TPU v7x, 32 devices: a whole 2x2x4 slice. The times are simulated.
32 devices in a mesh: dp: 4 (over y, core), wide: 4 (over z), narrow: 2 (over x).
Axes of the slice: x: 2, y: 2, z: 4, core: 2. Of those that a mesh axis runs over, the one named last changes fastest.
Arguments:
- patches: bfloat16 [2, 38535168], P('narrow', ('dp', 'wide')), may hold values from -6 to 6
- visible: int32 [512, 49], P(('dp', 'wide')), may hold values from 0 to 195, as said below
- w_qkv: bfloat16 [768, 3, 768], P('narrow', None, 'wide'), may hold values from -0.3125 to 0.3125
- b_qv: bfloat16 [2, 768], P(None, 'wide'), may hold values from -3 to 3
- w_out: bfloat16 [768, 768], P('wide', 'narrow'), may hold values from -0.875 to 0.875
- b_out: bfloat16 [768], P('narrow'), may hold values from -2 to 2
- w_up: bfloat16 [768, 3072], P('narrow', 'wide'), may hold values from -0.21875 to 0.21875
- b_up: bfloat16 [3072], P('wide'), may hold values from -3 to 3
- w_down: bfloat16 [768, 3072], P('narrow', 'wide'), may hold values from -0.15625 to 0.15625
- b_down: bfloat16 [768], P('narrow'), may hold values from -2 to 2
- gain_one: bfloat16 [768], P('narrow'), may hold values from 0.099609375 to 1.8984375
- shift_one: bfloat16 [768], P('narrow'), may hold values from -2 to 2
- gain_two: bfloat16 [768], P('narrow'), may hold values from 0.099609375 to 1.8984375
- shift_two: bfloat16 [768], P('narrow'), may hold values from -2 to 2
- cotangent: bfloat16 [2, 9633792], P('narrow', ('dp', 'wide')), may hold values from -6 to 6
Outputs:
- block_output: bfloat16 [2, 9633792], P('narrow', ('dp', 'wide'))
- grad_patches: float32 [2, 38535168], P('narrow', ('dp', 'wide'))
- grad_wqkv: float32 [768, 3, 768], P('narrow', None, 'wide')
- grad_bqv: float32 [2, 768], P(None, 'wide')
- grad_wout: float32 [768, 768], P('wide', 'narrow')
- grad_bout: float32 [768], P('narrow')
- grad_wup: float32 [768, 3072], P('narrow', 'wide')
- grad_bup: float32 [3072], P('wide')
- grad_wdown: float32 [768, 3072], P('narrow', 'wide')
- grad_bdown: float32 [768], P('narrow')
- grad_gain1: float32 [768], P('narrow')
- grad_shift1: float32 [768], P('narrow')
- grad_gain2: float32 [768], P('narrow')
- grad_shift2: float32 [768], P('narrow')
Inputs may be any that keep to these rules, and one draw needn't show every extreme that they name: `visible`: each image's 49 indices are distinct and increasing.
All inputs are finite; a program needn't handle non-finite values.
Results may differ from a plain program's by a relative error of at most 0.012.
The roundings to bfloat16 on the way count: a program that leaves them out, or rounds other values in their place, can miss the bound.
Values may be sent and summed in bfloat16 or wider, within the bound.
No kernel may reach another device: no remote copies, remote signals or barrier semaphores. Data moves between devices by JAX's collectives and lax.ppermute only.
A program may use at most 256 MiB of HBM per device.

v0:
```python
from functools import partial

import jax
import jax.numpy as jnp
from jax import lax
from jax.sharding import PartitionSpec as P

D = 768
HEAD_DIM = 64
PATCHES = 196
VISIBLE = 49


epsilon = 1e-06


def narrow_product(acts, weight):
    return lax.psum_scatter(
        jnp.dot(acts, weight, preferred_element_type=jnp.float32),
        "narrow",
        scatter_dimension=0,
        tiled=True,
    )


def normalize(values, gain, shift):
    totals = lax.psum((jnp.sum(values, 1), jnp.sum(values * values, 1)), "narrow")
    row_mean = totals[0] / D
    row_var = totals[1] / D - row_mean * row_mean
    inv_std = lax.rsqrt(row_var + epsilon)
    normed = (values - row_mean[:, None]) * inv_std[:, None]
    return (normed, inv_std, (normed * gain + shift).astype(jnp.bfloat16))


def norm_back(grad, normed, inv_std, gain):
    scaled = grad * gain
    totals = lax.psum((jnp.sum(scaled, 1), jnp.sum(scaled * normed, 1)), "narrow")
    back = inv_std[:, None] * (scaled - totals[0][:, None] / D - normed * (totals[1][:, None] / D))
    return (back, jnp.sum(grad * normed, 0), jnp.sum(grad, 0))


def wide_rows(acts):
    return lax.all_gather(acts, "wide", axis=0, tiled=True)


def narrow_rows(acts):
    return lax.all_gather(acts, "narrow", axis=0, tiled=True)


def wide_sum(partial_rows):
    return lax.psum_scatter(partial_rows, "wide", scatter_dimension=0, tiled=True)


def grad_wide_rows(acts):
    return lax.all_gather(acts, "wide", axis=0, tiled=True)


def grad_narrow_rows(acts):
    return lax.all_gather(acts, "narrow", axis=0, tiled=True)


def grad_wide_sum(partial_rows):
    return lax.psum_scatter(partial_rows, "wide", scatter_dimension=0, tiled=True)


def outer_sum(left, right):
    return lax.dot_general(
        left, right, (((0,), (0,)), ((), ())), preferred_element_type=jnp.float32
    )


def times_trans(left, weight):
    return lax.dot_general(
        left, weight, (((1,), (1,)), ((), ())), preferred_element_type=jnp.float32
    )


def attend(queries, keys_all, values_all, scale):
    scores = (
        jnp.einsum("nqhd,nkhd->nhqk", queries, keys_all, preferred_element_type=jnp.float32) * scale
    )
    top_score = jnp.max(scores, -1, keepdims=True)
    expo = jnp.exp(scores - top_score)
    total = jnp.sum(expo, -1, keepdims=True)
    prob_low = (expo / total).astype(jnp.bfloat16)
    mixed = jnp.einsum("nhqk,nkhd->nqhd", prob_low, values_all, preferred_element_type=jnp.float32)
    return (mixed, top_score + jnp.log(total))


def attend_back(queries, keys_all, values_all, log_total, grad_mixed, scale):
    scores = (
        jnp.einsum("nqhd,nkhd->nhqk", queries, keys_all, preferred_element_type=jnp.float32) * scale
    )
    attn_prob = jnp.exp(scores - log_total)
    grad_values = jnp.einsum(
        "nhqk,nqhd->nkhd",
        attn_prob.astype(jnp.bfloat16),
        grad_mixed,
        preferred_element_type=jnp.float32,
    )
    grad_prob = jnp.einsum(
        "nqhd,nkhd->nhqk", grad_mixed, values_all, preferred_element_type=jnp.float32
    )
    grad_scores = attn_prob * (grad_prob - jnp.sum(grad_prob * attn_prob, -1, keepdims=True))
    grad_scores = grad_scores.astype(jnp.bfloat16)
    grad_queries = (
        jnp.einsum("nhqk,nkhd->nqhd", grad_scores, keys_all, preferred_element_type=jnp.float32)
        * scale
    )
    grad_keys = (
        jnp.einsum("nhqk,nqhd->nkhd", grad_scores, queries, preferred_element_type=jnp.float32)
        * scale
    )
    return (grad_queries, grad_keys, grad_values)


def on_device(
    patches,
    visible,
    w_qkv,
    b_qv,
    w_out,
    b_out,
    w_up,
    b_up,
    w_down,
    b_down,
    gain_one,
    shift_one,
    gain_two,
    shift_two,
    cotangent,
):
    local_images = visible.shape[0]
    narrow_cols = w_qkv.shape[0]
    patch_rows = patches.reshape(local_images, PATCHES, narrow_cols)
    qkv_use, bqv_use, wout_use, wup_use, bup_use, wdown_use = (
        w_qkv,
        b_qv,
        w_out,
        w_up,
        b_up,
        w_down,
    )
    wide_cols = qkv_use.shape[2]
    head_count = wide_cols // HEAD_DIM
    scale = HEAD_DIM ** (-0.5)
    gain_a = gain_one.astype(jnp.float32)
    gain_b = gain_two.astype(jnp.float32)
    w_qkv_flat = qkv_use.reshape(narrow_cols, 3 * wide_cols)
    vis_rows = (
        jnp.take_along_axis(patch_rows, visible[:, :, None], axis=1)
        .reshape(-1, narrow_cols)
        .astype(jnp.float32)
    )
    normed_one, inv_one, hidden_one = normalize(vis_rows, gain_a, shift_one.astype(jnp.float32))
    hidden_one_all = wide_rows(hidden_one)
    bias_row = jnp.concatenate(
        [
            bqv_use[0].astype(jnp.float32),
            jnp.zeros((wide_cols,), jnp.float32),
            bqv_use[1].astype(jnp.float32),
        ]
    )
    triple = (narrow_product(hidden_one_all, w_qkv_flat) + bias_row).astype(jnp.bfloat16)
    image_count = triple.shape[0] // VISIBLE
    split = triple.reshape(image_count, VISIBLE, 3, head_count, HEAD_DIM)
    queries = split[:, :, 0]
    keys_all = split[:, :, 1]
    values_all = split[:, :, 2]
    mixed, log_total = attend(queries, keys_all, values_all, scale)
    mixed = mixed.reshape(-1, wide_cols).astype(jnp.bfloat16)
    mixed_all = narrow_rows(mixed)
    middle = vis_rows + (
        wide_sum(jnp.dot(mixed_all, wout_use, preferred_element_type=jnp.float32))
        + b_out.astype(jnp.float32)
    )
    normed_two, inv_two, hidden_two = normalize(middle, gain_b, shift_two.astype(jnp.float32))
    hidden_two_all = wide_rows(hidden_two)
    inner = narrow_product(hidden_two_all, wup_use) + bup_use.astype(jnp.float32)
    gelu_exact = partial(jax.nn.gelu, approximate=False)
    active = gelu_exact(inner).astype(jnp.bfloat16)
    active_all = narrow_rows(active)
    result = middle + (wide_sum(times_trans(active_all, wdown_use)) + b_down.astype(jnp.float32))
    block_output = result.astype(jnp.bfloat16).reshape(1, -1)
    cot_rows = cotangent.reshape(-1, narrow_cols)
    grad_out = cot_rows.astype(jnp.float32)
    grad_down_all = grad_wide_rows(cot_rows)
    gw_down = outer_sum(grad_down_all, active_all)
    gb_down = jnp.sum(grad_down_all, 0, dtype=jnp.float32)
    grad_active = narrow_product(grad_down_all, wdown_use)
    gelu_pull = jax.vjp(gelu_exact, inner)[1]
    grad_inner = gelu_pull(grad_active)[0].astype(jnp.bfloat16)
    grad_inner_all = grad_narrow_rows(grad_inner)
    gw_up = outer_sum(hidden_two_all, grad_inner_all)
    gb_up = jnp.sum(grad_inner_all, 0, dtype=jnp.float32)
    grad_hidden_two = grad_wide_sum(times_trans(grad_inner_all, wup_use))
    back_two, gg_two, gs_two = norm_back(grad_hidden_two, normed_two, inv_two, gain_b)
    grad_middle = grad_out + back_two
    grad_branch_all = grad_wide_rows(grad_middle.astype(jnp.bfloat16))
    gw_out = outer_sum(mixed_all, grad_branch_all)
    gb_out = jnp.sum(grad_branch_all, 0, dtype=jnp.float32)
    grad_mixed = narrow_product(grad_branch_all, wout_use.T).astype(jnp.bfloat16)
    grad_mixed = grad_mixed.reshape(image_count, VISIBLE, head_count, HEAD_DIM)
    grad_queries, grad_keys, grad_values = attend_back(
        queries, keys_all, values_all, log_total, grad_mixed, scale
    )
    grad_triple = (
        jnp.stack([grad_queries, grad_keys, grad_values], 2)
        .reshape(-1, 3 * wide_cols)
        .astype(jnp.bfloat16)
    )
    grad_triple_all = grad_narrow_rows(grad_triple)
    gw_qkv = outer_sum(hidden_one_all, grad_triple_all).reshape(narrow_cols, 3, wide_cols)
    bias_sums = jnp.sum(grad_triple_all, 0, dtype=jnp.float32).reshape(3, wide_cols)
    gb_qv = jnp.stack([bias_sums[0], bias_sums[2]])
    grad_hidden_one = grad_wide_sum(times_trans(grad_triple_all, w_qkv_flat))
    back_one, gg_one, gs_one = norm_back(grad_hidden_one, normed_one, inv_one, gain_a)
    grad_rows = grad_middle + back_one
    image_index = jnp.arange(local_images)[:, None]
    grad_patches = (
        jnp.zeros((local_images, PATCHES, narrow_cols), jnp.float32)
        .at[image_index, visible]
        .set(grad_rows.reshape(local_images, VISIBLE, narrow_cols))
    )
    grad_patches = grad_patches.reshape(1, -1)
    summed = lax.psum((gw_qkv, gb_qv, gw_out, gb_out, gw_up, gb_up, gw_down, gb_down), "dp")
    vectors = lax.psum((gg_one, gs_one, gg_two, gs_two), ("dp", "wide"))
    return (
        block_output,
        grad_patches,
        summed[0],
        summed[1],
        summed[2],
        summed[3],
        summed[4],
        summed[5],
        summed[6],
        summed[7],
        vectors[0],
        vectors[1],
        vectors[2],
        vectors[3],
    )


def solution(mesh):
    in_specs = (
        P("narrow", ("dp", "wide")),
        P(("dp", "wide"), None),
        P("narrow", None, "wide"),
        P(None, "wide"),
        P("wide", "narrow"),
        P("narrow"),
        P("narrow", "wide"),
        P("wide"),
        P("narrow", "wide"),
        P("narrow"),
        P("narrow"),
        P("narrow"),
        P("narrow"),
        P("narrow"),
        P("narrow", ("dp", "wide")),
    )
    out_specs = (
        P("narrow", ("dp", "wide")),
        P("narrow", ("dp", "wide")),
        P("narrow", None, "wide"),
        P(None, "wide"),
        P("wide", "narrow"),
        P("narrow"),
        P("narrow", "wide"),
        P("wide"),
        P("narrow", "wide"),
        P("narrow"),
        P("narrow"),
        P("narrow"),
        P("narrow"),
        P("narrow"),
    )
    return jax.shard_map(
        on_device, mesh=mesh, in_specs=in_specs, out_specs=out_specs, check_vma=False
    )
```

profile of v0, /device:TPU:0, one launch (start us, length us, event | category | flops | bytes accessed | tf_op | source)
XLA Modules:
  0.0 2732.8 jit_solution(15280021996956817729)
XLA Ops:
  10.3 103.4 %reduce.4 = bf16[2408448]{0:T(1024)(128)(2,1)} reduce(bf16[1,2408448]{1,0:T(2,128)(2,1)} %param.15, bf16[]{:T(256)} %constant.125), dimensions={0}, to_apply=%param.15.reduce_sub_computation | reduce | bytes 9633794 | tf_op args[0]
  126.9 22.4 gather_fusion
  163.7 91.1 %all-gather.11.cloned.1.call-done = bf16[6272,384]{1,0:T(8,128)(2,1)} async-done(((bf16[1568,384]{1,0:T(8,128)(2,1)}), bf16[6272,384]{1,0:T(8,128)(2,1)}) %all-gather.11.cloned.1.call-update) | async-done | bytes 4816912 | tf_op jit(solution)/shard_map/all_gather | solution.py:43
  265.4 179.2 %reduce-scatter.25.cloned.1.call-done = f32[3136,576]{1,0:T(8,128)} async-done(((f32[6272,576]{1,0:T(8,128)}), f32[3136,576]{1,0:T(8,128)}) %reduce-scatter.25.cloned.1.call-update) | async-done | bytes 7225360
  459.2 29.2 %reshape.125 = bf16[64,49,3,3,64]{1,0,4,3,2:T(8,128)(2,1)} reshape(bf16[3136,576]{0,1:T(8,128)(2,1)} %add_convert_fusion.1) | data formatting | bytes 7225344 | tf_op jit(solution)/shard_map/reshape | solution.py:167
  530.0 14.5 reshape.152
  544.6 37.3 %all-gather.23.cloned.1.call-done = bf16[2,3136,192]{1,2,0:T(8,128)(2,1)} async-done(((bf16[1,3136,192]{1,2,0:T(8,128)(2,1)}), bf16[2,3136,192]{1,2,0:T(8,128)(2,1)}) %all-gather.23.cloned.1.call-update) | async-done | bytes 2408464 | tf_op jit(solution)/shard_map/all_gather | solution.py:47
  599.7 26.0 reduce.5
  627.3 136.9 %reduce-scatter.13.cloned.1.call-done = f32[1568,384]{1,0:T(8,128)} async-done(((f32[6272,384]{1,0:T(8,128)}), f32[1568,384]{1,0:T(8,128)}) %reduce-scatter.13.cloned.1.call-update) | async-done | bytes 2408464 | tf_op jit(solution)/shard_map/reduce_scatter | solution.py:51
  779.7 77.9 %all-gather.17.cloned.1.call-done = bf16[6272,384]{1,0:T(8,128)(2,1)} async-done(((bf16[1568,384]{1,0:T(8,128)(2,1)}), bf16[6272,384]{1,0:T(8,128)(2,1)}) %all-gather.17.cloned.1.call-update) | async-done | bytes 4816912 | tf_op jit(solution)/shard_map/all_gather | solution.py:55
  869.2 79.9 %all-gather.13.cloned.1.call-done = bf16[6272,384]{1,0:T(8,128)(2,1)} async-done(((bf16[1568,384]{1,0:T(8,128)(2,1)}), bf16[6272,384]{1,0:T(8,128)(2,1)}) %all-gather.13.cloned.1.call-update) | async-done | bytes 4816912 | tf_op jit(solution)/shard_map/all_gather | solution.py:43
  961.3 204.5 %reduce-scatter.19.cloned.1.call-done = f32[3136,768]{1,0:T(8,128)} async-done(((f32[6272,768]{1,0:T(8,128)}), f32[3136,768]{1,0:T(8,128)}) %reduce-scatter.19.cloned.1.call-update) | async-done | bytes 9633808 | tf_op jit(solution)/shard_map/reduce_scatter | solution.py:18
  1165.7 218.2 %reduce-scatter.15.cloned.1.call-done = f32[3136,768]{1,0:T(8,128)} async-done(((f32[6272,768]{1,0:T(8,128)}), f32[3136,768]{1,0:T(8,128)}) %reduce-scatter.15.cloned.1.call-update) | async-done | bytes 9633808 | tf_op jit(solution)/shard_map/reduce_scatter | solution.py:18
  1384.0 25.5 add_convert_fusion
  1420.7 109.2 %all-gather.19.cloned.1.call-done = bf16[6272,768]{1,0:T(8,128)(2,1)} async-done(((bf16[3136,768]{1,0:T(8,128)(2,1)}), bf16[6272,768]{1,0:T(8,128)(2,1)}) %all-gather.19.cloned.1.call-update) | async-done | bytes 9633808 | tf_op jit(solution)/shard_map/all_gather | solution.py:59
  1541.4 110.0 %all-gather.15.cloned.1.call-done = bf16[6272,768]{1,0:T(8,128)(2,1)} async-done(((bf16[3136,768]{1,0:T(8,128)(2,1)}), bf16[6272,768]{1,0:T(8,128)(2,1)}) %all-gather.15.cloned.1.call-update) | async-done | bytes 9633808 | tf_op jit(solution)/shard_map/all_gather | solution.py:47
  1663.1 155.7 %reduce-scatter.21.cloned.1.call-done = f32[1568,384]{1,0:T(8,128)} async-done(((f32[6272,384]{1,0:T(8,128)}), f32[1568,384]{1,0:T(8,128)}) %reduce-scatter.21.cloned.1.call-update) | async-done | bytes 2408464 | tf_op jit(solution)/shard_map/reduce_scatter | solution.py:63
  1829.7 156.6 %reduce-scatter.17.cloned.1.call-done = f32[1568,384]{1,0:T(8,128)} async-done(((f32[6272,384]{1,0:T(8,128)}), f32[1568,384]{1,0:T(8,128)}) %reduce-scatter.17.cloned.1.call-update) | async-done | bytes 2408464 | tf_op jit(solution)/shard_map/reduce_scatter | solution.py:51
  1991.3 92.0 %all-gather.21.cloned.1.call-done = bf16[6272,384]{1,0:T(8,128)(2,1)} async-done(((bf16[1568,384]{1,0:T(8,128)(2,1)}), bf16[6272,384]{1,0:T(8,128)(2,1)}) %all-gather.21.cloned.1.call-update) | async-done | bytes 4816912 | tf_op jit(solution)/shard_map/all_gather | solution.py:55
  2090.6 76.8 %reduce-scatter.27.cloned.1.call-done = f32[3136,192]{1,0:T(8,128)} async-done(((f32[6272,192]{1,0:T(8,128)}), f32[3136,192]{1,0:T(8,128)}) %reduce-scatter.27.cloned.1.call-update) | async-done | bytes 2408464
  2204.5 13.5 copy.73
  2217.9 15.0 reshape.154
  2257.6 68.1 %all-gather.25.cloned.1.call-done = bf16[2,3136,576]{1,2,0:T(8,128)(2,1)} async-done(((bf16[1,3136,576]{1,2,0:T(8,128)(2,1)}), bf16[2,3136,576]{1,2,0:T(8,128)(2,1)}) %all-gather.25.cloned.1.call-update) | async-done | bytes 7225360 | tf_op jit(solution)/shard_map/all_gather | solution.py:59
  2325.7 39.5 %copy.74 = bf16[2,3136,576]{1,0,2:T(2,128)(2,1)} copy(bf16[2,3136,576]{1,2,0:T(8,128)(2,1)} %all-gather.25.cloned.1.call-done) | data formatting | bytes 14450688 | tf_op jit(solution)/shard_map/all_gather | solution.py:59
  2365.2 11.8 reshape.155
  2420.4 11.7 all-reduce.1
  2432.1 29.8 %all-reduce.9.cloned.1.call-done = (f32[384,3,192]{0,2,1:T(8,128)}, f32[192,384]{1,0:T(8,128)}, f32[384,768]{1,0:T(8,128)}, f32[384,768]{0,1:T(8,128)}) async-done(((f32[384,3,192]{0,2,1:T(8,128)}, f32[192,384]{1,0:T(8,128)}, f32[384,768]{1,0:T(8,128)}, f32[384,768]{0,1:T(8,128)}), (f32[384,3,192]{0,2,1:T(8,128)}, f32[192,384]{1,0:T(8,128)}, f32[384,768]{1,0:T(8,128)}, ...) | async-done | bytes 3538960 | tf_op jit(solution)/shard_map/psum | solution.py:227
  2464.6 164.8 %reduce-scatter.23.cloned.1.call-done = f32[1568,384]{1,0:T(8,128)} async-done(((f32[6272,384]{1,0:T(8,128)}), f32[1568,384]{1,0:T(8,128)}) %reduce-scatter.23.cloned.1.call-update) | async-done | bytes 2408464 | tf_op jit(solution)/shard_map/reduce_scatter | solution.py:63
  2640.5 18.2 scatter_custom_fusion
  2658.7 13.1 copy.75
  2671.8 18.9 reshape.130
  2690.7 32.5 %all-reduce = (f32[384]{0:T(512)}, f32[384]{0:T(512)}, f32[384]{0:T(512)}, f32[384]{0:T(512)}) all-reduce(f32[384]{0:T(512)S(1)} %get-tuple-element.72, f32[384]{0:T(512)S(1)} %get-tuple-element.77, f32[384]{0:T(512)S(1)} %get-tuple-element.70, f32[384]{0:T(512)S(1)} %get-tuple-element.76), channel_id=1, replica_groups=mesh['dp'=4,'wide'=4,'narrow'=2] {'dp','wide'}, use_global_device_ids=true, to_apply=%region_41.42 | all-reduce | flops 1536 | bytes 12288 | tf_op jit(solution)/shard_map/psum | solution.py:228
  (216 shorter events, 334.5 us)
Async XLA Ops:
  7.2 941.9 %copy-start = (bf16[384,768]{1,0:T(8,128)(2,1)S(1)}, bf16[384,768]{1,0:T(8,128)(2,1)}, u32[]{:S(2)}) copy-start(bf16[384,768]{1,0:T(8,128)(2,1)} %param.21) | copy-start | bytes 1769476
  7.2 247.6 %all-gather.11.cloned.1.call-start = ((), (), s32[]{:S(2)}) async-start(), calls=%async_computation.8 | async-start | bytes 6021120 | tf_op jit(solution)/shard_map/all_gather | solution.py:43
  9.4 151.4 %copy-start.27 = (f32[384]{0:T(512)}, f32[384]{0:T(512)S(1)}, u32[]{:S(2)}) copy-start(f32[384]{0:T(512)S(1)} %convert_element_type.103) | copy-start | bytes 4612
  10.2 754.0 %copy-start.25 = (pred[1568]{0:T(1024)(128)(4,1)}, pred[1568]{0:T(1024)(128)(4,1)S(1)}, u32[]{:S(2)}) copy-start(pred[1568]{0:T(1024)(128)(4,1)S(1)} %broadcast_in_dim.20) | copy-start | bytes 4708
  149.3 614.9 %copy-start.3 = (bf16[1568,384]{1,0:T(8,128)(2,1)}, bf16[1568,384]{1,0:T(8,128)(2,1)S(1)}, u32[]{:S(2)}) copy-start(bf16[1568,384]{1,0:T(8,128)(2,1)S(1)} %gather_fusion) | copy-start | bytes 3612676
  163.4 281.2 %reduce-scatter.25.cloned.1.call-start = ((), (), s32[]{:S(2)}) async-start(), calls=%async_computation.22 | async-start | bytes 24084480
  264.7 317.2 %all-gather.23.cloned.1.call-start = ((), (), s32[]{:S(2)}) async-start(), calls=%async_computation.20 | async-start | bytes 3686400 | tf_op jit(solution)/shard_map/all_gather | solution.py:47
  544.6 219.6 %reduce-scatter.13.cloned.1.call-start = ((), (), s32[]{:S(2)}) async-start(), calls=%async_computation.9 | async-start | bytes 12042240 | tf_op jit(solution)/shard_map/reduce_scatter | solution.py:51
  599.7 257.9 %all-gather.17.cloned.1.call-start = ((), (), s32[]{:S(2)}) async-start(), calls=%async_computation.14 | async-start | bytes 6021120 | tf_op jit(solution)/shard_map/all_gather | solution.py:55
  627.2 321.9 %all-gather.13.cloned.1.call-start = ((), (), s32[]{:S(2)}) async-start(), calls=%async_computation.10 | async-start | bytes 6021120 | tf_op jit(solution)/shard_map/all_gather | solution.py:43
  627.3 230.2 %copy-start.16 = (bf16[384,768]{1,0:T(8,128)(2,1)S(1)}, bf16[384,768]{1,0:T(8,128)(2,1)}, u32[]{:S(2)}) copy-start(bf16[384,768]{1,0:T(8,128)(2,1)} %param.23) | copy-start | bytes 1769476
  779.6 386.1 %reduce-scatter.19.cloned.1.call-start = ((), (), s32[]{:S(2)}) async-start(), calls=%async_computation.15 | async-start | bytes 28901376 | tf_op jit(solution)/shard_map/reduce_scatter | solution.py:18
  869.1 514.9 %reduce-scatter.15.cloned.1.call-start = ((), (), s32[]{:S(2)}) async-start(), calls=%async_computation.11 | async-start | bytes 28901376 | tf_op jit(solution)/shard_map/reduce_scatter | solution.py:18
  960.6 569.2 %all-gather.19.cloned.1.call-start = ((), (), s32[]{:S(2)}) async-start(), calls=%async_computation.16 | async-start | bytes 14450688 | tf_op jit(solution)/shard_map/all_gather | solution.py:59
  1409.5 241.9 %all-gather.15.cloned.1.call-start = ((), (), s32[]{:S(2)}) async-start(), calls=%async_computation.12 | async-start | bytes 14450688 | tf_op jit(solution)/shard_map/all_gather | solution.py:47
  1420.6 398.2 %reduce-scatter.21.cloned.1.call-start = ((), (), s32[]{:S(2)}) async-start(), calls=%async_computation.17 | async-start | bytes 12042240 | tf_op jit(solution)/shard_map/reduce_scatter | solution.py:63
  1541.4 445.0 %reduce-scatter.17.cloned.1.call-start = ((), (), s32[]{:S(2)}) async-start(), calls=%async_computation.13 | async-start | bytes 12042240 | tf_op jit(solution)/shard_map/reduce_scatter | solution.py:51
  1662.4 156.4 %copy-start.5 = (f32[1568,384]{1,0:T(8,128)S(1)}, f32[1568,384]{1,0:T(8,128)}, u32[]{:S(2)}) copy-start(f32[1568,384]{1,0:T(8,128)} %get-tuple-element.106) | copy-start | bytes 7225348
  1662.4 420.9 %all-gather.21.cloned.1.call-start = ((), (), s32[]{:S(2)}) async-start(), calls=%async_computation.18 | async-start | bytes 6021120 | tf_op jit(solution)/shard_map/all_gather | solution.py:55
  1991.3 176.1 %reduce-scatter.27.cloned.1.call-start = ((), (), s32[]{:S(2)}) async-start(), calls=%async_computation.23 | async-start | bytes 9633792
  2090.3 235.4 %all-gather.25.cloned.1.call-start = ((), (), s32[]{:S(2)}) async-start(), calls=%async_computation.21 | async-start | bytes 11059200 | tf_op jit(solution)/shard_map/all_gather | solution.py:59
  2233.0 228.9 %all-reduce.9.cloned.1.call-start = ((), (), s32[]{:S(2)}) async-start(), calls=%async_computation.24 | async-start | bytes 7077888 | tf_op jit(solution)/shard_map/psum | solution.py:227
  2386.4 243.0 %reduce-scatter.23.cloned.1.call-start = ((), (), s32[]{:S(2)}) async-start(), calls=%async_computation.19 | async-start | bytes 12042240 | tf_op jit(solution)/shard_map/reduce_scatter | solution.py:63
  2419.3 210.1 %copy-start.4 = (bf16[1568,384]{1,0:T(8,128)(2,1)S(1)}, bf16[1568,384]{1,0:T(8,128)(2,1)}, u32[]{:S(2)}) copy-start(bf16[1568,384]{1,0:T(8,128)(2,1)} %copy-done.3) | copy-start | bytes 3612676
  2419.3 210.1 %copy-start.22 = (f32[1568]{0:T(1024)S(1)}, f32[1568]{0:T(1024)}, u32[]{:S(2)}) copy-start(f32[1568]{0:T(1024)} %copy-done.21) | copy-start | bytes 18820
  2419.3 210.1 %copy-start.24 = (f32[1568]{0:T(1024)S(1)}, f32[1568]{0:T(1024)}, u32[]{:S(2)}) copy-start(f32[1568]{0:T(1024)} %copy-done.23) | copy-start | bytes 18820
  2419.3 210.1 %copy-start.26 = (pred[1568]{0:T(1024)(128)(4,1)S(1)}, pred[1568]{0:T(1024)(128)(4,1)}, u32[]{:S(2)}) copy-start(pred[1568]{0:T(1024)(128)(4,1)} %copy-done.25) | copy-start | bytes 4708
  2419.3 210.1 %copy-start.28 = (f32[384]{0:T(512)S(1)}, f32[384]{0:T(512)}, u32[]{:S(2)}) copy-start(f32[384]{0:T(512)} %copy-done.27) | copy-start | bytes 4612
  2671.8 51.4 %copy-start.15 = (f32[384,3,192]{0,2,1:T(8,128)S(1)}, f32[384,3,192]{0,2,1:T(8,128)}, u32[]{:S(2)}) copy-start(f32[384,3,192]{0,2,1:T(8,128)} %get-tuple-element.127) | copy-start | bytes 2654212
  2671.8 52.3 %copy-start.19 = (f32[192,384]{1,0:T(8,128)S(1)}, f32[192,384]{1,0:T(8,128)}, u32[]{:S(2)}) copy-start(f32[192,384]{1,0:T(8,128)} %get-tuple-element.129) | copy-start | bytes 884740
  2671.8 53.0 %copy-start.14 = (f32[384,768]{1,0:T(8,128)S(1)}, f32[384,768]{1,0:T(8,128)}, u32[]{:S(2)}) copy-start(f32[384,768]{1,0:T(8,128)} %get-tuple-element.131) | copy-start | bytes 3538948
  2671.8 54.0 %copy-start.1 = (bf16[384,768]{1,0:T(8,128)(2,1)S(1)}, bf16[384,768]{1,0:T(8,128)(2,1)}, u32[]{:S(2)}) copy-start(bf16[384,768]{1,0:T(8,128)(2,1)} %param.21) | copy-start | bytes 1769476
  (30 other events, 319.0 us)
Sparse Core Ops, SparseCore 0:
  163.6 91.2 all-gather.10
  264.8 179.8 reduce-scatter.24
  544.7 37.1 all-gather.22
  599.8 164.3 reduce-scatter.12
  765.6 91.9 all-gather.16
  859.6 89.4 all-gather.12
  951.4 214.3 reduce-scatter.18
  1168.0 215.8 reduce-scatter.14
  1409.6 120.1 all-gather.18
  1531.2 120.1 all-gather.14
  1654.4 164.3 reduce-scatter.20
  1821.0 165.2 reduce-scatter.16
  1991.4 91.9 all-gather.20
  2090.5 76.8 reduce-scatter.26
  2233.1 92.5 all-gather.24
  2386.5 75.3 all-reduce.8
  2464.9 164.4 reduce-scatter.22
where the time goes:
time: 2740 us; the launch traced here: 2730 us
  waiting for transfers between devices  1990 us (73%)
  local copies, waits for them, and re-layouts  283 us (10%)
  other arithmetic  233 us (9%)
  matrix products  134 us (5%)
  blocking collectives  78.4 us (3%)
    reduce_scatter x2, waiting for transfers between devices, narrow_product(): lax.psum_scatter(jnp.dot(acts, weight, preferred_element_type=jnp.float32...  423 us
    reduce_scatter x2, waiting for transfers between devices, grad_wide_sum(): lax.psum_scatter(partial_rows, 'wide', scatter_dimension=0, tiled=True)  320 us
    reduce_scatter x2, waiting for transfers between devices, wide_sum(): lax.psum_scatter(partial_rows, 'wide', scatter_dimension=0, tiled=True)  294 us
    unnamed x19, waiting for transfers between devices  256 us
    all_gather x2, waiting for transfers between devices, grad_narrow_rows(): return lax.all_gather(acts, 'narrow', axis=0, tiled=True)  177 us
    all_gather x2, waiting for transfers between devices, wide_rows(): return lax.all_gather(acts, 'wide', axis=0, tiled=True)  171 us
    all_gather x2, waiting for transfers between devices, grad_wide_rows(): return lax.all_gather(acts, 'wide', axis=0, tiled=True)  170 us
    unnamed x10, other arithmetic  148 us
  transfers between devices with their start and end apart: 17, of which 17 were waited for; matrix products, arithmetic and copies ran while one was open for 6% of the time, Pallas kernels for 0%

commit v1 on v0

v1 whole, which is shorter than its diff:
```python
from functools import partial

import jax
import jax.numpy as jnp
from jax import lax
from jax.experimental import pallas as pl
from jax.experimental.pallas import tpu as pltpu
from jax.sharding import PartitionSpec as P

D = 768
HEAD_DIM = 64
HEADS = 12
PATCHES = 196
VISIBLE = 49
PAIR = 2 * VISIBLE
ROWS = 112
TILE = 256
EPS = 1e-06
BF = jnp.bfloat16
F32 = jnp.float32
MB = 1024 * 1024


def dot(a, b, ca, cb):
    return lax.dot_general(a, b, (((ca,), (cb,)), ((), ())), preferred_element_type=F32)


def call(body, grid, ins, outs, shapes, scratch=(), prefetch=0, flops=0, nbytes=0, vmem=48):
    return pl.pallas_call(
        body,
        out_shape=shapes,
        grid_spec=pltpu.PrefetchScalarGridSpec(
            num_scalar_prefetch=prefetch,
            grid=grid,
            in_specs=ins,
            out_specs=outs,
            scratch_shapes=scratch,
        ),
        compiler_params=pltpu.CompilerParams(
            dimension_semantics=("arbitrary",) * len(grid), vmem_limit_bytes=vmem * MB
        ),
        cost_estimate=pl.CostEstimate(flops=flops, bytes_accessed=nbytes, transcendentals=0),
    )


def spec(shape, index):
    return pl.BlockSpec(shape, index)


def struct(shape, dtype):
    return jax.ShapeDtypeStruct(shape, dtype)


def pick_body(cols, patch_ref, cot_ref, index_ref, rows_ref, cot_rows_ref, wide_ref, cot_scr):
    lanes = cols // 128
    wide_ref[...] = patch_ref[...].astype(F32).reshape(wide_ref.shape)
    parts = [wide_ref[pl.ds(k, 2 * PATCHES, stride=lanes), :] for k in range(lanes)]
    both = jnp.concatenate(parts, axis=1).astype(BF)
    hit = index_ref[0] == lax.broadcasted_iota(jnp.int32, (ROWS, 2 * PATCHES), 1)
    rows_ref[...] = dot(hit.astype(BF), both, 1, 0).astype(BF)
    cot_scr[...] = cot_ref[...].astype(F32).reshape(cot_scr.shape)
    parts = [cot_scr[pl.ds(k, PAIR, stride=lanes), :] for k in range(lanes)]
    cot = jnp.concatenate(parts, axis=1)
    cot_rows_ref[...] = jnp.concatenate(
        [cot, jnp.zeros((ROWS - PAIR, cols), F32)], axis=0
    ).astype(BF)


def pick_rows(patches, cotangent, index, cols):
    pairs = index.shape[0]
    width = 2 * PATCHES * cols
    cot_width = PAIR * cols
    return call(
        partial(pick_body, cols),
        (pairs,),
        [
            spec((1, width), lambda i: (0, i)),
            spec((1, cot_width), lambda i: (0, i)),
            spec((1, ROWS, 1), lambda i: (i, 0, 0)),
        ],
        [spec((ROWS, cols), lambda i: (i, 0)), spec((ROWS, cols), lambda i: (i, 0))],
        [struct((pairs * ROWS, cols), BF), struct((pairs * ROWS, cols), BF)],
        [pltpu.VMEM((width // 128, 128), F32), pltpu.VMEM((cot_width // 128, 128), F32)],
        flops=2 * pairs * ROWS * 2 * PATCHES * cols,
        nbytes=pairs * (width + cot_width) * 4,
    )(patches, cotangent, index)


def put_body(cols, rows_ref, index_ref, out_ref):
    lanes = cols // 128
    hit = index_ref[0] == lax.broadcasted_iota(jnp.int32, (ROWS, 2 * PATCHES), 1)
    hit = hit.astype(BF)
    rest = rows_ref[...]
    total = None
    for _ in range(3):
        part = rest.astype(BF)
        rest = rest - part.astype(F32)
        term = dot(hit, part, 0, 0)
        total = term if total is None else total + term
    for k in range(lanes):
        out_ref[pl.ds(k, 2 * PATCHES, stride=lanes), :] = total[:, k * 128 : (k + 1) * 128]


def put_rows(rows, index, cols):
    pairs = index.shape[0]
    tall = 2 * PATCHES * cols // 128
    return call(
        partial(put_body, cols),
        (pairs,),
        [spec((ROWS, cols), lambda i: (i, 0)), spec((1, ROWS, 1), lambda i: (i, 0, 0))],
        spec((tall, 128), lambda i: (i, 0)),
        struct((pairs * tall, 128), F32),
        flops=6 * pairs * ROWS * 2 * PATCHES * cols,
        nbytes=pairs * (tall * 512 + ROWS * cols * 4),
    )(rows, index)


def flat_body(cols, rows_ref, out_ref, scr):
    lanes = cols // 128
    rows = rows_ref[...].astype(F32)
    for k in range(lanes):
        scr[pl.ds(k, PAIR, stride=lanes), :] = rows[:PAIR, k * 128 : (k + 1) * 128]
    out_ref[...] = scr[...].reshape(out_ref.shape).astype(BF)


def flat_rows(rows, cols):
    pairs = rows.shape[0] // ROWS
    width = PAIR * cols
    return call(
        partial(flat_body, cols),
        (pairs,),
        [spec((ROWS, cols), lambda i: (i, 0))],
        spec((1, width), lambda i: (0, i)),
        struct((1, pairs * width), BF),
        [pltpu.VMEM((width // 128, 128), F32)],
        nbytes=pairs * width * 6,
    )(rows)


def stats(rows):
    mean = jnp.mean(rows, 1, keepdims=True)
    off = rows - mean
    inv = lax.rsqrt(jnp.mean(off * off, 1, keepdims=True) + EPS)
    return off * inv, inv


def norm_body(rows_ref, gain_ref, shift_ref, out_ref):
    normed, _ = stats(rows_ref[...].astype(F32))
    out_ref[...] = (normed * gain_ref[...] + shift_ref[...]).astype(BF)


def norm(rows, gain, shift):
    r = rows.shape[0]
    return call(
        norm_body,
        (r // ROWS,),
        [
            spec((ROWS, D), lambda i: (i, 0)),
            spec((1, D), lambda i: (0, 0)),
            spec((1, D), lambda i: (0, 0)),
        ],
        spec((ROWS, D), lambda i: (i, 0)),
        struct((r, D), BF),
        nbytes=r * D * 4,
    )(rows, gain, shift)


def qkv_body(hidden_ref, w_ref, bias_ref, out_ref):
    out_ref[...] = (dot(hidden_ref[...], w_ref[...], 1, 1) + bias_ref[...]).astype(BF)


def qkv(hidden, w, bias):
    r = hidden.shape[0]
    return call(
        qkv_body,
        (3 * D // TILE,),
        [
            spec((r, D), lambda j: (0, 0)),
            spec((TILE, D), lambda j: (j, 0)),
            spec((1, TILE), lambda j: (0, j)),
        ],
        spec((r, TILE), lambda j: (0, j)),
        struct((r, 3 * D), BF),
        flops=2 * r * D * 3 * D,
        nbytes=r * D * 8 + 3 * D * D * 2,
    )(hidden, w, bias)


def same_image():
    at_row = lax.broadcasted_iota(jnp.int32, (ROWS, ROWS), 0)
    at_col = lax.broadcasted_iota(jnp.int32, (ROWS, ROWS), 1)

    def image(at):
        return (at >= VISIBLE).astype(jnp.int32) + (at >= PAIR).astype(jnp.int32)

    return image(at_row) == image(at_col)


def attend_body(triple_ref, mixed_ref, prob_ref):
    keep = same_image()
    left = lax.broadcasted_iota(jnp.int32, (ROWS, 128), 1) < HEAD_DIM
    for pair in range(HEADS // 2):
        q = triple_ref[:, pair * 128 : (pair + 1) * 128]
        k = triple_ref[:, D + pair * 128 : D + (pair + 1) * 128]
        v = triple_ref[:, 2 * D + pair * 128 : 2 * D + (pair + 1) * 128]
        halves = []
        for side in range(2):
            mine = left if side == 0 else jnp.logical_not(left)
            scores = dot(jnp.where(mine, q, jnp.zeros_like(q)), k, 1, 1) * HEAD_DIM**-0.5
            scores = jnp.where(keep, scores, -1e30)
            expo = jnp.exp(scores - jnp.max(scores, 1, keepdims=True))
            prob = expo / jnp.sum(expo, 1, keepdims=True)
            prob_ref[0, 2 * pair + side] = prob
            halves.append(dot(prob.astype(BF), v, 1, 0))
        mixed_ref[:, pair * 128 : (pair + 1) * 128] = jnp.where(left, halves[0], halves[1]).astype(
            BF
        )


def attend(triple):
    groups = triple.shape[0] // ROWS
    return call(
        attend_body,
        (groups,),
        [spec((ROWS, 3 * D), lambda g: (g, 0))],
        [spec((ROWS, D), lambda g: (g, 0)), spec((1, HEADS, ROWS, ROWS), lambda g: (g, 0, 0, 0))],
        [struct((groups * ROWS, D), BF), struct((groups, HEADS, ROWS, ROWS), F32)],
        flops=groups * HEADS * 4 * ROWS * ROWS * 128,
        nbytes=groups * ROWS * (8 * D + HEADS * 512),
    )(triple)


def mix_body(mixed_ref, w_ref, bias_ref, rows_ref, gain_ref, shift_ref, middle_ref, hidden_ref):
    middle = rows_ref[...].astype(F32) + (dot(mixed_ref[...], w_ref[...], 1, 0) + bias_ref[...])
    middle_ref[...] = middle
    normed, _ = stats(middle)
    hidden_ref[...] = (normed * gain_ref[...] + shift_ref[...]).astype(BF)


def row_tile(r):
    return r // 2


def mix(mixed, w, bias, rows, gain, shift):
    r = rows.shape[0]
    m = row_tile(r)
    vec = spec((1, D), lambda i: (0, 0))
    row = spec((m, D), lambda i: (i, 0))
    return call(
        mix_body,
        (r // m,),
        [row, spec((D, D), lambda i: (0, 0)), vec, row, vec, vec],
        [row, row],
        [struct((r, D), F32), struct((r, D), BF)],
        flops=2 * r * D * D,
        nbytes=r * D * 10 + D * D * 2,
    )(mixed, w, bias, rows, gain, shift)


def up_body(hidden_ref, w_ref, bias_ref, active_ref, slope_ref):
    inner = dot(hidden_ref[...], w_ref[...], 1, 0) + bias_ref[...]
    phi = 0.5 * (1.0 + lax.erf(inner * (0.5**0.5)))
    active_ref[...] = (inner * phi).astype(BF)
    slope_ref[...] = phi + inner * (jnp.exp(-0.5 * inner * inner) * 0.3989422804014327)


def up(hidden, w, bias):
    r = hidden.shape[0]
    units = w.shape[1]
    tile = spec((r, TILE), lambda j: (0, j))
    return call(
        up_body,
        (units // TILE,),
        [
            spec((r, D), lambda j: (0, 0)),
            spec((D, TILE), lambda j: (0, j)),
            spec((1, TILE), lambda j: (0, j)),
        ],
        [tile, tile],
        [struct((r, units), BF), struct((r, units), F32)],
        flops=2 * r * D * units,
        nbytes=r * D * 2 + D * units * 2 + r * units * 6,
    )(hidden, w, bias)


def down_body(active_ref, w_ref, bias_ref, middle_ref, out_ref):
    out = middle_ref[...] + (dot(active_ref[...], w_ref[...], 1, 1) + bias_ref[...])
    out_ref[...] = out.astype(BF)


def down(active, w, bias, middle):
    r, units = active.shape
    m = row_tile(r)
    return call(
        down_body,
        (r // m,),
        [
            spec((m, units), lambda i: (i, 0)),
            spec((D, units), lambda i: (0, 0)),
            spec((1, D), lambda i: (0, 0)),
            spec((m, D), lambda i: (i, 0)),
        ],
        spec((m, D), lambda i: (i, 0)),
        struct((r, D), BF),
        flops=2 * r * D * units,
        nbytes=r * units * 2 + D * units * 2 + r * D * 6,
    )(active, w, bias, middle)


def outer_body(left_ref, right_ref, out_ref, sum_ref, turned):
    @pl.when(pl.program_id(0) == 0)
    def _():
        turned[...] = left_ref[...].T

    right = right_ref[...]
    out_ref[...] = dot(turned[...], right, 1, 0).astype(BF)
    sum_ref[...] = jnp.sum(right.astype(F32), 0, keepdims=True)


def outer(left, right):
    r, width = right.shape
    rows = left.shape[1]
    return call(
        outer_body,
        (width // TILE,),
        [spec((r, rows), lambda j: (0, 0)), spec((r, TILE), lambda j: (0, j))],
        [spec((rows, TILE), lambda j: (0, j)), spec((1, TILE), lambda j: (0, j))],
        [struct((rows, width), BF), struct((1, width), F32)],
        [pltpu.VMEM((rows, r), BF)],
        flops=2 * r * rows * width,
        nbytes=r * rows * 2 + r * width * 2 + rows * width * 2,
    )(left, right)


def inner_back_body(cot_ref, w_ref, slope_ref, hidden_ref, grad_ref, gw_ref, gb_ref, turned):
    @pl.when(pl.program_id(0) == 0)
    def _():
        turned[...] = hidden_ref[...].T

    grad = (dot(cot_ref[...], w_ref[...], 1, 0) * slope_ref[...]).astype(BF)
    grad_ref[...] = grad
    gw_ref[...] = dot(turned[...], grad, 1, 0).astype(BF)
    gb_ref[...] = jnp.sum(grad.astype(F32), 0, keepdims=True)


def inner_back(cot, w, slope, hidden):
    r, units = slope.shape
    full = spec((r, D), lambda j: (0, 0))
    col = spec((D, TILE), lambda j: (0, j))
    tile = spec((r, TILE), lambda j: (0, j))
    return call(
        inner_back_body,
        (units // TILE,),
        [full, col, tile, full],
        [tile, col, spec((1, TILE), lambda j: (0, j))],
        [struct((r, units), BF), struct((D, units), BF), struct((1, units), F32)],
        [pltpu.VMEM((D, r), BF)],
        flops=4 * r * D * units,
        nbytes=r * D * 4 + D * units * 4 + r * units * 6,
    )(cot, w, slope, hidden)


def norm_pull(grad, normed, inv, gain):
    scaled = grad * gain
    return inv * (
        scaled
        - jnp.mean(scaled, 1, keepdims=True)
        - normed * jnp.mean(scaled * normed, 1, keepdims=True)
    )


def middle_back_body(
    grad_ref, w_ref, middle_ref, cot_ref, gain_ref, out_ref, branch_ref, gain_sum, shift_sum, out_sum
):
    grad = dot(grad_ref[...], w_ref[...], 1, 1)
    normed, inv = stats(middle_ref[...])
    total = cot_ref[...].astype(F32) + norm_pull(grad, normed, inv, gain_ref[...])
    out_ref[...] = total
    branch = total.astype(BF)
    branch_ref[...] = branch
    sums = (
        (gain_sum, jnp.sum(grad * normed, 0, keepdims=True)),
        (shift_sum, jnp.sum(grad, 0, keepdims=True)),
        (out_sum, jnp.sum(branch.astype(F32), 0, keepdims=True)),
    )
    for ref, value in sums:
        add_up(ref, value)


def add_up(ref, value):
    @pl.when(pl.program_id(0) == 0)
    def _():
        ref[...] = value

    @pl.when(pl.program_id(0) != 0)
    def _():
        ref[...] += value


def middle_back(grad, w, middle, cot, gain):
    r, units = grad.shape
    m = row_tile(r)
    vec = spec((1, D), lambda i: (0, 0))
    row = spec((m, D), lambda i: (i, 0))
    vec_out = struct((1, D), F32)
    return call(
        middle_back_body,
        (r // m,),
        [spec((m, units), lambda i: (i, 0)), spec((D, units), lambda i: (0, 0)), row, row, vec],
        [row, row, vec, vec, vec],
        [struct((r, D), F32), struct((r, D), BF), vec_out, vec_out, vec_out],
        flops=2 * r * D * units,
        nbytes=r * units * 2 + D * units * 2 + r * D * 12,
    )(grad, w, middle, cot, gain)


def mixed_back_body(branch_ref, tile_ref, w_ref, mixed_ref, grad_ref, gw_ref, turned):
    @pl.when(pl.program_id(0) == 0)
    def _():
        turned[...] = mixed_ref[...].T

    grad_ref[...] = dot(branch_ref[...], w_ref[...], 1, 1).astype(BF)
    gw_ref[...] = dot(turned[...], tile_ref[...], 1, 0).astype(BF)


def mixed_back(branch, w, mixed):
    r = branch.shape[0]
    full = spec((r, D), lambda j: (0, 0))
    tile = spec((r, TILE), lambda j: (0, j))
    return call(
        mixed_back_body,
        (D // TILE,),
        [full, tile, spec((TILE, D), lambda j: (j, 0)), full],
        [tile, spec((D, TILE), lambda j: (0, j))],
        [struct((r, D), BF), struct((D, D), BF)],
        [pltpu.VMEM((D, r), BF)],
        flops=4 * r * D * D,
        nbytes=r * D * 8 + D * D * 4,
    )(branch, branch, w, mixed)


def attend_back_body(triple_ref, prob_ref, grad_ref, out_ref):
    left = lax.broadcasted_iota(jnp.int32, (ROWS, 128), 1) < HEAD_DIM
    scale = HEAD_DIM**-0.5
    for pair in range(HEADS // 2):
        q = triple_ref[:, pair * 128 : (pair + 1) * 128]
        k = triple_ref[:, D + pair * 128 : D + (pair + 1) * 128]
        v = triple_ref[:, 2 * D + pair * 128 : 2 * D + (pair + 1) * 128]
        grad = grad_ref[:, pair * 128 : (pair + 1) * 128]
        gq, gk, gv = [], [], []
        for side in range(2):
            mine = left if side == 0 else jnp.logical_not(left)
            prob = prob_ref[0, 2 * pair + side]
            gv.append(dot(prob.astype(BF), grad, 0, 0))
            grad_prob = dot(jnp.where(mine, grad, jnp.zeros_like(grad)), v, 1, 1)
            inside = jnp.sum(grad_prob * prob, 1, keepdims=True)
            grad_scores = (prob * (grad_prob - inside)).astype(BF)
            gq.append(dot(grad_scores, k, 1, 0))
            gk.append(dot(grad_scores, q, 0, 0))
        for at, pieces, factor in ((0, gq, scale), (1, gk, scale), (2, gv, None)):
            both = jnp.where(left, pieces[0], pieces[1])
            if factor is not None:
                both = both * factor
            out_ref[:, at * D + pair * 128 : at * D + (pair + 1) * 128] = both.astype(BF)


def attend_back(triple, prob, grad):
    groups = triple.shape[0] // ROWS
    wide = spec((ROWS, 3 * D), lambda g: (g, 0))
    return call(
        attend_back_body,
        (groups,),
        [
            wide,
            spec((1, HEADS, ROWS, ROWS), lambda g: (g, 0, 0, 0)),
            spec((ROWS, D), lambda g: (g, 0)),
        ],
        wide,
        struct((groups * ROWS, 3 * D), BF),
        flops=groups * HEADS * 8 * ROWS * ROWS * 128,
        nbytes=groups * ROWS * (14 * D + HEADS * 512),
    )(triple, prob, grad)


def qkv_grad_body(grad_ref, hidden_ref, gw_ref, gb_ref):
    grad = grad_ref[...]
    gw_ref[...] = dot(grad.T, hidden_ref[...], 1, 0).astype(BF)
    gb_ref[...] = jnp.sum(grad.astype(F32), 0, keepdims=True)


def qkv_grad(grad, hidden):
    r, width = grad.shape
    return call(
        qkv_grad_body,
        (width // TILE,),
        [spec((r, TILE), lambda j: (0, j)), spec((r, D), lambda j: (0, 0))],
        [spec((TILE, D), lambda j: (j, 0)), spec((1, TILE), lambda j: (0, j))],
        [struct((width, D), BF), struct((1, width), F32)],
        flops=2 * r * D * width,
        nbytes=r * width * 2 + r * D * 2 + width * D * 2,
    )(grad, hidden)


def first_back_body(grad_ref, w_ref, rows_ref, middle_ref, gain_ref, out_ref, gain_sum, shift_sum):
    grad = dot(grad_ref[...], w_ref[...], 1, 0)
    normed, inv = stats(rows_ref[...].astype(F32))
    out_ref[...] = middle_ref[...] + norm_pull(grad, normed, inv, gain_ref[...])
    add_up(gain_sum, jnp.sum(grad * normed, 0, keepdims=True))
    add_up(shift_sum, jnp.sum(grad, 0, keepdims=True))


def first_back(grad, w, rows, grad_middle, gain):
    r, width = grad.shape
    m = row_tile(r)
    vec = spec((1, D), lambda i: (0, 0))
    row = spec((m, D), lambda i: (i, 0))
    vec_out = struct((1, D), F32)
    return call(
        first_back_body,
        (r // m,),
        [spec((m, width), lambda i: (i, 0)), spec((width, D), lambda i: (0, 0)), row, row, vec],
        [row, vec, vec],
        [struct((r, D), F32), vec_out, vec_out],
        flops=2 * r * D * width,
        nbytes=r * width * 2 + D * width * 2 + r * D * 10,
    )(grad, w, rows, grad_middle, gain)


def to_rows(blocks, narrow):
    got = lax.all_to_all(blocks, "narrow", 0, 0, tiled=True)
    return jnp.concatenate([got[n] for n in range(narrow)], axis=1)


def from_rows(rows, narrow):
    cols = rows.shape[1] // narrow
    blocks = jnp.stack([rows[:, n * cols : (n + 1) * cols] for n in range(narrow)])
    got = lax.all_to_all(blocks, "narrow", 0, 0, tiled=True)
    return got.reshape(-1, cols)


def gather_weight(shard, wide, narrow):
    got = lax.all_gather(shard.reshape(-1, 128), ("wide", "narrow"), axis=0, tiled=True)
    return got.reshape((wide, narrow) + shard.shape)


def scatter_grad(blocks):
    shape = blocks.shape[2:]
    got = lax.psum_scatter(
        blocks.reshape(-1, 128), ("wide", "narrow"), scatter_dimension=0, tiled=True
    )
    return lax.psum(got.astype(F32), "dp").reshape(shape)


def on_device(
    wide,
    narrow,
    patches,
    visible,
    w_qkv,
    b_qv,
    w_out,
    b_out,
    w_up,
    b_up,
    w_down,
    b_down,
    gain_one,
    shift_one,
    gain_two,
    shift_two,
    cotangent,
):
    images = visible.shape[0]
    pairs = images // 2
    cols = w_qkv.shape[0]
    heads_cols = w_qkv.shape[2]
    units = w_up.shape[1]

    index = (visible.reshape(pairs, 2, VISIBLE) + jnp.array([0, PATCHES])[None, :, None]).reshape(
        pairs, PAIR
    )
    index = jnp.pad(index, ((0, 0), (0, ROWS - PAIR)), constant_values=-1)[:, :, None]

    if cols % 128 == 0:
        rows_mine, cot_mine = pick_rows(patches, cotangent, index, cols)
    else:
        table = patches.reshape(images, PATCHES, cols)
        rows_mine = jnp.take_along_axis(table, visible[:, :, None], axis=1)
        rows_mine = jnp.pad(
            rows_mine.reshape(pairs, PAIR, cols), ((0, 0), (0, ROWS - PAIR), (0, 0))
        )
        cot_mine = jnp.pad(
            cotangent.reshape(pairs, PAIR, cols), ((0, 0), (0, ROWS - PAIR), (0, 0))
        )
    rows = to_rows(rows_mine.reshape(narrow, -1, cols), narrow)
    cot = to_rows(cot_mine.reshape(narrow, -1, cols), narrow)

    vec = jnp.concatenate(
        [gain_one, shift_one, gain_two, shift_two, b_out, b_down, b_qv.reshape(-1), b_up]
    )
    vec = lax.all_gather(vec, ("wide", "narrow"), axis=0, tiled=False).astype(F32)
    vec = vec.reshape(wide, narrow, -1)
    by_narrow = vec[0, :, : 6 * cols].reshape(narrow, 6, cols).transpose(1, 0, 2).reshape(6, 1, D)
    gain_a, shift_a, gain_b, shift_b, bias_out, bias_down = (by_narrow[i] for i in range(6))
    by_wide = vec[:, 0, 6 * cols :]
    bias_q = by_wide[:, :heads_cols].reshape(1, D)
    bias_v = by_wide[:, heads_cols : 2 * heads_cols].reshape(1, D)
    bias_qkv = jnp.concatenate([bias_q, jnp.zeros((1, D), F32), bias_v], axis=1)
    bias_up = by_wide[:, 2 * heads_cols :].reshape(1, -1)

    qkv_t = gather_weight(w_qkv.transpose(1, 2, 0), wide, narrow)
    qkv_t = qkv_t.transpose(2, 0, 3, 1, 4).reshape(3 * D, D)
    out_w = gather_weight(w_out, wide, narrow).transpose(0, 2, 1, 3).reshape(D, D)
    up_w = gather_weight(w_up, wide, narrow).transpose(1, 2, 0, 3).reshape(D, -1)
    down_w = gather_weight(w_down, wide, narrow).transpose(1, 2, 0, 3).reshape(D, -1)

    hidden_one = norm(rows, gain_a, shift_a)
    triple = qkv(hidden_one, qkv_t, bias_qkv)
    mixed, prob = attend(triple)
    middle, hidden_two = mix(mixed, out_w, bias_out, rows, gain_b, shift_b)
    active, slope = up(hidden_two, up_w, bias_up)
    result = down(active, down_w, bias_down, middle)

    gw_down, _ = outer(cot, active)
    gb_down = jnp.sum(cot, 0, dtype=F32)
    grad_inner, gw_up, gb_up = inner_back(cot, down_w, slope, hidden_two)
    grad_middle, branch, gg_two, gs_two, gb_out = middle_back(grad_inner, up_w, middle, cot, gain_b)
    grad_mixed, gw_out = mixed_back(branch, out_w, mixed)
    grad_triple = attend_back(triple, prob, grad_mixed)
    gw_qkv, gb_qkv = qkv_grad(grad_triple, hidden_one)
    grad_rows, gg_one, gs_one = first_back(grad_triple, qkv_t, rows, grad_middle, gain_a)

    result = from_rows(result, narrow)
    grad_rows = from_rows(grad_rows, narrow)
    if cols % 128 == 0:
        block_output = flat_rows(result, cols)
        grad_patches = put_rows(grad_rows, index, cols).reshape(1, -1)
    else:
        block_output = result.reshape(pairs, ROWS, cols)[:, :PAIR].reshape(1, -1)
        grad_rows = grad_rows.reshape(pairs, ROWS, cols)[:, :PAIR].reshape(images, VISIBLE, cols)
        grad_patches = (
            jnp.zeros((images, PATCHES, cols), F32)
            .at[jnp.arange(images)[:, None], visible]
            .set(grad_rows)
            .reshape(1, -1)
        )

    g_down = scatter_grad(gw_down.reshape(narrow, cols, wide, units).transpose(2, 0, 1, 3))
    g_up = scatter_grad(gw_up.reshape(narrow, cols, wide, units).transpose(2, 0, 1, 3))
    g_out = scatter_grad(gw_out.reshape(wide, heads_cols, narrow, cols).transpose(0, 2, 1, 3))
    g_qkv = scatter_grad(
        gw_qkv.reshape(3, wide, heads_cols, narrow, cols).transpose(1, 3, 0, 2, 4)
    )
    g_qkv = g_qkv.transpose(2, 0, 1)

    sums = jnp.concatenate(
        [
            gg_one[0],
            gs_one[0],
            gg_two[0],
            gs_two[0],
            gb_out[0],
            gb_down,
            gb_qkv[0, :D],
            gb_qkv[0, 2 * D :],
            gb_up[0],
        ]
    )
    sums = lax.psum(sums, ("dp", "wide", "narrow"))
    at_narrow = lax.axis_index("narrow") * cols
    at_wide = lax.axis_index("wide")

    def narrow_part(i):
        return lax.dynamic_slice_in_dim(sums, i * D + at_narrow, cols)

    g_bqv = jnp.stack(
        [
            lax.dynamic_slice_in_dim(sums, (6 + i) * D + at_wide * heads_cols, heads_cols)
            for i in range(2)
        ]
    )
    g_bup = lax.dynamic_slice_in_dim(sums, 8 * D + at_wide * units, units)
    return (
        block_output,
        grad_patches,
        g_qkv,
        g_bqv,
        g_out,
        narrow_part(4),
        g_up,
        g_bup,
        g_down,
        narrow_part(5),
        narrow_part(0),
        narrow_part(1),
        narrow_part(2),
        narrow_part(3),
    )


def solution(mesh):
    in_specs = (
        P("narrow", ("dp", "wide")),
        P(("dp", "wide"), None),
        P("narrow", None, "wide"),
        P(None, "wide"),
        P("wide", "narrow"),
        P("narrow"),
        P("narrow", "wide"),
        P("wide"),
        P("narrow", "wide"),
        P("narrow"),
        P("narrow"),
        P("narrow"),
        P("narrow"),
        P("narrow"),
        P("narrow", ("dp", "wide")),
    )
    out_specs = (
        P("narrow", ("dp", "wide")),
        P("narrow", ("dp", "wide")),
        P("narrow", None, "wide"),
        P(None, "wide"),
        P("wide", "narrow"),
        P("narrow"),
        P("narrow", "wide"),
        P("wide"),
        P("narrow", "wide"),
        P("narrow"),
        P("narrow"),
        P("narrow"),
        P("narrow"),
        P("narrow"),
    )
    body = partial(on_device, mesh.shape["wide"], mesh.shape["narrow"])
    return jax.shard_map(body, mesh=mesh, in_specs=in_specs, out_specs=out_specs, check_vma=False)
```

time: 2740 us -> 839 us (0.31)
  waiting for transfers between devices: 1990 us -> 313 us
  other arithmetic: 233 us -> 6.97 us
  Pallas kernels: 0 us -> 174 us
  matrix products: 134 us -> 0 us
  local copies, waits for them, and re-layouts: 283 us -> 192 us
  blocking collectives: 78.4 us -> 112 us
    reduce_scatter x6 -> x4, waiting for transfers between devices: 1040 us -> 180 us  [scatter_grad(): lax.psum_scatter(blocks.reshape(-1, 128), ('wide', 'narrow'), scatter_dim...]
    all_gather x8 -> x4, waiting for transfers between devices: 665 us -> 109 us  [gather_weight(): lax.all_gather(shard.reshape(-1, 128), ('wide', 'narrow'), axis=0, tiled=...]
    unnamed x19 -> x9, waiting for transfers between devices: 256 us -> 0.15 us
    pallas_call x0 -> x16, Pallas kernels: none -> 174 us  [the longest x1 31 us: attend_back(): call(attend_back_body, (groups,), [wide, spec((1, HEADS, ROWS, ROWS), lam...]
    unnamed x10 -> x3, other arithmetic: 148 us -> 0.01 us
    dot_general x16 -> x0, matrix products: 117 us -> none  [the longest x4 33.8 us: outer_sum(): lax.dot_general(left, right, (((0,), (0,)), ((), ())), preferred_element_...]
    convert_element_type x15 -> x0, other arithmetic: 55.6 us -> none  [the longest x1 25.5 us: on_device(): grad_inner = gelu_pull(grad_active)[0].astype(jnp.bfloat16)]
    unnamed x105 -> x109, local copies, waits for them, and re-layouts: 97.1 us -> 42.8 us
  transfers between devices with their start and end apart: 17 -> 13, of which waited for: 17 -> 6; matrix products, arithmetic and copies ran while one was open for 6% -> 16% of each run, Pallas kernels for 0% -> 15%
where the time goes in v1:
time: 839 us; the launch traced here: 830 us
  waiting for transfers between devices  313 us (37%)
  local copies, waits for them, and re-layouts  192 us (23%)
  Pallas kernels  174 us (21%)
  blocking collectives  112 us (13%)
  starting transfers between devices  17.6 us (2%)
  between operations  14.6 us (2%)
    reduce_scatter x4, waiting for transfers between devices, scatter_grad(): lax.psum_scatter(blocks.reshape(-1, 128), ('wide', 'narrow'), scatter_dim...  180 us
    all_gather x4, waiting for transfers between devices, gather_weight(): lax.all_gather(shard.reshape(-1, 128), ('wide', 'narrow'), axis=0, tiled=...  109 us
    psum x1, blocking collectives, on_device(): sums = lax.psum(sums, ('dp', 'wide', 'narrow'))  65.1 us
    all_gather x1, blocking collectives, on_device(): lax.all_gather(vec, ('wide', 'narrow'), axis=0, tiled=False).astype(F32)  47.3 us
    unnamed x109, local copies, waits for them, and re-layouts  42.8 us
    pallas_call x1, Pallas kernels, attend_back(): call(attend_back_body, (groups,), [wide, spec((1, HEADS, ROWS, ROWS), lam...  31 us
    reshape x4, local copies, waits for them, and re-layouts, gather_weight(): return got.reshape((wide, narrow) + shard.shape)  28.4 us
    reshape x4, local copies, waits for them, and re-layouts, scatter_grad(): blocks.reshape(-1, 128)  28.2 us
  transfers between devices with their start and end apart: 13, of which 6 were waited for; matrix products, arithmetic and copies ran while one was open for 16% of the time, Pallas kernels for 15%

profile of v1, /device:TPU:0, one launch (start us, length us, event | category | flops | bytes accessed | tf_op | source)
XLA Modules:
  0.0 830.2 jit_solution(16066907541353785781)
XLA Ops:
  15.6 15.9 %shard_map.263 = (bf16[1792,384]{1,0:T(8,128)(2,1)S(1)}, bf16[1792,384]{1,0:T(8,128)(2,1)}) custom-call(bf16[1,2408448]{1,0:T(2,128)(2,1)} %patch_ref.1, bf16[1,602112]{1,0:T(2,128)(2,1)S(1)} %copy-done.11, s32[16,112,1]{2,1,0:T(8,128)S(1)} %copy.40.index_ref), custom_call_target="tpu_custom_call" | custom-call | flops 539492352 | bytes 12042240 | tf_op jit(solution)/shard_map/pallas_call | solution.py:73
  38.9 47.3 %all-gather.1 = bf16[8,1,3456]{2,1,0:T(2,128)(2,1)S(1)} all-gather(bf16[1,1,3456]{2,1,0:T(2,128)(2,1)S(1)} %reshape.195), channel_id=2, replica_groups=mesh['dp'=4,'wide'=4,'narrow'=2] {'wide','narrow'}, dimensions={0}, use_global_device_ids=true | all-gather | bytes 62208 | tf_op jit(solution)/shard_map/all_gather | solution.py:601
  95.4 23.3 %all-to-all-done.2 = bf16[2,896,384]{2,1,0:T(8,128)(2,1)} async-done(((bf16[2,896,384]{2,1,0:T(8,128)(2,1)}), bf16[2,896,384]{2,1,0:T(8,128)(2,1)}, u32[]{:S(2)}, u32[]{:S(2)}) %all-to-all-start.2) | async-done | bytes 1376288 | tf_op jit(solution)/shard_map/all_to_all | solution.py:530
  127.3 6.3 all-gather.7.cloned.1.call-done
  133.6 6.6 reshape.159
  147.2 6.9 shard_map.265.triple_ref
  158.1 10.8 %shard_map.266 = (bf16[896,768]{1,0:T(8,128)(2,1)S(1)}, f32[8,12,112,112]{3,2,1,0:T(8,128)}) custom-call(bf16[896,2304]{1,0:T(8,128)(2,1)S(1)} %copy-done.1), custom_call_target="tpu_custom_call" | custom-call | flops 616562688 | bytes 11010048 | tf_op jit(solution)/shard_map/pallas_call | solution.py:222
  174.3 41.4 %all-gather.11.cloned.1.call-done = bf16[18432,128]{1,0:T(8,128)(2,1)} async-done(((bf16[2304,128]{1,0:T(8,128)(2,1)}), bf16[18432,128]{1,0:T(8,128)(2,1)}) %all-gather.11.cloned.1.call-update) | async-done | bytes 4718608 | tf_op jit(solution)/shard_map/all_gather | solution.py:542
  215.6 9.4 %reshape.167 = bf16[4,2,384,768]{3,2,1,0:T(8,128)(2,1)} reshape(bf16[18432,128]{1,0:T(8,128)(2,1)} %all-gather.11.cloned.1.call-done) | data formatting | bytes 9437184 | tf_op jit(solution)/shard_map/reshape | solution.py:543
  225.1 6.0 copy.43
  234.2 61.5 %all-gather.13.cloned.1.call-done = bf16[18432,128]{1,0:T(8,128)(2,1)} async-done(((bf16[2304,128]{1,0:T(8,128)(2,1)}), bf16[18432,128]{1,0:T(8,128)(2,1)}) %all-gather.13.cloned.1.call-update) | async-done | bytes 4718608 | tf_op jit(solution)/shard_map/all_gather | solution.py:542
  295.7 9.2 %reshape.171 = bf16[4,2,384,768]{3,2,1,0:T(8,128)(2,1)} reshape(bf16[18432,128]{1,0:T(8,128)(2,1)} %all-gather.13.cloned.1.call-done) | data formatting | bytes 9437184 | tf_op jit(solution)/shard_map/reshape | solution.py:543
  305.0 6.1 copy.44
  314.4 12.5 %shard_map.268 = (bf16[896,3072]{1,0:T(8,128)(2,1)}, f32[896,3072]{1,0:T(8,128)}) custom-call(bf16[896,768]{1,0:T(8,128)(2,1)S(1)} %copy-done.24, bf16[768,3072]{1,0:T(8,128)(2,1)S(1)} %bitcast.85, f32[1,3072]{1,0:T(1,128)S(1)} %bitcast.97), custom_call_target="tpu_custom_call" | custom-call | flops 4227858432 | bytes 22609920 | tf_op jit(solution)/shard_map/pallas_call | solution.py:271
  326.9 21.9 %shard_map.271 = (bf16[896,3072]{1,0:T(8,128)(2,1)}, bf16[768,3072]{1,0:T(8,128)(2,1)}, f32[1,3072]{1,0:T(1,128)S(1)}) custom-call(bf16[896,768]{1,0:T(8,128)(2,1)S(1)} %copy-done.12, bf16[768,3072]{1,0:T(8,128)(2,1)} %bitcast.109, f32[896,3072]{1,0:T(8,128)} %get-tuple-element.45.slope_ref, bf16[896,768]{1,0:T(8,128)(2,1)S(1)} %copy-done.24), custom_call_target="tpu_custom_call" | custom-call | flops 8455716864 | bytes 28704768 | tf_op jit(solution)/shard_map/pallas_call | solution.py:351
  348.8 10.5 %shard_map.272 = (f32[896,768]{1,0:T(8,128)S(1)}, bf16[896,768]{1,0:T(8,128)(2,1)S(1)}, f32[1,768]{1,0:T(1,128)S(1)}, f32[1,768]{1,0:T(1,128)S(1)}, f32[1,768]{1,0:T(1,128)S(1)}) custom-call(bf16[896,3072]{1,0:T(8,128)(2,1)} %get-tuple-element.46.grad_ref, bf16[768,3072]{1,0:T(8,128)(2,1)} %bitcast.82, f32[896,768]{1,0:T(8,128)} %get-tuple-element.42.middle_ref, ...), custom_call_target="tpu_custom_call" | custom-call | flops 4227858432 | bytes 18481152 | tf_op jit(solution)/shard_map/pallas_call | solution.py:406
  377.1 31.0 %shard_map.274.grad_ref = bf16[896,2304]{1,0:T(8,128)(2,1)S(1)} custom-call(bf16[896,2304]{1,0:T(8,128)(2,1)} %shard_map.265.triple_ref, f32[8,12,112,112]{3,2,1,0:T(8,128)} %get-tuple-element.43.prob_ref, bf16[896,768]{1,0:T(8,128)(2,1)S(1)} %copy-done.20), custom_call_target="tpu_custom_call" | custom-call | flops 1233125376 | bytes 15138816 | tf_op jit(solution)/shard_map/pallas_call | solution.py:470
  410.1 8.3 shard_map.277
  420.2 7.9 reshape.177
  432.6 6.7 reshape.178
  440.6 11.9 %shard_map.278 = (bf16[768,3072]{1,0:T(8,128)(2,1)S(1)}, f32[1,3072]{1,0:T(1,128)}) custom-call(bf16[896,768]{1,0:T(8,128)(2,1)S(1)} %copy-done.13, bf16[896,3072]{1,0:T(8,128)(2,1)} %get-tuple-element.41.active_ref.right_ref), custom_call_target="tpu_custom_call" | custom-call | flops 4227858432 | bytes 11599872 | tf_op jit(solution)/shard_map/pallas_call | solution.py:323
  454.7 9.8 %reshape.186 = bf16[2,384,4,768]{3,2,1,0:T(4,128)(2,1)} reshape(bf16[768,3072]{1,0:T(8,128)(2,1)} %copy-done.7) | data formatting | bytes 9437184 | tf_op jit(solution)/shard_map/reshape | solution.py:648
  469.7 9.3 %reshape.187 = bf16[18432,128]{1,0:T(8,128)(2,1)} reshape(bf16[4,2,384,768]{3,2,1,0:T(8,128)(2,1)} %bitcast.103) | data formatting | bytes 9437184 | tf_op jit(solution)/shard_map/reshape | solution.py:549
  479.1 9.8 %reshape.183 = bf16[2,384,4,768]{3,2,1,0:T(4,128)(2,1)} reshape(bf16[768,3072]{1,0:T(8,128)(2,1)} %get-tuple-element.60) | data formatting | bytes 9437184 | tf_op jit(solution)/shard_map/reshape | solution.py:649
  494.1 9.2 %reshape.184 = bf16[18432,128]{1,0:T(8,128)(2,1)} reshape(bf16[4,2,384,768]{3,2,1,0:T(8,128)(2,1)} %bitcast.104) | data formatting | bytes 9437184 | tf_op jit(solution)/shard_map/reshape | solution.py:549
  506.4 7.9 shard_map.269
  519.4 8.8 %shard_map.275 = (f32[896,768]{1,0:T(8,128)S(1)}, f32[1,768]{1,0:T(1,128)S(1)}, f32[1,768]{1,0:T(1,128)S(1)}) custom-call(bf16[896,2304]{1,0:T(8,128)(2,1)} %copy-done, bf16[2304,768]{1,0:T(8,128)(2,1)} %bitcast.79, bf16[896,768]{1,0:T(8,128)(2,1)S(1)} %pad_maximum_fusion.1.rows_ref, f32[896,768]{1,0:T(8,128)} %copy-done.9, f32[1,768]{1,0:T(1,128)S(1)} %bitcast.90), custom_call_target="tpu_custom_call" | custom-call | flops 3170893824 | bytes 14548992 | tf_op jit(solution)/shard_map/pallas_call | solution.py:518
  536.7 83.0 %reduce-scatter.11.cloned.1.call-done = bf16[2304,128]{1,0:T(8,128)(2,1)} async-done(((bf16[18432,128]{1,0:T(8,128)(2,1)}), bf16[2304,128]{1,0:T(8,128)(2,1)}) %reduce-scatter.11.cloned.1.call-update) | async-done | bytes 589840 | tf_op jit(solution)/shard_map/reduce_scatter | solution.py:548
  622.2 96.9 %reduce-scatter.9.cloned.1.call-done = bf16[2304,128]{1,0:T(8,128)(2,1)} async-done(((bf16[18432,128]{1,0:T(8,128)(2,1)}), bf16[2304,128]{1,0:T(8,128)(2,1)}) %reduce-scatter.9.cloned.1.call-update) | async-done | bytes 589840 | tf_op jit(solution)/shard_map/reduce_scatter | solution.py:548
  730.1 65.1 %psum.36 = f32[9216]{0:T(1024)S(1)} all-reduce(f32[9216]{0:T(1024)S(1)} %constant_dynamic-update-slice_fusion), channel_id=1, replica_groups=mesh['dp'=4,'wide'=4,'narrow'=2] {'dp','wide','narrow'}, use_global_device_ids=true, to_apply=%region_3.4 | all-reduce | flops 9216 | bytes 73728 | tf_op jit(solution)/shard_map/psum | solution.py:669
  798.5 6.1 shard_map.270
  805.8 11.7 %shard_map.276 = f32[18816,128]{1,0:T(8,128)} custom-call(f32[1792,384]{1,0:T(8,128)S(1)} %bitcast.80, s32[16,112,1]{2,1,0:T(8,128)S(1)} %copy-done.4), custom_call_target="tpu_custom_call" | custom-call | flops 1618477056 | bytes 12386304 | tf_op jit(solution)/shard_map/pallas_call | solution.py:107
  (202 shorter events, 136.5 us)
Async XLA Ops:
  7.2 6.4 copy-start.29
  7.2 8.0 copy-start.30
  7.2 114.3 %all-gather.9.cloned.1.call-start = ((), (), s32[]{:S(2)}) async-start(), calls=%async_computation.9 | async-start | bytes 1327104 | tf_op jit(solution)/shard_map/all_gather | solution.py:542
  9.0 124.6 %all-gather.7.cloned.1.call-start = ((), (), s32[]{:S(2)}) async-start(), calls=%async_computation.8 | async-start | bytes 3981312 | tf_op jit(solution)/shard_map/all_gather | solution.py:542
  9.0 6.6 copy-start.11
  11.2 204.4 %all-gather.11.cloned.1.call-start = ((), (), s32[]{:S(2)}) async-start(), calls=%async_computation.10 | async-start | bytes 5308416 | tf_op jit(solution)/shard_map/all_gather | solution.py:542
  13.6 282.1 %all-gather.13.cloned.1.call-start = ((), (), s32[]{:S(2)}) async-start(), calls=%async_computation.11 | async-start | bytes 5308416 | tf_op jit(solution)/shard_map/all_gather | solution.py:542
  15.6 15.9 %copy-start.3 = (s32[16,112,1]{2,1,0:T(8,128)}, s32[16,112,1]{2,1,0:T(8,128)S(1)}, u32[]{:S(2)}) copy-start(s32[16,112,1]{2,1,0:T(8,128)S(1)} %copy.40.index_ref) | copy-start | bytes 21508
  32.6 4.4 copy-start.32
  32.6 4.5 copy-start.33
  32.6 4.7 copy-start.34
  32.6 4.9 copy-start.35
  32.6 5.1 copy-start.36
  32.7 5.3 copy-start.37
  32.7 5.6 copy-start.38
  32.7 6.0 copy-start.31
  32.7 54.2 %all-to-all-start = ((bf16[2,896,384]{2,1,0:T(8,128)(2,1)}), bf16[2,896,384]{2,1,0:T(8,128)(2,1)S(1)}, u32[]{:S(2)}, u32[]{:S(2)}) async-start(bf16[2,896,384]{2,1,0:T(8,128)(2,1)} %bitcast.88), calls=%async_computation | async-start | bytes 2752512 | tf_op jit(solution)/shard_map/all_to_all | solution.py:530
  86.9 31.9 %all-to-all-start.2 = ((bf16[2,896,384]{2,1,0:T(8,128)(2,1)}), bf16[2,896,384]{2,1,0:T(8,128)(2,1)}, u32[]{:S(2)}, u32[]{:S(2)}) async-start(bf16[2,896,384]{2,1,0:T(8,128)(2,1)} %bitcast.19), calls=%async_computation.2 | async-start | bytes 2752512 | tf_op jit(solution)/shard_map/all_to_all | solution.py:530
  91.4 441.4 %reduce-scatter.7.cloned.1.call-start = ((), (), s32[]{:S(2)}) async-start(), calls=%async_computation.13 | async-start | bytes 1327104 | tf_op jit(solution)/shard_map/reduce_scatter | solution.py:548
  120.2 6.9 copy-start.25
  305.0 9.4 %slice-start = ((s8[4718592]{0:T(1024)(128)(4,1)}), s8[4194304]{0:T(1024)(128)(4,1)S(1)}, s32[]{:S(2)}) async-start(s8[4718592]{0:T(1024)(128)(4,1)} %bitcast.83), calls=%async_computation.17 | async-start | bytes 8388608
  314.4 12.6 %copy-start.12 = (bf16[896,768]{1,0:T(8,128)(2,1)S(1)}, bf16[896,768]{1,0:T(8,128)(2,1)}, u32[]{:S(2)}) copy-start(bf16[896,768]{1,0:T(8,128)(2,1)} %pad_maximum_fusion.3.cot_ref.left_ref) | copy-start | bytes 4128772
  371.4 5.7 copy-start.20
  377.0 157.6 %reduce-scatter.5.cloned.1.call-start = ((), (), s32[]{:S(2)}) async-start(), calls=%async_computation.12 | async-start | bytes 3981312 | tf_op jit(solution)/shard_map/reduce_scatter | solution.py:548
  377.1 33.0 %copy-start.16 = (bf16[896,768]{1,0:T(8,128)(2,1)S(1)}, bf16[896,768]{1,0:T(8,128)(2,1)}, u32[]{:S(2)}) copy-start(bf16[896,768]{1,0:T(8,128)(2,1)} %copy-done.14) | copy-start | bytes 4128772
  439.3 180.4 %reduce-scatter.11.cloned.1.call-start = ((), (), s32[]{:S(2)}) async-start(), calls=%async_computation.15 | async-start | bytes 5308416 | tf_op jit(solution)/shard_map/reduce_scatter | solution.py:548
  479.0 240.1 %reduce-scatter.9.cloned.1.call-start = ((), (), s32[]{:S(2)}) async-start(), calls=%async_computation.14 | async-start | bytes 5308416 | tf_op jit(solution)/shard_map/reduce_scatter | solution.py:548
  515.7 209.0 %all-to-all-start.1 = ((bf16[2,896,384]{2,1,0:T(8,128)(2,1)}), bf16[2,896,384]{2,1,0:T(8,128)(2,1)S(1)}, u32[]{:S(2)}, u32[]{:S(2)}) async-start(bf16[2,896,384]{2,1,0:T(8,128)(2,1)} %pad_maximum_fusion.2), calls=%async_computation.1 | async-start | bytes 2752512 | tf_op jit(solution)/shard_map/all_to_all | solution.py:537
  519.4 298.2 %all-reduce.4.cloned.1.call-start = ((), (), s32[]{:S(2)}) async-start(), calls=%async_computation.16 | async-start | bytes 7077888 | tf_op jit(solution)/shard_map/psum | solution.py:551
  725.7 78.9 %all-to-all-start.3 = ((f32[2,896,384]{2,1,0:T(8,128)}), f32[2,896,384]{2,1,0:T(8,128)S(1)}, u32[]{:S(2)}, u32[]{:S(2)}) async-start(f32[2,896,384]{2,1,0:T(8,128)} %pad_maximum_fusion), calls=%async_computation.3 | async-start | bytes 5505024 | tf_op jit(solution)/shard_map/all_to_all | solution.py:537
  817.5 4.0 copy-start.28
  817.5 5.0 copy-start.27
  (22 other events, 35.2 us)
Sparse Core Ops, SparseCore 0:
  10.8 49.3 all-gather.8
  62.4 71.2 all-gather.6
  136.4 79.1 all-gather.10
  217.7 78.0 all-gather.12
  377.1 62.3 reduce-scatter.6
  443.0 78.1 reduce-scatter.4
  524.9 94.7 reduce-scatter.10
  623.9 95.1 reduce-scatter.8
  722.9 76.2 all-reduce.3

commit v2 on v1

--- a/solution.py
+++ b/solution.py
@@ -51,7 +51,9 @@
     return jax.ShapeDtypeStruct(shape, dtype)
 
 
-def pick_body(cols, patch_ref, cot_ref, index_ref, rows_ref, cot_rows_ref, wide_ref, cot_scr):
+def pick_body(
+    cols, at_ref, patch_ref, cot_ref, index_ref, rows_ref, cot_rows_ref, wide_ref, cot_scr
+):
     lanes = cols // 128
     wide_ref[...] = patch_ref[...].astype(F32).reshape(wide_ref.shape)
     parts = [wide_ref[pl.ds(k, 2 * PATCHES, stride=lanes), :] for k in range(lanes)]
@@ -66,31 +68,43 @@
     ).astype(BF)
 
 
-def pick_rows(patches, cotangent, index, cols):
+def pick_rows(at, patches, cotangent, index, cols):
     pairs = index.shape[0]
+    own = pairs // 2
     width = 2 * PATCHES * cols
     cot_width = PAIR * cols
+
+    def source(i, at):
+        return (i // own ^ 1 ^ at[1]) * own + i % own
+
     return call(
         partial(pick_body, cols),
         (pairs,),
         [
-            spec((1, width), lambda i: (0, i)),
-            spec((1, cot_width), lambda i: (0, i)),
-            spec((1, ROWS, 1), lambda i: (i, 0, 0)),
+            spec((1, width), lambda i, at: (0, source(i, at))),
+            spec((1, cot_width), lambda i, at: (0, source(i, at))),
+            spec((1, ROWS, 1), lambda i, at: (source(i, at), 0, 0)),
         ],
-        [spec((ROWS, cols), lambda i: (i, 0)), spec((ROWS, cols), lambda i: (i, 0))],
+        [spec((ROWS, cols), lambda i, at: (i, 0)), spec((ROWS, cols), lambda i, at: (i, 0))],
         [struct((pairs * ROWS, cols), BF), struct((pairs * ROWS, cols), BF)],
         [pltpu.VMEM((width // 128, 128), F32), pltpu.VMEM((cot_width // 128, 128), F32)],
+        prefetch=1,
         flops=2 * pairs * ROWS * 2 * PATCHES * cols,
         nbytes=pairs * (width + cot_width) * 4,
-    )(patches, cotangent, index)
-
-
-def put_body(cols, rows_ref, index_ref, out_ref):
+    )(at, patches, cotangent, index)
+
+
+def own_block(at_ref, keep_ref, got_ref):
+    own = pl.num_programs(0) // 2
+    mine = pl.program_id(0) // own == at_ref[1]
+    return jnp.where(mine, keep_ref[...].astype(F32), got_ref[...].astype(F32))
+
+
+def put_body(cols, at_ref, keep_ref, got_ref, index_ref, out_ref):
     lanes = cols // 128
     hit = index_ref[0] == lax.broadcasted_iota(jnp.int32, (ROWS, 2 * PATCHES), 1)
     hit = hit.astype(BF)
-    rest = rows_ref[...]
+    rest = own_block(at_ref, keep_ref, got_ref)
     total = None
     for _ in range(3):
         part = rest.astype(BF)
@@ -101,40 +115,46 @@
         out_ref[pl.ds(k, 2 * PATCHES, stride=lanes), :] = total[:, k * 128 : (k + 1) * 128]
 
 
-def put_rows(rows, index, cols):
+def put_rows(at, keep, got, index, cols):
     pairs = index.shape[0]
+    own = pairs // 2
     tall = 2 * PATCHES * cols // 128
+    rows = spec((ROWS, cols), lambda i, at: (i % own, 0))
     return call(
         partial(put_body, cols),
         (pairs,),
-        [spec((ROWS, cols), lambda i: (i, 0)), spec((1, ROWS, 1), lambda i: (i, 0, 0))],
-        spec((tall, 128), lambda i: (i, 0)),
+        [rows, rows, spec((1, ROWS, 1), lambda i, at: (i, 0, 0))],
+        spec((tall, 128), lambda i, at: (i, 0)),
         struct((pairs * tall, 128), F32),
+        prefetch=1,
         flops=6 * pairs * ROWS * 2 * PATCHES * cols,
         nbytes=pairs * (tall * 512 + ROWS * cols * 4),
-    )(rows, index)
-
-
-def flat_body(cols, rows_ref, out_ref, scr):
+    )(at, keep, got, index)
+
+
+def flat_body(cols, at_ref, keep_ref, got_ref, out_ref, scr):
     lanes = cols // 128
-    rows = rows_ref[...].astype(F32)
+    rows = own_block(at_ref, keep_ref, got_ref)
     for k in range(lanes):
         scr[pl.ds(k, PAIR, stride=lanes), :] = rows[:PAIR, k * 128 : (k + 1) * 128]
     out_ref[...] = scr[...].reshape(out_ref.shape).astype(BF)
 
 
-def flat_rows(rows, cols):
-    pairs = rows.shape[0] // ROWS
+def flat_rows(at, keep, got, cols):
+    own = keep.shape[0] // ROWS
+    pairs = 2 * own
     width = PAIR * cols
+    rows = spec((ROWS, cols), lambda i, at: (i % own, 0))
     return call(
         partial(flat_body, cols),
         (pairs,),
-        [spec((ROWS, cols), lambda i: (i, 0))],
-        spec((1, width), lambda i: (0, i)),
+        [rows, rows],
+        spec((1, width), lambda i, at: (0, i)),
         struct((1, pairs * width), BF),
         [pltpu.VMEM((width // 128, 128), F32)],
+        prefetch=1,
         nbytes=pairs * width * 6,
-    )(rows)
+    )(at, keep, got)
 
 
 def stats(rows):
@@ -524,6 +544,160 @@
         flops=2 * r * D * width,
         nbytes=r * width * 2 + D * width * 2 + r * D * 10,
     )(grad, w, rows, grad_middle, gain)
+
+
+WIDE, NARROW, DP = "wide", "narrow", "dp"
+
+
+def swap(value, axis, bit):
+    size = lax.axis_size(axis)
+    return lax.ppermute(value, axis, [(i, i ^ bit) for i in range(size)])
+
+
+def gather_pieces(piece, steps):
+    stack, tags = piece[None], [(0, 0, 0)]
+    for axis, bit in steps:
+        got = swap(stack, axis, bit)
+        move = (bit if axis == WIDE else 0, bit if axis == NARROW else 0, 0)
+        stack = jnp.concatenate([stack, got])
+        tags = tags + [tuple(a ^ b for a, b in zip(tag, move)) for tag in tags]
+    other = swap(stack, DP, 1)
+    return [(stack, tags), (other, [(a, b, 1) for a, b, _ in tags])]
+
+
+def qkv_plan(cols, heads_cols):
+    half = heads_cols // 2
+
+    def plan(w, n, h):
+        return [
+            (0, (pl.ds(p * half, half), slice(None)), (p * D + w * heads_cols + h * half, n * cols))
+            for p in range(3)
+        ]
+
+    return plan
+
+
+def flat_plan(cols, units):
+    half = cols // 2
+
+    def plan(w, n, h):
+        return [(0, (pl.ds(0, half), slice(None)), (n * cols + h * half, w * units))]
+
+    return plan
+
+
+def up_out_plan(cols, units, heads_cols):
+    half = cols // 2
+    part = heads_cols // 4
+
+    def plan(w, n, h):
+        moves = flat_plan(cols, units)(w, n, h)
+        for s in range(2):
+            at = (pl.ds(half, part), pl.ds(s * cols, cols))
+            moves.append((1, at, (w * heads_cols + h * 2 * part + s * part, n * cols)))
+        return moves
+
+    return plan
+
+
+def build_body(plan, tag_lists, n_out, inverse, at_ref, *refs):
+    arrays, outs, sem = refs[: len(tag_lists)], refs[len(tag_lists) : -1], refs[-1]
+    if inverse:
+        outs, arrays = refs[:n_out], refs[n_out:-1]
+    copies = []
+    for array, tags in zip(arrays, tag_lists):
+        for k, (dw, dn, dc) in enumerate(tags):
+            w, n, h = at_ref[0] ^ dw, at_ref[1] ^ dn, at_ref[2] ^ dc
+            for which, src, (row, lane) in plan(w, n, h):
+                piece = array.at[(k,) + src]
+                shape = piece.shape
+                whole = outs[which].at[
+                    pl.ds(pl.multiple_of(row, 16), shape[-2]),
+                    pl.ds(pl.multiple_of(lane, 128), shape[-1]),
+                ]
+                ends = (whole, piece) if inverse else (piece, whole)
+                copies.append(pltpu.make_async_copy(*ends, sem.at[len(copies)]))
+    for copy in copies:
+        copy.start()
+    for copy in copies:
+        copy.wait()
+
+
+ANY = pl.BlockSpec(memory_space=pl.ANY)
+
+
+def build_weights(at, pieces, plan, shapes):
+    arrays = [stack for stack, _ in pieces]
+    tags = [t for _, t in pieces]
+    moves = sum(len(t) for t in tags) * len(plan(0, 0, 0))
+    return pl.pallas_call(
+        partial(build_body, plan, tags, len(shapes), False),
+        out_shape=[struct(shape, BF) for shape in shapes],
+        grid_spec=pltpu.PrefetchScalarGridSpec(
+            num_scalar_prefetch=1,
+            grid=(1,),
+            in_specs=[ANY] * len(arrays),
+            out_specs=[ANY] * len(shapes),
+            scratch_shapes=[pltpu.SemaphoreType.DMA((moves,))],
+        ),
+        compiler_params=pltpu.CompilerParams(vmem_limit_bytes=4 * MB),
+        cost_estimate=pl.CostEstimate(
+            flops=0, bytes_accessed=2 * sum(a.size * 2 for a in arrays), transcendentals=0
+        ),
+    )(at, *arrays)
+
+
+def cut_grads(at, grads, plan, tags, shape):
+    tag_lists = [[(w, n, dc) for w, n in tags] for dc in range(2)]
+    moves = 2 * len(tags) * len(plan(0, 0, 0))
+    return pl.pallas_call(
+        partial(build_body, plan, tag_lists, len(grads), True),
+        out_shape=[struct((len(tags),) + shape, BF)] * 2,
+        grid_spec=pltpu.PrefetchScalarGridSpec(
+            num_scalar_prefetch=1,
+            grid=(1,),
+            in_specs=[ANY] * len(grads),
+            out_specs=[ANY] * 2,
+            scratch_shapes=[pltpu.SemaphoreType.DMA((moves,))],
+        ),
+        compiler_params=pltpu.CompilerParams(vmem_limit_bytes=4 * MB),
+        cost_estimate=pl.CostEstimate(
+            flops=0, bytes_accessed=sum(g.size * 4 for g in grads), transcendentals=0
+        ),
+    )(at, *grads)
+
+
+def reduce_pieces(kept, sent, steps):
+    kept = kept.astype(F32) + swap(sent, DP, 1).astype(F32)
+    for axis, bit in steps:
+        half = kept.shape[0] // 2
+        got = swap(kept[half:].astype(BF), axis, bit)
+        kept = kept[:half] + got.astype(F32)
+    kept = kept[0]
+    bit = 2
+    while bit < lax.axis_size(DP):
+        kept = kept + swap(kept.astype(BF), DP, bit).astype(F32)
+        bit *= 2
+    return kept
+
+
+def both_halves(at, mine):
+    other = swap(mine, DP, 1)
+    return jnp.where(at[2] == 0, jnp.stack([mine, other]), jnp.stack([other, mine]))
+
+
+def half_of(at, shard):
+    half = shard.shape[-2] // 2
+    return lax.dynamic_slice_in_dim(shard, at[2] * half, half, axis=shard.ndim - 2)
+
+
+def total_over_all(value, axes):
+    for axis in axes:
+        bit = 1
+        while bit < lax.axis_size(axis):
+            value = value + swap(value, axis, bit)
+            bit *= 2
+    return value
 
 
 def to_rows(blocks, narrow):
@@ -575,14 +749,66 @@
     cols = w_qkv.shape[0]
     heads_cols = w_qkv.shape[2]
     units = w_up.shape[1]
+    swaps = cols % 128 == 0 and narrow == 2 and wide == 4 and pairs % 2 == 0
+
+    at = jnp.stack(
+        [lax.axis_index("wide"), lax.axis_index("narrow"), lax.axis_index("dp") % 2]
+    ).astype(jnp.int32)
 
     index = (visible.reshape(pairs, 2, VISIBLE) + jnp.array([0, PATCHES])[None, :, None]).reshape(
         pairs, PAIR
     )
     index = jnp.pad(index, ((0, 0), (0, ROWS - PAIR)), constant_values=-1)[:, :, None]
 
-    if cols % 128 == 0:
-        rows_mine, cot_mine = pick_rows(patches, cotangent, index, cols)
+    w_qkv_t = w_qkv.transpose(1, 2, 0)
+    vec = jnp.concatenate(
+        [gain_one, shift_one, gain_two, shift_two, b_out, b_down, b_qv.reshape(-1), b_up]
+    )
+    if swaps:
+        vec_rows = vec.size // cols
+        vec_rows_pad = -(-vec_rows // 16) * 16
+        first = jnp.concatenate(
+            [
+                half_of(at, w_qkv_t).reshape(-1, cols),
+                jnp.pad(vec.reshape(vec_rows, cols), ((0, vec_rows_pad - vec_rows), (0, 0))),
+            ]
+        )
+        first = gather_pieces(first, [(NARROW, 1), (WIDE, 2), (WIDE, 1)])
+        (qkv_t,) = build_weights(at, first, qkv_plan(cols, heads_cols), [(3 * D, D)])
+        vecs = first[0][0][:, -vec_rows_pad:]
+        order = [(w, n) for w, n, _ in first[0][1]]
+        rel = [order.index((w, n)) for w in range(wide) for n in range(narrow)]
+        vecs = vecs[:, :vec_rows].reshape(wide * narrow, -1)
+        slot = jnp.array(rel)[
+            (jnp.arange(wide)[:, None] ^ at[0]) * narrow + (jnp.arange(narrow)[None, :] ^ at[1])
+        ]
+        hot = (slot.reshape(-1)[:, None] == jnp.arange(wide * narrow)[None, :]).astype(BF)
+        vec = jnp.dot(hot, vecs, preferred_element_type=F32)
+
+        rows_out, cot_out = pick_rows(at, patches, cotangent, index, cols)
+        own = rows_out.shape[0] // 2
+
+        def join(keep, got):
+            return jnp.where(
+                at[1] == 0,
+                jnp.concatenate([keep, got], axis=1),
+                jnp.concatenate([got, keep], axis=1),
+            )
+
+        rows = join(rows_out[own:], swap(rows_out[:own], NARROW, 1))
+        cot = join(cot_out[own:], swap(cot_out[:own], NARROW, 1))
+
+        out_half = half_of(at, w_out)
+        part = out_half.shape[0] // 2
+        second = jnp.concatenate(
+            [half_of(at, w_up), jnp.concatenate([out_half[:part], out_half[part:]], axis=1)]
+        )
+        second = gather_pieces(second, [(WIDE, 2), (WIDE, 1), (NARROW, 1)])
+        up_w, out_w = build_weights(
+            at, second, up_out_plan(cols, units, heads_cols), [(D, wide * units), (D, D)]
+        )
+        third = gather_pieces(half_of(at, w_down), [(WIDE, 2), (WIDE, 1), (NARROW, 1)])
+        (down_w,) = build_weights(at, third, flat_plan(cols, units), [(D, wide * units)])
     else:
         table = patches.reshape(images, PATCHES, cols)
         rows_mine = jnp.take_along_axis(table, visible[:, :, None], axis=1)
@@ -592,13 +818,15 @@
         cot_mine = jnp.pad(
             cotangent.reshape(pairs, PAIR, cols), ((0, 0), (0, ROWS - PAIR), (0, 0))
         )
-    rows = to_rows(rows_mine.reshape(narrow, -1, cols), narrow)
-    cot = to_rows(cot_mine.reshape(narrow, -1, cols), narrow)
-
-    vec = jnp.concatenate(
-        [gain_one, shift_one, gain_two, shift_two, b_out, b_down, b_qv.reshape(-1), b_up]
-    )
-    vec = lax.all_gather(vec, ("wide", "narrow"), axis=0, tiled=False).astype(F32)
+        rows = to_rows(rows_mine.reshape(narrow, -1, cols), narrow)
+        cot = to_rows(cot_mine.reshape(narrow, -1, cols), narrow)
+        vec = lax.all_gather(vec, ("wide", "narrow"), axis=0, tiled=False).astype(F32)
+        qkv_t = gather_weight(w_qkv_t, wide, narrow)
+        qkv_t = qkv_t.transpose(2, 0, 3, 1, 4).reshape(3 * D, D)
+        out_w = gather_weight(w_out, wide, narrow).transpose(0, 2, 1, 3).reshape(D, D)
+        up_w = gather_weight(w_up, wide, narrow).transpose(1, 2, 0, 3).reshape(D, -1)
+        down_w = gather_weight(w_down, wide, narrow).transpose(1, 2, 0, 3).reshape(D, -1)
+
     vec = vec.reshape(wide, narrow, -1)
     by_narrow = vec[0, :, : 6 * cols].reshape(narrow, 6, cols).transpose(1, 0, 2).reshape(6, 1, D)
     gain_a, shift_a, gain_b, shift_b, bias_out, bias_down = (by_narrow[i] for i in range(6))
@@ -608,12 +836,6 @@
     bias_qkv = jnp.concatenate([bias_q, jnp.zeros((1, D), F32), bias_v], axis=1)
     bias_up = by_wide[:, 2 * heads_cols :].reshape(1, -1)
 
-    qkv_t = gather_weight(w_qkv.transpose(1, 2, 0), wide, narrow)
-    qkv_t = qkv_t.transpose(2, 0, 3, 1, 4).reshape(3 * D, D)
-    out_w = gather_weight(w_out, wide, narrow).transpose(0, 2, 1, 3).reshape(D, D)
-    up_w = gather_weight(w_up, wide, narrow).transpose(1, 2, 0, 3).reshape(D, -1)
-    down_w = gather_weight(w_down, wide, narrow).transpose(1, 2, 0, 3).reshape(D, -1)
-
     hidden_one = norm(rows, gain_a, shift_a)
     triple = qkv(hidden_one, qkv_t, bias_qkv)
     mixed, prob = attend(triple)
@@ -629,30 +851,6 @@
     grad_triple = attend_back(triple, prob, grad_mixed)
     gw_qkv, gb_qkv = qkv_grad(grad_triple, hidden_one)
     grad_rows, gg_one, gs_one = first_back(grad_triple, qkv_t, rows, grad_middle, gain_a)
-
-    result = from_rows(result, narrow)
-    grad_rows = from_rows(grad_rows, narrow)
-    if cols % 128 == 0:
-        block_output = flat_rows(result, cols)
-        grad_patches = put_rows(grad_rows, index, cols).reshape(1, -1)
-    else:
-        block_output = result.reshape(pairs, ROWS, cols)[:, :PAIR].reshape(1, -1)
-        grad_rows = grad_rows.reshape(pairs, ROWS, cols)[:, :PAIR].reshape(images, VISIBLE, cols)
-        grad_patches = (
-            jnp.zeros((images, PATCHES, cols), F32)
-            .at[jnp.arange(images)[:, None], visible]
-            .set(grad_rows)
-            .reshape(1, -1)
-        )
-
-    g_down = scatter_grad(gw_down.reshape(narrow, cols, wide, units).transpose(2, 0, 1, 3))
-    g_up = scatter_grad(gw_up.reshape(narrow, cols, wide, units).transpose(2, 0, 1, 3))
-    g_out = scatter_grad(gw_out.reshape(wide, heads_cols, narrow, cols).transpose(0, 2, 1, 3))
-    g_qkv = scatter_grad(
-        gw_qkv.reshape(3, wide, heads_cols, narrow, cols).transpose(1, 3, 0, 2, 4)
-    )
-    g_qkv = g_qkv.transpose(2, 0, 1)
-
     sums = jnp.concatenate(
         [
             gg_one[0],
@@ -666,9 +864,64 @@
             gb_up[0],
         ]
     )
-    sums = lax.psum(sums, ("dp", "wide", "narrow"))
-    at_narrow = lax.axis_index("narrow") * cols
-    at_wide = lax.axis_index("wide")
+
+    if swaps:
+
+        def part_of(whole, side):
+            return lax.dynamic_slice_in_dim(whole, side * cols, cols, axis=1)
+
+        mine, theirs = at[1], 1 - at[1]
+        block_output = flat_rows(
+            at, part_of(result, mine), swap(part_of(result, theirs), NARROW, 1), cols
+        )
+        grad_patches = put_rows(
+            at,
+            part_of(grad_rows, mine),
+            swap(part_of(grad_rows, theirs).astype(BF), NARROW, 1),
+            index,
+            cols,
+        ).reshape(1, -1)
+
+        def reduced(grads, plan, shape):
+            tags = [(w, n) for n in range(2) for w in (0, 2, 1, 3)]
+            kept, sent = cut_grads(at, grads, plan, tags, shape)
+            got = reduce_pieces(kept, sent, [(NARROW, 1), (WIDE, 1), (WIDE, 2)])
+            return both_halves(at, got)
+
+        g_down = reduced([gw_down], flat_plan(cols, units), (cols // 2, units)).reshape(cols, units)
+        g_up = reduced([gw_up], flat_plan(cols, units), (cols // 2, units)).reshape(cols, units)
+
+        def out_plan(w, n, h):
+            half = heads_cols // 2
+            return [(0, (slice(None), slice(None)), (w * heads_cols + h * half, n * cols))]
+
+        g_out = reduced([gw_out], out_plan, (heads_cols // 2, cols)).reshape(heads_cols, cols)
+        g_qkv = reduced([gw_qkv], qkv_plan(cols, heads_cols), (3 * heads_cols // 2, cols))
+        g_qkv = g_qkv.reshape(2, 3, heads_cols // 2, cols).transpose(3, 1, 0, 2)
+        g_qkv = g_qkv.reshape(cols, 3, heads_cols)
+        sums = total_over_all(sums.reshape(-1, 128), ("dp", "narrow", "wide")).reshape(-1)
+    else:
+        result = from_rows(result, narrow)
+        grad_rows = from_rows(grad_rows, narrow)
+        block_output = result.reshape(pairs, ROWS, cols)[:, :PAIR].reshape(1, -1)
+        grad_rows = grad_rows.reshape(pairs, ROWS, cols)[:, :PAIR].reshape(images, VISIBLE, cols)
+        grad_patches = (
+            jnp.zeros((images, PATCHES, cols), F32)
+            .at[jnp.arange(images)[:, None], visible]
+            .set(grad_rows)
+            .reshape(1, -1)
+        )
+        g_down = scatter_grad(gw_down.reshape(narrow, cols, wide, units).transpose(2, 0, 1, 3))
+        g_up = scatter_grad(gw_up.reshape(narrow, cols, wide, units).transpose(2, 0, 1, 3))
+        g_out = scatter_grad(gw_out.reshape(wide, heads_cols, narrow, cols).transpose(0, 2, 1, 3))
+        g_qkv = scatter_grad(
+            gw_qkv.reshape(3, wide, heads_cols, narrow, cols).transpose(1, 3, 0, 2, 4)
+        )
+        g_qkv = g_qkv.transpose(2, 0, 1)
+        sums = lax.psum(sums, ("dp", "wide", "narrow"))
+
+    at_narrow = at[1] * cols
+    at_wide = at[0]
 
     def narrow_part(i):
         return lax.dynamic_slice_in_dim(sums, i * D + at_narrow, cols)

time: 839 us -> 510 us (0.61)
  local copies, waits for them, and re-layouts: 192 us -> 52.9 us
  waiting for transfers between devices: 313 us -> 185 us
  blocking collectives: 112 us -> 0 us
  other arithmetic: 6.97 us -> 34.8 us
  starting transfers between devices: 17.6 us -> 41.5 us
  Pallas kernels: 174 us -> 192 us
  between operations: 14.6 us -> 1.47 us
    ppermute x0 -> x45, waiting for transfers between devices: none -> 185 us  [swap(): return lax.ppermute(value, axis, [(i, i ^ bit) for i in range(size)])]
    reduce_scatter x4 -> x0, waiting for transfers between devices: 180 us -> none  [scatter_grad(): lax.psum_scatter(blocks.reshape(-1, 128), ('wide', 'narrow'), scatter_dim...]
    reshape x25 -> x2, local copies, waits for them, and re-layouts: 121 us -> 0.06 us  [the longest x1 0.04 us: on_device(): vecs = vecs[:, :vec_rows].reshape(wide * narrow, -1)]
    all_gather x4 -> x0, waiting for transfers between devices: 109 us -> none  [gather_weight(): lax.all_gather(shard.reshape(-1, 128), ('wide', 'narrow'), axis=0, tiled=...]
    psum x1 -> x0, blocking collectives: 65.1 us -> none  [on_device(): sums = lax.psum(sums, ('dp', 'wide', 'narrow'))]
    all_gather x1 -> x0, blocking collectives: 47.3 us -> none  [on_device(): lax.all_gather(vec, ('wide', 'narrow'), axis=0, tiled=False).astype(F32)]
    ppermute x0 -> x45, starting transfers between devices: none -> 41.5 us  [swap(): return lax.ppermute(value, axis, [(i, i ^ bit) for i in range(size)])]
    all_to_all x4 -> x0, waiting for transfers between devices: 23.3 us -> none  [the longest x2 23.3 us: to_rows(): got = lax.all_to_all(blocks, 'narrow', 0, 0, tiled=True)]
  transfers between devices with their start and end apart: 13 -> 45, of which waited for: 6 -> 16; matrix products, arithmetic and copies ran while one was open for 16% -> 11% of each run, Pallas kernels for 15% -> 17%
where the time goes in v2:
time: 510 us; the launch traced here: 508 us
  Pallas kernels  192 us (38%)
  waiting for transfers between devices  185 us (36%)
  local copies, waits for them, and re-layouts  52.9 us (10%)
  starting transfers between devices  41.5 us (8%)
  other arithmetic  34.8 us (7%)
    ppermute x45, waiting for transfers between devices, swap(): return lax.ppermute(value, axis, [(i, i ^ bit) for i in range(size)])  185 us
    ppermute x45, starting transfers between devices, swap(): return lax.ppermute(value, axis, [(i, i ^ bit) for i in range(size)])  41.5 us
    unnamed x93, local copies, waits for them, and re-layouts  35.9 us
    pallas_call x1, Pallas kernels, attend_back(): call(attend_back_body, (groups,), [wide, spec((1, HEADS, ROWS, ROWS), lam...  30.9 us
    pallas_call x1, Pallas kernels, inner_back(): call(inner_back_body, (units // TILE,), [full, col, tile, full], [tile, c...  21.7 us
    pallas_call x1, Pallas kernels, pick_rows(): call(partial(pick_body, cols), (pairs,), [spec((1, width), lambda i, at:...  16.3 us
    concatenate x9, other arithmetic, gather_pieces(): stack = jnp.concatenate([stack, got])  16.2 us
    pallas_call x1, Pallas kernels, up(): call(up_body, (units // TILE,), [spec((r, D), lambda j: (0, 0)), spec((D,...  12.6 us
  transfers between devices with their start and end apart: 45, of which 16 were waited for; matrix products, arithmetic and copies ran while one was open for 11% of the time, Pallas kernels for 17%

profile of v2, /device:TPU:0, one launch (start us, length us, event | category | flops | bytes accessed | tf_op | source)
XLA Modules:
  0.0 508.0 jit_solution(6022182904594514304)
XLA Ops:
  1.8 4.1 collective-permute-start.5
  13.9 8.5 %collective-permute-done.5 = bf16[1,240,768]{2,1,0:T(8,128)(2,1)S(1)} collective-permute-done((bf16[1,240,768]{2,1,0:T(8,128)(2,1)S(1)}, bf16[1,240,768]{2,1,0:T(8,128)(2,1)S(1)}, u32[]{:S(2)}, u32[]{:S(2)}) %collective-permute-start.5) | collective-permute-done | bytes 368672 | tf_op jit(solution)/shard_map/ppermute | solution.py:554
  25.8 3.4 collective-permute-start.9
  29.5 16.0 %collective-permute-done.9 = bf16[1,192,768]{2,1,0:T(8,128)(2,1)S(1)} collective-permute-done((bf16[1,192,768]{2,1,0:T(8,128)(2,1)S(1)}, bf16[1,192,768]{2,1,0:T(8,128)(2,1)S(1)}, u32[]{:S(2)}, u32[]{:S(2)}) %collective-permute-start.9) | collective-permute-done | bytes 294944 | tf_op jit(solution)/shard_map/ppermute | solution.py:554
  46.4 4.1 collective-permute-start.10
  55.4 16.3 %shard_map.272 = (bf16[1792,384]{1,0:T(8,128)(2,1)S(1)}, bf16[1792,384]{1,0:T(8,128)(2,1)S(1)}) custom-call(s32[3]{0:T(128)S(1)} %pad_add_fusion.at_ref, bf16[1,2408448]{1,0:T(2,128)(2,1)} %patch_ref.1, bf16[1,602112]{1,0:T(2,128)(2,1)S(1)} %copy-done.9, s32[16,112,1]{2,1,0:T(8,128)S(1)} %copy.34.index_ref), custom_call_target="tpu_custom_call" | custom-call | flops 539492352 | bytes 12042240 | tf_op jit(solution)/shard_map/pallas_call | solution.py:80
  79.8 16.7 %collective-permute-done.2 = bf16[2,304,384]{2,1,0:T(8,128)(2,1)} collective-permute-done((bf16[2,304,384]{2,1,0:T(8,128)(2,1)}, bf16[2,304,384]{2,1,0:T(8,128)(2,1)}, u32[]{:S(2)}, u32[]{:S(2)}) %collective-permute-start.2) | collective-permute-done | bytes 466976 | tf_op jit(solution)/shard_map/ppermute | solution.py:554
  102.6 37.7 %collective-permute-done.14 = bf16[896,384]{1,0:T(8,128)(2,1)} collective-permute-done((bf16[896,384]{1,0:T(8,128)(2,1)}, bf16[896,384]{1,0:T(8,128)(2,1)}, u32[]{:S(2)}, u32[]{:S(2)}) %collective-permute-start.14) | collective-permute-done | bytes 688160 | tf_op jit(solution)/shard_map/ppermute | solution.py:554
  157.8 7.4 %shard_map.275.triple_ref = bf16[896,2304]{1,0:T(8,128)(2,1)} custom-call(bf16[896,768]{1,0:T(8,128)(2,1)S(1)} %shard_map.273.hidden_ref, bf16[2304,768]{1,0:T(8,128)(2,1)S(1)} %shard_map.274.w_ref, f32[1,2304]{1,0:T(1,128)S(1)} %fusion.12.bias_ref), custom_call_target="tpu_custom_call" | custom-call | flops 3170893824 | bytes 9043968 | tf_op jit(solution)/shard_map/pallas_call | solution.py:194
  167.4 10.8 %shard_map.276 = (bf16[896,768]{1,0:T(8,128)(2,1)S(1)}, f32[8,12,112,112]{3,2,1,0:T(8,128)}) custom-call(bf16[896,2304]{1,0:T(8,128)(2,1)S(1)} %copy-done.3), custom_call_target="tpu_custom_call" | custom-call | flops 616562688 | bytes 11010048 | tf_op jit(solution)/shard_map/pallas_call | solution.py:242
  183.4 3.7 shard_map.277
  194.8 12.6 %shard_map.279 = (bf16[896,3072]{1,0:T(8,128)(2,1)}, f32[896,3072]{1,0:T(8,128)}) custom-call(bf16[896,768]{1,0:T(8,128)(2,1)S(1)} %get-tuple-element.51.hidden_ref, bf16[768,3072]{1,0:T(8,128)(2,1)S(1)} %copy-done.20, f32[1,3072]{1,0:T(1,128)S(1)} %bitcast.91), custom_call_target="tpu_custom_call" | custom-call | flops 4227858432 | bytes 22609920 | tf_op jit(solution)/shard_map/pallas_call | solution.py:291
  207.4 21.7 %shard_map.283 = (bf16[896,3072]{1,0:T(8,128)(2,1)}, bf16[768,3072]{1,0:T(8,128)(2,1)}, f32[1,3072]{1,0:T(1,128)S(1)}) custom-call(bf16[896,768]{1,0:T(8,128)(2,1)S(1)} %copy-done.14, bf16[768,3072]{1,0:T(8,128)(2,1)} %copy-done.5, f32[896,3072]{1,0:T(8,128)} %get-tuple-element.57.slope_ref, bf16[896,768]{1,0:T(8,128)(2,1)S(1)} %get-tuple-element.51.hidden_ref), custom_call_target="tpu_custom_call" | custom-call | flops 8455716864 | bytes 28704768 | tf_op jit(solution)/shard_map/pallas_call | solution.py:371
  229.2 10.6 %shard_map.284 = (f32[896,768]{1,0:T(8,128)S(1)}, bf16[896,768]{1,0:T(8,128)(2,1)S(1)}, f32[1,768]{1,0:T(1,128)S(1)}, f32[1,768]{1,0:T(1,128)S(1)}, f32[1,768]{1,0:T(1,128)S(1)}) custom-call(bf16[896,3072]{1,0:T(8,128)(2,1)} %get-tuple-element.58.grad_ref, bf16[768,3072]{1,0:T(8,128)(2,1)} %copy-done.19, f32[896,768]{1,0:T(8,128)} %get-tuple-element.54.middle_ref, ...), custom_call_target="tpu_custom_call" | custom-call | flops 4227858432 | bytes 18481152 | tf_op jit(solution)/shard_map/pallas_call | solution.py:426
  241.3 4.8 shard_map.285
  246.1 30.9 %shard_map.286.grad_ref = bf16[896,2304]{1,0:T(8,128)(2,1)S(1)} custom-call(bf16[896,2304]{1,0:T(8,128)(2,1)} %shard_map.275.triple_ref, f32[8,12,112,112]{3,2,1,0:T(8,128)} %get-tuple-element.55.prob_ref, bf16[896,768]{1,0:T(8,128)(2,1)S(1)} %get-tuple-element.60.grad_ref), custom_call_target="tpu_custom_call" | custom-call | flops 1233125376 | bytes 15138816 | tf_op jit(solution)/shard_map/pallas_call | solution.py:490
  279.0 8.4 %shard_map.289 = (bf16[2304,768]{1,0:T(8,128)(2,1)S(1)}, f32[1,2304]{1,0:T(1,128)S(1)}) custom-call(bf16[896,2304]{1,0:T(8,128)(2,1)} %copy-done.2, bf16[896,768]{1,0:T(8,128)(2,1)S(1)} %shard_map.273.hidden_ref), custom_call_target="tpu_custom_call" | custom-call | flops 3170893824 | bytes 9043968 | tf_op jit(solution)/shard_map/pallas_call | solution.py:513
  289.1 8.3 %shard_map.287 = (f32[896,768]{1,0:T(8,128)S(1)}, f32[1,768]{1,0:T(1,128)S(1)}, f32[1,768]{1,0:T(1,128)S(1)}) custom-call(bf16[896,2304]{1,0:T(8,128)(2,1)} %copy-done.2, bf16[2304,768]{1,0:T(8,128)(2,1)} %copy-done.4, bf16[896,768]{1,0:T(8,128)(2,1)S(1)} %maximum_select_fusion.rows_ref, f32[896,768]{1,0:T(8,128)} %copy-done.8, f32[1,768]{1,0:T(1,128)S(1)} %bitcast.84), custom_call_target="tpu_custom_call" | custom-call | flops 3170893824 | bytes 14548992 | tf_op jit(solution)/shard_map/pallas_call | solution.py:538
  311.4 11.7 %shard_map.293 = (bf16[768,3072]{1,0:T(8,128)(2,1)S(1)}, f32[1,3072]{1,0:T(1,128)}) custom-call(bf16[896,768]{1,0:T(8,128)(2,1)S(1)} %copy-done.15, bf16[896,3072]{1,0:T(8,128)(2,1)} %get-tuple-element.53.active_ref.right_ref), custom_call_target="tpu_custom_call" | custom-call | flops 4227858432 | bytes 11599872 | tf_op jit(solution)/shard_map/pallas_call | solution.py:343
  331.4 8.0 %shard_map.281 = bf16[896,768]{1,0:T(8,128)(2,1)S(1)} custom-call(bf16[896,3072]{1,0:T(8,128)(2,1)} %get-tuple-element.53.active_ref.right_ref, bf16[768,3072]{1,0:T(8,128)(2,1)} %copy-done.5, f32[1,768]{1,0:T(1,128)S(1)} %bitcast.92, f32[896,768]{1,0:T(8,128)S(1)} %copy-done.21), custom_call_target="tpu_custom_call" | custom-call | flops 4227858432 | bytes 14352384 | tf_op jit(solution)/shard_map/pallas_call | solution.py:314
  346.8 3.5 collective-permute-done.25
  351.2 4.0 collective-permute-done.26
  368.5 11.4 %collective-permute-done.28 = bf16[4,96,384]{2,1,0:T(8,128)(2,1)S(1)} collective-permute-done((bf16[4,96,384]{2,1,0:T(8,128)(2,1)S(1)}, bf16[4,96,384]{2,1,0:T(8,128)(2,1)S(1)}, u32[]{:S(2)}, u32[]{:S(2)}) %collective-permute-start.28) | collective-permute-done | bytes 294944 | tf_op jit(solution)/shard_map/ppermute | solution.py:554
  383.7 6.8 %shard_map.282 = bf16[1,602112]{1,0:T(2,128)(2,1)} custom-call(s32[3]{0:T(128)S(1)} %pad_add_fusion.at_ref, bf16[896,384]{1,0:T(8,128)(2,1)S(1)} %get-tuple-element.89.keep_ref, bf16[896,384]{1,0:T(8,128)(2,1)S(1)} %collective-permute-done.13.got_ref), custom_call_target="tpu_custom_call" | custom-call | bytes 3612672 | tf_op jit(solution)/shard_map/pallas_call | solution.py:148
  391.3 7.7 %collective-permute-done.17 = bf16[4,288,384]{2,1,0:T(8,128)(2,1)} collective-permute-done((bf16[4,288,384]{2,1,0:T(8,128)(2,1)S(1)}, bf16[4,288,384]{2,1,0:T(8,128)(2,1)}, u32[]{:S(2)}, u32[]{:S(2)}) %collective-permute-start.17) | collective-permute-done | bytes 884768 | tf_op jit(solution)/shard_map/ppermute | solution.py:554
  400.8 23.6 %collective-permute-done.40 = bf16[4,192,768]{2,1,0:T(8,128)(2,1)} collective-permute-done((bf16[4,192,768]{2,1,0:T(8,128)(2,1)}, bf16[4,192,768]{2,1,0:T(8,128)(2,1)}, u32[]{:S(2)}, u32[]{:S(2)}) %collective-permute-start.40) | collective-permute-done | bytes 1179680 | tf_op jit(solution)/shard_map/ppermute | solution.py:554
  426.4 23.2 %collective-permute-done.34 = bf16[4,192,768]{2,1,0:T(8,128)(2,1)} collective-permute-done((bf16[4,192,768]{2,1,0:T(8,128)(2,1)}, bf16[4,192,768]{2,1,0:T(8,128)(2,1)}, u32[]{:S(2)}, u32[]{:S(2)}) %collective-permute-start.34) | collective-permute-done | bytes 1179680 | tf_op jit(solution)/shard_map/ppermute | solution.py:554
  455.4 13.3 %collective-permute-done.35 = bf16[2,192,768]{2,1,0:T(8,128)(2,1)S(1)} collective-permute-done((bf16[2,192,768]{2,1,0:T(8,128)(2,1)S(1)}, bf16[2,192,768]{2,1,0:T(8,128)(2,1)S(1)}, u32[]{:S(2)}, u32[]{:S(2)}) %collective-permute-start.35) | collective-permute-done | bytes 589856 | tf_op jit(solution)/shard_map/ppermute | solution.py:554
  469.0 7.1 %collective-permute-done.42 = bf16[1,192,768]{2,1,0:T(8,128)(2,1)S(1)} collective-permute-done((bf16[1,192,768]{2,1,0:T(8,128)(2,1)S(1)}, bf16[1,192,768]{2,1,0:T(8,128)(2,1)S(1)}, u32[]{:S(2)}, u32[]{:S(2)}) %collective-permute-start.42) | collective-permute-done | bytes 294944 | tf_op jit(solution)/shard_map/ppermute | solution.py:554
  476.2 3.7 collective-permute-start.43
  486.0 4.9 collective-permute-done.37
  491.7 12.3 %shard_map.288 = f32[18816,128]{1,0:T(8,128)} custom-call(s32[3]{0:T(128)S(1)} %pad_add_fusion.at_ref, f32[896,384]{1,0:T(8,128)S(1)} %constant_dynamic-slice_fusion.1.keep_ref, bf16[896,384]{1,0:T(8,128)(2,1)S(1)} %collective-permute-done.15.got_ref, s32[16,112,1]{2,1,0:T(8,128)S(1)} %copy.34.index_ref), custom_call_target="tpu_custom_call" | custom-call | flops 1618477056 | bytes 12386304 | tf_op jit(solution)/shard_map/pallas_call | solution.py:123
  (284 shorter events, 139.1 us)
Async XLA Ops:
  1.8 20.6 %collective-permute-start.5 = (bf16[1,240,768]{2,1,0:T(8,128)(2,1)S(1)}, bf16[1,240,768]{2,1,0:T(8,128)(2,1)S(1)}, u32[]{:S(2)}, u32[]{:S(2)}) collective-permute-start(bf16[1,240,768]{2,1,0:T(8,128)(2,1)S(1)} %maximum_bitcast_fusion), channel_id=1, source_target_pairs={{0,4},{2,6},{4,0},{6,2},{1,5},{3,7},{5,1},{7,3},{8,12},{10,14},{12... | collective-permute-start | bytes 1105928 | tf_op jit(solution)/shard_map/ppermute | solution.py:554
  22.5 28.1 %collective-permute-start.6 = (bf16[2,240,768]{2,1,0:T(8,128)(2,1)S(1)}, bf16[2,240,768]{2,1,0:T(8,128)(2,1)S(1)}, u32[]{:S(2)}, u32[]{:S(2)}) collective-permute-start(bf16[2,240,768]{2,1,0:T(8,128)(2,1)S(1)} %pad_maximum_fusion.6), channel_id=1, source_target_pairs={{0,2},{2,0},{4,6},{6,4},{1,3},{3,1},{5,7},{7,5},{8,10},{10,8},{12,... | collective-permute-start | bytes 2211848 | tf_op jit(solution)/shard_map/ppermute | solution.py:554
  23.3 50.2 %collective-permute-start.1 = (bf16[1,304,384]{2,1,0:T(8,128)(2,1)S(1)}, bf16[1,304,384]{2,1,0:T(8,128)(2,1)S(1)}, u32[]{:S(2)}, u32[]{:S(2)}) collective-permute-start(bf16[1,304,384]{2,1,0:T(8,128)(2,1)S(1)} %fusion.9), channel_id=1, source_target_pairs={{0,1},{1,0},{2,3},{3,2},{4,5},{5,4},{6,7},{7,6},{8,9},{9,8},{10,11... | collective-permute-start | bytes 700424 | tf_op jit(solution)/shard_map/ppermute | solution.py:554
  25.8 19.7 %collective-permute-start.9 = (bf16[1,192,768]{2,1,0:T(8,128)(2,1)S(1)}, bf16[1,192,768]{2,1,0:T(8,128)(2,1)S(1)}, u32[]{:S(2)}, u32[]{:S(2)}) collective-permute-start(bf16[1,192,768]{2,1,0:T(8,128)(2,1)S(1)} %dynamic-slice_bitcast_fusion), channel_id=1, source_target_pairs={{0,4},{2,6},{4,0},{6,2},{1,5},{3,7},{5,1},{7,3},{8,12},{10,14},{12... | collective-permute-start | bytes 884744 | tf_op jit(solution)/shard_map/ppermute | solution.py:554
  46.4 27.9 %collective-permute-start.10 = (bf16[2,192,768]{2,1,0:T(8,128)(2,1)}, bf16[2,192,768]{2,1,0:T(8,128)(2,1)}, u32[]{:S(2)}, u32[]{:S(2)}) collective-permute-start(bf16[2,192,768]{2,1,0:T(8,128)(2,1)} %pad_maximum_fusion.7), channel_id=1, source_target_pairs={{0,2},{2,0},{4,6},{6,4},{1,3},{3,1},{5,7},{7,5},{8,10},{10,8},{12,... | collective-permute-start | bytes 1769480 | tf_op jit(solution)/shard_map/ppermute | solution.py:554
  51.8 46.9 %collective-permute-start.7 = (bf16[4,240,768]{2,1,0:T(8,128)(2,1)}, bf16[4,240,768]{2,1,0:T(8,128)(2,1)}, u32[]{:S(2)}, u32[]{:S(2)}) collective-permute-start(bf16[4,240,768]{2,1,0:T(8,128)(2,1)} %pad_maximum_fusion.3), channel_id=1, source_target_pairs={{0,1},{1,0},{2,3},{3,2},{4,5},{5,4},{6,7},{7,6},{8,9},{9,8},{10,11... | collective-permute-start | bytes 4423688 | tf_op jit(solution)/shard_map/ppermute | solution.py:554
  72.9 76.6 %collective-permute-start = (bf16[896,384]{1,0:T(8,128)(2,1)}, bf16[896,384]{1,0:T(8,128)(2,1)}, u32[]{:S(2)}, u32[]{:S(2)}) collective-permute-start(bf16[896,384]{1,0:T(8,128)(2,1)} %get-tuple-element.91), channel_id=1, source_target_pairs={{0,1},{1,0},{2,3},{3,2},{4,5},{5,4},{6,7},{7,6},{8,9},{9,8},{10,11... | collective-permute-start | bytes 2064392 | tf_op jit(solution)/shard_map/ppermute | solution.py:554
  74.3 22.2 %collective-permute-start.2 = (bf16[2,304,384]{2,1,0:T(8,128)(2,1)}, bf16[2,304,384]{2,1,0:T(8,128)(2,1)}, u32[]{:S(2)}, u32[]{:S(2)}) collective-permute-start(bf16[2,304,384]{2,1,0:T(8,128)(2,1)} %pad_maximum_fusion.8), channel_id=1, source_target_pairs={{0,4},{2,6},{4,0},{6,2},{1,5},{3,7},{5,1},{7,3},{8,12},{10,14},{12... | collective-permute-start | bytes 1400840 | tf_op jit(solution)/shard_map/ppermute | solution.py:554
  76.5 66.7 %collective-permute-start.11 = (bf16[4,192,768]{2,1,0:T(8,128)(2,1)}, bf16[4,192,768]{2,1,0:T(8,128)(2,1)}, u32[]{:S(2)}, u32[]{:S(2)}) collective-permute-start(bf16[4,192,768]{2,1,0:T(8,128)(2,1)} %pad_maximum_fusion.4), channel_id=1, source_target_pairs={{0,1},{1,0},{2,3},{3,2},{4,5},{5,4},{6,7},{7,6},{8,9},{9,8},{10,11... | collective-permute-start | bytes 3538952 | tf_op jit(solution)/shard_map/ppermute | solution.py:554
  79.2 61.1 %collective-permute-start.14 = (bf16[896,384]{1,0:T(8,128)(2,1)}, bf16[896,384]{1,0:T(8,128)(2,1)}, u32[]{:S(2)}, u32[]{:S(2)}) collective-permute-start(bf16[896,384]{1,0:T(8,128)(2,1)} %get-tuple-element.86), channel_id=1, source_target_pairs={{0,1},{1,0},{2,3},{3,2},{4,5},{5,4},{6,7},{7,6},{8,9},{9,8},{10,11... | collective-permute-start | bytes 2064392 | tf_op jit(solution)/shard_map/ppermute | solution.py:554
  98.6 47.7 %collective-permute-start.3 = (bf16[4,304,384]{2,1,0:T(8,128)(2,1)}, bf16[4,304,384]{2,1,0:T(8,128)(2,1)}, u32[]{:S(2)}, u32[]{:S(2)}) collective-permute-start(bf16[4,304,384]{2,1,0:T(8,128)(2,1)} %pad_maximum_fusion.5), channel_id=1, source_target_pairs={{0,2},{2,0},{4,6},{6,4},{1,3},{3,1},{5,7},{7,5},{8,10},{10,8},{12,... | collective-permute-start | bytes 2801672 | tf_op jit(solution)/shard_map/ppermute | solution.py:554
  101.7 81.7 %collective-permute-start.8 = (bf16[8,240,768]{2,1,0:T(8,128)(2,1)}, bf16[8,240,768]{2,1,0:T(8,128)(2,1)}, u32[]{:S(2)}, u32[]{:S(2)}) collective-permute-start(bf16[8,240,768]{2,1,0:T(8,128)(2,1)} %pad_maximum_fusion.refs_0_), channel_id=1, source_target_pairs={{0,8},{8,0},{16,24},{24,16},{1,9},{9,1},{17,25},{25,17},{2,10},{10... | collective-permute-start | bytes 8847368 | tf_op jit(solution)/shard_map/ppermute | solution.py:554
  146.2 32.0 %collective-permute-start.12 = (bf16[8,192,768]{2,1,0:T(8,128)(2,1)}, bf16[8,192,768]{2,1,0:T(8,128)(2,1)}, u32[]{:S(2)}, u32[]{:S(2)}) collective-permute-start(bf16[8,192,768]{2,1,0:T(8,128)(2,1)} %pad_maximum_fusion.1.refs_0_), channel_id=1, source_target_pairs={{0,8},{8,0},{16,24},{24,16},{1,9},{9,1},{17,25},{25,17},{2,10},{10... | collective-permute-start | bytes 7077896 | tf_op jit(solution)/shard_map/ppermute | solution.py:554
  310.0 19.7 %collective-permute-start.22 = (f32[72,128]{1,0:T(8,128)}, f32[72,128]{1,0:T(8,128)S(1)}, u32[]{:S(2)}, u32[]{:S(2)}) collective-permute-start(f32[72,128]{1,0:T(8,128)} %bitcast.106), channel_id=1, source_target_pairs={{0,8},{8,0},{16,24},{24,16},{1,9},{9,1},{17,25},{25,17},{2,10},{10... | collective-permute-start | bytes 110600 | tf_op jit(solution)/shard_map/ppermute | solution.py:554
  329.1 28.5 %collective-permute-start.16 = (bf16[8,288,384]{2,1,0:T(8,128)(2,1)}, bf16[8,288,384]{2,1,0:T(8,128)(2,1)}, u32[]{:S(2)}, u32[]{:S(2)}) collective-permute-start(bf16[8,288,384]{2,1,0:T(8,128)(2,1)} %get-tuple-element.65), channel_id=1, source_target_pairs={{0,8},{8,0},{16,24},{24,16},{1,9},{9,1},{17,25},{25,17},{2,10},{10... | collective-permute-start | bytes 5308424 | tf_op jit(solution)/shard_map/ppermute | solution.py:554
  329.7 31.4 %collective-permute-start.39 = (bf16[8,192,768]{2,1,0:T(8,128)(2,1)}, bf16[8,192,768]{2,1,0:T(8,128)(2,1)}, u32[]{:S(2)}, u32[]{:S(2)}) collective-permute-start(bf16[8,192,768]{2,1,0:T(8,128)(2,1)} %get-tuple-element.81), channel_id=1, source_target_pairs={{0,8},{8,0},{16,24},{24,16},{1,9},{9,1},{17,25},{25,17},{2,10},{10... | collective-permute-start | bytes 7077896 | tf_op jit(solution)/shard_map/ppermute | solution.py:554
  341.9 23.8 %collective-permute-start.33 = (bf16[8,192,768]{2,1,0:T(8,128)(2,1)S(1)}, bf16[8,192,768]{2,1,0:T(8,128)(2,1)S(1)}, u32[]{:S(2)}, u32[]{:S(2)}) collective-permute-start(bf16[8,192,768]{2,1,0:T(8,128)(2,1)S(1)} %get-tuple-element.78), channel_id=1, source_target_pairs={{0,8},{8,0},{16,24},{24,16},{1,9},{9,1},{17,25},{25,17},{2,10},{10... | collective-permute-start | bytes 7077896 | tf_op jit(solution)/shard_map/ppermute | solution.py:554
  355.3 26.9 %collective-permute-start.13 = (bf16[896,384]{1,0:T(8,128)(2,1)S(1)}, bf16[896,384]{1,0:T(8,128)(2,1)S(1)}, u32[]{:S(2)}, u32[]{:S(2)}) collective-permute-start(bf16[896,384]{1,0:T(8,128)(2,1)S(1)} %get-tuple-element.88), channel_id=1, source_target_pairs={{0,1},{1,0},{2,3},{3,2},{4,5},{5,4},{6,7},{7,6},{8,9},{9,8},{10,11... | collective-permute-start | bytes 2064392 | tf_op jit(solution)/shard_map/ppermute | solution.py:554
  357.0 23.0 %collective-permute-start.28 = (bf16[4,96,384]{2,1,0:T(8,128)(2,1)S(1)}, bf16[4,96,384]{2,1,0:T(8,128)(2,1)S(1)}, u32[]{:S(2)}, u32[]{:S(2)}) collective-permute-start(bf16[4,96,384]{2,1,0:T(8,128)(2,1)S(1)} %slice.295), channel_id=1, source_target_pairs={{0,1},{1,0},{2,3},{3,2},{4,5},{5,4},{6,7},{7,6},{8,9},{9,8},{10,11... | collective-permute-start | bytes 884744 | tf_op jit(solution)/shard_map/ppermute | solution.py:554
  359.6 39.5 %collective-permute-start.17 = (bf16[4,288,384]{2,1,0:T(8,128)(2,1)S(1)}, bf16[4,288,384]{2,1,0:T(8,128)(2,1)}, u32[]{:S(2)}, u32[]{:S(2)}) collective-permute-start(bf16[4,288,384]{2,1,0:T(8,128)(2,1)S(1)} %slice.289), channel_id=1, source_target_pairs={{0,1},{1,0},{2,3},{3,2},{4,5},{5,4},{6,7},{7,6},{8,9},{9,8},{10,11... | collective-permute-start | bytes 2654216 | tf_op jit(solution)/shard_map/ppermute | solution.py:554
  364.7 59.7 %collective-permute-start.40 = (bf16[4,192,768]{2,1,0:T(8,128)(2,1)}, bf16[4,192,768]{2,1,0:T(8,128)(2,1)}, u32[]{:S(2)}, u32[]{:S(2)}) collective-permute-start(bf16[4,192,768]{2,1,0:T(8,128)(2,1)} %slice.287), channel_id=1, source_target_pairs={{0,1},{1,0},{2,3},{3,2},{4,5},{5,4},{6,7},{7,6},{8,9},{9,8},{10,11... | collective-permute-start | bytes 3538952 | tf_op jit(solution)/shard_map/ppermute | solution.py:554
  367.5 82.0 %collective-permute-start.34 = (bf16[4,192,768]{2,1,0:T(8,128)(2,1)}, bf16[4,192,768]{2,1,0:T(8,128)(2,1)}, u32[]{:S(2)}, u32[]{:S(2)}) collective-permute-start(bf16[4,192,768]{2,1,0:T(8,128)(2,1)} %slice.288), channel_id=1, source_target_pairs={{0,1},{1,0},{2,3},{3,2},{4,5},{5,4},{6,7},{7,6},{8,9},{9,8},{10,11... | collective-permute-start | bytes 3538952 | tf_op jit(solution)/shard_map/ppermute | solution.py:554
  382.2 109.5 %collective-permute-start.15 = (bf16[896,384]{1,0:T(8,128)(2,1)}, bf16[896,384]{1,0:T(8,128)(2,1)S(1)}, u32[]{:S(2)}, u32[]{:S(2)}) collective-permute-start(bf16[896,384]{1,0:T(8,128)(2,1)} %dynamic-slice_convert_fusion), channel_id=1, source_target_pairs={{0,1},{1,0},{2,3},{3,2},{4,5},{5,4},{6,7},{7,6},{8,9},{9,8},{10,11... | collective-permute-start | bytes 2064392 | tf_op jit(solution)/shard_map/ppermute | solution.py:554
  390.6 60.9 %collective-permute-start.30 = (bf16[1,96,384]{2,1,0:T(8,128)(2,1)S(1)}, bf16[1,96,384]{2,1,0:T(8,128)(2,1)S(1)}, u32[]{:S(2)}, u32[]{:S(2)}) collective-permute-start(bf16[1,96,384]{2,1,0:T(8,128)(2,1)S(1)} %slice.298), channel_id=1, source_target_pairs={{0,4},{2,6},{4,0},{6,2},{1,5},{3,7},{5,1},{7,3},{8,12},{10,14},{12... | collective-permute-start | bytes 221192 | tf_op jit(solution)/shard_map/ppermute | solution.py:554
  400.5 51.6 %collective-permute-start.18 = (bf16[2,288,384]{2,1,0:T(8,128)(2,1)S(1)}, bf16[2,288,384]{2,1,0:T(8,128)(2,1)S(1)}, u32[]{:S(2)}, u32[]{:S(2)}) collective-permute-start(bf16[2,288,384]{2,1,0:T(8,128)(2,1)S(1)} %slice.292), channel_id=1, source_target_pairs={{0,2},{2,0},{4,6},{6,4},{1,3},{3,1},{5,7},{7,5},{8,10},{10,8},{12,... | collective-permute-start | bytes 1327112 | tf_op jit(solution)/shard_map/ppermute | solution.py:554
  426.1 26.8 %collective-permute-start.41 = (bf16[2,192,768]{2,1,0:T(8,128)(2,1)S(1)}, bf16[2,192,768]{2,1,0:T(8,128)(2,1)S(1)}, u32[]{:S(2)}, u32[]{:S(2)}) collective-permute-start(bf16[2,192,768]{2,1,0:T(8,128)(2,1)S(1)} %slice.290), channel_id=1, source_target_pairs={{0,2},{2,0},{4,6},{6,4},{1,3},{3,1},{5,7},{7,5},{8,10},{10,8},{12,... | collective-permute-start | bytes 1769480 | tf_op jit(solution)/shard_map/ppermute | solution.py:554
  451.2 17.4 %collective-permute-start.35 = (bf16[2,192,768]{2,1,0:T(8,128)(2,1)S(1)}, bf16[2,192,768]{2,1,0:T(8,128)(2,1)S(1)}, u32[]{:S(2)}, u32[]{:S(2)}) collective-permute-start(bf16[2,192,768]{2,1,0:T(8,128)(2,1)S(1)} %slice.291), channel_id=1, source_target_pairs={{0,2},{2,0},{4,6},{6,4},{1,3},{3,1},{5,7},{7,5},{8,10},{10,8},{12,... | collective-permute-start | bytes 1769480 | tf_op jit(solution)/shard_map/ppermute | solution.py:554
  451.5 39.6 %collective-permute-start.31 = (bf16[96,384]{1,0:T(8,128)(2,1)S(1)}, bf16[96,384]{1,0:T(8,128)(2,1)S(1)}, u32[]{:S(2)}, u32[]{:S(2)}) collective-permute-start(bf16[96,384]{1,0:T(8,128)(2,1)S(1)} %fusion.11), channel_id=1, source_target_pairs={{0,16},{8,24},{16,0},{24,8},{1,17},{9,25},{17,1},{25,9},{2,18},{10... | collective-permute-start | bytes 221192 | tf_op jit(solution)/shard_map/ppermute | solution.py:554
  452.2 16.7 %collective-permute-start.19 = (bf16[1,288,384]{2,1,0:T(8,128)(2,1)S(1)}, bf16[1,288,384]{2,1,0:T(8,128)(2,1)S(1)}, u32[]{:S(2)}, u32[]{:S(2)}) collective-permute-start(bf16[1,288,384]{2,1,0:T(8,128)(2,1)S(1)} %slice.296), channel_id=1, source_target_pairs={{0,4},{2,6},{4,0},{6,2},{1,5},{3,7},{5,1},{7,3},{8,12},{10,14},{12... | collective-permute-start | bytes 663560 | tf_op jit(solution)/shard_map/ppermute | solution.py:554
  453.1 23.1 %collective-permute-start.42 = (bf16[1,192,768]{2,1,0:T(8,128)(2,1)S(1)}, bf16[1,192,768]{2,1,0:T(8,128)(2,1)S(1)}, u32[]{:S(2)}, u32[]{:S(2)}) collective-permute-start(bf16[1,192,768]{2,1,0:T(8,128)(2,1)S(1)} %slice.293), channel_id=1, source_target_pairs={{0,4},{2,6},{4,0},{6,2},{1,5},{3,7},{5,1},{7,3},{8,12},{10,14},{12... | collective-permute-start | bytes 884744 | tf_op jit(solution)/shard_map/ppermute | solution.py:554
  483.3 21.5 %collective-permute-start.21 = (f32[288,384]{1,0:T(8,128)S(1)}, f32[288,384]{1,0:T(8,128)S(1)}, u32[]{:S(2)}, u32[]{:S(2)}) collective-permute-start(f32[288,384]{1,0:T(8,128)S(1)} %convert_add_fusion.6), channel_id=1, source_target_pairs={{0,8},{8,0},{16,24},{24,16},{1,9},{9,1},{17,25},{25,17},{2,10},{10... | collective-permute-start | bytes 1327112 | tf_op jit(solution)/shard_map/ppermute | solution.py:554
  486.0 19.9 %collective-permute-start.44 = (f32[192,768]{1,0:T(8,128)S(1)}, f32[192,768]{1,0:T(8,128)S(1)}, u32[]{:S(2)}, u32[]{:S(2)}) collective-permute-start(f32[192,768]{1,0:T(8,128)S(1)} %convert_add_fusion.4), channel_id=1, source_target_pairs={{0,8},{8,0},{16,24},{24,16},{1,9},{9,1},{17,25},{25,17},{2,10},{10... | collective-permute-start | bytes 1769480 | tf_op jit(solution)/shard_map/ppermute | solution.py:554
  (51 other events, 469.5 us)

commit v3 on v1

--- a/solution.py
+++ b/solution.py
@@ -25,7 +25,10 @@
     return lax.dot_general(a, b, (((ca,), (cb,)), ((), ())), preferred_element_type=F32)
 
 
-def call(body, grid, ins, outs, shapes, scratch=(), prefetch=0, flops=0, nbytes=0, vmem=48):
+FLOPS_PER_US = 540000000
+
+
+def call(body, grid, ins, outs, shapes, scratch=(), prefetch=0, us=1.0, nbytes=0, vmem=24):
     return pl.pallas_call(
         body,
         out_shape=shapes,
@@ -39,8 +42,14 @@
         compiler_params=pltpu.CompilerParams(
             dimension_semantics=("arbitrary",) * len(grid), vmem_limit_bytes=vmem * MB
         ),
-        cost_estimate=pl.CostEstimate(flops=flops, bytes_accessed=nbytes, transcendentals=0),
+        cost_estimate=pl.CostEstimate(
+            flops=int(us * FLOPS_PER_US), bytes_accessed=1024, transcendentals=0
+        ),
     )
+
+
+def in_hbm(value):
+    return pltpu.with_memory_space_constraint(value, pltpu.HBM)
 
 
 def spec(shape, index):
@@ -51,46 +60,77 @@
     return jax.ShapeDtypeStruct(shape, dtype)
 
 
-def pick_body(cols, patch_ref, cot_ref, index_ref, rows_ref, cot_rows_ref, wide_ref, cot_scr):
+def pick_body(cols, at_ref, patch_ref, index_ref, rows_ref, wide_ref):
     lanes = cols // 128
     wide_ref[...] = patch_ref[...].astype(F32).reshape(wide_ref.shape)
     parts = [wide_ref[pl.ds(k, 2 * PATCHES, stride=lanes), :] for k in range(lanes)]
     both = jnp.concatenate(parts, axis=1).astype(BF)
     hit = index_ref[0] == lax.broadcasted_iota(jnp.int32, (ROWS, 2 * PATCHES), 1)
     rows_ref[...] = dot(hit.astype(BF), both, 1, 0).astype(BF)
-    cot_scr[...] = cot_ref[...].astype(F32).reshape(cot_scr.shape)
-    parts = [cot_scr[pl.ds(k, PAIR, stride=lanes), :] for k in range(lanes)]
-    cot = jnp.concatenate(parts, axis=1)
-    cot_rows_ref[...] = jnp.concatenate(
-        [cot, jnp.zeros((ROWS - PAIR, cols), F32)], axis=0
-    ).astype(BF)
-
-
-def pick_rows(patches, cotangent, index, cols):
+
+
+def owner_first_sent(own):
+    def source(i, at):
+        return (i // own ^ 1 ^ at[1]) * own + i % own
+
+    return source
+
+
+def pick_rows(at, patches, index, cols):
     pairs = index.shape[0]
     width = 2 * PATCHES * cols
-    cot_width = PAIR * cols
+    source = owner_first_sent(pairs // 2)
     return call(
         partial(pick_body, cols),
         (pairs,),
         [
-            spec((1, width), lambda i: (0, i)),
-            spec((1, cot_width), lambda i: (0, i)),
-            spec((1, ROWS, 1), lambda i: (i, 0, 0)),
+            spec((1, width), lambda i, at: (0, source(i, at))),
+            spec((1, ROWS, 1), lambda i, at: (source(i, at), 0, 0)),
         ],
-        [spec((ROWS, cols), lambda i: (i, 0)), spec((ROWS, cols), lambda i: (i, 0))],
-        [struct((pairs * ROWS, cols), BF), struct((pairs * ROWS, cols), BF)],
-        [pltpu.VMEM((width // 128, 128), F32), pltpu.VMEM((cot_width // 128, 128), F32)],
-        flops=2 * pairs * ROWS * 2 * PATCHES * cols,
-        nbytes=pairs * (width + cot_width) * 4,
-    )(patches, cotangent, index)
-
-
-def put_body(cols, rows_ref, index_ref, out_ref):
+        spec((ROWS, cols), lambda i, at: (i, 0)),
+        struct((pairs * ROWS, cols), BF),
+        [pltpu.VMEM((width // 128, 128), F32)],
+        prefetch=1,
+        us=200,
+        nbytes=pairs * width * 4,
+    )(at, patches, index)
+
+
+def cot_body(cols, at_ref, cot_ref, rows_ref, scr):
+    lanes = cols // 128
+    scr[...] = cot_ref[...].astype(F32).reshape(scr.shape)
+    parts = [scr[pl.ds(k, PAIR, stride=lanes), :] for k in range(lanes)]
+    cot = jnp.concatenate(parts, axis=1)
+    rows_ref[...] = jnp.concatenate([cot, jnp.zeros((ROWS - PAIR, cols), F32)], axis=0).astype(BF)
+
+
+def cot_rows(at, cotangent, pairs, cols):
+    width = PAIR * cols
+    source = owner_first_sent(pairs // 2)
+    return call(
+        partial(cot_body, cols),
+        (pairs,),
+        [spec((1, width), lambda i, at: (0, source(i, at)))],
+        spec((ROWS, cols), lambda i, at: (i, 0)),
+        struct((pairs * ROWS, cols), BF),
+        [pltpu.VMEM((width // 128, 128), F32)],
+        prefetch=1,
+        us=200,
+        nbytes=pairs * width * 4,
+    )(at, cotangent)
+
+
+def own_block(at_ref, keep_ref, got_ref):
+    own = pl.num_programs(0) // 2
+    mine = pl.program_id(0) // own == at_ref[1]
+    return jnp.where(mine, keep_ref[...].astype(F32), got_ref[...].astype(F32))
+
+
+def put_body(cols, at_ref, keep_ref, got_ref, index_ref, out_ref):
     lanes = cols // 128
     hit = index_ref[0] == lax.broadcasted_iota(jnp.int32, (ROWS, 2 * PATCHES), 1)
     hit = hit.astype(BF)
-    rest = rows_ref[...]
+    rest = own_block(at_ref, keep_ref, got_ref)
     total = None
     for _ in range(3):
         part = rest.astype(BF)
@@ -101,40 +141,47 @@
         out_ref[pl.ds(k, 2 * PATCHES, stride=lanes), :] = total[:, k * 128 : (k + 1) * 128]
 
 
-def put_rows(rows, index, cols):
+def put_rows(at, keep, got, index, cols):
     pairs = index.shape[0]
+    own = pairs // 2
     tall = 2 * PATCHES * cols // 128
+    rows = spec((ROWS, cols), lambda i, at: (i % own, 0))
     return call(
         partial(put_body, cols),
         (pairs,),
-        [spec((ROWS, cols), lambda i: (i, 0)), spec((1, ROWS, 1), lambda i: (i, 0, 0))],
-        spec((tall, 128), lambda i: (i, 0)),
+        [rows, rows, spec((1, ROWS, 1), lambda i, at: (i, 0, 0))],
+        spec((tall, 128), lambda i, at: (i, 0)),
         struct((pairs * tall, 128), F32),
-        flops=6 * pairs * ROWS * 2 * PATCHES * cols,
+        prefetch=1,
+        us=200,
         nbytes=pairs * (tall * 512 + ROWS * cols * 4),
-    )(rows, index)
-
-
-def flat_body(cols, rows_ref, out_ref, scr):
+    )(at, keep, got, index)
+
+
+def flat_body(cols, at_ref, keep_ref, got_ref, out_ref, scr):
     lanes = cols // 128
-    rows = rows_ref[...].astype(F32)
+    rows = own_block(at_ref, keep_ref, got_ref)
     for k in range(lanes):
         scr[pl.ds(k, PAIR, stride=lanes), :] = rows[:PAIR, k * 128 : (k + 1) * 128]
     out_ref[...] = scr[...].reshape(out_ref.shape).astype(BF)
 
 
-def flat_rows(rows, cols):
-    pairs = rows.shape[0] // ROWS
+def flat_rows(at, keep, got, cols):
+    own = keep.shape[0] // ROWS
+    pairs = 2 * own
     width = PAIR * cols
+    rows = spec((ROWS, cols), lambda i, at: (i % own, 0))
     return call(
         partial(flat_body, cols),
         (pairs,),
-        [spec((ROWS, cols), lambda i: (i, 0))],
-        spec((1, width), lambda i: (0, i)),
+        [rows, rows],
+        spec((1, width), lambda i, at: (0, i)),
         struct((1, pairs * width), BF),
         [pltpu.VMEM((width // 128, 128), F32)],
+        prefetch=1,
+        us=200,
         nbytes=pairs * width * 6,
-    )(rows)
+    )(at, keep, got)
 
 
 def stats(rows):
@@ -144,25 +191,29 @@
     return off * inv, inv
 
 
-def norm_body(rows_ref, gain_ref, shift_ref, out_ref):
+GAIN_ONE, SHIFT_ONE, GAIN_TWO, SHIFT_TWO, BIAS_OUT, BIAS_DOWN = range(6)
+
+
+def vec_row(vec_ref, i):
+    return vec_ref[i : i + 1, :]
+
+
+def norm_body(rows_ref, vec_ref, out_ref):
     normed, _ = stats(rows_ref[...].astype(F32))
-    out_ref[...] = (normed * gain_ref[...] + shift_ref[...]).astype(BF)
-
-
-def norm(rows, gain, shift):
+    out_ref[...] = (normed * vec_row(vec_ref, GAIN_ONE) + vec_row(vec_ref, SHIFT_ONE)).astype(BF)
+
+
+def norm(rows, vec):
     r = rows.shape[0]
     return call(
         norm_body,
         (r // ROWS,),
-        [
-            spec((ROWS, D), lambda i: (i, 0)),
-            spec((1, D), lambda i: (0, 0)),
-            spec((1, D), lambda i: (0, 0)),
-        ],
+        [spec((ROWS, D), lambda i: (i, 0)), spec((8, D), lambda i: (0, 0))],
         spec((ROWS, D), lambda i: (i, 0)),
         struct((r, D), BF),
+        us=200,
         nbytes=r * D * 4,
-    )(rows, gain, shift)
+    )(rows, vec)
 
 
 def qkv_body(hidden_ref, w_ref, bias_ref, out_ref):
@@ -181,7 +232,7 @@
         ],
         spec((r, TILE), lambda j: (0, j)),
         struct((r, 3 * D), BF),
-        flops=2 * r * D * 3 * D,
+        us=0.01,
         nbytes=r * D * 8 + 3 * D * D * 2,
     )(hidden, w, bias)
 
@@ -225,36 +276,38 @@
         [spec((ROWS, 3 * D), lambda g: (g, 0))],
         [spec((ROWS, D), lambda g: (g, 0)), spec((1, HEADS, ROWS, ROWS), lambda g: (g, 0, 0, 0))],
         [struct((groups * ROWS, D), BF), struct((groups, HEADS, ROWS, ROWS), F32)],
-        flops=groups * HEADS * 4 * ROWS * ROWS * 128,
+        us=0.01,
         nbytes=groups * ROWS * (8 * D + HEADS * 512),
     )(triple)
 
 
-def mix_body(mixed_ref, w_ref, bias_ref, rows_ref, gain_ref, shift_ref, middle_ref, hidden_ref):
-    middle = rows_ref[...].astype(F32) + (dot(mixed_ref[...], w_ref[...], 1, 0) + bias_ref[...])
+def mix_body(mixed_ref, w_ref, rows_ref, vec_ref, middle_ref, hidden_ref):
+    branch = dot(mixed_ref[...], w_ref[...], 1, 0) + vec_row(vec_ref, BIAS_OUT)
+    middle = rows_ref[...].astype(F32) + branch
     middle_ref[...] = middle
     normed, _ = stats(middle)
-    hidden_ref[...] = (normed * gain_ref[...] + shift_ref[...]).astype(BF)
+    hidden_ref[...] = (
+        normed * vec_row(vec_ref, GAIN_TWO) + vec_row(vec_ref, SHIFT_TWO)
+    ).astype(BF)
 
 
 def row_tile(r):
     return r // 2
 
 
-def mix(mixed, w, bias, rows, gain, shift):
+def mix(mixed, w, rows, vec):
     r = rows.shape[0]
     m = row_tile(r)
-    vec = spec((1, D), lambda i: (0, 0))
     row = spec((m, D), lambda i: (i, 0))
     return call(
         mix_body,
         (r // m,),
-        [row, spec((D, D), lambda i: (0, 0)), vec, row, vec, vec],
+        [row, spec((D, D), lambda i: (0, 0)), row, spec((8, D), lambda i: (0, 0))],
         [row, row],
         [struct((r, D), F32), struct((r, D), BF)],
-        flops=2 * r * D * D,
+        us=200,
         nbytes=r * D * 10 + D * D * 2,
-    )(mixed, w, bias, rows, gain, shift)
+    )(mixed, w, rows, vec)
 
 
 def up_body(hidden_ref, w_ref, bias_ref, active_ref, slope_ref):
@@ -278,17 +331,17 @@
         ],
         [tile, tile],
         [struct((r, units), BF), struct((r, units), F32)],
-        flops=2 * r * D * units,
+        us=200,
         nbytes=r * D * 2 + D * units * 2 + r * units * 6,
     )(hidden, w, bias)
 
 
-def down_body(active_ref, w_ref, bias_ref, middle_ref, out_ref):
-    out = middle_ref[...] + (dot(active_ref[...], w_ref[...], 1, 1) + bias_ref[...])
-    out_ref[...] = out.astype(BF)
-
-
-def down(active, w, bias, middle):
+def down_body(active_ref, w_ref, vec_ref, middle_ref, out_ref):
+    branch = dot(active_ref[...], w_ref[...], 1, 1) + vec_row(vec_ref, BIAS_DOWN)
+    out_ref[...] = (middle_ref[...] + branch).astype(BF)
+
+
+def down(active, w, vec, middle):
     r, units = active.shape
     m = row_tile(r)
     return call(
@@ -297,14 +350,14 @@
         [
             spec((m, units), lambda i: (i, 0)),
             spec((D, units), lambda i: (0, 0)),
-            spec((1, D), lambda i: (0, 0)),
+            spec((8, D), lambda i: (0, 0)),
             spec((m, D), lambda i: (i, 0)),
         ],
         spec((m, D), lambda i: (i, 0)),
         struct((r, D), BF),
-        flops=2 * r * D * units,
+        us=200,
         nbytes=r * units * 2 + D * units * 2 + r * D * 6,
-    )(active, w, bias, middle)
+    )(active, w, vec, middle)
 
 
 def outer_body(left_ref, right_ref, out_ref, sum_ref, turned):
@@ -327,7 +380,7 @@
         [spec((rows, TILE), lambda j: (0, j)), spec((1, TILE), lambda j: (0, j))],
         [struct((rows, width), BF), struct((1, width), F32)],
         [pltpu.VMEM((rows, r), BF)],
-        flops=2 * r * rows * width,
+        us=0.01,
         nbytes=r * rows * 2 + r * width * 2 + rows * width * 2,
     )(left, right)
 
@@ -355,7 +408,7 @@
         [tile, col, spec((1, TILE), lambda j: (0, j))],
         [struct((r, units), BF), struct((D, units), BF), struct((1, units), F32)],
         [pltpu.VMEM((D, r), BF)],
-        flops=4 * r * D * units,
+        us=200,
         nbytes=r * D * 4 + D * units * 4 + r * units * 6,
     )(cot, w, slope, hidden)
 
@@ -370,11 +423,13 @@
 
 
 def middle_back_body(
-    grad_ref, w_ref, middle_ref, cot_ref, gain_ref, out_ref, branch_ref, gain_sum, shift_sum, out_sum
+    grad_ref, w_ref, middle_ref, cot_ref, vec_ref, out_ref, branch_ref, gain_sum, shift_sum, out_sum
 ):
     grad = dot(grad_ref[...], w_ref[...], 1, 1)
     normed, inv = stats(middle_ref[...])
-    total = cot_ref[...].astype(F32) + norm_pull(grad, normed, inv, gain_ref[...])
+    total = cot_ref[...].astype(F32) + norm_pull(
+        grad, normed, inv, vec_row(vec_ref, GAIN_TWO)
+    )
     out_ref[...] = total
     branch = total.astype(BF)
     branch_ref[...] = branch
@@ -397,7 +452,7 @@
         ref[...] += value
 
 
-def middle_back(grad, w, middle, cot, gain):
+def middle_back(grad, w, middle, cot, vecs):
     r, units = grad.shape
     m = row_tile(r)
     vec = spec((1, D), lambda i: (0, 0))
@@ -406,12 +461,18 @@
     return call(
         middle_back_body,
         (r // m,),
-        [spec((m, units), lambda i: (i, 0)), spec((D, units), lambda i: (0, 0)), row, row, vec],
+        [
+            spec((m, units), lambda i: (i, 0)),
+            spec((D, units), lambda i: (0, 0)),
+            row,
+            row,
+            spec((8, D), lambda i: (0, 0)),
+        ],
         [row, row, vec, vec, vec],
         [struct((r, D), F32), struct((r, D), BF), vec_out, vec_out, vec_out],
-        flops=2 * r * D * units,
+        us=0.01,
         nbytes=r * units * 2 + D * units * 2 + r * D * 12,
-    )(grad, w, middle, cot, gain)
+    )(grad, w, middle, cot, vecs)
 
 
 def mixed_back_body(branch_ref, tile_ref, w_ref, mixed_ref, grad_ref, gw_ref, turned):
@@ -434,12 +495,13 @@
         [tile, spec((D, TILE), lambda j: (0, j))],
         [struct((r, D), BF), struct((D, D), BF)],
         [pltpu.VMEM((D, r), BF)],
-        flops=4 * r * D * D,
+        us=0.01,
         nbytes=r * D * 8 + D * D * 4,
     )(branch, branch, w, mixed)
 
 
-def attend_back_body(triple_ref, prob_ref, grad_ref, out_ref):
+def attend_back_body(triple_ref, prob_ref, grad_ref, *rest):
+    out_ref = rest[-1]
     left = lax.broadcasted_iota(jnp.int32, (ROWS, 128), 1) < HEAD_DIM
     scale = HEAD_DIM**-0.5
     for pair in range(HEADS // 2):
@@ -464,22 +526,32 @@
             out_ref[:, at * D + pair * 128 : at * D + (pair + 1) * 128] = both.astype(BF)
 
 
-def attend_back(triple, prob, grad):
-    groups = triple.shape[0] // ROWS
-    wide = spec((ROWS, 3 * D), lambda g: (g, 0))
-    return call(
+def attend_back(triple, prob, grad, start, stop, partial_out=None):
+    wide = spec((ROWS, 3 * D), lambda g: (g + start, 0))
+    count = stop - start
+    given = [] if partial_out is None else [partial_out]
+    return pl.pallas_call(
         attend_back_body,
-        (groups,),
-        [
-            wide,
-            spec((1, HEADS, ROWS, ROWS), lambda g: (g, 0, 0, 0)),
-            spec((ROWS, D), lambda g: (g, 0)),
-        ],
-        wide,
-        struct((groups * ROWS, 3 * D), BF),
-        flops=groups * HEADS * 8 * ROWS * ROWS * 128,
-        nbytes=groups * ROWS * (14 * D + HEADS * 512),
-    )(triple, prob, grad)
+        out_shape=struct(triple.shape, BF),
+        grid_spec=pltpu.PrefetchScalarGridSpec(
+            num_scalar_prefetch=0,
+            grid=(count,),
+            in_specs=[
+                wide,
+                spec((1, HEADS, ROWS, ROWS), lambda g: (g + start, 0, 0, 0)),
+                spec((ROWS, D), lambda g: (g + start, 0)),
+            ]
+            + [ANY] * len(given),
+            out_specs=wide,
+        ),
+        input_output_aliases={3: 0} if given else {},
+        compiler_params=pltpu.CompilerParams(
+            dimension_semantics=("arbitrary",), vmem_limit_bytes=24 * MB
+        ),
+        cost_estimate=pl.CostEstimate(
+            flops=200 * FLOPS_PER_US, bytes_accessed=1024, transcendentals=0
+        ),
+    )(triple, prob, grad, *given)
 
 
 def qkv_grad_body(grad_ref, hidden_ref, gw_ref, gb_ref):
@@ -496,20 +568,21 @@
         [spec((r, TILE), lambda j: (0, j)), spec((r, D), lambda j: (0, 0))],
         [spec((TILE, D), lambda j: (j, 0)), spec((1, TILE), lambda j: (0, j))],
         [struct((width, D), BF), struct((1, width), F32)],
-        flops=2 * r * D * width,
+        us=200,
         nbytes=r * width * 2 + r * D * 2 + width * D * 2,
     )(grad, hidden)
 
 
-def first_back_body(grad_ref, w_ref, rows_ref, middle_ref, gain_ref, out_ref, gain_sum, shift_sum):
+def first_back_body(grad_ref, w_ref, rows_ref, middle_ref, vec_ref, out_ref, gain_sum, shift_sum):
     grad = dot(grad_ref[...], w_ref[...], 1, 0)
     normed, inv = stats(rows_ref[...].astype(F32))
-    out_ref[...] = middle_ref[...] + norm_pull(grad, normed, inv, gain_ref[...])
+    pulled = norm_pull(grad, normed, inv, vec_row(vec_ref, GAIN_ONE))
+    out_ref[...] = middle_ref[...] + pulled
     add_up(gain_sum, jnp.sum(grad * normed, 0, keepdims=True))
     add_up(shift_sum, jnp.sum(grad, 0, keepdims=True))
 
 
-def first_back(grad, w, rows, grad_middle, gain):
+def first_back(grad, w, rows, grad_middle, vecs):
     r, width = grad.shape
     m = row_tile(r)
     vec = spec((1, D), lambda i: (0, 0))
@@ -518,12 +591,313 @@
     return call(
         first_back_body,
         (r // m,),
-        [spec((m, width), lambda i: (i, 0)), spec((width, D), lambda i: (0, 0)), row, row, vec],
+        [
+            spec((m, width), lambda i: (i, 0)),
+            spec((width, D), lambda i: (0, 0)),
+            row,
+            row,
+            spec((8, D), lambda i: (0, 0)),
+        ],
         [row, vec, vec],
         [struct((r, D), F32), vec_out, vec_out],
-        flops=2 * r * D * width,
+        us=200,
         nbytes=r * width * 2 + D * width * 2 + r * D * 10,
-    )(grad, w, rows, grad_middle, gain)
+    )(grad, w, rows, grad_middle, vecs)
+
+
+WIDE, NARROW, DP = "wide", "narrow", "dp"
+
+
+def swap(value, axis, bit):
+    size = lax.axis_size(axis)
+    return lax.ppermute(value, axis, [(i, i ^ bit) for i in range(size)])
+
+
+def hold(value, *deps):
+    return lax.optimization_barrier((value, deps))[0]
+
+
+class Pieces:
+    def __init__(self, stack, tags):
+        self.stack, self.tags = stack, tags
+
+    def fetch(self, axis, bit, *deps):
+        move = [bit if axis == name else 0 for name in (WIDE, NARROW, DP)]
+        tags = [tuple(a ^ b for a, b in zip(tag, move)) for tag in self.tags]
+        return Pieces(swap(hold(self.stack, *deps), axis, bit), tags)
+
+    def after(self, *deps):
+        return Pieces(hold(self.stack, *deps), self.tags)
+
+    def rows(self, start, stop):
+        return Pieces(self.stack[:, start:stop], self.tags)
+
+    def join(self, *others):
+        stack = jnp.concatenate([self.stack] + [o.stack for o in others])
+        return Pieces(stack, sum([o.tags for o in others], self.tags))
+
+
+def first_piece(piece):
+    return Pieces(piece[None], [(0, 0, 0)])
+
+
+def dp_sum(total):
+    total = total.astype(F32)
+    bit = 2
+    while bit < lax.axis_size(DP):
+        total = total + swap(total.astype(BF), DP, bit).astype(F32)
+        bit *= 2
+    return total
+
+
+def qkv_plan(cols, heads_cols, parts, spots=None):
+    rows = heads_cols // parts
+    spots = spots or [(p * rows, 0) for p in range(3)]
+
+    def plan(w, n, q):
+        return [
+            (spot, (rows, cols), (p * D + w * heads_cols + q * rows, n * cols))
+            for p, spot in enumerate(spots)
+        ]
+
+    return plan
+
+
+def out_plan(cols, heads_cols, parts, spot=(0, 0)):
+    rows = heads_cols // parts
+    return lambda w, n, q: [(spot, (rows, cols), (w * heads_cols + q * rows, n * cols))]
+
+
+def flat_plan(cols, units, parts, spot=(0, 0)):
+    rows = cols // parts
+    return lambda w, n, q: [(spot, (rows, units), (n * cols + q * rows, w * units))]
+
+
+def prep_body(cols, rows, at_ref, *refs):
+    qkv_ref, out_ref, vectors = refs[0], refs[1], refs[2:10]
+    piece_ref, held, sem = refs[10], refs[11:-1], refs[-1]
+    start = pl.multiple_of(at_ref[2] * rows, 16)
+    copies = [
+        pltpu.make_async_copy(
+            qkv_ref.at[p, pl.ds(start, rows)], piece_ref.at[pl.ds(p * rows, rows)], sem.at[p]
+        )
+        for p in range(3)
+    ]
+    copies.append(
+        pltpu.make_async_copy(
+            out_ref.at[pl.ds(start, rows)], piece_ref.at[pl.ds(3 * rows + 16, rows)], sem.at[3]
+        )
+    )
+    copies += [
+        pltpu.make_async_copy(vector, scratch, sem.at[4 + k])
+        for k, (vector, scratch) in enumerate(zip(vectors, held))
+    ]
+    for copy in copies:
+        copy.start()
+    for copy in copies:
+        copy.wait()
+    lines = [ref[...].astype(F32).reshape(1, -1) for ref in held[:6]]
+    both = held[6][...].astype(F32)
+    lines.append(jnp.concatenate([both[:1], both[1:]], axis=1))
+    wide_line = held[7][...].astype(F32).reshape(1, -1)
+    lines += [wide_line[:, k : k + cols] for k in range(0, wide_line.shape[1], cols)]
+    lines.append(jnp.zeros((16 - len(lines), cols), F32))
+    piece_ref[3 * rows : 3 * rows + 16, :] = jnp.concatenate(lines, axis=0).astype(BF)
+
+
+def prep(at, qkv_t, w_out, *vectors):
+    cols = qkv_t.shape[2]
+    rows = qkv_t.shape[1] // 2
+    return pl.pallas_call(
+        partial(prep_body, cols, rows),
+        out_shape=struct((4 * rows + 16, cols), BF),
+        grid_spec=pltpu.PrefetchScalarGridSpec(
+            num_scalar_prefetch=1,
+            grid=(1,),
+            in_specs=[IN_HBM] * (2 + len(vectors)),
+            out_specs=pl.BlockSpec(memory_space=pltpu.VMEM),
+            scratch_shapes=[pltpu.VMEM(v.shape, BF) for v in vectors]
+            + [pltpu.SemaphoreType.DMA((4 + len(vectors),))],
+        ),
+        compiler_params=pltpu.CompilerParams(vmem_limit_bytes=8 * MB),
+        cost_estimate=pl.CostEstimate(
+            flops=FLOPS_PER_US // 100, bytes_accessed=1024, transcendentals=0
+        ),
+    )(at, *[in_hbm(v) for v in (qkv_t, w_out, *vectors)])
+
+
+def vec_body(wide, narrow, cols, first, tag_lists, at_ref, *refs):
+    arrays, (vec_ref, qkv_bias_ref, up_bias_ref, held, sem) = refs[:-5], refs[-5:]
+    copies = []
+    for array, tags in zip(arrays, tag_lists):
+        for k, (dw, dn, _) in enumerate(tags):
+            slot = (at_ref[0] ^ dw) * narrow + (at_ref[1] ^ dn)
+            source = array.at[k, pl.ds(first, 16)]
+            copies.append(pltpu.make_async_copy(source, held.at[slot], sem.at[len(copies)]))
+    for copy in copies:
+        copy.start()
+    for copy in copies:
+        copy.wait()
+    lines = [held[k].astype(F32) for k in range(wide * narrow)]
+    for n in range(narrow):
+        vec_ref[:, n * cols : (n + 1) * cols] = lines[n][:8]
+    by_wide = [lines[w * narrow] for w in range(wide)]
+    half = cols // 2
+    q = jnp.concatenate([line[6:7, :half] for line in by_wide], axis=1)
+    v = jnp.concatenate([line[6:7, half:] for line in by_wide], axis=1)
+    qkv_bias_ref[...] = jnp.concatenate([q, jnp.zeros_like(q), v], axis=1)
+    up_bias_ref[...] = jnp.concatenate(
+        [line[i : i + 1] for line in by_wide for i in (7, 8)], axis=1
+    )
+
+
+def vectors_of(at, pieces, first, wide, narrow, cols, units):
+    vmem = pl.BlockSpec(memory_space=pltpu.VMEM)
+    return pl.pallas_call(
+        partial(vec_body, wide, narrow, cols, first, [p.tags for p in pieces]),
+        out_shape=[struct((8, D), F32), struct((1, 3 * D), F32), struct((1, wide * units), F32)],
+        grid_spec=pltpu.PrefetchScalarGridSpec(
+            num_scalar_prefetch=1,
+            grid=(1,),
+            in_specs=[ANY] * len(pieces),
+            out_specs=[vmem] * 3,
+            scratch_shapes=[
+                pltpu.VMEM((wide * narrow, 16, cols), BF),
+                pltpu.SemaphoreType.DMA((wide * narrow,)),
+            ],
+        ),
+        compiler_params=pltpu.CompilerParams(vmem_limit_bytes=8 * MB),
+        cost_estimate=pl.CostEstimate(flops=FLOPS_PER_US // 100, bytes_accessed=1024, transcendentals=0),
+    )(at, *[p.stack for p in pieces])
+
+
+def pack_body(*refs):
+    out = refs[-1]
+    at = 0
+    for ref in refs[:-1]:
+        for k in range(0, ref.shape[1], D):
+            out[at : at + 1, :] = ref[:, k : k + D]
+            at += 1
+    if at < out.shape[0]:
+        out[at:, :] = jnp.zeros((out.shape[0] - at, D), F32)
+
+
+def pack(*rows):
+    count = -(-sum(r.shape[1] for r in rows) // (8 * D)) * 8
+    vmem = pl.BlockSpec(memory_space=pltpu.VMEM)
+    return pl.pallas_call(
+        pack_body,
+        out_shape=struct((count, D), F32),
+        in_specs=[vmem] * len(rows),
+        out_specs=vmem,
+        compiler_params=pltpu.CompilerParams(vmem_limit_bytes=8 * MB),
+        cost_estimate=pl.CostEstimate(flops=FLOPS_PER_US // 100, bytes_accessed=1024, transcendentals=0),
+    )(*rows)
+
+
+ANY = pl.BlockSpec(memory_space=pl.ANY)
+IN_HBM = pl.BlockSpec(memory_space=pltpu.HBM)
+
+
+CORE, DP_INDEX = 2, 3
+
+
+def build_body(plan, tag_lists, inverse, part_at, at_ref, *refs):
+    sem = refs[-1]
+    if inverse:
+        whole_ref, arrays = refs[0], refs[1:-1]
+    else:
+        arrays, whole_ref = refs[:-2], refs[-2]
+    copies = []
+    for array, tags in zip(arrays, tag_lists):
+        for k, (dw, dn, dq) in enumerate(tags):
+            w, n, q = at_ref[0] ^ dw, at_ref[1] ^ dn, at_ref[part_at] ^ dq
+            for (at_row, at_lane), (rows, lanes), (row, lane) in plan(w, n, q):
+                piece = array.at[k, pl.ds(at_row, rows), pl.ds(at_lane, lanes)]
+                whole = whole_ref.at[
+                    pl.ds(pl.multiple_of(row, 16), rows), pl.ds(pl.multiple_of(lane, 128), lanes)
+                ]
+                ends = (whole, piece) if inverse else (piece, whole)
+                copies.append(pltpu.make_async_copy(*ends, sem.at[len(copies)]))
+    for copy in copies:
+        copy.start()
+    for copy in copies:
+        copy.wait()
+
+
+def move_pieces(at, arrays, plan, tag_lists, inverse, part_at, shapes):
+    moves = sum(len(tags) for tags in tag_lists) * len(plan(0, 0, 0))
+    return pl.pallas_call(
+        partial(build_body, plan, tag_lists, inverse, part_at),
+        out_shape=[struct(shape, BF) for shape in shapes],
+        grid_spec=pltpu.PrefetchScalarGridSpec(
+            num_scalar_prefetch=1,
+            grid=(1,),
+            in_specs=[ANY] * len(arrays),
+            out_specs=[ANY] * len(shapes),
+            scratch_shapes=[pltpu.SemaphoreType.DMA((moves,))],
+        ),
+        compiler_params=pltpu.CompilerParams(vmem_limit_bytes=4 * MB),
+        cost_estimate=pl.CostEstimate(
+            flops=FLOPS_PER_US // 100, bytes_accessed=1024, transcendentals=0
+        ),
+    )(at, *arrays)
+
+
+def build_weights(at, pieces, plan, shape, part_at=CORE):
+    arrays, tags = [p.stack for p in pieces], [p.tags for p in pieces]
+    arrays = [in_hbm(a) for a in arrays]
+    return move_pieces(at, arrays, plan, tags, False, part_at, [shape])[0]
+
+
+def cut_grads(at, grad, plan, tags, shape, part_at=CORE):
+    tag_lists = [[(w, n, q ^ dc) for w, n, q in tags] for dc in range(2)]
+    return move_pieces(at, [grad], plan, tag_lists, True, part_at, [(len(tags),) + shape] * 2)
+
+
+class Chain:
+    def __init__(self, at, grad, plan, tags, shape, part_at=CORE):
+        self.keep, self.send = cut_grads(at, grad, plan, tags, shape, part_at)
+
+    def go(self, axis, bit):
+        self.got = swap(self.send, axis, bit)
+
+    def fold(self, *deps):
+        self.keep, self.send = halves_summed(self.keep, hold(self.got, *deps))
+
+    def total(self, *deps):
+        return self.keep[0].astype(F32) + hold(self.got, *deps)[0].astype(F32)
+
+
+def doubled(value, bit, index):
+    other = swap(value, DP, bit)
+    return jnp.where(index == 0, jnp.stack([value, other]), jnp.stack([other, value]))
+
+
+def halves_summed(kept, got):
+    half = kept.shape[0] // 2
+    keep = kept[:half].astype(F32) + got[:half].astype(F32)
+    send = (kept[half:].astype(F32) + got[half:].astype(F32)).astype(BF)
+    return keep, send
+
+
+def core_half(at, shard):
+    rows = shard.shape[0] // 2
+    return lax.dynamic_slice_in_dim(shard, at[2] * rows, rows, axis=0)
+
+
+def quarter(at, shard):
+    rows = shard.shape[0] // 4
+    return lax.dynamic_slice_in_dim(shard, at[3] * rows, rows, axis=0)
+
+
+def total_over_all(value, axes):
+    for axis in axes:
+        bit = 1
+        while bit < lax.axis_size(axis):
+            value = value + swap(value, axis, bit)
+            bit *= 2
+    return value
 
 
 def to_rows(blocks, narrow):
@@ -575,14 +949,210 @@
     cols = w_qkv.shape[0]
     heads_cols = w_qkv.shape[2]
     units = w_up.shape[1]
+    swaps = cols % 128 == 0 and narrow == 2 and wide == 4 and lax.axis_size(DP) == 4
+    swaps = swaps and pairs % 2 == 0
+
+    at = jnp.stack(
+        [
+            lax.axis_index("wide"),
+            lax.axis_index("narrow"),
+            lax.axis_index("dp") % 2,
+            lax.axis_index("dp"),
+        ]
+    ).astype(jnp.int32)
 
     index = (visible.reshape(pairs, 2, VISIBLE) + jnp.array([0, PATCHES])[None, :, None]).reshape(
         pairs, PAIR
     )
     index = jnp.pad(index, ((0, 0), (0, ROWS - PAIR)), constant_values=-1)[:, :, None]
 
-    if cols % 128 == 0:
-        rows_mine, cot_mine = pick_rows(patches, cotangent, index, cols)
+    w_qkv_t = w_qkv.transpose(1, 2, 0)
+    if swaps:
+        first = first_piece(
+            prep(
+                at,
+                w_qkv_t,
+                w_out,
+                gain_one,
+                shift_one,
+                gain_two,
+                shift_two,
+                b_out,
+                b_down,
+                b_qv,
+                b_up,
+            )
+        )
+
+        def part_of(whole, side):
+            return lax.dynamic_slice_in_dim(whole, side * cols, cols, axis=1)
+
+        def join_cols(keep, got):
+            return jnp.where(
+                at[1] == 0,
+                jnp.concatenate([keep, got], axis=1),
+                jnp.concatenate([got, keep], axis=1),
+            )
+
+        mine, theirs = at[1], 1 - at[1]
+        whole = (D, wide * units)
+
+        first_z = [first.fetch(WIDE, bit) for bit in (1, 2, 3)]
+        rows_out = pick_rows(hold(at, first.stack), patches, index, cols)
+        own = rows_out.shape[0] // 2
+        rows_send = rows_out[:own]
+        rows_got = swap(rows_send, NARROW, 1)
+        cot_out = cot_rows(hold(at, rows_send), cotangent, pairs, cols)
+
+        first = first.join(*[p.after(cot_out) for p in first_z])
+        up_p = first_piece(hold(core_half(at, w_up), first.stack))
+        up_z = [up_p.fetch(WIDE, bit) for bit in (1, 2, 3)]
+        rows = join_cols(rows_out[own:], hold(rows_got, up_p.stack))
+        first_x = first.fetch(NARROW, 1, rows)
+        up_p = up_p.join(*[p.after(rows) for p in up_z])
+
+        first = first.join(first_x.after(up_p.stack))
+        first_c = first.fetch(DP, 1)
+        up_x = up_p.fetch(NARROW, 1)
+        down_p = first_piece(hold(quarter(at, w_down), first.stack))
+        down_z = [down_p.fetch(WIDE, bit) for bit in (1, 2, 3)]
+        vec_at = 3 * heads_cols // 2
+        out_at = (vec_at + 16, 0)
+        vecs, bias_qkv, bias_up = vectors_of(at, [first], vec_at, wide, narrow, cols, units)
+        hidden_one = norm(rows, vecs)
+        all_first = [first, first_c.after(hidden_one)]
+        qkv_t = build_weights(at, all_first, qkv_plan(cols, heads_cols, 2), (3 * D, D))
+        out_w = build_weights(at, all_first, out_plan(cols, heads_cols, 2, out_at), (D, D))
+        down_p = down_p.join(*[p.after(qkv_t) for p in down_z])
+        down_x = down_p.fetch(NARROW, 1)
+        triple = qkv(hold(hidden_one, down_p.stack), qkv_t, bias_qkv)
+        mixed, prob = attend(triple)
+        half_flat, part_flat = flat_plan(cols, units, 2), flat_plan(cols, units, 4)
+        up_x = up_x.after(mixed)
+        up_c = up_p.fetch(DP, 1, up_x.stack)
+        up_xc = up_x.fetch(DP, 1)
+        down_p = down_p.join(down_x.after(mixed))
+        down_y = down_p.fetch(DP, 2)
+        cot_send = hold(cot_out[:own], down_p.stack)
+        cot_got = swap(cot_send, NARROW, 1)
+        middle, hidden_two = mix(
+            hold(mixed, up_x.stack, down_p.stack, cot_send), out_w, rows, vecs
+        )
+        up_c, up_xc = up_c.after(hidden_two), up_xc.after(hidden_two)
+        up_w = build_weights(at, [up_p, up_x, up_c, up_xc], half_flat, whole)
+        active, slope = up(hidden_two, up_w, bias_up)
+        cot = join_cols(cot_out[own:], hold(cot_got, active))
+        gw_down, _ = outer(cot, active)
+        gb_down = jnp.sum(cot, 0, dtype=F32)[None]
+        x_first = [(w, n, 0) for n in range(2) for w in (0, 2, 1, 3)]
+        y_first = [(w, n, dy) for dy in (0, 2) for n in range(2) for w in (0, 2, 1, 3)]
+        g_d = Chain(at, gw_down, half_flat, x_first, (cols // 2, units))
+        g_d.go(DP, 1)
+        down_y = down_y.after(g_d.send)
+        down_c = [p.fetch(DP, 1, down_y.stack) for p in (down_p, down_y)]
+        down_w = build_weights(at, [down_p, down_y] + down_c, part_flat, whole, DP_INDEX)
+        g_d.fold(down_w)
+        g_d.go(NARROW, 1)
+        grad_inner, gw_up, gb_up = inner_back(
+            cot, hold(down_w, g_d.send), in_hbm(slope), hidden_two
+        )
+
+        g_u = Chain(at, gw_up, part_flat, y_first, (cols // 4, units), DP_INDEX)
+        g_u.go(DP, 1)
+        g_d.fold(g_u.send)
+        g_d.go(WIDE, 1)
+        result = down(hold(active, g_d.send), down_w, vecs, middle)
+        grad_middle, branch, gg_two, gs_two, gb_out = middle_back(
+            hold(grad_inner, result), up_w, middle, cot, vecs
+        )
+        grad_mixed, gw_out = mixed_back(branch, out_w, mixed)
+
+        g_o = Chain(at, gw_out, out_plan(cols, heads_cols, 2), x_first, (heads_cols // 2, cols))
+        g_o.go(DP, 1)
+        g_u.fold(g_o.send)
+        g_u.go(DP, 2)
+        g_d.fold(g_o.send)
+        g_d.go(WIDE, 2)
+        result_got = swap(hold(part_of(result, theirs), g_o.send), NARROW, 1)
+        groups = rows.shape[0] // ROWS
+        grad_triple = attend_back(
+            triple, in_hbm(prob), hold(grad_mixed, g_u.send, g_d.send), 0, groups
+        )
+
+        d_sum = g_d.total(grad_triple)
+        d_got = swap(d_sum.astype(BF), DP, 2)
+        g_u.fold(grad_triple)
+        g_u.go(NARROW, 1)
+        g_o.fold(grad_triple)
+        g_o.go(NARROW, 1)
+        result_got = hold(result_got, grad_triple)
+        gw_qkv, gb_qkv = qkv_grad(hold(grad_triple, d_sum, g_u.send, g_o.send), hidden_one)
+
+        g_q = Chain(
+            at,
+            gw_qkv,
+            qkv_plan(cols, heads_cols, 4),
+            y_first,
+            (3 * heads_cols // 4, cols),
+            DP_INDEX,
+        )
+        g_q.go(DP, 1)
+        d_sum = d_sum + hold(d_got, g_q.send).astype(F32)
+        d_got = swap(d_sum, DP, 1)
+        g_u.fold(g_q.send)
+        g_u.go(WIDE, 1)
+        g_o.fold(g_q.send)
+        g_o.go(WIDE, 1)
+        grad_rows, gg_one, gs_one = first_back(
+            grad_triple, hold(qkv_t, d_sum, g_u.send, g_o.send), rows, grad_middle, vecs
+        )
+
+        g_q.fold(grad_rows)
+        g_q.go(DP, 2)
+        rows_send = part_of(grad_rows, theirs).astype(BF)
+        rows_back = swap(rows_send, NARROW, 1)
+        g_u.fold(grad_rows)
+        g_u.go(WIDE, 2)
+        g_o.fold(grad_rows)
+        g_o.go(WIDE, 2)
+        sums = pack(gg_one, gs_one, gg_two, gs_two, gb_out, gb_down, gb_qkv, gb_up)
+        sums_got = swap(sums, DP, 1)
+        keep = part_of(result, mine)
+        block_output = flat_rows(
+            at, hold(keep, g_q.send, rows_send, g_u.send, g_o.send, sums), result_got, cols
+        )
+
+        g_q.fold(block_output)
+        g_q.go(NARROW, 1)
+        u_sum = g_u.total(block_output)
+        u_got = swap(u_sum, DP, 2)
+        o_sum = g_o.total(block_output)
+        o_got = swap(o_sum.astype(BF), DP, 2)
+        sums = sums + hold(sums_got, block_output)
+        sums_got = swap(sums, DP, 2)
+        rows_back = hold(rows_back, block_output, g_q.send, u_sum, o_sum, sums)
+        grad_patches = put_rows(at, part_of(grad_rows, mine), rows_back, index, cols)
+
+        def in_order(value, other, index):
+            return jnp.where(index == 0, jnp.stack([value, other]), jnp.stack([other, value]))
+
+        g_q.fold(grad_patches)
+        g_q.go(WIDE, 1)
+        u_sum = in_order(u_sum, hold(u_got, grad_patches), at[3] // 2)
+        u_got = swap(u_sum, DP, 1)
+        o_sum = o_sum + hold(o_got, grad_patches).astype(F32)
+        o_got = swap(o_sum, DP, 1)
+        sums = sums + hold(sums_got, grad_patches)
+        sums = total_over_all(sums, ("narrow", "wide"))
+        g_down = in_order(d_sum, d_got, at[2]).reshape(cols, units)
+        g_q.fold()
+        g_q.go(WIDE, 2)
+        g_up = in_order(u_sum, u_got, at[2]).transpose(1, 0, 2, 3).reshape(cols, units)
+        g_out = in_order(o_sum, o_got, at[2]).reshape(heads_cols, cols)
+        q_sum = doubled(doubled(g_q.total(), 2, at[3] // 2), 1, at[2])
+        g_qkv = q_sum.reshape(2, 2, 3, heads_cols // 4, cols).transpose(4, 2, 1, 0, 3)
+        g_qkv = g_qkv.reshape(cols, 3, heads_cols)
+        grad_patches = grad_patches.reshape(1, -1)
     else:
         table = patches.reshape(images, PATCHES, cols)
         rows_mine = jnp.take_along_axis(table, visible[:, :, None], axis=1)
@@ -592,50 +1162,46 @@
         cot_mine = jnp.pad(
             cotangent.reshape(pairs, PAIR, cols), ((0, 0), (0, ROWS - PAIR), (0, 0))
         )
-    rows = to_rows(rows_mine.reshape(narrow, -1, cols), narrow)
-    cot = to_rows(cot_mine.reshape(narrow, -1, cols), narrow)
-
-    vec = jnp.concatenate(
-        [gain_one, shift_one, gain_two, shift_two, b_out, b_down, b_qv.reshape(-1), b_up]
-    )
-    vec = lax.all_gather(vec, ("wide", "narrow"), axis=0, tiled=False).astype(F32)
-    vec = vec.reshape(wide, narrow, -1)
-    by_narrow = vec[0, :, : 6 * cols].reshape(narrow, 6, cols).transpose(1, 0, 2).reshape(6, 1, D)
-    gain_a, shift_a, gain_b, shift_b, bias_out, bias_down = (by_narrow[i] for i in range(6))
-    by_wide = vec[:, 0, 6 * cols :]
-    bias_q = by_wide[:, :heads_cols].reshape(1, D)
-    bias_v = by_wide[:, heads_cols : 2 * heads_cols].reshape(1, D)
-    bias_qkv = jnp.concatenate([bias_q, jnp.zeros((1, D), F32), bias_v], axis=1)
-    bias_up = by_wide[:, 2 * heads_cols :].reshape(1, -1)
-
-    qkv_t = gather_weight(w_qkv.transpose(1, 2, 0), wide, narrow)
-    qkv_t = qkv_t.transpose(2, 0, 3, 1, 4).reshape(3 * D, D)
-    out_w = gather_weight(w_out, wide, narrow).transpose(0, 2, 1, 3).reshape(D, D)
-    up_w = gather_weight(w_up, wide, narrow).transpose(1, 2, 0, 3).reshape(D, -1)
-    down_w = gather_weight(w_down, wide, narrow).transpose(1, 2, 0, 3).reshape(D, -1)
-
-    hidden_one = norm(rows, gain_a, shift_a)
-    triple = qkv(hidden_one, qkv_t, bias_qkv)
-    mixed, prob = attend(triple)
-    middle, hidden_two = mix(mixed, out_w, bias_out, rows, gain_b, shift_b)
-    active, slope = up(hidden_two, up_w, bias_up)
-    result = down(active, down_w, bias_down, middle)
-
-    gw_down, _ = outer(cot, active)
-    gb_down = jnp.sum(cot, 0, dtype=F32)
-    grad_inner, gw_up, gb_up = inner_back(cot, down_w, slope, hidden_two)
-    grad_middle, branch, gg_two, gs_two, gb_out = middle_back(grad_inner, up_w, middle, cot, gain_b)
-    grad_mixed, gw_out = mixed_back(branch, out_w, mixed)
-    grad_triple = attend_back(triple, prob, grad_mixed)
-    gw_qkv, gb_qkv = qkv_grad(grad_triple, hidden_one)
-    grad_rows, gg_one, gs_one = first_back(grad_triple, qkv_t, rows, grad_middle, gain_a)
-
-    result = from_rows(result, narrow)
-    grad_rows = from_rows(grad_rows, narrow)
-    if cols % 128 == 0:
-        block_output = flat_rows(result, cols)
-        grad_patches = put_rows(grad_rows, index, cols).reshape(1, -1)
-    else:
+        rows = to_rows(rows_mine.reshape(narrow, -1, cols), narrow)
+        cot = to_rows(cot_mine.reshape(narrow, -1, cols), narrow)
+        vec = jnp.concatenate(
+            [gain_one, shift_one, gain_two, shift_two, b_out, b_down, b_qv.reshape(-1), b_up]
+        )
+        vec = lax.all_gather(vec, ("wide", "narrow"), axis=0, tiled=False).astype(F32)
+        qkv_t = gather_weight(w_qkv_t, wide, narrow)
+        qkv_t = qkv_t.transpose(2, 0, 3, 1, 4).reshape(3 * D, D)
+        out_w = gather_weight(w_out, wide, narrow).transpose(0, 2, 1, 3).reshape(D, D)
+        up_w = gather_weight(w_up, wide, narrow).transpose(1, 2, 0, 3).reshape(D, -1)
+        down_w = gather_weight(w_down, wide, narrow).transpose(1, 2, 0, 3).reshape(D, -1)
+        vec = vec.reshape(wide, narrow, -1)
+        vecs = vec[0, :, : 6 * cols].reshape(narrow, 6, cols).transpose(1, 0, 2).reshape(6, D)
+        vecs = jnp.pad(vecs, ((0, 2), (0, 0)))
+        by_wide = vec[:, 0, 6 * cols :]
+        bias_q = by_wide[:, :heads_cols].reshape(1, D)
+        bias_v = by_wide[:, heads_cols : 2 * heads_cols].reshape(1, D)
+        bias_qkv = jnp.concatenate([bias_q, jnp.zeros((1, D), F32), bias_v], axis=1)
+        bias_up = by_wide[:, 2 * heads_cols :].reshape(1, -1)
+
+        hidden_one = norm(rows, vecs)
+        triple = qkv(hidden_one, qkv_t, bias_qkv)
+        mixed, prob = attend(triple)
+        middle, hidden_two = mix(mixed, out_w, rows, vecs)
+        active, slope = up(hidden_two, up_w, bias_up)
+        result = down(active, down_w, vecs, middle)
+        gw_down, _ = outer(cot, active)
+        gb_down = jnp.sum(cot, 0, dtype=F32)[None]
+        grad_inner, gw_up, gb_up = inner_back(cot, down_w, slope, hidden_two)
+        grad_middle, branch, gg_two, gs_two, gb_out = middle_back(
+            grad_inner, up_w, middle, cot, vecs
+        )
+        grad_mixed, gw_out = mixed_back(branch, out_w, mixed)
+        grad_triple = attend_back(triple, prob, grad_mixed, 0, rows.shape[0] // ROWS)
+        gw_qkv, gb_qkv = qkv_grad(grad_triple, hidden_one)
+        grad_rows, gg_one, gs_one = first_back(grad_triple, qkv_t, rows, grad_middle, vecs)
+        sums = pack(gg_one, gs_one, gg_two, gs_two, gb_out, gb_down, gb_qkv, gb_up)
+
+        result = from_rows(result, narrow)
+        grad_rows = from_rows(grad_rows, narrow)
         block_output = result.reshape(pairs, ROWS, cols)[:, :PAIR].reshape(1, -1)
         grad_rows = grad_rows.reshape(pairs, ROWS, cols)[:, :PAIR].reshape(images, VISIBLE, cols)
         grad_patches = (
@@ -644,31 +1210,18 @@
             .set(grad_rows)
             .reshape(1, -1)
         )
-
-    g_down = scatter_grad(gw_down.reshape(narrow, cols, wide, units).transpose(2, 0, 1, 3))
-    g_up = scatter_grad(gw_up.reshape(narrow, cols, wide, units).transpose(2, 0, 1, 3))
-    g_out = scatter_grad(gw_out.reshape(wide, heads_cols, narrow, cols).transpose(0, 2, 1, 3))
-    g_qkv = scatter_grad(
-        gw_qkv.reshape(3, wide, heads_cols, narrow, cols).transpose(1, 3, 0, 2, 4)
-    )
-    g_qkv = g_qkv.transpose(2, 0, 1)
-
-    sums = jnp.concatenate(
-        [
-            gg_one[0],
-            gs_one[0],
-            gg_two[0],
-            gs_two[0],
-            gb_out[0],
-            gb_down,
-            gb_qkv[0, :D],
-            gb_qkv[0, 2 * D :],
-            gb_up[0],
-        ]
-    )
-    sums = lax.psum(sums, ("dp", "wide", "narrow"))
-    at_narrow = lax.axis_index("narrow") * cols
-    at_wide = lax.axis_index("wide")
+        g_down = scatter_grad(gw_down.reshape(narrow, cols, wide, units).transpose(2, 0, 1, 3))
+        g_up = scatter_grad(gw_up.reshape(narrow, cols, wide, units).transpose(2, 0, 1, 3))
+        g_out = scatter_grad(gw_out.reshape(wide, heads_cols, narrow, cols).transpose(0, 2, 1, 3))
+        g_qkv = scatter_grad(
+            gw_qkv.reshape(3, wide, heads_cols, narrow, cols).transpose(1, 3, 0, 2, 4)
+        )
+        g_qkv = g_qkv.transpose(2, 0, 1)
+        sums = lax.psum(sums, ("dp", "wide", "narrow"))
+
+    sums = sums.reshape(-1)
+    at_narrow = at[1] * cols
+    at_wide = at[0]
 
     def narrow_part(i):
         return lax.dynamic_slice_in_dim(sums, i * D + at_narrow, cols)
@@ -676,10 +1229,10 @@
     g_bqv = jnp.stack(
         [
             lax.dynamic_slice_in_dim(sums, (6 + i) * D + at_wide * heads_cols, heads_cols)
-            for i in range(2)
+            for i in (0, 2)
         ]
     )
-    g_bup = lax.dynamic_slice_in_dim(sums, 8 * D + at_wide * units, units)
+    g_bup = lax.dynamic_slice_in_dim(sums, 9 * D + at_wide * units, units)
     return (
         block_output,
         grad_patches,

time: 839 us -> 358 us (0.43)
  waiting for transfers between devices: 313 us -> 74.2 us
  local copies, waits for them, and re-layouts: 192 us -> 39.3 us
  blocking collectives: 112 us -> 0 us
  starting transfers between devices: 17.6 us -> 51.7 us
  between operations: 14.6 us -> 1.62 us
  other arithmetic: 6.97 us -> 16.6 us
    reduce_scatter x4 -> x0, waiting for transfers between devices: 180 us -> none  [scatter_grad(): lax.psum_scatter(blocks.reshape(-1, 128), ('wide', 'narrow'), scatter_dim...]
    reshape x28 -> x1, local copies, waits for them, and re-layouts: 122 us -> 0.01 us  [on_device(): sums = sums.reshape(-1)]
    all_gather x4 -> x0, waiting for transfers between devices: 109 us -> none  [gather_weight(): lax.all_gather(shard.reshape(-1, 128), ('wide', 'narrow'), axis=0, tiled=...]
    ppermute x0 -> x53, waiting for transfers between devices: none -> 74.2 us  [swap(): return lax.ppermute(value, axis, [(i, i ^ bit) for i in range(size)])]
    psum x1 -> x0, blocking collectives: 65.1 us -> none  [on_device(): sums = lax.psum(sums, ('dp', 'wide', 'narrow'))]
    ppermute x0 -> x53, starting transfers between devices: none -> 51.7 us  [swap(): return lax.ppermute(value, axis, [(i, i ^ bit) for i in range(size)])]
    all_gather x1 -> x0, blocking collectives: 47.3 us -> none  [on_device(): lax.all_gather(vec, ('wide', 'narrow'), axis=0, tiled=False).astype(F32)]
    all_to_all x4 -> x0, waiting for transfers between devices: 23.3 us -> none  [the longest x2 23.3 us: to_rows(): got = lax.all_to_all(blocks, 'narrow', 0, 0, tiled=True)]
  transfers between devices with their start and end apart: 13 -> 53, of which waited for: 6 -> 17; matrix products, arithmetic and copies ran while one was open for 16% -> 8% of each run, Pallas kernels for 15% -> 48%
where the time goes in v3:
time: 358 us; the launch traced here: 357 us
  Pallas kernels  173 us (48%)
  waiting for transfers between devices  74.2 us (21%)
  starting transfers between devices  51.7 us (14%)
  local copies, waits for them, and re-layouts  39.3 us (11%)
  other arithmetic  16.6 us (5%)
    ppermute x53, waiting for transfers between devices, swap(): return lax.ppermute(value, axis, [(i, i ^ bit) for i in range(size)])  74.2 us
    ppermute x53, starting transfers between devices, swap(): return lax.ppermute(value, axis, [(i, i ^ bit) for i in range(size)])  51.7 us
    pallas_call x1, Pallas kernels, attend_back(): pl.pallas_call(attend_back_body, out_shape=struct(triple.shape, BF), grid...  30.8 us
    unnamed x100, local copies, waits for them, and re-layouts  27.8 us
    pallas_call x1, Pallas kernels, inner_back(): call(inner_back_body, (units // TILE,), [full, col, tile, full], [tile, c...  22.2 us
    pallas_call x8, Pallas kernels, move_pieces(): pl.pallas_call(partial(build_body, plan, tag_lists, inverse, part_at), ou...  19.2 us
    pallas_call x1, Pallas kernels, put_rows(): call(partial(put_body, cols), (pairs,), [rows, rows, spec((1, ROWS, 1), l...  12.3 us
    pallas_call x1, Pallas kernels, pick_rows(): call(partial(pick_body, cols), (pairs,), [spec((1, width), lambda i, at:...  11 us
  transfers between devices with their start and end apart: 53, of which 17 were waited for; matrix products, arithmetic and copies ran while one was open for 8% of the time, Pallas kernels for 48%

profile of v3, /device:TPU:0, one launch (start us, length us, event | category | flops | bytes accessed | tf_op | source)
XLA Modules:
  0.0 356.8 jit_solution(1439482899930012341)
XLA Ops:
  3.2 5.1 %collective-permute-start.3 = (bf16[1,400,384]{2,1,0:T(8,128)(2,1)}, bf16[1,400,384]{2,1,0:T(8,128)(2,1)}, u32[]{:S(2)}, u32[]{:S(2)}) collective-permute-start(bf16[1,400,384]{2,1,0:T(8,128)(2,1)} %bitcast.5), channel_id=1, source_target_pairs={{0,6},{2,4},{4,2},{6,0},{1,7},{3,5},{5,3},{7,1},{8,14},{10,12},{12... | collective-permute-start | bytes 921608 | tf_op jit(solution)/shard_map/ppermute | solution.py:613
  10.3 3.7 %copy-done.27 = bf16[1,2408448]{1,0:T(2,128)(2,1)S(1)} copy-done((bf16[1,2408448]{1,0:T(2,128)(2,1)S(1)}, bf16[1,2408448]{1,0:T(2,128)(2,1)}, u32[]{:S(2)}) %copy-start.27) | copy-done | bytes 4816920
  14.0 11.0 %shard_map.264 = bf16[1792,384]{1,0:T(8,128)(2,1)S(1)} custom-call(s32[4]{0:T(128)S(1)} %pad_add_fusion.at_ref, bf16[1,2408448]{1,0:T(2,128)(2,1)S(1)} %copy-done.27, s32[16,112,1]{2,1,0:T(8,128)S(1)} %copy.31.index_ref), custom_call_target="tpu_custom_call" | custom-call | flops 108000002048 | bytes 1024 | tf_op jit(solution)/shard_map/pallas_call | solution.py:83
  31.2 3.6 %collective-permute-done.2 = bf16[1,400,384]{2,1,0:T(8,128)(2,1)} collective-permute-done((bf16[1,400,384]{2,1,0:T(8,128)(2,1)}, bf16[1,400,384]{2,1,0:T(8,128)(2,1)}, u32[]{:S(2)}, u32[]{:S(2)}) %collective-permute-start.2) | collective-permute-done | bytes 307232 | tf_op jit(solution)/shard_map/ppermute | solution.py:613
  37.3 5.7 %collective-permute-done = bf16[896,384]{1,0:T(8,128)(2,1)} collective-permute-done((bf16[896,384]{1,0:T(8,128)(2,1)}, bf16[896,384]{1,0:T(8,128)(2,1)}, u32[]{:S(2)}, u32[]{:S(2)}) %collective-permute-start) | collective-permute-done | bytes 688160 | tf_op jit(solution)/shard_map/ppermute | solution.py:613
  48.2 3.5 collective-permute-start.7
  55.7 4.6 %collective-permute-done.7 = bf16[1,192,768]{2,1,0:T(8,128)(2,1)S(1)} collective-permute-done((bf16[1,192,768]{2,1,0:T(8,128)(2,1)}, bf16[1,192,768]{2,1,0:T(8,128)(2,1)S(1)}, u32[]{:S(2)}, u32[]{:S(2)}) %collective-permute-start.7) | collective-permute-done | bytes 294944 | tf_op jit(solution)/shard_map/ppermute | solution.py:613
  60.3 14.9 %collective-permute-done.6 = bf16[1,192,768]{2,1,0:T(8,128)(2,1)S(1)} collective-permute-done((bf16[1,192,768]{2,1,0:T(8,128)(2,1)}, bf16[1,192,768]{2,1,0:T(8,128)(2,1)S(1)}, u32[]{:S(2)}, u32[]{:S(2)}) %collective-permute-start.6) | collective-permute-done | bytes 294944 | tf_op jit(solution)/shard_map/ppermute | solution.py:613
  89.1 3.0 shard_map.268.w_ref
  95.7 5.3 %shard_map.269.triple_ref = bf16[896,2304]{1,0:T(8,128)(2,1)S(1)} custom-call(bf16[896,768]{1,0:T(8,128)(2,1)S(1)} %shard_map.267.hidden_ref, bf16[2304,768]{1,0:T(8,128)(2,1)S(1)} %shard_map.268.w_ref, f32[1,2304]{1,0:T(1,128)S(1)} %get-tuple-element.126.bias_ref), custom_call_target="tpu_custom_call" | custom-call | flops 5400000 | bytes 1024 | tf_op jit(solution)/shard_map/pallas_call | solution.py:225
  101.0 10.1 %shard_map.270 = (bf16[896,768]{1,0:T(8,128)(2,1)S(1)}, f32[8,12,112,112]{3,2,1,0:T(8,128)S(1)}) custom-call(bf16[896,2304]{1,0:T(8,128)(2,1)S(1)} %shard_map.269.triple_ref), custom_call_target="tpu_custom_call" | custom-call | flops 5400000 | bytes 1024 | tf_op jit(solution)/shard_map/pallas_call | solution.py:273
  127.0 3.0 shard_map.273.w_ref
  130.0 10.9 %shard_map.274 = (bf16[896,3072]{1,0:T(8,128)(2,1)S(1)}, f32[896,3072]{1,0:T(8,128)S(1)}) custom-call(bf16[896,768]{1,0:T(8,128)(2,1)S(1)} %get-tuple-element.132.hidden_ref, bf16[768,3072]{1,0:T(8,128)(2,1)S(1)} %shard_map.273.w_ref, f32[1,3072]{1,0:T(1,128)S(1)} %get-tuple-element.136.bias_ref), custom_call_target="tpu_custom_call" | custom-call | flops 108000002048 | bytes 1024 | tf_op jit(solution)/shard_map/pallas_call | solution.py:324
  141.0 4.0 %copy-done.32 = f32[896,3072]{1,0:T(8,128)} copy-done((f32[896,3072]{1,0:T(8,128)}, f32[896,3072]{1,0:T(8,128)S(1)}, u32[]{:S(2)}) %copy-start.32) | copy-done | bytes 11010072
  146.8 9.2 %shard_map.275 = (bf16[768,3072]{1,0:T(8,128)(2,1)S(1)}, f32[1,3072]{1,0:T(1,128)}) custom-call(bf16[896,768]{1,0:T(8,128)(2,1)S(1)} %get-tuple-element.203.left_ref.cot_ref, bf16[896,3072]{1,0:T(8,128)(2,1)S(1)} %get-tuple-element.151.right_ref.active_ref), custom_call_target="tpu_custom_call" | custom-call | flops 5400000 | bytes 1024 | tf_op jit(solution)/shard_map/pallas_call | solution.py:376
  162.6 6.0 %collective-permute-done.19.refs_2_ = bf16[8,96,768]{2,1,0:T(8,128)(2,1)} collective-permute-done((bf16[8,96,768]{2,1,0:T(8,128)(2,1)}, bf16[8,96,768]{2,1,0:T(8,128)(2,1)}, u32[]{:S(2)}, u32[]{:S(2)}) %collective-permute-start.19) | collective-permute-done | bytes 1179680 | tf_op jit(solution)/shard_map/ppermute | solution.py:613
  170.4 3.4 shard_map.277.w_ref
  177.5 22.2 %shard_map.278 = (bf16[896,3072]{1,0:T(8,128)(2,1)S(1)}, bf16[768,3072]{1,0:T(8,128)(2,1)S(1)}, f32[1,3072]{1,0:T(1,128)S(1)}) custom-call(bf16[896,768]{1,0:T(8,128)(2,1)S(1)} %get-tuple-element.203.left_ref.cot_ref, bf16[768,3072]{1,0:T(8,128)(2,1)S(1)} %shard_map.277.w_ref, f32[896,3072]{1,0:T(8,128)} %copy-done.32, ...), custom_call_target="tpu_custom_call" | custom-call | flops 108000002048 | bytes 1024 | tf_op jit(solution)/shard_map/pallas_call | solution.py:404
  205.4 4.7 %shard_map.280 = bf16[896,768]{1,0:T(8,128)(2,1)S(1)} custom-call(bf16[896,3072]{1,0:T(8,128)(2,1)S(1)} %bitcast.46, bf16[768,3072]{1,0:T(8,128)(2,1)S(1)} %shard_map.277.w_ref, f32[8,768]{1,0:T(8,128)S(1)} %copy-done.26, f32[896,768]{1,0:T(8,128)S(1)} %copy-done.12), custom_call_target="tpu_custom_call" | custom-call | flops 108000002048 | bytes 1024 | tf_op jit(solution)/shard_map/pallas_call | solution.py:347
  210.1 6.2 %shard_map.281 = (f32[896,768]{1,0:T(8,128)S(1)}, bf16[896,768]{1,0:T(8,128)(2,1)S(1)}, f32[1,768]{1,0:T(1,128)S(1)}, f32[1,768]{1,0:T(1,128)S(1)}, f32[1,768]{1,0:T(1,128)S(1)}) custom-call(bf16[896,3072]{1,0:T(8,128)(2,1)S(1)} %get-tuple-element.155.grad_ref, bf16[768,3072]{1,0:T(8,128)(2,1)S(1)} %bitcast.44, f32[896,768]{1,0:T(8,128)S(1)} %copy-done.12, ...), custom_call_target="tpu_custom_call" | custom-call | flops 5400000 | bytes 1024 | tf_op jit(solution)/shard_map/pallas_call | solution.py:461
  216.3 3.5 shard_map.282
  222.5 2.8 collective-permute-start.24
  228.3 30.8 %shard_map.284.grad_ref = bf16[896,2304]{1,0:T(8,128)(2,1)S(1)} custom-call(bf16[896,2304]{1,0:T(8,128)(2,1)S(1)} %copy-done.5, f32[8,12,112,112]{3,2,1,0:T(8,128)} %copy-done.28, bf16[896,768]{1,0:T(8,128)(2,1)S(1)} %get-tuple-element.163.grad_ref), custom_call_target="tpu_custom_call" | custom-call | flops 108000002048 | bytes 1024 | tf_op jit(solution)/shard_map/pallas_call | solution.py:533
  263.9 6.0 %shard_map.285 = (bf16[2304,768]{1,0:T(8,128)(2,1)S(1)}, f32[1,2304]{1,0:T(1,128)S(1)}) custom-call(bf16[896,2304]{1,0:T(8,128)(2,1)S(1)} %shard_map.284.grad_ref, bf16[896,768]{1,0:T(8,128)(2,1)S(1)} %copy-done.22), custom_call_target="tpu_custom_call" | custom-call | flops 108000002048 | bytes 1024 | tf_op jit(solution)/shard_map/pallas_call | solution.py:565
  269.9 2.8 shard_map.286
  273.6 8.4 %collective-permute-done.29 = bf16[4,96,768]{2,1,0:T(8,128)(2,1)S(1)} collective-permute-done((bf16[4,96,768]{2,1,0:T(8,128)(2,1)S(1)}, bf16[4,96,768]{2,1,0:T(8,128)(2,1)S(1)}, u32[]{:S(2)}, u32[]{:S(2)}) %collective-permute-start.29) | collective-permute-done | bytes 589856 | tf_op jit(solution)/shard_map/ppermute | solution.py:613
  282.2 5.0 %shard_map.287 = (f32[896,768]{1,0:T(8,128)S(1)}, f32[1,768]{1,0:T(1,128)S(1)}, f32[1,768]{1,0:T(1,128)S(1)}) custom-call(bf16[896,2304]{1,0:T(8,128)(2,1)S(1)} %shard_map.284.grad_ref, bf16[2304,768]{1,0:T(8,128)(2,1)S(1)} %copy-done.7, bf16[896,768]{1,0:T(8,128)(2,1)S(1)} %copy-done.18, f32[896,768]{1,0:T(8,128)S(1)} %get-tuple-element.176.middle_ref, ...), custom_call_target="tpu_custom_call" | custom-call | flops 108000002048 | bytes 1024 | tf_op jit(solution)/shard_map/pallas_call | solution.py:591
  293.9 6.8 %shard_map.289 = bf16[1,602112]{1,0:T(2,128)(2,1)} custom-call(s32[4]{0:T(128)S(1)} %pad_add_fusion.at_ref, bf16[896,384]{1,0:T(8,128)(2,1)S(1)} %get-tuple-element.188.keep_ref, bf16[896,384]{1,0:T(8,128)(2,1)S(1)} %copy-done.31), custom_call_target="tpu_custom_call" | custom-call | flops 108000002048 | bytes 1024 | tf_op jit(solution)/shard_map/pallas_call | solution.py:174
  304.6 11.0 %collective-permute-done.35 = bf16[8,144,384]{2,1,0:T(8,128)(2,1)S(1)} collective-permute-done((bf16[8,144,384]{2,1,0:T(8,128)(2,1)S(1)}, bf16[8,144,384]{2,1,0:T(8,128)(2,1)S(1)}, u32[]{:S(2)}, u32[]{:S(2)}) %collective-permute-start.35) | collective-permute-done | bytes 884768 | tf_op jit(solution)/shard_map/ppermute | solution.py:613
  317.1 12.3 %shard_map.290 = f32[18816,128]{1,0:T(8,128)} custom-call(s32[4]{0:T(128)S(1)} %pad_add_fusion.at_ref, f32[896,384]{1,0:T(8,128)S(1)} %constant_dynamic-slice_fusion.keep_ref, bf16[896,384]{1,0:T(8,128)(2,1)S(1)} %collective-permute-done.34.got_ref, s32[16,112,1]{2,1,0:T(8,128)S(1)} %copy-done.24), custom_call_target="tpu_custom_call" | custom-call | flops 108000002048 | bytes 1024 | tf_op jit(solution)/shard_map/pallas_call | solution.py:149
  340.9 4.8 %collective-permute-done.47 = f32[16,768]{1,0:T(8,128)S(1)} collective-permute-done((f32[16,768]{1,0:T(8,128)S(1)}, f32[16,768]{1,0:T(8,128)S(1)}, u32[]{:S(2)}, u32[]{:S(2)}) %collective-permute-start.47) | collective-permute-done | bytes 49184 | tf_op jit(solution)/shard_map/ppermute | solution.py:613
  348.5 4.6 %collective-permute-done.42 = f32[144,384]{1,0:T(8,128)S(1)} collective-permute-done((f32[144,384]{1,0:T(8,128)S(1)}, f32[144,384]{1,0:T(8,128)S(1)}, u32[]{:S(2)}, u32[]{:S(2)}) %collective-permute-start.42) | collective-permute-done | bytes 221216 | tf_op jit(solution)/shard_map/ppermute | solution.py:613
  (267 shorter events, 116.2 us)
Async XLA Ops:
  3.2 28.0 %collective-permute-start.3 = (bf16[1,400,384]{2,1,0:T(8,128)(2,1)}, bf16[1,400,384]{2,1,0:T(8,128)(2,1)}, u32[]{:S(2)}, u32[]{:S(2)}) collective-permute-start(bf16[1,400,384]{2,1,0:T(8,128)(2,1)} %bitcast.5), channel_id=1, source_target_pairs={{0,6},{2,4},{4,2},{6,0},{1,7},{3,5},{5,3},{7,1},{8,14},{10,12},{12... | collective-permute-start | bytes 921608 | tf_op jit(solution)/shard_map/ppermute | solution.py:613
  8.3 26.5 %collective-permute-start.2 = (bf16[1,400,384]{2,1,0:T(8,128)(2,1)}, bf16[1,400,384]{2,1,0:T(8,128)(2,1)}, u32[]{:S(2)}, u32[]{:S(2)}) collective-permute-start(bf16[1,400,384]{2,1,0:T(8,128)(2,1)} %bitcast.5), channel_id=1, source_target_pairs={{0,4},{2,6},{4,0},{6,2},{1,5},{3,7},{5,1},{7,3},{8,12},{10,14},{12... | collective-permute-start | bytes 921608 | tf_op jit(solution)/shard_map/ppermute | solution.py:613
  8.3 26.5 %collective-permute-start.1 = (bf16[1,400,384]{2,1,0:T(8,128)(2,1)}, bf16[1,400,384]{2,1,0:T(8,128)(2,1)}, u32[]{:S(2)}, u32[]{:S(2)}) collective-permute-start(bf16[1,400,384]{2,1,0:T(8,128)(2,1)} %bitcast.5), channel_id=1, source_target_pairs={{0,2},{2,0},{4,6},{6,4},{1,3},{3,1},{5,7},{7,5},{8,10},{10,8},{12,... | collective-permute-start | bytes 921608 | tf_op jit(solution)/shard_map/ppermute | solution.py:613
  26.0 16.9 %collective-permute-start = (bf16[896,384]{1,0:T(8,128)(2,1)}, bf16[896,384]{1,0:T(8,128)(2,1)}, u32[]{:S(2)}, u32[]{:S(2)}) collective-permute-start(bf16[896,384]{1,0:T(8,128)(2,1)} %get-tuple-element.225), channel_id=1, source_target_pairs={{0,1},{1,0},{2,3},{3,2},{4,5},{5,4},{6,7},{7,6},{8,9},{9,8},{10,11... | collective-permute-start | bytes 2064392 | tf_op jit(solution)/shard_map/ppermute | solution.py:613
  44.6 31.5 %collective-permute-start.4 = (bf16[4,400,384]{2,1,0:T(8,128)(2,1)}, bf16[4,400,384]{2,1,0:T(8,128)(2,1)}, u32[]{:S(2)}, u32[]{:S(2)}) collective-permute-start(bf16[4,400,384]{2,1,0:T(8,128)(2,1)} %pad_maximum_fusion), channel_id=1, source_target_pairs={{0,1},{1,0},{2,3},{3,2},{4,5},{5,4},{6,7},{7,6},{8,9},{9,8},{10,11... | collective-permute-start | bytes 3686408 | tf_op jit(solution)/shard_map/ppermute | solution.py:613
  51.7 23.5 %collective-permute-start.6 = (bf16[1,192,768]{2,1,0:T(8,128)(2,1)}, bf16[1,192,768]{2,1,0:T(8,128)(2,1)S(1)}, u32[]{:S(2)}, u32[]{:S(2)}) collective-permute-start(bf16[1,192,768]{2,1,0:T(8,128)(2,1)} %bitcast.57), channel_id=1, source_target_pairs={{0,4},{2,6},{4,0},{6,2},{1,5},{3,7},{5,1},{7,3},{8,12},{10,14},{12... | collective-permute-start | bytes 884744 | tf_op jit(solution)/shard_map/ppermute | solution.py:613
  51.7 23.5 %collective-permute-start.5 = (bf16[1,192,768]{2,1,0:T(8,128)(2,1)}, bf16[1,192,768]{2,1,0:T(8,128)(2,1)S(1)}, u32[]{:S(2)}, u32[]{:S(2)}) collective-permute-start(bf16[1,192,768]{2,1,0:T(8,128)(2,1)} %bitcast.58), channel_id=1, source_target_pairs={{0,2},{2,0},{4,6},{6,4},{1,3},{3,1},{5,7},{7,5},{8,10},{10,8},{12,... | collective-permute-start | bytes 884744 | tf_op jit(solution)/shard_map/ppermute | solution.py:613
  75.4 38.1 %collective-permute-start.12 = (bf16[4,192,768]{2,1,0:T(8,128)(2,1)S(1)}, bf16[4,192,768]{2,1,0:T(8,128)(2,1)S(1)}, u32[]{:S(2)}, u32[]{:S(2)}) collective-permute-start(bf16[4,192,768]{2,1,0:T(8,128)(2,1)S(1)} %pad_maximum_fusion.1.refs_0_), channel_id=1, source_target_pairs={{0,1},{1,0},{2,3},{3,2},{4,5},{5,4},{6,7},{7,6},{8,9},{9,8},{10,11... | collective-permute-start | bytes 3538952 | tf_op jit(solution)/shard_map/ppermute | solution.py:613
  78.5 13.6 %collective-permute-start.11 = (bf16[1,96,768]{2,1,0:T(8,128)(2,1)S(1)}, bf16[1,96,768]{2,1,0:T(8,128)(2,1)S(1)}, u32[]{:S(2)}, u32[]{:S(2)}) collective-permute-start(bf16[1,96,768]{2,1,0:T(8,128)(2,1)S(1)} %bitcast.52), channel_id=1, source_target_pairs={{0,6},{2,4},{4,2},{6,0},{1,7},{3,5},{5,3},{7,1},{8,14},{10,12},{12... | collective-permute-start | bytes 442376 | tf_op jit(solution)/shard_map/ppermute | solution.py:613
  92.4 25.8 %collective-permute-start.13 = (bf16[4,96,768]{2,1,0:T(8,128)(2,1)S(1)}, bf16[4,96,768]{2,1,0:T(8,128)(2,1)S(1)}, u32[]{:S(2)}, u32[]{:S(2)}) collective-permute-start(bf16[4,96,768]{2,1,0:T(8,128)(2,1)S(1)} %pad_maximum_fusion.2), channel_id=1, source_target_pairs={{0,1},{1,0},{2,3},{3,2},{4,5},{5,4},{6,7},{7,6},{8,9},{9,8},{10,11... | collective-permute-start | bytes 1769480 | tf_op jit(solution)/shard_map/ppermute | solution.py:613
  119.1 26.0 %collective-permute-start.16 = (bf16[896,384]{1,0:T(8,128)(2,1)}, bf16[896,384]{1,0:T(8,128)(2,1)}, u32[]{:S(2)}, u32[]{:S(2)}) collective-permute-start(bf16[896,384]{1,0:T(8,128)(2,1)} %get-tuple-element.130), channel_id=1, source_target_pairs={{0,1},{1,0},{2,3},{3,2},{4,5},{5,4},{6,7},{7,6},{8,9},{9,8},{10,11... | collective-permute-start | bytes 2064392 | tf_op jit(solution)/shard_map/ppermute | solution.py:613
  119.8 42.4 %collective-permute-start.18 = (bf16[8,96,768]{2,1,0:T(8,128)(2,1)}, bf16[8,96,768]{2,1,0:T(8,128)(2,1)}, u32[]{:S(2)}, u32[]{:S(2)}) collective-permute-start(bf16[8,96,768]{2,1,0:T(8,128)(2,1)} %constant_dynamic-update-slice_fusion.5.refs_0_), channel_id=1, source_target_pairs={{0,16},{8,24},{16,0},{24,8},{1,17},{9,25},{17,1},{25,9},{2,18},{10... | collective-permute-start | bytes 3538952 | tf_op jit(solution)/shard_map/ppermute | solution.py:613
  176.1 28.1 %collective-permute-start.21 = (bf16[4,192,768]{2,1,0:T(8,128)(2,1)S(1)}, bf16[4,192,768]{2,1,0:T(8,128)(2,1)S(1)}, u32[]{:S(2)}, u32[]{:S(2)}) collective-permute-start(bf16[4,192,768]{2,1,0:T(8,128)(2,1)S(1)} %get-tuple-element.208), channel_id=1, source_target_pairs={{0,1},{1,0},{2,3},{3,2},{4,5},{5,4},{6,7},{7,6},{8,9},{9,8},{10,11... | collective-permute-start | bytes 3538952 | tf_op jit(solution)/shard_map/ppermute | solution.py:613
  203.0 22.4 %collective-permute-start.22 = (bf16[16,96,768]{2,1,0:T(8,128)(2,1)S(1)}, bf16[16,96,768]{2,1,0:T(8,128)(2,1)}, u32[]{:S(2)}, u32[]{:S(2)}) collective-permute-start(bf16[16,96,768]{2,1,0:T(8,128)(2,1)S(1)} %get-tuple-element.149), channel_id=1, source_target_pairs={{0,8},{8,0},{16,24},{24,16},{1,9},{9,1},{17,25},{25,17},{2,10},{10... | collective-permute-start | bytes 7077896 | tf_op jit(solution)/shard_map/ppermute | solution.py:613
  205.3 17.1 %collective-permute-start.23 = (bf16[2,192,768]{2,1,0:T(8,128)(2,1)}, bf16[2,192,768]{2,1,0:T(8,128)(2,1)S(1)}, u32[]{:S(2)}, u32[]{:S(2)}) collective-permute-start(bf16[2,192,768]{2,1,0:T(8,128)(2,1)} %get-tuple-element.215), channel_id=1, source_target_pairs={{0,2},{2,0},{4,6},{6,4},{1,3},{3,1},{5,7},{7,5},{8,10},{10,8},{12,... | collective-permute-start | bytes 1769480 | tf_op jit(solution)/shard_map/ppermute | solution.py:613
  220.8 38.3 %collective-permute-start.26 = (bf16[8,96,384]{2,1,0:T(8,128)(2,1)S(1)}, bf16[8,96,384]{2,1,0:T(8,128)(2,1)S(1)}, u32[]{:S(2)}, u32[]{:S(2)}) collective-permute-start(bf16[8,96,384]{2,1,0:T(8,128)(2,1)S(1)} %get-tuple-element.160), channel_id=1, source_target_pairs={{0,8},{8,0},{16,24},{24,16},{1,9},{9,1},{17,25},{25,17},{2,10},{10... | collective-permute-start | bytes 1769480 | tf_op jit(solution)/shard_map/ppermute | solution.py:613
  221.1 40.8 %collective-permute-start.33 = (bf16[896,384]{1,0:T(8,128)(2,1)S(1)}, bf16[896,384]{1,0:T(8,128)(2,1)S(1)}, u32[]{:S(2)}, u32[]{:S(2)}) collective-permute-start(bf16[896,384]{1,0:T(8,128)(2,1)S(1)} %get-tuple-element.189), channel_id=1, source_target_pairs={{0,1},{1,0},{2,3},{3,2},{4,5},{5,4},{6,7},{7,6},{8,9},{9,8},{10,11... | collective-permute-start | bytes 2064392 | tf_op jit(solution)/shard_map/ppermute | solution.py:613
  222.5 36.6 %collective-permute-start.24 = (bf16[1,192,768]{2,1,0:T(8,128)(2,1)S(1)}, bf16[1,192,768]{2,1,0:T(8,128)(2,1)S(1)}, u32[]{:S(2)}, u32[]{:S(2)}) collective-permute-start(bf16[1,192,768]{2,1,0:T(8,128)(2,1)S(1)} %fusion.8), channel_id=1, source_target_pairs={{0,4},{2,6},{4,0},{6,2},{1,5},{3,7},{5,1},{7,3},{8,12},{10,14},{12... | collective-permute-start | bytes 884744 | tf_op jit(solution)/shard_map/ppermute | solution.py:613
  227.7 34.2 %collective-permute-start.25 = (bf16[8,96,768]{2,1,0:T(8,128)(2,1)S(1)}, bf16[8,96,768]{2,1,0:T(8,128)(2,1)S(1)}, u32[]{:S(2)}, u32[]{:S(2)}) collective-permute-start(bf16[8,96,768]{2,1,0:T(8,128)(2,1)S(1)} %get-tuple-element.207), channel_id=1, source_target_pairs={{0,16},{8,24},{16,0},{24,8},{1,17},{9,25},{17,1},{25,9},{2,18},{10... | collective-permute-start | bytes 3538952 | tf_op jit(solution)/shard_map/ppermute | solution.py:613
  259.2 13.5 %collective-permute-start.28 = (bf16[192,768]{1,0:T(8,128)(2,1)S(1)}, bf16[192,768]{1,0:T(8,128)(2,1)S(1)}, u32[]{:S(2)}, u32[]{:S(2)}) collective-permute-start(bf16[192,768]{1,0:T(8,128)(2,1)S(1)} %get-tuple-element.204), channel_id=1, source_target_pairs={{0,16},{8,24},{16,0},{24,8},{1,17},{9,25},{17,1},{25,9},{2,18},{10... | collective-permute-start | bytes 884744 | tf_op jit(solution)/shard_map/ppermute | solution.py:613
  262.8 19.2 %collective-permute-start.29 = (bf16[4,96,768]{2,1,0:T(8,128)(2,1)S(1)}, bf16[4,96,768]{2,1,0:T(8,128)(2,1)S(1)}, u32[]{:S(2)}, u32[]{:S(2)}) collective-permute-start(bf16[4,96,768]{2,1,0:T(8,128)(2,1)S(1)} %get-tuple-element.213), channel_id=1, source_target_pairs={{0,1},{1,0},{2,3},{3,2},{4,5},{5,4},{6,7},{7,6},{8,9},{9,8},{10,11... | collective-permute-start | bytes 1769480 | tf_op jit(solution)/shard_map/ppermute | solution.py:613
  272.7 19.9 %collective-permute-start.27 = (bf16[16,144,384]{2,1,0:T(8,128)(2,1)S(1)}, bf16[16,144,384]{2,1,0:T(8,128)(2,1)S(1)}, u32[]{:S(2)}, u32[]{:S(2)}) collective-permute-start(bf16[16,144,384]{2,1,0:T(8,128)(2,1)S(1)} %get-tuple-element.171), channel_id=1, source_target_pairs={{0,8},{8,0},{16,24},{24,16},{1,9},{9,1},{17,25},{25,17},{2,10},{10... | collective-permute-start | bytes 5308424 | tf_op jit(solution)/shard_map/ppermute | solution.py:613
  272.9 14.3 %collective-permute-start.32 = (bf16[2,96,384]{2,1,0:T(8,128)(2,1)S(1)}, bf16[2,96,384]{2,1,0:T(8,128)(2,1)S(1)}, u32[]{:S(2)}, u32[]{:S(2)}) collective-permute-start(bf16[2,96,384]{2,1,0:T(8,128)(2,1)S(1)} %get-tuple-element.231), channel_id=1, source_target_pairs={{0,2},{2,0},{4,6},{6,4},{1,3},{3,1},{5,7},{7,5},{8,10},{10,8},{12,... | collective-permute-start | bytes 442376 | tf_op jit(solution)/shard_map/ppermute | solution.py:613
  273.0 17.1 %collective-permute-start.52 = (f32[192,768]{1,0:T(8,128)S(1)}, f32[192,768]{1,0:T(8,128)S(1)}, u32[]{:S(2)}, u32[]{:S(2)}) collective-permute-start(f32[192,768]{1,0:T(8,128)S(1)} %convert_add_fusion.4), channel_id=1, source_target_pairs={{0,8},{8,0},{16,24},{24,16},{1,9},{9,1},{17,25},{25,17},{2,10},{10... | collective-permute-start | bytes 1769480 | tf_op jit(solution)/shard_map/ppermute | solution.py:613
  287.3 29.8 %collective-permute-start.34 = (bf16[896,384]{1,0:T(8,128)(2,1)S(1)}, bf16[896,384]{1,0:T(8,128)(2,1)S(1)}, u32[]{:S(2)}, u32[]{:S(2)}) collective-permute-start(bf16[896,384]{1,0:T(8,128)(2,1)S(1)} %dynamic-slice_convert_fusion), channel_id=1, source_target_pairs={{0,1},{1,0},{2,3},{3,2},{4,5},{5,4},{6,7},{7,6},{8,9},{9,8},{10,11... | collective-permute-start | bytes 2064392 | tf_op jit(solution)/shard_map/ppermute | solution.py:613
  293.1 22.5 %collective-permute-start.35 = (bf16[8,144,384]{2,1,0:T(8,128)(2,1)S(1)}, bf16[8,144,384]{2,1,0:T(8,128)(2,1)S(1)}, u32[]{:S(2)}, u32[]{:S(2)}) collective-permute-start(bf16[8,144,384]{2,1,0:T(8,128)(2,1)S(1)} %get-tuple-element.211), channel_id=1, source_target_pairs={{0,16},{8,24},{16,0},{24,8},{1,17},{9,25},{17,1},{25,9},{2,18},{10... | collective-permute-start | bytes 2654216 | tf_op jit(solution)/shard_map/ppermute | solution.py:613
  301.6 27.8 %collective-permute-start.44 = (f32[16,768]{1,0:T(8,128)S(1)}, f32[16,768]{1,0:T(8,128)S(1)}, u32[]{:S(2)}, u32[]{:S(2)}) collective-permute-start(f32[16,768]{1,0:T(8,128)S(1)} %add.248), channel_id=1, source_target_pairs={{0,16},{8,24},{16,0},{24,8},{1,17},{9,25},{17,1},{25,9},{2,18},{10... | collective-permute-start | bytes 147464 | tf_op jit(solution)/shard_map/ppermute | solution.py:613
  302.4 28.0 %collective-permute-start.48 = (bf16[96,384]{1,0:T(8,128)(2,1)S(1)}, bf16[96,384]{1,0:T(8,128)(2,1)S(1)}, u32[]{:S(2)}, u32[]{:S(2)}) collective-permute-start(bf16[96,384]{1,0:T(8,128)(2,1)S(1)} %get-tuple-element.200), channel_id=1, source_target_pairs={{0,16},{8,24},{16,0},{24,8},{1,17},{9,25},{17,1},{25,9},{2,18},{10... | collective-permute-start | bytes 221192 | tf_op jit(solution)/shard_map/ppermute | solution.py:613
  303.8 28.6 %collective-permute-start.50 = (f32[96,768]{1,0:T(8,128)S(1)}, f32[96,768]{1,0:T(8,128)S(1)}, u32[]{:S(2)}, u32[]{:S(2)}) collective-permute-start(f32[96,768]{1,0:T(8,128)S(1)} %bitcast.47), channel_id=1, source_target_pairs={{0,16},{8,24},{16,0},{24,8},{1,17},{9,25},{17,1},{25,9},{2,18},{10... | collective-permute-start | bytes 884744 | tf_op jit(solution)/shard_map/ppermute | solution.py:613
  315.8 14.5 %collective-permute-start.39 = (bf16[4,144,384]{2,1,0:T(8,128)(2,1)S(1)}, bf16[4,144,384]{2,1,0:T(8,128)(2,1)S(1)}, u32[]{:S(2)}, u32[]{:S(2)}) collective-permute-start(bf16[4,144,384]{2,1,0:T(8,128)(2,1)S(1)} %get-tuple-element.217), channel_id=1, source_target_pairs={{0,1},{1,0},{2,3},{3,2},{4,5},{5,4},{6,7},{7,6},{8,9},{9,8},{10,11... | collective-permute-start | bytes 1327112 | tf_op jit(solution)/shard_map/ppermute | solution.py:613
  332.3 21.4 %collective-permute-start.49 = (f32[96,384]{1,0:T(8,128)S(1)}, f32[96,384]{1,0:T(8,128)S(1)}, u32[]{:S(2)}, u32[]{:S(2)}) collective-permute-start(f32[96,384]{1,0:T(8,128)S(1)} %convert_add_fusion.5), channel_id=1, source_target_pairs={{0,8},{8,0},{16,24},{24,16},{1,9},{9,1},{17,25},{25,17},{2,10},{10... | collective-permute-start | bytes 442376 | tf_op jit(solution)/shard_map/ppermute | solution.py:613
  335.4 19.0 %collective-permute-start.51 = (f32[2,96,768]{2,1,0:T(8,128)S(1)}, f32[2,96,768]{2,1,0:T(8,128)S(1)}, u32[]{:S(2)}, u32[]{:S(2)}) collective-permute-start(f32[2,96,768]{2,1,0:T(8,128)S(1)} %maximum_select_fusion.6), channel_id=1, source_target_pairs={{0,8},{8,0},{16,24},{24,16},{1,9},{9,1},{17,25},{25,17},{2,10},{10... | collective-permute-start | bytes 1769480 | tf_op jit(solution)/shard_map/ppermute | solution.py:613
  (67 other events, 687.5 us)

commit v4 on v3

--- a/solution.py
+++ b/solution.py
@@ -14,7 +14,7 @@
 VISIBLE = 49
 PAIR = 2 * VISIBLE
 ROWS = 112
-TILE = 256
+TILE = 768
 EPS = 1e-06
 BF = jnp.bfloat16
 F32 = jnp.float32
@@ -28,7 +28,7 @@
 FLOPS_PER_US = 540000000
 
 
-def call(body, grid, ins, outs, shapes, scratch=(), prefetch=0, us=1.0, nbytes=0, vmem=24):
+def call(body, grid, ins, outs, shapes, scratch=(), prefetch=0, us=1.0, nbytes=0, vmem=32):
     return pl.pallas_call(
         body,
         out_shape=shapes,
@@ -247,25 +247,32 @@
     return image(at_row) == image(at_col)
 
 
+def side_by_side(block):
+    left = lax.broadcasted_iota(jnp.int32, (ROWS, 128), 1) < HEAD_DIM
+    none = jnp.zeros_like(block)
+    return jnp.concatenate([jnp.where(left, block, none), jnp.where(left, none, block)])
+
+
+def both_heads(stack):
+    left = lax.broadcasted_iota(jnp.int32, (ROWS, 128), 1) < HEAD_DIM
+    return jnp.where(left, stack[:ROWS], stack[ROWS:])
+
+
+def pair_of(ref, part, pair):
+    return ref[:, part * D + pair * 128 : part * D + (pair + 1) * 128]
+
+
 def attend_body(triple_ref, mixed_ref, prob_ref):
-    keep = same_image()
-    left = lax.broadcasted_iota(jnp.int32, (ROWS, 128), 1) < HEAD_DIM
+    keep = same_image()[None]
     for pair in range(HEADS // 2):
-        q = triple_ref[:, pair * 128 : (pair + 1) * 128]
-        k = triple_ref[:, D + pair * 128 : D + (pair + 1) * 128]
-        v = triple_ref[:, 2 * D + pair * 128 : 2 * D + (pair + 1) * 128]
-        halves = []
-        for side in range(2):
-            mine = left if side == 0 else jnp.logical_not(left)
-            scores = dot(jnp.where(mine, q, jnp.zeros_like(q)), k, 1, 1) * HEAD_DIM**-0.5
-            scores = jnp.where(keep, scores, -1e30)
-            expo = jnp.exp(scores - jnp.max(scores, 1, keepdims=True))
-            prob = expo / jnp.sum(expo, 1, keepdims=True)
-            prob_ref[0, 2 * pair + side] = prob
-            halves.append(dot(prob.astype(BF), v, 1, 0))
-        mixed_ref[:, pair * 128 : (pair + 1) * 128] = jnp.where(left, halves[0], halves[1]).astype(
-            BF
-        )
+        q, k, v = (pair_of(triple_ref, part, pair) for part in range(3))
+        scores = dot(side_by_side(k), q, 1, 1).reshape(2, ROWS, ROWS) * HEAD_DIM**-0.5
+        scores = jnp.where(keep, scores, -1e30)
+        expo = jnp.exp(scores - jnp.max(scores, 1, keepdims=True))
+        prob = expo / jnp.sum(expo, 1, keepdims=True)
+        prob_ref[0, 2 * pair : 2 * pair + 2] = prob
+        low = prob.astype(BF).reshape(2 * ROWS, ROWS)
+        mixed_ref[:, pair * 128 : (pair + 1) * 128] = dot(low, side_by_side(v), 0, 0).astype(BF)
 
 
 def attend(triple):
@@ -275,7 +282,7 @@
         (groups,),
         [spec((ROWS, 3 * D), lambda g: (g, 0))],
         [spec((ROWS, D), lambda g: (g, 0)), spec((1, HEADS, ROWS, ROWS), lambda g: (g, 0, 0, 0))],
-        [struct((groups * ROWS, D), BF), struct((groups, HEADS, ROWS, ROWS), F32)],
+        [struct((groups * ROWS, D), BF), pltpu.HBM((groups, HEADS, ROWS, ROWS), F32)],
         us=0.01,
         nbytes=groups * ROWS * (8 * D + HEADS * 512),
     )(triple)
@@ -330,8 +337,8 @@
             spec((1, TILE), lambda j: (0, j)),
         ],
         [tile, tile],
-        [struct((r, units), BF), struct((r, units), F32)],
-        us=200,
+        [pltpu.HBM((r, units), BF), pltpu.HBM((r, units), F32)],
+        us=0.01,
         nbytes=r * D * 2 + D * units * 2 + r * units * 6,
     )(hidden, w, bias)
 
@@ -380,7 +387,7 @@
         [spec((rows, TILE), lambda j: (0, j)), spec((1, TILE), lambda j: (0, j))],
         [struct((rows, width), BF), struct((1, width), F32)],
         [pltpu.VMEM((rows, r), BF)],
-        us=0.01,
+        us=200,
         nbytes=r * rows * 2 + r * width * 2 + rows * width * 2,
     )(left, right)
 
@@ -406,7 +413,7 @@
         (units // TILE,),
         [full, col, tile, full],
         [tile, col, spec((1, TILE), lambda j: (0, j))],
-        [struct((r, units), BF), struct((D, units), BF), struct((1, units), F32)],
+        [pltpu.HBM((r, units), BF), struct((D, units), BF), struct((1, units), F32)],
         [pltpu.VMEM((D, r), BF)],
         us=200,
         nbytes=r * D * 4 + D * units * 4 + r * units * 6,
@@ -502,28 +509,21 @@
 
 def attend_back_body(triple_ref, prob_ref, grad_ref, *rest):
     out_ref = rest[-1]
-    left = lax.broadcasted_iota(jnp.int32, (ROWS, 128), 1) < HEAD_DIM
     scale = HEAD_DIM**-0.5
     for pair in range(HEADS // 2):
-        q = triple_ref[:, pair * 128 : (pair + 1) * 128]
-        k = triple_ref[:, D + pair * 128 : D + (pair + 1) * 128]
-        v = triple_ref[:, 2 * D + pair * 128 : 2 * D + (pair + 1) * 128]
-        grad = grad_ref[:, pair * 128 : (pair + 1) * 128]
-        gq, gk, gv = [], [], []
-        for side in range(2):
-            mine = left if side == 0 else jnp.logical_not(left)
-            prob = prob_ref[0, 2 * pair + side]
-            gv.append(dot(prob.astype(BF), grad, 0, 0))
-            grad_prob = dot(jnp.where(mine, grad, jnp.zeros_like(grad)), v, 1, 1)
-            inside = jnp.sum(grad_prob * prob, 1, keepdims=True)
-            grad_scores = (prob * (grad_prob - inside)).astype(BF)
-            gq.append(dot(grad_scores, k, 1, 0))
-            gk.append(dot(grad_scores, q, 0, 0))
-        for at, pieces, factor in ((0, gq, scale), (1, gk, scale), (2, gv, None)):
-            both = jnp.where(left, pieces[0], pieces[1])
-            if factor is not None:
-                both = both * factor
-            out_ref[:, at * D + pair * 128 : at * D + (pair + 1) * 128] = both.astype(BF)
+        q, k, v = (pair_of(triple_ref, part, pair) for part in range(3))
+        grad = pair_of(grad_ref, 0, pair)
+        prob = prob_ref[0, 2 * pair : 2 * pair + 2]
+        grad_prob = dot(side_by_side(v), grad, 1, 1).reshape(2, ROWS, ROWS)
+        inside = jnp.sum(grad_prob * prob, 1, keepdims=True)
+        grad_scores = (prob * (grad_prob - inside)).astype(BF).reshape(2 * ROWS, ROWS)
+        grads = (
+            dot(grad_scores, side_by_side(k), 0, 0) * scale,
+            both_heads(dot(grad_scores, q, 1, 0)) * scale,
+            both_heads(dot(prob.astype(BF).reshape(2 * ROWS, ROWS), grad, 1, 0)),
+        )
+        for part, value in enumerate(grads):
+            out_ref[:, part * D + pair * 128 : part * D + (pair + 1) * 128] = value.astype(BF)
 
 
 def attend_back(triple, prob, grad, start, stop, partial_out=None):
@@ -600,7 +600,7 @@
         ],
         [row, vec, vec],
         [struct((r, D), F32), vec_out, vec_out],
-        us=200,
+        us=0.01,
         nbytes=r * width * 2 + D * width * 2 + r * D * 10,
     )(grad, w, rows, grad_middle, vecs)
 
@@ -650,27 +650,34 @@
     return total
 
 
-def qkv_plan(cols, heads_cols, parts, spots=None):
+def qkv_plan(cols, heads_cols, parts, spots):
     rows = heads_cols // parts
-    spots = spots or [(p * rows, 0) for p in range(3)]
 
     def plan(w, n, q):
         return [
-            (spot, (rows, cols), (p * D + w * heads_cols + q * rows, n * cols))
-            for p, spot in enumerate(spots)
+            (0, spot, (rows, cols), (p * D + w * heads_cols + q * rows, n * cols))
+            for p, spot in spots.items()
         ]
 
     return plan
 
 
-def out_plan(cols, heads_cols, parts, spot=(0, 0)):
+def out_plan(cols, heads_cols, parts, spot, which=0):
     rows = heads_cols // parts
-    return lambda w, n, q: [(spot, (rows, cols), (w * heads_cols + q * rows, n * cols))]
-
-
-def flat_plan(cols, units, parts, spot=(0, 0)):
+    return lambda w, n, q: [(which, spot, (rows, cols), (w * heads_cols + q * rows, n * cols))]
+
+
+def flat_plan(cols, units, parts):
     rows = cols // parts
-    return lambda w, n, q: [(spot, (rows, units), (n * cols + q * rows, w * units))]
+    return lambda w, n, q: [(0, (0, 0), (rows, units), (n * cols + q * rows, w * units))]
+
+
+def sums_plan(cols, narrow, spot, which):
+    return lambda w, n, q: [(which, spot, (16, cols), ((w * narrow + n) * 16, 0))]
+
+
+def joined(*plans):
+    return lambda w, n, q: [move for plan in plans for move in plan(w, n, q)]
 
 
 def prep_body(cols, rows, at_ref, *refs):
@@ -802,19 +809,51 @@
 CORE, DP_INDEX = 2, 3
 
 
+def owner_sums_body(wide, narrow, cols, *refs):
+    out = refs[-1]
+    narrow_refs, qkv_ref, up_ref = refs[:6], refs[6], refs[7]
+    part, units = D // wide, up_ref.shape[1] // wide
+    for w in range(wide):
+        for n in range(narrow):
+            lines = [ref[:, n * cols : (n + 1) * cols] for ref in narrow_refs]
+            lines.append(
+                jnp.concatenate(
+                    [qkv_ref[:, p * D + w * part : p * D + (w + 1) * part] for p in (0, 2)], axis=1
+                )
+            )
+            lines += [
+                up_ref[:, w * units + k : w * units + k + cols] for k in range(0, units, cols)
+            ]
+            lines.append(jnp.zeros((16 - len(lines), cols), F32))
+            at = (w * narrow + n) * 16
+            out[at : at + 16, :] = jnp.concatenate(lines, axis=0).astype(BF)
+
+
+def owner_sums(wide, narrow, cols, *rows):
+    vmem = pl.BlockSpec(memory_space=pltpu.VMEM)
+    return pl.pallas_call(
+        partial(owner_sums_body, wide, narrow, cols),
+        out_shape=struct((wide * narrow * 16, cols), BF),
+        in_specs=[vmem] * len(rows),
+        out_specs=vmem,
+        compiler_params=pltpu.CompilerParams(vmem_limit_bytes=8 * MB),
+        cost_estimate=pl.CostEstimate(
+            flops=FLOPS_PER_US // 100, bytes_accessed=1024, transcendentals=0
+        ),
+    )(*rows)
+
+
 def build_body(plan, tag_lists, inverse, part_at, at_ref, *refs):
-    sem = refs[-1]
-    if inverse:
-        whole_ref, arrays = refs[0], refs[1:-1]
-    else:
-        arrays, whole_ref = refs[:-2], refs[-2]
+    refs, sem = refs[:-1], refs[-1]
+    count = len(tag_lists)
+    wholes, arrays = (refs[:-count], refs[-count:]) if inverse else (refs[count:], refs[:count])
     copies = []
     for array, tags in zip(arrays, tag_lists):
         for k, (dw, dn, dq) in enumerate(tags):
             w, n, q = at_ref[0] ^ dw, at_ref[1] ^ dn, at_ref[part_at] ^ dq
-            for (at_row, at_lane), (rows, lanes), (row, lane) in plan(w, n, q):
+            for which, (at_row, at_lane), (rows, lanes), (row, lane) in plan(w, n, q):
                 piece = array.at[k, pl.ds(at_row, rows), pl.ds(at_lane, lanes)]
-                whole = whole_ref.at[
+                whole = wholes[which].at[
                     pl.ds(pl.multiple_of(row, 16), rows), pl.ds(pl.multiple_of(lane, 128), lanes)
                 ]
                 ends = (whole, piece) if inverse else (piece, whole)
@@ -844,26 +883,60 @@
     )(at, *arrays)
 
 
+CORE, DP_INDEX = 2, 3
+
+
 def build_weights(at, pieces, plan, shape, part_at=CORE):
-    arrays, tags = [p.stack for p in pieces], [p.tags for p in pieces]
-    arrays = [in_hbm(a) for a in arrays]
+    arrays, tags = [in_hbm(p.stack) for p in pieces], [p.tags for p in pieces]
     return move_pieces(at, arrays, plan, tags, False, part_at, [shape])[0]
 
 
-def cut_grads(at, grad, plan, tags, shape, part_at=CORE):
+def cut_grads(at, grads, plan, tags, shape, part_at=CORE):
     tag_lists = [[(w, n, q ^ dc) for w, n, q in tags] for dc in range(2)]
-    return move_pieces(at, [grad], plan, tag_lists, True, part_at, [(len(tags),) + shape] * 2)
+    return move_pieces(at, grads, plan, tag_lists, True, part_at, [(len(tags),) + shape] * 2)
+
+
+def fence_body(x_ref, out_ref):
+    out_ref[...] = x_ref[...]
+
+
+def fence(token):
+    vmem = pl.BlockSpec(memory_space=pltpu.VMEM)
+    return pl.pallas_call(
+        fence_body,
+        out_shape=struct(token.shape, token.dtype),
+        in_specs=[vmem],
+        out_specs=vmem,
+        compiler_params=pltpu.CompilerParams(vmem_limit_bytes=MB, has_side_effects=True),
+        cost_estimate=pl.CostEstimate(
+            flops=200 * FLOPS_PER_US, bytes_accessed=1024, transcendentals=0
+        ),
+    )(token)
 
 
 class Chain:
-    def __init__(self, at, grad, plan, tags, shape, part_at=CORE):
-        self.keep, self.send = cut_grads(at, grad, plan, tags, shape, part_at)
+    def __init__(self, at, grads, plan, tags, shape, part_at=CORE):
+        self.keep, self.send = cut_grads(at, grads, plan, tags, shape, part_at)
 
     def go(self, axis, bit):
         self.got = swap(self.send, axis, bit)
 
     def fold(self, *deps):
         self.keep, self.send = halves_summed(self.keep, hold(self.got, *deps))
+
+    def spread(self, *deps):
+        got = hold(self.got, *deps)
+        order = (0, 2, 1, 3)
+        total = [k.astype(F32) + g.astype(F32) for k, g in zip(self.keep, got)]
+        self.keep = total[0]
+        self.send = [total[order.index(bit)].astype(BF) for bit in range(1, len(total))]
+        self.got = [swap(piece, WIDE, bit) for bit, piece in enumerate(self.send, 1)]
+
+    def all_of(self, *deps):
+        total = self.keep
+        for got in hold(self.got, *deps):
+            total = total + got.astype(F32)
+        return total
 
     def total(self, *deps):
         return self.keep[0].astype(F32) + hold(self.got, *deps)[0].astype(F32)
@@ -889,15 +962,6 @@
 def quarter(at, shard):
     rows = shard.shape[0] // 4
     return lax.dynamic_slice_in_dim(shard, at[3] * rows, rows, axis=0)
-
-
-def total_over_all(value, axes):
-    for axis in axes:
-        bit = 1
-        while bit < lax.axis_size(axis):
-            value = value + swap(value, axis, bit)
-            bit *= 2
-    return value
 
 
 def to_rows(blocks, narrow):
@@ -1021,7 +1085,9 @@
         vecs, bias_qkv, bias_up = vectors_of(at, [first], vec_at, wide, narrow, cols, units)
         hidden_one = norm(rows, vecs)
         all_first = [first, first_c.after(hidden_one)]
-        qkv_t = build_weights(at, all_first, qkv_plan(cols, heads_cols, 2), (3 * D, D))
+        half = heads_cols // 2
+        first_plan = qkv_plan(cols, heads_cols, 2, {p: (p * half, 0) for p in range(3)})
+        qkv_t = build_weights(at, all_first, first_plan, (3 * D, D))
         out_w = build_weights(at, all_first, out_plan(cols, heads_cols, 2, out_at), (D, D))
         down_p = down_p.join(*[p.after(qkv_t) for p in down_z])
         down_x = down_p.fetch(NARROW, 1)
@@ -1042,22 +1108,24 @@
         up_w = build_weights(at, [up_p, up_x, up_c, up_xc], half_flat, whole)
         active, slope = up(hidden_two, up_w, bias_up)
         cot = join_cols(cot_out[own:], hold(cot_got, active))
-        gw_down, _ = outer(cot, active)
-        gb_down = jnp.sum(cot, 0, dtype=F32)[None]
+        down_y = down_y.after(active)
+        down_c = [p.fetch(DP, 1, down_y.stack) for p in (down_p, down_y)]
+
         x_first = [(w, n, 0) for n in range(2) for w in (0, 2, 1, 3)]
         y_first = [(w, n, dy) for dy in (0, 2) for n in range(2) for w in (0, 2, 1, 3)]
-        g_d = Chain(at, gw_down, half_flat, x_first, (cols // 2, units))
+        gw_down, _ = outer(hold(cot, *[p.stack for p in (down_p, down_y)]), active)
+        gb_down = jnp.sum(cot, 0, dtype=F32)[None]
+        down_c = [p.after(gw_down) for p in down_c]
+        down_w = build_weights(at, [down_p, down_y] + down_c, part_flat, whole, DP_INDEX)
+        g_d = Chain(at, [hold(gw_down, down_w)], half_flat, x_first, (cols // 2, units))
         g_d.go(DP, 1)
-        down_y = down_y.after(g_d.send)
-        down_c = [p.fetch(DP, 1, down_y.stack) for p in (down_p, down_y)]
-        down_w = build_weights(at, [down_p, down_y] + down_c, part_flat, whole, DP_INDEX)
-        g_d.fold(down_w)
+        g_d.fold()
         g_d.go(NARROW, 1)
         grad_inner, gw_up, gb_up = inner_back(
             cot, hold(down_w, g_d.send), in_hbm(slope), hidden_two
         )
 
-        g_u = Chain(at, gw_up, part_flat, y_first, (cols // 4, units), DP_INDEX)
+        g_u = Chain(at, [gw_up], part_flat, y_first, (cols // 4, units), DP_INDEX)
         g_u.go(DP, 1)
         g_d.fold(g_u.send)
         g_d.go(WIDE, 1)
@@ -1067,92 +1135,113 @@
         )
         grad_mixed, gw_out = mixed_back(branch, out_w, mixed)
 
-        g_o = Chain(at, gw_out, out_plan(cols, heads_cols, 2), x_first, (heads_cols // 2, cols))
-        g_o.go(DP, 1)
-        g_u.fold(g_o.send)
+        g_u.fold(grad_mixed)
         g_u.go(DP, 2)
-        g_d.fold(g_o.send)
+        g_d.fold(grad_mixed)
         g_d.go(WIDE, 2)
-        result_got = swap(hold(part_of(result, theirs), g_o.send), NARROW, 1)
+        result_send = hold(part_of(result, theirs), grad_mixed)
+        result_got = swap(result_send, NARROW, 1)
         groups = rows.shape[0] // ROWS
         grad_triple = attend_back(
-            triple, in_hbm(prob), hold(grad_mixed, g_u.send, g_d.send), 0, groups
-        )
-
-        d_sum = g_d.total(grad_triple)
+            triple, in_hbm(prob), hold(grad_mixed, g_u.send, g_d.send, result_send), 0, groups
+        )
+        grad_rows, gg_one, gs_one = first_back(grad_triple, qkv_t, rows, grad_middle, vecs)
+
+        d_sum = g_d.total(grad_rows)
         d_got = swap(d_sum.astype(BF), DP, 2)
-        g_u.fold(grad_triple)
+        g_u.fold(grad_rows)
         g_u.go(NARROW, 1)
-        g_o.fold(grad_triple)
-        g_o.go(NARROW, 1)
-        result_got = hold(result_got, grad_triple)
-        gw_qkv, gb_qkv = qkv_grad(hold(grad_triple, d_sum, g_u.send, g_o.send), hidden_one)
-
+        result_got = hold(result_got, grad_rows)
+        gw_qkv, gb_qkv = qkv_grad(hold(grad_triple, d_sum, g_u.send, result_got), hidden_one)
+        sums = owner_sums(
+            wide,
+            narrow,
+            cols,
+            gg_one,
+            gs_one,
+            gg_two,
+            gs_two,
+            gb_out,
+            gb_down,
+            gb_qkv,
+            gb_up,
+        )
+
+        part = heads_cols // 4
         g_q = Chain(
             at,
-            gw_qkv,
-            qkv_plan(cols, heads_cols, 4),
+            [gw_qkv],
+            qkv_plan(cols, heads_cols, 4, {0: (0, 0), 1: (part, 0)}),
             y_first,
-            (3 * heads_cols // 4, cols),
+            (2 * part, cols),
             DP_INDEX,
         )
         g_q.go(DP, 1)
-        d_sum = d_sum + hold(d_got, g_q.send).astype(F32)
+        rest_plan = joined(
+            qkv_plan(cols, heads_cols, 2, {2: (0, 0)}),
+            out_plan(cols, heads_cols, 2, (half, 0), 1),
+            sums_plan(cols, narrow, (2 * half, 0), 2),
+        )
+        g_r = Chain(at, [gw_qkv, gw_out, sums], rest_plan, x_first, (2 * half + 16, cols))
+        g_r.go(DP, 1)
+        d_sum = d_sum + hold(d_got, g_r.send).astype(F32)
         d_got = swap(d_sum, DP, 1)
-        g_u.fold(g_q.send)
+        g_u.fold(g_r.send)
         g_u.go(WIDE, 1)
-        g_o.fold(g_q.send)
-        g_o.go(WIDE, 1)
-        grad_rows, gg_one, gs_one = first_back(
-            grad_triple, hold(qkv_t, d_sum, g_u.send, g_o.send), rows, grad_middle, vecs
-        )
-
-        g_q.fold(grad_rows)
+        rows_send = hold(part_of(grad_rows, theirs), g_r.send).astype(BF)
+        rows_back = swap(rows_send, NARROW, 1)
+        keep = hold(part_of(result, mine), g_q.send, d_sum, g_u.send, rows_send)
+        block_output = flat_rows(at, keep, result_got, cols)
+
+        g_q.fold(block_output)
         g_q.go(DP, 2)
-        rows_send = part_of(grad_rows, theirs).astype(BF)
-        rows_back = swap(rows_send, NARROW, 1)
-        g_u.fold(grad_rows)
+        g_r.fold(block_output)
+        g_r.go(NARROW, 1)
+        g_u.fold(g_q.send, g_r.send)
         g_u.go(WIDE, 2)
-        g_o.fold(grad_rows)
-        g_o.go(WIDE, 2)
-        sums = pack(gg_one, gs_one, gg_two, gs_two, gb_out, gb_down, gb_qkv, gb_up)
-        sums_got = swap(sums, DP, 1)
-        keep = part_of(result, mine)
-        block_output = flat_rows(
-            at, hold(keep, g_q.send, rows_send, g_u.send, g_o.send, sums), result_got, cols
-        )
-
-        g_q.fold(block_output)
-        g_q.go(NARROW, 1)
-        u_sum = g_u.total(block_output)
-        u_got = swap(u_sum, DP, 2)
-        o_sum = g_o.total(block_output)
-        o_got = swap(o_sum.astype(BF), DP, 2)
-        sums = sums + hold(sums_got, block_output)
-        sums_got = swap(sums, DP, 2)
-        rows_back = hold(rows_back, block_output, g_q.send, u_sum, o_sum, sums)
+        rows_back = hold(rows_back, g_u.send)
         grad_patches = put_rows(at, part_of(grad_rows, mine), rows_back, index, cols)
 
         def in_order(value, other, index):
             return jnp.where(index == 0, jnp.stack([value, other]), jnp.stack([other, value]))
 
         g_q.fold(grad_patches)
-        g_q.go(WIDE, 1)
-        u_sum = in_order(u_sum, hold(u_got, grad_patches), at[3] // 2)
+        g_q.go(NARROW, 1)
+        g_r.spread(grad_patches)
+        u_sum = g_u.total(g_q.send, *g_r.send)
+        u_got = swap(u_sum.astype(BF), DP, 2)
+        token = fence(hold(vecs, g_q.send, u_sum, *g_r.send))
+        g_q.spread(token)
+        r_sum = g_r.all_of(token)
+        r_got = swap(r_sum.astype(BF), DP, 2)
+        u_sum = in_order(u_sum, hold(u_got, token).astype(F32), at[3] // 2)
         u_got = swap(u_sum, DP, 1)
-        o_sum = o_sum + hold(o_got, grad_patches).astype(F32)
-        o_got = swap(o_sum, DP, 1)
-        sums = sums + hold(sums_got, grad_patches)
-        sums = total_over_all(sums, ("narrow", "wide"))
+        token = fence(hold(token, r_sum, u_sum, *g_q.send))
+        q_sum = g_q.all_of(token)
+        q_got = [swap(q_sum.astype(BF), DP, bit) for bit in (1, 2, 3)]
+        r_sum = r_sum + hold(r_got, token).astype(F32)
+        r_got = swap(r_sum[: 2 * half], DP, 1)
         g_down = in_order(d_sum, d_got, at[2]).reshape(cols, units)
-        g_q.fold()
-        g_q.go(WIDE, 2)
-        g_up = in_order(u_sum, u_got, at[2]).transpose(1, 0, 2, 3).reshape(cols, units)
-        g_out = in_order(o_sum, o_got, at[2]).reshape(heads_cols, cols)
-        q_sum = doubled(doubled(g_q.total(), 2, at[3] // 2), 1, at[2])
-        g_qkv = q_sum.reshape(2, 2, 3, heads_cols // 4, cols).transpose(4, 2, 1, 0, 3)
-        g_qkv = g_qkv.reshape(cols, 3, heads_cols)
+        g_up = in_order(u_sum, hold(u_got, token), at[2]).transpose(1, 0, 2, 3)
+        g_up = g_up.reshape(cols, units)
+        q_got = [got.astype(F32) for got in q_got]
+        pairs_of = [in_order(q_sum, q_got[0], at[2]), in_order(q_got[1], q_got[2], at[2])]
+        q_sum = in_order(*pairs_of, at[3] // 2).reshape(4, 2, part, cols)
+        g_rest = in_order(r_sum[: 2 * half], r_got, at[2]).reshape(2, 2, half, cols)
+        g_out = g_rest[:, 1].reshape(heads_cols, cols)
+        g_qkv = jnp.stack(
+            [
+                q_sum[:, 0].reshape(heads_cols, cols),
+                q_sum[:, 1].reshape(heads_cols, cols),
+                g_rest[:, 0].reshape(heads_cols, cols),
+            ]
+        )
+        g_qkv = g_qkv.transpose(2, 0, 1)
         grad_patches = grad_patches.reshape(1, -1)
+        lines = r_sum[2 * half :]
+        vector_grads = [lines[i] for i in range(6)]
+        g_bqv = lines[6].reshape(2, heads_cols)
+        g_bup = lines[7:9].reshape(units)
     else:
         table = patches.reshape(images, PATCHES, cols)
         rows_mine = jnp.take_along_axis(table, visible[:, :, None], axis=1)
@@ -1218,36 +1307,33 @@
         )
         g_qkv = g_qkv.transpose(2, 0, 1)
         sums = lax.psum(sums, ("dp", "wide", "narrow"))
-
-    sums = sums.reshape(-1)
-    at_narrow = at[1] * cols
-    at_wide = at[0]
-
-    def narrow_part(i):
-        return lax.dynamic_slice_in_dim(sums, i * D + at_narrow, cols)
-
-    g_bqv = jnp.stack(
-        [
-            lax.dynamic_slice_in_dim(sums, (6 + i) * D + at_wide * heads_cols, heads_cols)
-            for i in (0, 2)
+        sums = sums.reshape(-1)
+        vector_grads = [
+            lax.dynamic_slice_in_dim(sums, i * D + at[1] * cols, cols) for i in range(6)
         ]
-    )
-    g_bup = lax.dynamic_slice_in_dim(sums, 9 * D + at_wide * units, units)
+        g_bqv = jnp.stack(
+            [
+                lax.dynamic_slice_in_dim(sums, (6 + i) * D + at[0] * heads_cols, heads_cols)
+                for i in (0, 2)
+            ]
+        )
+        g_bup = lax.dynamic_slice_in_dim(sums, 9 * D + at[0] * units, units)
+
     return (
         block_output,
         grad_patches,
         g_qkv,
         g_bqv,
         g_out,
-        narrow_part(4),
+        vector_grads[4],
         g_up,
         g_bup,
         g_down,
-        narrow_part(5),
-        narrow_part(0),
-        narrow_part(1),
-        narrow_part(2),
-        narrow_part(3),
+        vector_grads[5],
+        vector_grads[0],
+        vector_grads[1],
+        vector_grads[2],
+        vector_grads[3],
     )
 
 

time: 358 us -> 328 us (0.916)
  Pallas kernels: 173 us -> 137 us
  waiting for transfers between devices: 74.2 us -> 85 us
  local copies, waits for them, and re-layouts: 39.3 us -> 34.7 us
    pallas_call x1, Pallas kernels: 30.8 us -> 12 us  [attend_back(): pl.pallas_call(attend_back_body, out_shape=struct(triple.shape, BF), grid...]
    ppermute x53 -> x51, waiting for transfers between devices: 74.2 us -> 85 us  [swap(): return lax.ppermute(value, axis, [(i, i ^ bit) for i in range(size)])]
    pallas_call x1, Pallas kernels: 22.2 us -> 12.9 us  [inner_back(): call(inner_back_body, (units // TILE,), [full, col, tile, full], [tile, c...]
    pallas_call x1, Pallas kernels: 10.1 us -> 6.43 us  [attend(): call(attend_body, (groups,), [spec((ROWS, 3 * D), lambda g: (g, 0))], [sp...]
    unnamed x100 -> x104, local copies, waits for them, and re-layouts: 27.8 us -> 24.9 us
    ppermute x53 -> x51, starting transfers between devices: 51.7 us -> 54.5 us  [swap(): return lax.ppermute(value, axis, [(i, i ^ bit) for i in range(size)])]
  transfers between devices with their start and end apart: 53 -> 51, of which waited for: 17 -> 18; matrix products, arithmetic and copies ran while one was open for 8% -> 7% of each run, Pallas kernels for 48% -> 39%
where the time goes in v4:
time: 328 us; the launch traced here: 327 us
  Pallas kernels  137 us (42%)
  waiting for transfers between devices  85 us (26%)
  starting transfers between devices  54.5 us (17%)
  local copies, waits for them, and re-layouts  34.7 us (11%)
  other arithmetic  14.7 us (4%)
    ppermute x51, waiting for transfers between devices, swap(): return lax.ppermute(value, axis, [(i, i ^ bit) for i in range(size)])  85 us
    ppermute x51, starting transfers between devices, swap(): return lax.ppermute(value, axis, [(i, i ^ bit) for i in range(size)])  54.5 us
    unnamed x104, local copies, waits for them, and re-layouts  24.9 us
    pallas_call x8, Pallas kernels, move_pieces(): pl.pallas_call(partial(build_body, plan, tag_lists, inverse, part_at), ou...  20 us
    pallas_call x1, Pallas kernels, inner_back(): call(inner_back_body, (units // TILE,), [full, col, tile, full], [tile, c...  12.9 us
    pallas_call x1, Pallas kernels, put_rows(): call(partial(put_body, cols), (pairs,), [rows, rows, spec((1, ROWS, 1), l...  12.3 us
    pallas_call x1, Pallas kernels, attend_back(): pl.pallas_call(attend_back_body, out_shape=struct(triple.shape, BF), grid...  12 us
    pallas_call x1, Pallas kernels, pick_rows(): call(partial(pick_body, cols), (pairs,), [spec((1, width), lambda i, at:...  11 us
  transfers between devices with their start and end apart: 51, of which 18 were waited for; matrix products, arithmetic and copies ran while one was open for 7% of the time, Pallas kernels for 39%

profile of v4, /device:TPU:0, one launch (start us, length us, event | category | flops | bytes accessed | tf_op | source)
XLA Modules:
  0.0 327.4 jit_solution(5616212432152947913)
XLA Ops:
  3.2 5.1 %collective-permute-start.3 = (bf16[1,400,384]{2,1,0:T(8,128)(2,1)}, bf16[1,400,384]{2,1,0:T(8,128)(2,1)}, u32[]{:S(2)}, u32[]{:S(2)}) collective-permute-start(bf16[1,400,384]{2,1,0:T(8,128)(2,1)} %bitcast.5), channel_id=1, source_target_pairs={{0,6},{2,4},{4,2},{6,0},{1,7},{3,5},{5,3},{7,1},{8,14},{10,12},{12... | collective-permute-start | bytes 921608 | tf_op jit(solution)/shard_map/ppermute | solution.py:613
  10.3 3.7 %copy-done.28 = bf16[1,2408448]{1,0:T(2,128)(2,1)S(1)} copy-done((bf16[1,2408448]{1,0:T(2,128)(2,1)S(1)}, bf16[1,2408448]{1,0:T(2,128)(2,1)}, u32[]{:S(2)}) %copy-start.28) | copy-done | bytes 4816920
  14.0 11.0 %shard_map.264 = bf16[1792,384]{1,0:T(8,128)(2,1)S(1)} custom-call(s32[4]{0:T(128)S(1)} %pad_add_fusion.at_ref, bf16[1,2408448]{1,0:T(2,128)(2,1)S(1)} %copy-done.28, s32[16,112,1]{2,1,0:T(8,128)S(1)} %copy.30.index_ref), custom_call_target="tpu_custom_call" | custom-call | flops 108000002048 | bytes 1024 | tf_op jit(solution)/shard_map/pallas_call | solution.py:83
  31.2 3.6 %collective-permute-done.2 = bf16[1,400,384]{2,1,0:T(8,128)(2,1)} collective-permute-done((bf16[1,400,384]{2,1,0:T(8,128)(2,1)}, bf16[1,400,384]{2,1,0:T(8,128)(2,1)}, u32[]{:S(2)}, u32[]{:S(2)}) %collective-permute-start.2) | collective-permute-done | bytes 307232 | tf_op jit(solution)/shard_map/ppermute | solution.py:613
  37.3 5.7 %collective-permute-done = bf16[896,384]{1,0:T(8,128)(2,1)} collective-permute-done((bf16[896,384]{1,0:T(8,128)(2,1)}, bf16[896,384]{1,0:T(8,128)(2,1)}, u32[]{:S(2)}, u32[]{:S(2)}) %collective-permute-start) | collective-permute-done | bytes 688160 | tf_op jit(solution)/shard_map/ppermute | solution.py:613
  48.2 3.5 %collective-permute-start.7 = (bf16[1,192,768]{2,1,0:T(8,128)(2,1)}, bf16[1,192,768]{2,1,0:T(8,128)(2,1)S(1)}, u32[]{:S(2)}, u32[]{:S(2)}) collective-permute-start(bf16[1,192,768]{2,1,0:T(8,128)(2,1)} %bitcast.94), channel_id=1, source_target_pairs={{0,6},{2,4},{4,2},{6,0},{1,7},{3,5},{5,3},{7,1},{8,14},{10,12},{12... | collective-permute-start | bytes 884744 | tf_op jit(solution)/shard_map/ppermute | solution.py:613
  55.7 4.6 %collective-permute-done.7 = bf16[1,192,768]{2,1,0:T(8,128)(2,1)S(1)} collective-permute-done((bf16[1,192,768]{2,1,0:T(8,128)(2,1)}, bf16[1,192,768]{2,1,0:T(8,128)(2,1)S(1)}, u32[]{:S(2)}, u32[]{:S(2)}) %collective-permute-start.7) | collective-permute-done | bytes 294944 | tf_op jit(solution)/shard_map/ppermute | solution.py:613
  60.3 14.9 %collective-permute-done.6 = bf16[1,192,768]{2,1,0:T(8,128)(2,1)S(1)} collective-permute-done((bf16[1,192,768]{2,1,0:T(8,128)(2,1)}, bf16[1,192,768]{2,1,0:T(8,128)(2,1)S(1)}, u32[]{:S(2)}, u32[]{:S(2)}) %collective-permute-start.6) | collective-permute-done | bytes 294944 | tf_op jit(solution)/shard_map/ppermute | solution.py:613
  89.0 3.0 shard_map.268.w_ref
  94.0 4.1 %shard_map.269.triple_ref = bf16[896,2304]{1,0:T(8,128)(2,1)S(1)} custom-call(bf16[896,768]{1,0:T(8,128)(2,1)S(1)} %shard_map.267.hidden_ref, bf16[2304,768]{1,0:T(8,128)(2,1)S(1)} %shard_map.268.w_ref, f32[1,2304]{1,0:T(1,128)S(1)} %get-tuple-element.134.bias_ref), custom_call_target="tpu_custom_call" | custom-call | flops 5400000 | bytes 1024 | tf_op jit(solution)/shard_map/pallas_call | solution.py:225
  98.1 6.4 %shard_map.270 = (bf16[896,768]{1,0:T(8,128)(2,1)S(1)}, f32[8,12,112,112]{3,2,1,0:T(8,128)}) custom-call(bf16[896,2304]{1,0:T(8,128)(2,1)S(1)} %shard_map.269.triple_ref), custom_call_target="tpu_custom_call" | custom-call | flops 5400000 | bytes 1024 | tf_op jit(solution)/shard_map/pallas_call | solution.py:280
  107.3 7.8 %collective-permute-done.13 = bf16[4,96,768]{2,1,0:T(8,128)(2,1)S(1)} collective-permute-done((bf16[4,96,768]{2,1,0:T(8,128)(2,1)S(1)}, bf16[4,96,768]{2,1,0:T(8,128)(2,1)S(1)}, u32[]{:S(2)}, u32[]{:S(2)}) %collective-permute-start.13) | collective-permute-done | bytes 589856 | tf_op jit(solution)/shard_map/ppermute | solution.py:613
  126.1 10.1 %shard_map.274 = (bf16[896,3072]{1,0:T(8,128)(2,1)}, f32[896,3072]{1,0:T(8,128)}) custom-call(bf16[896,768]{1,0:T(8,128)(2,1)S(1)} %get-tuple-element.140.hidden_ref, bf16[768,3072]{1,0:T(8,128)(2,1)S(1)} %shard_map.273.w_ref, f32[1,3072]{1,0:T(1,128)S(1)} %get-tuple-element.144.bias_ref), custom_call_target="tpu_custom_call" | custom-call | flops 5400000 | bytes 1024 | tf_op jit(solution)/shard_map/pallas_call | solution.py:331
  136.7 4.6 %collective-permute-done.17.refs_1_ = bf16[8,96,768]{2,1,0:T(8,128)(2,1)S(1)} collective-permute-done((bf16[8,96,768]{2,1,0:T(8,128)(2,1)S(1)}, bf16[8,96,768]{2,1,0:T(8,128)(2,1)S(1)}, u32[]{:S(2)}, u32[]{:S(2)}) %collective-permute-start.17) | collective-permute-done | bytes 1179680 | tf_op jit(solution)/shard_map/ppermute | solution.py:613
  144.4 7.2 %shard_map.275 = (bf16[768,3072]{1,0:T(8,128)(2,1)S(1)}, f32[1,3072]{1,0:T(1,128)}) custom-call(bf16[896,768]{1,0:T(8,128)(2,1)S(1)} %get-tuple-element.148.left_ref.cot_ref, bf16[896,3072]{1,0:T(8,128)(2,1)S(1)} %copy-done.29), custom_call_target="tpu_custom_call" | custom-call | flops 108000002048 | bytes 1024 | tf_op jit(solution)/shard_map/pallas_call | solution.py:383
  153.6 3.2 shard_map.276.w_ref
  162.9 4.8 %collective-permute-done.20 = bf16[8,192,768]{2,1,0:T(8,128)(2,1)} collective-permute-done((bf16[8,192,768]{2,1,0:T(8,128)(2,1)}, bf16[8,192,768]{2,1,0:T(8,128)(2,1)}, u32[]{:S(2)}, u32[]{:S(2)}) %collective-permute-start.20) | collective-permute-done | bytes 2359328 | tf_op jit(solution)/shard_map/ppermute | solution.py:613
  167.7 3.0 add_convert_fusion.1
  172.5 12.9 %shard_map.278 = (bf16[896,3072]{1,0:T(8,128)(2,1)}, bf16[768,3072]{1,0:T(8,128)(2,1)S(1)}, f32[1,3072]{1,0:T(1,128)S(1)}) custom-call(bf16[896,768]{1,0:T(8,128)(2,1)S(1)} %get-tuple-element.148.left_ref.cot_ref, bf16[768,3072]{1,0:T(8,128)(2,1)S(1)} %copy-done.9, f32[896,3072]{1,0:T(8,128)} %get-tuple-element.158.slope_ref, bf16[896,768]{1,0:T(8,128)(2,1)S(1)} %copy-done.21), custom_call_target="tpu_custom_call" | custom-call | flops 108000002048 | bytes 1024 | tf_op jit(solution)/shard_map/pallas_call | solution.py:411
  188.0 10.8 %collective-permute-done.21 = bf16[4,192,768]{2,1,0:T(8,128)(2,1)S(1)} collective-permute-done((bf16[4,192,768]{2,1,0:T(8,128)(2,1)S(1)}, bf16[4,192,768]{2,1,0:T(8,128)(2,1)S(1)}, u32[]{:S(2)}, u32[]{:S(2)}) %collective-permute-start.21) | collective-permute-done | bytes 1179680 | tf_op jit(solution)/shard_map/ppermute | solution.py:613
  199.3 3.2 copy-done.30
  202.5 4.7 %shard_map.280 = bf16[896,768]{1,0:T(8,128)(2,1)S(1)} custom-call(bf16[896,3072]{1,0:T(8,128)(2,1)S(1)} %copy-done.30, bf16[768,3072]{1,0:T(8,128)(2,1)S(1)} %copy-done.10, f32[8,768]{1,0:T(8,128)S(1)} %copy-done.27, f32[896,768]{1,0:T(8,128)S(1)} %copy-done.14), custom_call_target="tpu_custom_call" | custom-call | flops 108000002048 | bytes 1024 | tf_op jit(solution)/shard_map/pallas_call | solution.py:354
  207.2 6.3 %shard_map.281 = (f32[896,768]{1,0:T(8,128)S(1)}, bf16[896,768]{1,0:T(8,128)(2,1)S(1)}, f32[1,768]{1,0:T(1,128)S(1)}, f32[1,768]{1,0:T(1,128)S(1)}, f32[1,768]{1,0:T(1,128)S(1)}) custom-call(bf16[896,3072]{1,0:T(8,128)(2,1)S(1)} %bitcast.86, bf16[768,3072]{1,0:T(8,128)(2,1)S(1)} %bitcast.84, f32[896,768]{1,0:T(8,128)S(1)} %copy-done.14, ...), custom_call_target="tpu_custom_call" | custom-call | flops 5400000 | bytes 1024 | tf_op jit(solution)/shard_map/pallas_call | solution.py:468
  223.1 12.0 %shard_map.283.grad_ref = bf16[896,2304]{1,0:T(8,128)(2,1)S(1)} custom-call(bf16[896,2304]{1,0:T(8,128)(2,1)S(1)} %copy-done.7, f32[8,12,112,112]{3,2,1,0:T(8,128)} %get-tuple-element.164.prob_ref, bf16[896,768]{1,0:T(8,128)(2,1)S(1)} %get-tuple-element.173.grad_ref), custom_call_target="tpu_custom_call" | custom-call | flops 108000002048 | bytes 1024 | tf_op jit(solution)/shard_map/pallas_call | solution.py:533
  235.1 5.0 %shard_map.284 = (f32[896,768]{1,0:T(8,128)S(1)}, f32[1,768]{1,0:T(1,128)S(1)}, f32[1,768]{1,0:T(1,128)S(1)}) custom-call(bf16[896,2304]{1,0:T(8,128)(2,1)S(1)} %shard_map.283.grad_ref, bf16[2304,768]{1,0:T(8,128)(2,1)S(1)} %copy-done.4, bf16[896,768]{1,0:T(8,128)(2,1)S(1)} %maximum_select_fusion.rows_ref, f32[896,768]{1,0:T(8,128)S(1)} %get-tuple-element.174.middle_ref, ...), custom_call_target="tpu_custom_call" | custom-call | flops 5400000 | bytes 1024 | tf_op jit(solution)/shard_map/pallas_call | solution.py:591
  241.0 9.5 %collective-permute-done.25 = bf16[8,96,768]{2,1,0:T(8,128)(2,1)S(1)} collective-permute-done((bf16[8,96,768]{2,1,0:T(8,128)(2,1)S(1)}, bf16[8,96,768]{2,1,0:T(8,128)(2,1)S(1)}, u32[]{:S(2)}, u32[]{:S(2)}) %collective-permute-start.25) | collective-permute-done | bytes 1179680 | tf_op jit(solution)/shard_map/ppermute | solution.py:613
  251.8 4.7 %shard_map.285 = (bf16[2304,768]{1,0:T(8,128)(2,1)S(1)}, f32[1,2304]{1,0:T(1,128)S(1)}) custom-call(bf16[896,2304]{1,0:T(8,128)(2,1)S(1)} %shard_map.283.grad_ref, bf16[896,768]{1,0:T(8,128)(2,1)S(1)} %copy-done.23), custom_call_target="tpu_custom_call" | custom-call | flops 108000002048 | bytes 1024 | tf_op jit(solution)/shard_map/pallas_call | solution.py:565
  263.0 6.8 %shard_map.289 = bf16[1,602112]{1,0:T(2,128)(2,1)} custom-call(s32[4]{0:T(128)S(1)} %pad_add_fusion.at_ref, bf16[896,384]{1,0:T(8,128)(2,1)S(1)} %get-tuple-element.194.keep_ref, bf16[896,384]{1,0:T(8,128)(2,1)S(1)} %collective-permute-done.26.got_ref), custom_call_target="tpu_custom_call" | custom-call | flops 108000002048 | bytes 1024 | tf_op jit(solution)/shard_map/pallas_call | solution.py:174
  277.4 12.3 %shard_map.290 = f32[18816,128]{1,0:T(8,128)} custom-call(s32[4]{0:T(128)S(1)} %pad_add_fusion.at_ref, f32[896,384]{1,0:T(8,128)S(1)} %constant_dynamic-slice_fusion.keep_ref, bf16[896,384]{1,0:T(8,128)(2,1)S(1)} %collective-permute-done.29.got_ref, s32[16,112,1]{2,1,0:T(8,128)S(1)} %copy-done.25), custom_call_target="tpu_custom_call" | custom-call | flops 108000002048 | bytes 1024 | tf_op jit(solution)/shard_map/pallas_call | solution.py:149
  297.5 3.3 %collective-permute-done.43 = bf16[96,768]{1,0:T(8,128)(2,1)S(1)} collective-permute-done((bf16[96,768]{1,0:T(8,128)(2,1)S(1)}, bf16[96,768]{1,0:T(8,128)(2,1)S(1)}, u32[]{:S(2)}, u32[]{:S(2)}) %collective-permute-start.43) | collective-permute-done | bytes 147488 | tf_op jit(solution)/shard_map/ppermute | solution.py:613
  306.6 4.4 %collective-permute-done.41 = bf16[208,384]{1,0:T(8,128)(2,1)S(1)} collective-permute-done((bf16[208,384]{1,0:T(8,128)(2,1)S(1)}, bf16[208,384]{1,0:T(8,128)(2,1)S(1)}, u32[]{:S(2)}, u32[]{:S(2)}) %collective-permute-start.41) | collective-permute-done | bytes 159776 | tf_op jit(solution)/shard_map/ppermute | solution.py:613
  317.2 4.8 %collective-permute-done.45 = bf16[96,384]{1,0:T(8,128)(2,1)S(1)} collective-permute-done((bf16[96,384]{1,0:T(8,128)(2,1)S(1)}, bf16[96,384]{1,0:T(8,128)(2,1)S(1)}, u32[]{:S(2)}, u32[]{:S(2)}) %collective-permute-start.45) | collective-permute-done | bytes 73760 | tf_op jit(solution)/shard_map/ppermute | solution.py:613
  (268 shorter events, 118.7 us)
Async XLA Ops:
  3.2 28.0 %collective-permute-start.3 = (bf16[1,400,384]{2,1,0:T(8,128)(2,1)}, bf16[1,400,384]{2,1,0:T(8,128)(2,1)}, u32[]{:S(2)}, u32[]{:S(2)}) collective-permute-start(bf16[1,400,384]{2,1,0:T(8,128)(2,1)} %bitcast.5), channel_id=1, source_target_pairs={{0,6},{2,4},{4,2},{6,0},{1,7},{3,5},{5,3},{7,1},{8,14},{10,12},{12... | collective-permute-start | bytes 921608 | tf_op jit(solution)/shard_map/ppermute | solution.py:613
  8.3 26.5 %collective-permute-start.2 = (bf16[1,400,384]{2,1,0:T(8,128)(2,1)}, bf16[1,400,384]{2,1,0:T(8,128)(2,1)}, u32[]{:S(2)}, u32[]{:S(2)}) collective-permute-start(bf16[1,400,384]{2,1,0:T(8,128)(2,1)} %bitcast.5), channel_id=1, source_target_pairs={{0,4},{2,6},{4,0},{6,2},{1,5},{3,7},{5,1},{7,3},{8,12},{10,14},{12... | collective-permute-start | bytes 921608 | tf_op jit(solution)/shard_map/ppermute | solution.py:613
  8.3 26.5 %collective-permute-start.1 = (bf16[1,400,384]{2,1,0:T(8,128)(2,1)}, bf16[1,400,384]{2,1,0:T(8,128)(2,1)}, u32[]{:S(2)}, u32[]{:S(2)}) collective-permute-start(bf16[1,400,384]{2,1,0:T(8,128)(2,1)} %bitcast.5), channel_id=1, source_target_pairs={{0,2},{2,0},{4,6},{6,4},{1,3},{3,1},{5,7},{7,5},{8,10},{10,8},{12,... | collective-permute-start | bytes 921608 | tf_op jit(solution)/shard_map/ppermute | solution.py:613
  26.0 16.9 %collective-permute-start = (bf16[896,384]{1,0:T(8,128)(2,1)}, bf16[896,384]{1,0:T(8,128)(2,1)}, u32[]{:S(2)}, u32[]{:S(2)}) collective-permute-start(bf16[896,384]{1,0:T(8,128)(2,1)} %get-tuple-element.255), channel_id=1, source_target_pairs={{0,1},{1,0},{2,3},{3,2},{4,5},{5,4},{6,7},{7,6},{8,9},{9,8},{10,11... | collective-permute-start | bytes 2064392 | tf_op jit(solution)/shard_map/ppermute | solution.py:613
  44.6 31.4 %collective-permute-start.4 = (bf16[4,400,384]{2,1,0:T(8,128)(2,1)}, bf16[4,400,384]{2,1,0:T(8,128)(2,1)}, u32[]{:S(2)}, u32[]{:S(2)}) collective-permute-start(bf16[4,400,384]{2,1,0:T(8,128)(2,1)} %pad_maximum_fusion), channel_id=1, source_target_pairs={{0,1},{1,0},{2,3},{3,2},{4,5},{5,4},{6,7},{7,6},{8,9},{9,8},{10,11... | collective-permute-start | bytes 3686408 | tf_op jit(solution)/shard_map/ppermute | solution.py:613
  48.2 12.1 %collective-permute-start.7 = (bf16[1,192,768]{2,1,0:T(8,128)(2,1)}, bf16[1,192,768]{2,1,0:T(8,128)(2,1)S(1)}, u32[]{:S(2)}, u32[]{:S(2)}) collective-permute-start(bf16[1,192,768]{2,1,0:T(8,128)(2,1)} %bitcast.94), channel_id=1, source_target_pairs={{0,6},{2,4},{4,2},{6,0},{1,7},{3,5},{5,3},{7,1},{8,14},{10,12},{12... | collective-permute-start | bytes 884744 | tf_op jit(solution)/shard_map/ppermute | solution.py:613
  51.7 23.5 %collective-permute-start.6 = (bf16[1,192,768]{2,1,0:T(8,128)(2,1)}, bf16[1,192,768]{2,1,0:T(8,128)(2,1)S(1)}, u32[]{:S(2)}, u32[]{:S(2)}) collective-permute-start(bf16[1,192,768]{2,1,0:T(8,128)(2,1)} %bitcast.95), channel_id=1, source_target_pairs={{0,4},{2,6},{4,0},{6,2},{1,5},{3,7},{5,1},{7,3},{8,12},{10,14},{12... | collective-permute-start | bytes 884744 | tf_op jit(solution)/shard_map/ppermute | solution.py:613
  51.7 23.5 %collective-permute-start.5 = (bf16[1,192,768]{2,1,0:T(8,128)(2,1)}, bf16[1,192,768]{2,1,0:T(8,128)(2,1)S(1)}, u32[]{:S(2)}, u32[]{:S(2)}) collective-permute-start(bf16[1,192,768]{2,1,0:T(8,128)(2,1)} %bitcast.96), channel_id=1, source_target_pairs={{0,2},{2,0},{4,6},{6,4},{1,3},{3,1},{5,7},{7,5},{8,10},{10,8},{12,... | collective-permute-start | bytes 884744 | tf_op jit(solution)/shard_map/ppermute | solution.py:613
  75.4 29.2 %collective-permute-start.12 = (bf16[4,192,768]{2,1,0:T(8,128)(2,1)S(1)}, bf16[4,192,768]{2,1,0:T(8,128)(2,1)S(1)}, u32[]{:S(2)}, u32[]{:S(2)}) collective-permute-start(bf16[4,192,768]{2,1,0:T(8,128)(2,1)S(1)} %pad_maximum_fusion.1.refs_0_), channel_id=1, source_target_pairs={{0,1},{1,0},{2,3},{3,2},{4,5},{5,4},{6,7},{7,6},{8,9},{9,8},{10,11... | collective-permute-start | bytes 3538952 | tf_op jit(solution)/shard_map/ppermute | solution.py:613
  78.4 13.7 %collective-permute-start.11 = (bf16[1,96,768]{2,1,0:T(8,128)(2,1)S(1)}, bf16[1,96,768]{2,1,0:T(8,128)(2,1)S(1)}, u32[]{:S(2)}, u32[]{:S(2)}) collective-permute-start(bf16[1,96,768]{2,1,0:T(8,128)(2,1)S(1)} %bitcast.90), channel_id=1, source_target_pairs={{0,6},{2,4},{4,2},{6,0},{1,7},{3,5},{5,3},{7,1},{8,14},{10,12},{12... | collective-permute-start | bytes 442376 | tf_op jit(solution)/shard_map/ppermute | solution.py:613
  92.2 22.8 %collective-permute-start.13 = (bf16[4,96,768]{2,1,0:T(8,128)(2,1)S(1)}, bf16[4,96,768]{2,1,0:T(8,128)(2,1)S(1)}, u32[]{:S(2)}, u32[]{:S(2)}) collective-permute-start(bf16[4,96,768]{2,1,0:T(8,128)(2,1)S(1)} %pad_maximum_fusion.2), channel_id=1, source_target_pairs={{0,1},{1,0},{2,3},{3,2},{4,5},{5,4},{6,7},{7,6},{8,9},{9,8},{10,11... | collective-permute-start | bytes 1769480 | tf_op jit(solution)/shard_map/ppermute | solution.py:613
  104.6 16.4 %collective-permute-start.14 = (bf16[4,192,768]{2,1,0:T(8,128)(2,1)S(1)}, bf16[4,192,768]{2,1,0:T(8,128)(2,1)S(1)}, u32[]{:S(2)}, u32[]{:S(2)}) collective-permute-start(bf16[4,192,768]{2,1,0:T(8,128)(2,1)S(1)} %pad_maximum_fusion.1.refs_0_), channel_id=1, source_target_pairs={{0,8},{8,0},{16,24},{24,16},{1,9},{9,1},{17,25},{25,17},{2,10},{10... | collective-permute-start | bytes 3538952 | tf_op jit(solution)/shard_map/ppermute | solution.py:613
  104.6 16.4 %collective-permute-start.15 = (bf16[4,192,768]{2,1,0:T(8,128)(2,1)S(1)}, bf16[4,192,768]{2,1,0:T(8,128)(2,1)S(1)}, u32[]{:S(2)}, u32[]{:S(2)}) collective-permute-start(bf16[4,192,768]{2,1,0:T(8,128)(2,1)S(1)} %collective-permute-done.12.refs_1_), channel_id=1, source_target_pairs={{0,8},{8,0},{16,24},{24,16},{1,9},{9,1},{17,25},{25,17},{2,10},{10... | collective-permute-start | bytes 3538952 | tf_op jit(solution)/shard_map/ppermute | solution.py:613
  115.1 21.1 %collective-permute-start.16 = (bf16[896,384]{1,0:T(8,128)(2,1)S(1)}, bf16[896,384]{1,0:T(8,128)(2,1)S(1)}, u32[]{:S(2)}, u32[]{:S(2)}) collective-permute-start(bf16[896,384]{1,0:T(8,128)(2,1)S(1)} %get-tuple-element.138), channel_id=1, source_target_pairs={{0,1},{1,0},{2,3},{3,2},{4,5},{5,4},{6,7},{7,6},{8,9},{9,8},{10,11... | collective-permute-start | bytes 2064392 | tf_op jit(solution)/shard_map/ppermute | solution.py:613
  115.6 25.7 %collective-permute-start.17 = (bf16[8,96,768]{2,1,0:T(8,128)(2,1)S(1)}, bf16[8,96,768]{2,1,0:T(8,128)(2,1)S(1)}, u32[]{:S(2)}, u32[]{:S(2)}) collective-permute-start(bf16[8,96,768]{2,1,0:T(8,128)(2,1)S(1)} %constant_dynamic-update-slice_fusion.5.refs_0_), channel_id=1, source_target_pairs={{0,16},{8,24},{16,0},{24,8},{1,17},{9,25},{17,1},{25,9},{2,18},{10... | collective-permute-start | bytes 3538952 | tf_op jit(solution)/shard_map/ppermute | solution.py:613
  170.7 28.1 %collective-permute-start.21 = (bf16[4,192,768]{2,1,0:T(8,128)(2,1)S(1)}, bf16[4,192,768]{2,1,0:T(8,128)(2,1)S(1)}, u32[]{:S(2)}, u32[]{:S(2)}) collective-permute-start(bf16[4,192,768]{2,1,0:T(8,128)(2,1)S(1)} %get-tuple-element.233), channel_id=1, source_target_pairs={{0,1},{1,0},{2,3},{3,2},{4,5},{5,4},{6,7},{7,6},{8,9},{9,8},{10,11... | collective-permute-start | bytes 3538952 | tf_op jit(solution)/shard_map/ppermute | solution.py:613
  188.0 31.2 %collective-permute-start.22 = (bf16[16,96,768]{2,1,0:T(8,128)(2,1)}, bf16[16,96,768]{2,1,0:T(8,128)(2,1)}, u32[]{:S(2)}, u32[]{:S(2)}) collective-permute-start(bf16[16,96,768]{2,1,0:T(8,128)(2,1)} %get-tuple-element.160), channel_id=1, source_target_pairs={{0,8},{8,0},{16,24},{24,16},{1,9},{9,1},{17,25},{25,17},{2,10},{10... | collective-permute-start | bytes 7077896 | tf_op jit(solution)/shard_map/ppermute | solution.py:613
  199.1 18.8 %collective-permute-start.23 = (bf16[2,192,768]{2,1,0:T(8,128)(2,1)S(1)}, bf16[2,192,768]{2,1,0:T(8,128)(2,1)S(1)}, u32[]{:S(2)}, u32[]{:S(2)}) collective-permute-start(bf16[2,192,768]{2,1,0:T(8,128)(2,1)S(1)} %get-tuple-element.238), channel_id=1, source_target_pairs={{0,2},{2,0},{4,6},{6,4},{1,3},{3,1},{5,7},{7,5},{8,10},{10,8},{12,... | collective-permute-start | bytes 1769480 | tf_op jit(solution)/shard_map/ppermute | solution.py:613
  216.2 23.9 %collective-permute-start.26 = (bf16[896,384]{1,0:T(8,128)(2,1)S(1)}, bf16[896,384]{1,0:T(8,128)(2,1)S(1)}, u32[]{:S(2)}, u32[]{:S(2)}) collective-permute-start(bf16[896,384]{1,0:T(8,128)(2,1)S(1)} %get-tuple-element.172), channel_id=1, source_target_pairs={{0,1},{1,0},{2,3},{3,2},{4,5},{5,4},{6,7},{7,6},{8,9},{9,8},{10,11... | collective-permute-start | bytes 2064392 | tf_op jit(solution)/shard_map/ppermute | solution.py:613
  218.0 22.1 %collective-permute-start.24 = (bf16[1,192,768]{2,1,0:T(8,128)(2,1)S(1)}, bf16[1,192,768]{2,1,0:T(8,128)(2,1)S(1)}, u32[]{:S(2)}, u32[]{:S(2)}) collective-permute-start(bf16[1,192,768]{2,1,0:T(8,128)(2,1)S(1)} %fusion.7), channel_id=1, source_target_pairs={{0,4},{2,6},{4,0},{6,2},{1,5},{3,7},{5,1},{7,3},{8,12},{10,14},{12... | collective-permute-start | bytes 884744 | tf_op jit(solution)/shard_map/ppermute | solution.py:613
  221.5 29.0 %collective-permute-start.25 = (bf16[8,96,768]{2,1,0:T(8,128)(2,1)S(1)}, bf16[8,96,768]{2,1,0:T(8,128)(2,1)S(1)}, u32[]{:S(2)}, u32[]{:S(2)}) collective-permute-start(bf16[8,96,768]{2,1,0:T(8,128)(2,1)S(1)} %get-tuple-element.232), channel_id=1, source_target_pairs={{0,16},{8,24},{16,0},{24,8},{1,17},{9,25},{17,1},{25,9},{2,18},{10... | collective-permute-start | bytes 3538952 | tf_op jit(solution)/shard_map/ppermute | solution.py:613
  240.2 18.2 %collective-permute-start.27 = (bf16[192,768]{1,0:T(8,128)(2,1)S(1)}, bf16[192,768]{1,0:T(8,128)(2,1)S(1)}, u32[]{:S(2)}, u32[]{:S(2)}) collective-permute-start(bf16[192,768]{1,0:T(8,128)(2,1)S(1)} %get-tuple-element.229), channel_id=1, source_target_pairs={{0,16},{8,24},{16,0},{24,8},{1,17},{9,25},{17,1},{25,9},{2,18},{10... | collective-permute-start | bytes 884744 | tf_op jit(solution)/shard_map/ppermute | solution.py:613
  258.4 14.3 %collective-permute-start.32 = (bf16[8,208,384]{2,1,0:T(8,128)(2,1)S(1)}, bf16[8,208,384]{2,1,0:T(8,128)(2,1)S(1)}, u32[]{:S(2)}, u32[]{:S(2)}) collective-permute-start(bf16[8,208,384]{2,1,0:T(8,128)(2,1)S(1)} %get-tuple-element.190), channel_id=1, source_target_pairs={{0,8},{8,0},{16,24},{24,16},{1,9},{9,1},{17,25},{25,17},{2,10},{10... | collective-permute-start | bytes 3833864 | tf_op jit(solution)/shard_map/ppermute | solution.py:613
  259.1 18.3 %collective-permute-start.29 = (bf16[896,384]{1,0:T(8,128)(2,1)S(1)}, bf16[896,384]{1,0:T(8,128)(2,1)S(1)}, u32[]{:S(2)}, u32[]{:S(2)}) collective-permute-start(bf16[896,384]{1,0:T(8,128)(2,1)S(1)} %constant_dynamic-slice_fusion.1), channel_id=1, source_target_pairs={{0,1},{1,0},{2,3},{3,2},{4,5},{5,4},{6,7},{7,6},{8,9},{9,8},{10,11... | collective-permute-start | bytes 2064392 | tf_op jit(solution)/shard_map/ppermute | solution.py:613
  262.2 11.9 %collective-permute-start.30 = (bf16[2,96,768]{2,1,0:T(8,128)(2,1)S(1)}, bf16[2,96,768]{2,1,0:T(8,128)(2,1)S(1)}, u32[]{:S(2)}, u32[]{:S(2)}) collective-permute-start(bf16[2,96,768]{2,1,0:T(8,128)(2,1)S(1)} %get-tuple-element.249), channel_id=1, source_target_pairs={{0,2},{2,0},{4,6},{6,4},{1,3},{3,1},{5,7},{7,5},{8,10},{10,8},{12,... | collective-permute-start | bytes 884744 | tf_op jit(solution)/shard_map/ppermute | solution.py:613
  271.1 18.6 %collective-permute-start.33 = (bf16[8,96,384]{2,1,0:T(8,128)(2,1)S(1)}, bf16[8,96,384]{2,1,0:T(8,128)(2,1)S(1)}, u32[]{:S(2)}, u32[]{:S(2)}) collective-permute-start(bf16[8,96,384]{2,1,0:T(8,128)(2,1)S(1)} %get-tuple-element.242), channel_id=1, source_target_pairs={{0,16},{8,24},{16,0},{24,8},{1,17},{9,25},{17,1},{25,9},{2,18},{10... | collective-permute-start | bytes 1769480 | tf_op jit(solution)/shard_map/ppermute | solution.py:613
  273.0 17.9 %collective-permute-start.36 = (bf16[4,208,384]{2,1,0:T(8,128)(2,1)S(1)}, bf16[4,208,384]{2,1,0:T(8,128)(2,1)S(1)}, u32[]{:S(2)}, u32[]{:S(2)}) collective-permute-start(bf16[4,208,384]{2,1,0:T(8,128)(2,1)S(1)} %get-tuple-element.240), channel_id=1, source_target_pairs={{0,1},{1,0},{2,3},{3,2},{4,5},{5,4},{6,7},{7,6},{8,9},{9,8},{10,11... | collective-permute-start | bytes 1916936 | tf_op jit(solution)/shard_map/ppermute | solution.py:613
  274.1 21.4 %collective-permute-start.35 = (bf16[1,96,768]{2,1,0:T(8,128)(2,1)S(1)}, bf16[1,96,768]{2,1,0:T(8,128)(2,1)S(1)}, u32[]{:S(2)}, u32[]{:S(2)}) collective-permute-start(bf16[1,96,768]{2,1,0:T(8,128)(2,1)S(1)} %fusion.16), channel_id=1, source_target_pairs={{0,4},{2,6},{4,0},{6,2},{1,5},{3,7},{5,1},{7,3},{8,12},{10,14},{12... | collective-permute-start | bytes 442376 | tf_op jit(solution)/shard_map/ppermute | solution.py:613
  291.1 12.6 %collective-permute-start.42 = (bf16[208,384]{1,0:T(8,128)(2,1)S(1)}, bf16[208,384]{1,0:T(8,128)(2,1)S(1)}, u32[]{:S(2)}, u32[]{:S(2)}) collective-permute-start(bf16[208,384]{1,0:T(8,128)(2,1)S(1)} %get-tuple-element.243), channel_id=1, source_target_pairs={{0,6},{2,4},{4,2},{6,0},{1,7},{3,5},{5,3},{7,1},{8,14},{10,12},{12... | collective-permute-start | bytes 479240 | tf_op jit(solution)/shard_map/ppermute | solution.py:613
  293.8 17.3 %collective-permute-start.41 = (bf16[208,384]{1,0:T(8,128)(2,1)S(1)}, bf16[208,384]{1,0:T(8,128)(2,1)S(1)}, u32[]{:S(2)}, u32[]{:S(2)}) collective-permute-start(bf16[208,384]{1,0:T(8,128)(2,1)S(1)} %get-tuple-element.244), channel_id=1, source_target_pairs={{0,4},{2,6},{4,0},{6,2},{1,5},{3,7},{5,1},{7,3},{8,12},{10,14},{12... | collective-permute-start | bytes 479240 | tf_op jit(solution)/shard_map/ppermute | solution.py:613
  293.8 17.3 %collective-permute-start.40 = (bf16[208,384]{1,0:T(8,128)(2,1)S(1)}, bf16[208,384]{1,0:T(8,128)(2,1)S(1)}, u32[]{:S(2)}, u32[]{:S(2)}) collective-permute-start(bf16[208,384]{1,0:T(8,128)(2,1)S(1)} %get-tuple-element.245), channel_id=1, source_target_pairs={{0,2},{2,0},{4,6},{6,4},{1,3},{3,1},{5,7},{7,5},{8,10},{10,8},{12,... | collective-permute-start | bytes 479240 | tf_op jit(solution)/shard_map/ppermute | solution.py:613
  311.0 15.2 %collective-permute-start.49 = (f32[2,96,768]{2,1,0:T(8,128)S(1)}, f32[2,96,768]{2,1,0:T(8,128)S(1)}, u32[]{:S(2)}, u32[]{:S(2)}) collective-permute-start(f32[2,96,768]{2,1,0:T(8,128)S(1)} %maximum_select_fusion.4), channel_id=1, source_target_pairs={{0,8},{8,0},{16,24},{24,16},{1,9},{9,1},{17,25},{25,17},{2,10},{10... | collective-permute-start | bytes 1769480 | tf_op jit(solution)/shard_map/ppermute | solution.py:613
  (67 other events, 571.2 us)

commit v5 on v4

--- a/solution.py
+++ b/solution.py
@@ -60,16 +60,30 @@
     return jax.ShapeDtypeStruct(shape, dtype)
 
 
-def pick_body(cols, at_ref, patch_ref, index_ref, rows_ref, wide_ref):
+def together(own):
+    return next(count for count in (4, 2, 1) if own % count == 0)
+
+
+def strided(start, count, lanes):
+    return [pl.ds(start + k, count, stride=lanes) for k in range(lanes)]
+
+
+def one_hot(index):
+    return (index == lax.broadcasted_iota(jnp.int32, (ROWS, 2 * PATCHES), 1)).astype(BF)
+
+
+def pick_body(cols, count, at_ref, patch_ref, index_ref, rows_ref, wide_ref):
     lanes = cols // 128
     wide_ref[...] = patch_ref[...].astype(F32).reshape(wide_ref.shape)
-    parts = [wide_ref[pl.ds(k, 2 * PATCHES, stride=lanes), :] for k in range(lanes)]
-    both = jnp.concatenate(parts, axis=1).astype(BF)
-    hit = index_ref[0] == lax.broadcasted_iota(jnp.int32, (ROWS, 2 * PATCHES), 1)
-    rows_ref[...] = dot(hit.astype(BF), both, 1, 0).astype(BF)
-
-
-def owner_first_sent(own):
+    for j in range(count):
+        places = strided(j * 2 * PATCHES * lanes, 2 * PATCHES, lanes)
+        both = jnp.concatenate([wide_ref[place, :] for place in places], axis=1).astype(BF)
+        rows_ref[j * ROWS : (j + 1) * ROWS, :] = dot(one_hot(index_ref[j]), both, 1, 0).astype(BF)
+
+
+def owner_first_sent(steps):
+    own = steps // 2
+
     def source(i, at):
         return (i // own ^ 1 ^ at[1]) * own + i % own
 
@@ -78,16 +92,17 @@
 
 def pick_rows(at, patches, index, cols):
     pairs = index.shape[0]
-    width = 2 * PATCHES * cols
-    source = owner_first_sent(pairs // 2)
-    return call(
-        partial(pick_body, cols),
-        (pairs,),
+    count = together(pairs // 2)
+    width = 2 * PATCHES * cols * count
+    source = owner_first_sent(pairs // count)
+    return call(
+        partial(pick_body, cols, count),
+        (pairs // count,),
         [
             spec((1, width), lambda i, at: (0, source(i, at))),
-            spec((1, ROWS, 1), lambda i, at: (source(i, at), 0, 0)),
+            spec((count, ROWS, 1), lambda i, at: (source(i, at), 0, 0)),
         ],
-        spec((ROWS, cols), lambda i, at: (i, 0)),
+        spec((count * ROWS, cols), lambda i, at: (i, 0)),
         struct((pairs * ROWS, cols), BF),
         [pltpu.VMEM((width // 128, 128), F32)],
         prefetch=1,
@@ -96,22 +111,26 @@
     )(at, patches, index)
 
 
-def cot_body(cols, at_ref, cot_ref, rows_ref, scr):
+def cot_body(cols, count, at_ref, cot_ref, rows_ref, scr):
     lanes = cols // 128
     scr[...] = cot_ref[...].astype(F32).reshape(scr.shape)
-    parts = [scr[pl.ds(k, PAIR, stride=lanes), :] for k in range(lanes)]
-    cot = jnp.concatenate(parts, axis=1)
-    rows_ref[...] = jnp.concatenate([cot, jnp.zeros((ROWS - PAIR, cols), F32)], axis=0).astype(BF)
+    for j in range(count):
+        places = strided(j * PAIR * lanes, PAIR, lanes)
+        cot = jnp.concatenate([scr[place, :] for place in places], axis=1)
+        rows_ref[j * ROWS : (j + 1) * ROWS, :] = jnp.concatenate(
+            [cot, jnp.zeros((ROWS - PAIR, cols), F32)], axis=0
+        ).astype(BF)
 
 
 def cot_rows(at, cotangent, pairs, cols):
-    width = PAIR * cols
-    source = owner_first_sent(pairs // 2)
-    return call(
-        partial(cot_body, cols),
-        (pairs,),
+    count = together(pairs // 2)
+    width = PAIR * cols * count
+    source = owner_first_sent(pairs // count)
+    return call(
+        partial(cot_body, cols, count),
+        (pairs // count,),
         [spec((1, width), lambda i, at: (0, source(i, at)))],
-        spec((ROWS, cols), lambda i, at: (i, 0)),
+        spec((count * ROWS, cols), lambda i, at: (i, 0)),
         struct((pairs * ROWS, cols), BF),
         [pltpu.VMEM((width // 128, 128), F32)],
         prefetch=1,
@@ -120,63 +139,66 @@
     )(at, cotangent)
 
 
-def own_block(at_ref, keep_ref, got_ref):
+def own_block(at_ref, keep_ref, got_ref, j):
     own = pl.num_programs(0) // 2
     mine = pl.program_id(0) // own == at_ref[1]
-    return jnp.where(mine, keep_ref[...].astype(F32), got_ref[...].astype(F32))
-
-
-def put_body(cols, at_ref, keep_ref, got_ref, index_ref, out_ref):
+    rows = slice(j * ROWS, (j + 1) * ROWS)
+    return jnp.where(mine, keep_ref[rows, :].astype(F32), got_ref[rows, :].astype(F32))
+
+
+def put_body(cols, count, at_ref, keep_ref, got_ref, index_ref, out_ref):
     lanes = cols // 128
-    hit = index_ref[0] == lax.broadcasted_iota(jnp.int32, (ROWS, 2 * PATCHES), 1)
-    hit = hit.astype(BF)
-    rest = own_block(at_ref, keep_ref, got_ref)
-    total = None
-    for _ in range(3):
-        part = rest.astype(BF)
-        rest = rest - part.astype(F32)
-        term = dot(hit, part, 0, 0)
-        total = term if total is None else total + term
-    for k in range(lanes):
-        out_ref[pl.ds(k, 2 * PATCHES, stride=lanes), :] = total[:, k * 128 : (k + 1) * 128]
+    for j in range(count):
+        hit = one_hot(index_ref[j])
+        rest = own_block(at_ref, keep_ref, got_ref, j)
+        parts = []
+        for _ in range(3):
+            parts.append(rest.astype(BF))
+            rest = rest - parts[-1].astype(F32)
+        total = dot(jnp.concatenate([hit] * 3), jnp.concatenate(parts), 0, 0)
+        for k, place in enumerate(strided(j * 2 * PATCHES * lanes, 2 * PATCHES, lanes)):
+            out_ref[place, :] = total[:, k * 128 : (k + 1) * 128]
 
 
 def put_rows(at, keep, got, index, cols):
     pairs = index.shape[0]
-    own = pairs // 2
-    tall = 2 * PATCHES * cols // 128
-    rows = spec((ROWS, cols), lambda i, at: (i % own, 0))
-    return call(
-        partial(put_body, cols),
-        (pairs,),
-        [rows, rows, spec((1, ROWS, 1), lambda i, at: (i, 0, 0))],
+    count = together(pairs // 2)
+    own = pairs // count // 2
+    tall = count * 2 * PATCHES * cols // 128
+    rows = spec((count * ROWS, cols), lambda i, at: (i % own, 0))
+    return call(
+        partial(put_body, cols, count),
+        (pairs // count,),
+        [rows, rows, spec((count, ROWS, 1), lambda i, at: (i, 0, 0))],
         spec((tall, 128), lambda i, at: (i, 0)),
-        struct((pairs * tall, 128), F32),
+        struct((pairs // count * tall, 128), F32),
         prefetch=1,
         us=200,
         nbytes=pairs * (tall * 512 + ROWS * cols * 4),
     )(at, keep, got, index)
 
 
-def flat_body(cols, at_ref, keep_ref, got_ref, out_ref, scr):
+def flat_body(cols, count, at_ref, keep_ref, got_ref, out_ref, scr):
     lanes = cols // 128
-    rows = own_block(at_ref, keep_ref, got_ref)
-    for k in range(lanes):
-        scr[pl.ds(k, PAIR, stride=lanes), :] = rows[:PAIR, k * 128 : (k + 1) * 128]
+    for j in range(count):
+        rows = own_block(at_ref, keep_ref, got_ref, j)
+        for k, place in enumerate(strided(j * PAIR * lanes, PAIR, lanes)):
+            scr[place, :] = rows[:PAIR, k * 128 : (k + 1) * 128]
     out_ref[...] = scr[...].reshape(out_ref.shape).astype(BF)
 
 
 def flat_rows(at, keep, got, cols):
-    own = keep.shape[0] // ROWS
-    pairs = 2 * own
-    width = PAIR * cols
-    rows = spec((ROWS, cols), lambda i, at: (i % own, 0))
-    return call(
-        partial(flat_body, cols),
-        (pairs,),
+    pairs = 2 * (keep.shape[0] // ROWS)
+    count = together(pairs // 2)
+    own = pairs // count // 2
+    width = PAIR * cols * count
+    rows = spec((count * ROWS, cols), lambda i, at: (i % own, 0))
+    return call(
+        partial(flat_body, cols, count),
+        (pairs // count,),
         [rows, rows],
         spec((1, width), lambda i, at: (0, i)),
-        struct((1, pairs * width), BF),
+        struct((1, pairs // count * width), BF),
         [pltpu.VMEM((width // 128, 128), F32)],
         prefetch=1,
         us=200,
@@ -232,7 +254,7 @@
         ],
         spec((r, TILE), lambda j: (0, j)),
         struct((r, 3 * D), BF),
-        us=0.01,
+        us=13,
         nbytes=r * D * 8 + 3 * D * D * 2,
     )(hidden, w, bias)
 
@@ -283,7 +305,7 @@
         [spec((ROWS, 3 * D), lambda g: (g, 0))],
         [spec((ROWS, D), lambda g: (g, 0)), spec((1, HEADS, ROWS, ROWS), lambda g: (g, 0, 0, 0))],
         [struct((groups * ROWS, D), BF), pltpu.HBM((groups, HEADS, ROWS, ROWS), F32)],
-        us=0.01,
+        us=200,
         nbytes=groups * ROWS * (8 * D + HEADS * 512),
     )(triple)
 
@@ -312,7 +334,7 @@
         [row, spec((D, D), lambda i: (0, 0)), row, spec((8, D), lambda i: (0, 0))],
         [row, row],
         [struct((r, D), F32), struct((r, D), BF)],
-        us=200,
+        us=16,
         nbytes=r * D * 10 + D * D * 2,
     )(mixed, w, rows, vec)
 
@@ -362,7 +384,7 @@
         ],
         spec((m, D), lambda i: (i, 0)),
         struct((r, D), BF),
-        us=200,
+        us=0.01,
         nbytes=r * units * 2 + D * units * 2 + r * D * 6,
     )(active, w, vec, middle)
 
@@ -387,7 +409,7 @@
         [spec((rows, TILE), lambda j: (0, j)), spec((1, TILE), lambda j: (0, j))],
         [struct((rows, width), BF), struct((1, width), F32)],
         [pltpu.VMEM((rows, r), BF)],
-        us=200,
+        us=0.01,
         nbytes=r * rows * 2 + r * width * 2 + rows * width * 2,
     )(left, right)
 
@@ -477,7 +499,7 @@
         ],
         [row, row, vec, vec, vec],
         [struct((r, D), F32), struct((r, D), BF), vec_out, vec_out, vec_out],
-        us=0.01,
+        us=200,
         nbytes=r * units * 2 + D * units * 2 + r * D * 12,
     )(grad, w, middle, cot, vecs)
 
@@ -549,7 +571,7 @@
             dimension_semantics=("arbitrary",), vmem_limit_bytes=24 * MB
         ),
         cost_estimate=pl.CostEstimate(
-            flops=200 * FLOPS_PER_US, bytes_accessed=1024, transcendentals=0
+            flops=FLOPS_PER_US // 100, bytes_accessed=1024, transcendentals=0
         ),
     )(triple, prob, grad, *given)
 
@@ -667,9 +689,8 @@
     return lambda w, n, q: [(which, spot, (rows, cols), (w * heads_cols + q * rows, n * cols))]
 
 
-def flat_plan(cols, units, parts):
-    rows = cols // parts
-    return lambda w, n, q: [(0, (0, 0), (rows, units), (n * cols + q * rows, w * units))]
+def flat_plan(cols, units, rows, base=0):
+    return lambda w, n, q: [(0, (0, 0), (rows, units), (n * cols + base + q * rows, w * units))]
 
 
 def sums_plan(cols, narrow, spot, which):
@@ -680,25 +701,29 @@
     return lambda w, n, q: [move for plan in plans for move in plan(w, n, q)]
 
 
-def prep_body(cols, rows, at_ref, *refs):
-    qkv_ref, out_ref, vectors = refs[0], refs[1], refs[2:10]
-    piece_ref, held, sem = refs[10], refs[11:-1], refs[-1]
-    start = pl.multiple_of(at_ref[2] * rows, 16)
-    copies = [
-        pltpu.make_async_copy(
-            qkv_ref.at[p, pl.ds(start, rows)], piece_ref.at[pl.ds(p * rows, rows)], sem.at[p]
-        )
-        for p in range(3)
+def prep_body(cols, at_ref, *refs):
+    (qkv_ref, out_ref, up_ref, down_ref), vectors = refs[:4], refs[4:12]
+    first_ref, second_ref, up_a_ref, up_b_ref, down_part_ref = refs[12:17]
+    held, sem = refs[17:-1], refs[-1]
+    core, q = at_ref[2], at_ref[3]
+
+    def block(ref, index, rows, base=0):
+        return ref.at[pl.ds(pl.multiple_of(base + index * rows, 16), rows)]
+
+    half = qkv_ref.shape[1] // 2
+    ends = [
+        (block(qkv_ref.at[0], core, half), first_ref.at[pl.ds(0, half)]),
+        (block(out_ref, core, half), first_ref.at[pl.ds(half + 16, half)]),
     ]
-    copies.append(
-        pltpu.make_async_copy(
-            out_ref.at[pl.ds(start, rows)], piece_ref.at[pl.ds(3 * rows + 16, rows)], sem.at[3]
-        )
-    )
-    copies += [
-        pltpu.make_async_copy(vector, scratch, sem.at[4 + k])
-        for k, (vector, scratch) in enumerate(zip(vectors, held))
+    part = half // 2
+    ends += [
+        (block(qkv_ref.at[1 + p], q, part), second_ref.at[pl.ds(p * part, part)]) for p in range(2)
     ]
+    ends.append((block(up_ref, core, up_a_ref.shape[0]), up_a_ref))
+    ends.append((block(up_ref, q, up_b_ref.shape[0], up_ref.shape[0] // 2), up_b_ref))
+    ends.append((block(down_ref, q, down_part_ref.shape[0]), down_part_ref))
+    ends += list(zip(vectors, held))
+    copies = [pltpu.make_async_copy(a, b, sem.at[k]) for k, (a, b) in enumerate(ends)]
     for copy in copies:
         copy.start()
     for copy in copies:
@@ -709,28 +734,35 @@
     wide_line = held[7][...].astype(F32).reshape(1, -1)
     lines += [wide_line[:, k : k + cols] for k in range(0, wide_line.shape[1], cols)]
     lines.append(jnp.zeros((16 - len(lines), cols), F32))
-    piece_ref[3 * rows : 3 * rows + 16, :] = jnp.concatenate(lines, axis=0).astype(BF)
-
-
-def prep(at, qkv_t, w_out, *vectors):
-    cols = qkv_t.shape[2]
-    rows = qkv_t.shape[1] // 2
+    first_ref[half : half + 16, :] = jnp.concatenate(lines, axis=0).astype(BF)
+
+
+def prep(at, qkv_t, w_out, w_up, w_down, *vectors):
+    cols, half = qkv_t.shape[2], qkv_t.shape[1] // 2
+    rows, units = w_up.shape
+    shapes = [
+        (2 * half + 16, cols),
+        (half, cols),
+        (rows // 4, units),
+        (rows // 8, units),
+        (rows // 4, units),
+    ]
     return pl.pallas_call(
-        partial(prep_body, cols, rows),
-        out_shape=struct((4 * rows + 16, cols), BF),
+        partial(prep_body, cols),
+        out_shape=[struct(shape, BF) for shape in shapes],
         grid_spec=pltpu.PrefetchScalarGridSpec(
             num_scalar_prefetch=1,
             grid=(1,),
-            in_specs=[IN_HBM] * (2 + len(vectors)),
-            out_specs=pl.BlockSpec(memory_space=pltpu.VMEM),
+            in_specs=[IN_HBM] * (4 + len(vectors)),
+            out_specs=[pl.BlockSpec(memory_space=pltpu.VMEM)] * len(shapes),
             scratch_shapes=[pltpu.VMEM(v.shape, BF) for v in vectors]
-            + [pltpu.SemaphoreType.DMA((4 + len(vectors),))],
+            + [pltpu.SemaphoreType.DMA((7 + len(vectors),))],
         ),
         compiler_params=pltpu.CompilerParams(vmem_limit_bytes=8 * MB),
         cost_estimate=pl.CostEstimate(
             flops=FLOPS_PER_US // 100, bytes_accessed=1024, transcendentals=0
         ),
-    )(at, *[in_hbm(v) for v in (qkv_t, w_out, *vectors)])
+    )(at, *[in_hbm(v) for v in (qkv_t, w_out, w_up, w_down, *vectors)])
 
 
 def vec_body(wide, narrow, cols, first, tag_lists, at_ref, *refs):
@@ -843,14 +875,14 @@
     )(*rows)
 
 
-def build_body(plan, tag_lists, inverse, part_at, at_ref, *refs):
+def build_body(plans, tag_lists, inverse, parts_by, at_ref, *refs):
     refs, sem = refs[:-1], refs[-1]
     count = len(tag_lists)
     wholes, arrays = (refs[:-count], refs[-count:]) if inverse else (refs[count:], refs[:count])
     copies = []
-    for array, tags in zip(arrays, tag_lists):
+    for array, tags, plan, by in zip(arrays, tag_lists, plans, parts_by):
         for k, (dw, dn, dq) in enumerate(tags):
-            w, n, q = at_ref[0] ^ dw, at_ref[1] ^ dn, at_ref[part_at] ^ dq
+            w, n, q = at_ref[0] ^ dw, at_ref[1] ^ dn, at_ref[by] ^ dq
             for which, (at_row, at_lane), (rows, lanes), (row, lane) in plan(w, n, q):
                 piece = array.at[k, pl.ds(at_row, rows), pl.ds(at_lane, lanes)]
                 whole = wholes[which].at[
@@ -864,10 +896,10 @@
         copy.wait()
 
 
-def move_pieces(at, arrays, plan, tag_lists, inverse, part_at, shapes):
-    moves = sum(len(tags) for tags in tag_lists) * len(plan(0, 0, 0))
+def move_pieces(at, arrays, plans, tag_lists, inverse, parts_by, shapes):
+    moves = sum(len(tags) * len(plan(0, 0, 0)) for tags, plan in zip(tag_lists, plans))
     return pl.pallas_call(
-        partial(build_body, plan, tag_lists, inverse, part_at),
+        partial(build_body, plans, tag_lists, inverse, parts_by),
         out_shape=[struct(shape, BF) for shape in shapes],
         grid_spec=pltpu.PrefetchScalarGridSpec(
             num_scalar_prefetch=1,
@@ -886,21 +918,30 @@
 CORE, DP_INDEX = 2, 3
 
 
-def build_weights(at, pieces, plan, shape, part_at=CORE):
-    arrays, tags = [in_hbm(p.stack) for p in pieces], [p.tags for p in pieces]
-    return move_pieces(at, arrays, plan, tags, False, part_at, [shape])[0]
-
-
-def cut_grads(at, grads, plan, tags, shape, part_at=CORE):
-    tag_lists = [[(w, n, q ^ dc) for w, n, q in tags] for dc in range(2)]
-    return move_pieces(at, grads, plan, tag_lists, True, part_at, [(len(tags),) + shape] * 2)
+def build_weights(at, shape, *groups):
+    lists = [(p, plan, by) for pieces, plan, by in groups for p in pieces]
+    arrays, tags = [p.stack for p, _, _ in lists], [p.tags for p, _, _ in lists]
+    plans, parts_by = [plan for _, plan, _ in lists], [by for _, _, by in lists]
+    return move_pieces(at, arrays, plans, tags, False, parts_by, [shape])[0]
+
+
+def cut_grads(at, grads, plan, tags, shape, part_at=CORE, split=False):
+    half = len(tags) // 2
+    some = (tags[:half], tags[half:]) if split else (tags,)
+    tag_lists = [[(w, n, q ^ dc) for w, n, q in part] for dc in range(2) for part in some]
+    shapes = [(len(part),) + shape for part in tag_lists]
+    count = len(tag_lists)
+    out = move_pieces(
+        at, grads, [plan] * count, tag_lists, True, [part_at] * count, shapes
+    )
+    return (out[:2], out[2:]) if split else out
 
 
 def fence_body(x_ref, out_ref):
     out_ref[...] = x_ref[...]
 
 
-def fence(token):
+def fence(token, us=200):
     vmem = pl.BlockSpec(memory_space=pltpu.VMEM)
     return pl.pallas_call(
         fence_body,
@@ -909,17 +950,20 @@
         out_specs=vmem,
         compiler_params=pltpu.CompilerParams(vmem_limit_bytes=MB, has_side_effects=True),
         cost_estimate=pl.CostEstimate(
-            flops=200 * FLOPS_PER_US, bytes_accessed=1024, transcendentals=0
+            flops=us * FLOPS_PER_US, bytes_accessed=1024, transcendentals=0
         ),
     )(token)
 
 
 class Chain:
-    def __init__(self, at, grads, plan, tags, shape, part_at=CORE):
-        self.keep, self.send = cut_grads(at, grads, plan, tags, shape, part_at)
+    def __init__(self, *args, **options):
+        self.keep, self.send = cut_grads(*args, **options)
 
     def go(self, axis, bit):
-        self.got = swap(self.send, axis, bit)
+        if isinstance(self.send, (list, tuple)):
+            self.got = [swap(part, axis, bit) for part in self.send]
+        else:
+            self.got = swap(self.send, axis, bit)
 
     def fold(self, *deps):
         self.keep, self.send = halves_summed(self.keep, hold(self.got, *deps))
@@ -948,10 +992,14 @@
 
 
 def halves_summed(kept, got):
-    half = kept.shape[0] // 2
-    keep = kept[:half].astype(F32) + got[:half].astype(F32)
-    send = (kept[half:].astype(F32) + got[half:].astype(F32)).astype(BF)
-    return keep, send
+    def halves(stack):
+        if isinstance(stack, (list, tuple)):
+            return stack
+        half = stack.shape[0] // 2
+        return stack[:half], stack[half:]
+
+    first, second = [a.astype(F32) + b.astype(F32) for a, b in zip(halves(kept), halves(got))]
+    return first, second.astype(BF)
 
 
 def core_half(at, shard):
@@ -1032,21 +1080,22 @@
 
     w_qkv_t = w_qkv.transpose(1, 2, 0)
     if swaps:
-        first = first_piece(
-            prep(
-                at,
-                w_qkv_t,
-                w_out,
-                gain_one,
-                shift_one,
-                gain_two,
-                shift_two,
-                b_out,
-                b_down,
-                b_qv,
-                b_up,
-            )
-        )
+        pieces = prep(
+            at,
+            w_qkv_t,
+            w_out,
+            w_up,
+            w_down,
+            gain_one,
+            shift_one,
+            gain_two,
+            shift_two,
+            b_out,
+            b_down,
+            b_qv,
+            b_up,
+        )
+        a_p, b_p, u_p, v_p, d_p = [first_piece(piece) for piece in pieces]
 
         def part_of(whole, side):
             return lax.dynamic_slice_in_dim(whole, side * cols, cols, axis=1)
@@ -1061,89 +1110,136 @@
         mine, theirs = at[1], 1 - at[1]
         whole = (D, wide * units)
 
-        first_z = [first.fetch(WIDE, bit) for bit in (1, 2, 3)]
-        rows_out = pick_rows(hold(at, first.stack), patches, index, cols)
+        b_z = [b_p.fetch(WIDE, bit) for bit in (1, 2, 3)]
+        a_x, d_x = a_p.fetch(NARROW, 1), d_p.fetch(NARROW, 1)
+        token = fence(hold(at, a_p.stack, b_p.stack, d_p.stack))
+        a_p, d_p = a_p.join(a_x.after(token)), d_p.join(d_x.after(token))
+        b_p = b_p.join(*[p.after(token) for p in b_z])
+
+        b_x, a_z = b_p.fetch(NARROW, 1), a_p.fetch(WIDE, 2)
+        rows_out = pick_rows(
+            hold(at, a_p.stack, b_p.stack, d_p.stack), patches, index, cols
+        )
         own = rows_out.shape[0] // 2
         rows_send = rows_out[:own]
+        a_p, b_p = a_p.join(a_z.after(rows_send)), b_p.join(b_x.after(rows_send))
+
+        b_y, a_z = b_p.fetch(DP, 2), a_p.fetch(WIDE, 1)
+        v_z = v_p.fetch(WIDE, 2, rows_send)
         rows_got = swap(rows_send, NARROW, 1)
-        cot_out = cot_rows(hold(at, rows_send), cotangent, pairs, cols)
-
-        first = first.join(*[p.after(cot_out) for p in first_z])
-        up_p = first_piece(hold(core_half(at, w_up), first.stack))
-        up_z = [up_p.fetch(WIDE, bit) for bit in (1, 2, 3)]
-        rows = join_cols(rows_out[own:], hold(rows_got, up_p.stack))
-        first_x = first.fetch(NARROW, 1, rows)
-        up_p = up_p.join(*[p.after(rows) for p in up_z])
-
-        first = first.join(first_x.after(up_p.stack))
-        first_c = first.fetch(DP, 1)
-        up_x = up_p.fetch(NARROW, 1)
-        down_p = first_piece(hold(quarter(at, w_down), first.stack))
-        down_z = [down_p.fetch(WIDE, bit) for bit in (1, 2, 3)]
-        vec_at = 3 * heads_cols // 2
-        out_at = (vec_at + 16, 0)
-        vecs, bias_qkv, bias_up = vectors_of(at, [first], vec_at, wide, narrow, cols, units)
-        hidden_one = norm(rows, vecs)
-        all_first = [first, first_c.after(hidden_one)]
+        cot_out = cot_rows(hold(at, rows_send, a_p.stack, b_p.stack), cotangent, pairs, cols)
+        a_p, b_p = a_p.join(a_z.after(cot_out)), b_p.join(b_y.after(cot_out))
+        v_p = v_p.join(v_z.after(cot_out))
+        rows = join_cols(rows_out[own:], hold(rows_got, cot_out))
+
+        started = [a_p.stack, b_p.stack, v_p.stack, rows]
+        a_c, b_c = a_p.fetch(DP, 1, *started), b_p.fetch(DP, 1, *started)
+        u_z, v_z = u_p.fetch(WIDE, 2, *started), v_p.fetch(WIDE, 1, *started)
+        cot_send = hold(cot_out[:own], *started)
+        cot_got = swap(cot_send, NARROW, 1)
         half = heads_cols // 2
-        first_plan = qkv_plan(cols, heads_cols, 2, {p: (p * half, 0) for p in range(3)})
-        qkv_t = build_weights(at, all_first, first_plan, (3 * D, D))
-        out_w = build_weights(at, all_first, out_plan(cols, heads_cols, 2, out_at), (D, D))
-        down_p = down_p.join(*[p.after(qkv_t) for p in down_z])
-        down_x = down_p.fetch(NARROW, 1)
-        triple = qkv(hold(hidden_one, down_p.stack), qkv_t, bias_qkv)
-        mixed, prob = attend(triple)
-        half_flat, part_flat = flat_plan(cols, units, 2), flat_plan(cols, units, 4)
-        up_x = up_x.after(mixed)
-        up_c = up_p.fetch(DP, 1, up_x.stack)
-        up_xc = up_x.fetch(DP, 1)
-        down_p = down_p.join(down_x.after(mixed))
-        down_y = down_p.fetch(DP, 2)
-        cot_send = hold(cot_out[:own], down_p.stack)
-        cot_got = swap(cot_send, NARROW, 1)
-        middle, hidden_two = mix(
-            hold(mixed, up_x.stack, down_p.stack, cot_send), out_w, rows, vecs
-        )
-        up_c, up_xc = up_c.after(hidden_two), up_xc.after(hidden_two)
-        up_w = build_weights(at, [up_p, up_x, up_c, up_xc], half_flat, whole)
+        vecs, bias_qkv, bias_up = vectors_of(at, [a_p], half, wide, narrow, cols, units)
+        hidden_one = norm(hold(rows, *started, cot_send), vecs)
+        u_p, v_p = u_p.join(u_z.after(hidden_one)), v_p.join(v_z.after(hidden_one))
+        a_c, b_c = a_c.after(hidden_one), b_c.after(hidden_one)
+
+        u_z, v_x = u_p.fetch(WIDE, 1), v_p.fetch(NARROW, 1)
+        started = [u_p.stack, v_p.stack]
+        d_z = d_p.fetch(WIDE, 2, *started)
+        part = heads_cols // 4
+        qkv_t = build_weights(
+            at,
+            (3 * D, D),
+            ([a_p, a_c], qkv_plan(cols, heads_cols, 2, {0: (0, 0)}), CORE),
+            (
+                [b_p, b_c],
+                qkv_plan(cols, heads_cols, 4, {1: (0, 0), 2: (part, 0)}),
+                DP_INDEX,
+            ),
+        )
+        out_w = build_weights(
+            at, (D, D), ([a_p, a_c], out_plan(cols, heads_cols, 2, (half + 16, 0)), CORE)
+        )
+        triple = qkv(hold(hidden_one, *started), qkv_t, bias_qkv)
+        u_p, v_p = u_p.join(u_z.after(triple)), v_p.join(v_x.after(triple))
+        d_p = d_p.join(d_z.after(triple))
+        cot = join_cols(cot_out[own:], hold(cot_got, triple))
+
+        u_x, v_y, d_z = u_p.fetch(NARROW, 1), v_p.fetch(DP, 2), d_p.fetch(WIDE, 1)
+        mixed, prob = attend(hold(triple, u_p.stack, v_p.stack, d_p.stack, cot))
+        d_p = d_p.join(d_z.after(mixed))
+        u_x, v_y = u_x.after(mixed), v_y.after(mixed)
+
+        u_all, v_all = [u_p, u_x], [v_p, v_y]
+        started = [d_p.stack, u_x.stack, v_y.stack]
+        d_y = d_p.fetch(DP, 2)
+        u_c = [p.fetch(DP, 1, *started) for p in u_all]
+        v_c = [p.fetch(DP, 1, *started) for p in v_all]
+        middle, hidden_two = mix(hold(mixed, *started), out_w, rows, vecs)
+        half_flat = flat_plan(cols, units, cols // 2)
+        part_flat = flat_plan(cols, units, cols // 4)
+        up_w = build_weights(
+            at,
+            whole,
+            (u_all + [p.after(hidden_two) for p in u_c], part_flat, CORE),
+            (
+                v_all + [p.after(hidden_two) for p in v_c],
+                flat_plan(cols, units, cols // 8, cols // 2),
+                DP_INDEX,
+            ),
+        )
         active, slope = up(hidden_two, up_w, bias_up)
-        cot = join_cols(cot_out[own:], hold(cot_got, active))
-        down_y = down_y.after(active)
-        down_c = [p.fetch(DP, 1, down_y.stack) for p in (down_p, down_y)]
 
         x_first = [(w, n, 0) for n in range(2) for w in (0, 2, 1, 3)]
         y_first = [(w, n, dy) for dy in (0, 2) for n in range(2) for w in (0, 2, 1, 3)]
-        gw_down, _ = outer(hold(cot, *[p.stack for p in (down_p, down_y)]), active)
+        gw_down, _ = outer(cot, in_hbm(active))
         gb_down = jnp.sum(cot, 0, dtype=F32)[None]
-        down_c = [p.after(gw_down) for p in down_c]
-        down_w = build_weights(at, [down_p, down_y] + down_c, part_flat, whole, DP_INDEX)
-        g_d = Chain(at, [hold(gw_down, down_w)], half_flat, x_first, (cols // 2, units))
+        d_y = d_y.after(gw_down)
+        d_c = [p.fetch(DP, 1, d_y.stack) for p in (d_p, d_y)]
+        g_d = Chain(
+            at,
+            [hold(gw_down, d_y.stack)],
+            half_flat,
+            x_first,
+            (cols // 2, units),
+            split=True,
+        )
         g_d.go(DP, 1)
-        g_d.fold()
+        d_c = [p.after(*g_d.send) for p in d_c]
+        down_w = build_weights(at, whole, ([d_p, d_y] + d_c, part_flat, DP_INDEX))
+        g_d.fold(down_w)
         g_d.go(NARROW, 1)
         grad_inner, gw_up, gb_up = inner_back(
             cot, hold(down_w, g_d.send), in_hbm(slope), hidden_two
         )
 
-        g_u = Chain(at, [gw_up], part_flat, y_first, (cols // 4, units), DP_INDEX)
+        result = down(hold(in_hbm(active), grad_inner), down_w, vecs, middle)
+        g_u = Chain(
+            at,
+            [hold(gw_up, result)],
+            part_flat,
+            y_first,
+            (cols // 4, units),
+            DP_INDEX,
+            split=True,
+        )
         g_u.go(DP, 1)
-        g_d.fold(g_u.send)
+        g_d.fold(*g_u.send)
         g_d.go(WIDE, 1)
-        result = down(hold(active, g_d.send), down_w, vecs, middle)
+        g_u.fold(g_d.send)
+        g_u.go(DP, 2)
         grad_middle, branch, gg_two, gs_two, gb_out = middle_back(
-            hold(grad_inner, result), up_w, middle, cot, vecs
+            hold(grad_inner, g_d.send, g_u.send), up_w, middle, cot, vecs
         )
         grad_mixed, gw_out = mixed_back(branch, out_w, mixed)
 
-        g_u.fold(grad_mixed)
-        g_u.go(DP, 2)
         g_d.fold(grad_mixed)
         g_d.go(WIDE, 2)
         result_send = hold(part_of(result, theirs), grad_mixed)
         result_got = swap(result_send, NARROW, 1)
         groups = rows.shape[0] // ROWS
         grad_triple = attend_back(
-            triple, in_hbm(prob), hold(grad_mixed, g_u.send, g_d.send, result_send), 0, groups
+            triple, in_hbm(prob), hold(grad_mixed, g_d.send, result_send), 0, groups
         )
         grad_rows, gg_one, gs_one = first_back(grad_triple, qkv_t, rows, grad_middle, vecs)
 
@@ -1171,18 +1267,16 @@
         g_q = Chain(
             at,
             [gw_qkv],
-            qkv_plan(cols, heads_cols, 4, {0: (0, 0), 1: (part, 0)}),
+            qkv_plan(cols, heads_cols, 4, {p: (p * part, 0) for p in range(3)}),
             y_first,
-            (2 * part, cols),
+            (3 * part, cols),
             DP_INDEX,
         )
         g_q.go(DP, 1)
         rest_plan = joined(
-            qkv_plan(cols, heads_cols, 2, {2: (0, 0)}),
-            out_plan(cols, heads_cols, 2, (half, 0), 1),
-            sums_plan(cols, narrow, (2 * half, 0), 2),
-        )
-        g_r = Chain(at, [gw_qkv, gw_out, sums], rest_plan, x_first, (2 * half + 16, cols))
+            out_plan(cols, heads_cols, 2, (0, 0), 0), sums_plan(cols, narrow, (half, 0), 1)
+        )
+        g_r = Chain(at, [gw_out, sums], rest_plan, x_first, (half + 16, cols))
         g_r.go(DP, 1)
         d_sum = d_sum + hold(d_got, g_r.send).astype(F32)
         d_got = swap(d_sum, DP, 1)
@@ -1209,36 +1303,27 @@
         g_q.go(NARROW, 1)
         g_r.spread(grad_patches)
         u_sum = g_u.total(g_q.send, *g_r.send)
-        u_got = swap(u_sum.astype(BF), DP, 2)
         token = fence(hold(vecs, g_q.send, u_sum, *g_r.send))
         g_q.spread(token)
         r_sum = g_r.all_of(token)
         r_got = swap(r_sum.astype(BF), DP, 2)
-        u_sum = in_order(u_sum, hold(u_got, token).astype(F32), at[3] // 2)
-        u_got = swap(u_sum, DP, 1)
+        u_got = swap(u_sum.astype(BF), DP, 2)
         token = fence(hold(token, r_sum, u_sum, *g_q.send))
         q_sum = g_q.all_of(token)
         q_got = [swap(q_sum.astype(BF), DP, bit) for bit in (1, 2, 3)]
         r_sum = r_sum + hold(r_got, token).astype(F32)
-        r_got = swap(r_sum[: 2 * half], DP, 1)
+        r_got = swap(r_sum[:half], DP, 1)
+        u_sum = in_order(u_sum, hold(u_got, token).astype(F32), at[3] // 2)
+        u_got = swap(u_sum, DP, 1)
         g_down = in_order(d_sum, d_got, at[2]).reshape(cols, units)
-        g_up = in_order(u_sum, hold(u_got, token), at[2]).transpose(1, 0, 2, 3)
-        g_up = g_up.reshape(cols, units)
+        g_up = in_order(u_sum, u_got, at[2]).transpose(1, 0, 2, 3).reshape(cols, units)
         q_got = [got.astype(F32) for got in q_got]
         pairs_of = [in_order(q_sum, q_got[0], at[2]), in_order(q_got[1], q_got[2], at[2])]
-        q_sum = in_order(*pairs_of, at[3] // 2).reshape(4, 2, part, cols)
-        g_rest = in_order(r_sum[: 2 * half], r_got, at[2]).reshape(2, 2, half, cols)
-        g_out = g_rest[:, 1].reshape(heads_cols, cols)
-        g_qkv = jnp.stack(
-            [
-                q_sum[:, 0].reshape(heads_cols, cols),
-                q_sum[:, 1].reshape(heads_cols, cols),
-                g_rest[:, 0].reshape(heads_cols, cols),
-            ]
-        )
-        g_qkv = g_qkv.transpose(2, 0, 1)
+        q_sum = in_order(*pairs_of, at[3] // 2).reshape(4, 3, part, cols)
+        g_out = in_order(r_sum[:half], r_got, at[2]).reshape(heads_cols, cols)
+        g_qkv = q_sum.transpose(3, 1, 0, 2).reshape(cols, 3, heads_cols)
         grad_patches = grad_patches.reshape(1, -1)
-        lines = r_sum[2 * half :]
+        lines = r_sum[half:]
         vector_grads = [lines[i] for i in range(6)]
         g_bqv = lines[6].reshape(2, heads_cols)
         g_bup = lines[7:9].reshape(units)

time: 328 us -> 282 us (0.86); the launches traced: 327 us -> 277 us
  waiting for transfers between devices: 85 us -> 57 us
  local copies, waits for them, and re-layouts: 34.7 us -> 17.4 us
  Pallas kernels: 137 us -> 128 us
    ppermute x51 -> x62, waiting for transfers between devices: 85 us -> 57 us  [swap(): return lax.ppermute(value, axis, [(i, i ^ bit) for i in range(size)])]
    pallas_call x13, Pallas kernels: 55.3 us -> 33.9 us  [the longest x8 14.7 us: move_pieces(): pl.pallas_call(partial(build_body, plans, tag_lists, inverse, parts_by),...]
    unnamed x104 -> x81, local copies, waits for them, and re-layouts: 24.9 us -> 12 us
    pallas_call x1, Pallas kernels: 6.28 us -> 16.3 us  [middle_back(): call(middle_back_body, (r // m,), [spec((m, units), lambda i: (i, 0)), sp...]
    ppermute x51 -> x62, starting transfers between devices: 54.5 us -> 56.2 us  [swap(): return lax.ppermute(value, axis, [(i, i ^ bit) for i in range(size)])]
  transfers between devices with their start and end apart: 51 -> 62, of which waited for: 18 -> 24; matrix products, arithmetic and copies ran while one was open for 7% -> 7% of each run, Pallas kernels for 39% -> 45%
where the time goes in v5:
time: 282 us; the launch traced here: 277 us
  Pallas kernels  128 us (45%)
  waiting for transfers between devices  57 us (20%)
  starting transfers between devices  56.2 us (20%)
  local copies, waits for them, and re-layouts  17.4 us (6%)
  other arithmetic  16.1 us (6%)
    ppermute x62, waiting for transfers between devices, swap(): return lax.ppermute(value, axis, [(i, i ^ bit) for i in range(size)])  57 us
    ppermute x62, starting transfers between devices, swap(): return lax.ppermute(value, axis, [(i, i ^ bit) for i in range(size)])  56.2 us
    pallas_call x1, Pallas kernels, middle_back(): call(middle_back_body, (r // m,), [spec((m, units), lambda i: (i, 0)), sp...  16.3 us
    pallas_call x8, Pallas kernels, move_pieces(): pl.pallas_call(partial(build_body, plans, tag_lists, inverse, parts_by),...  14.7 us
    pallas_call x1, Pallas kernels, inner_back(): call(inner_back_body, (units // TILE,), [full, col, tile, full], [tile, c...  12.9 us
    unnamed x81, local copies, waits for them, and re-layouts  12 us
    pallas_call x1, Pallas kernels, attend_back(): pl.pallas_call(attend_back_body, out_shape=struct(triple.shape, BF), grid...  11.9 us
    pallas_call x1, Pallas kernels, up(): call(up_body, (units // TILE,), [spec((r, D), lambda j: (0, 0)), spec((D,...  10.2 us
  transfers between devices with their start and end apart: 62, of which 24 were waited for; matrix products, arithmetic and copies ran while one was open for 7% of the time, Pallas kernels for 45%

profile of v5, /device:TPU:0, one launch (start us, length us, event | category | flops | bytes accessed | tf_op | source)
XLA Modules:
  0.0 276.8 jit_solution(4599540400563828593)
XLA Ops:
  2.7 5.1 %collective-permute-start.3 = (bf16[1,96,384]{2,1,0:T(8,128)(2,1)S(1)}, bf16[1,96,384]{2,1,0:T(8,128)(2,1)S(1)}, u32[]{:S(2)}, u32[]{:S(2)}) collective-permute-start(bf16[1,96,384]{2,1,0:T(8,128)(2,1)S(1)} %bitcast.101), channel_id=1, source_target_pairs={{0,6},{2,4},{4,2},{6,0},{1,7},{3,5},{5,3},{7,1},{8,14},{10,12},{12... | collective-permute-start | bytes 221192 | tf_op jit(solution)/shard_map/ppermute | solution.py:635
  18.4 2.7 collective-permute-start.6
  21.0 3.7 %copy-done.23 = bf16[1,2408448]{1,0:T(2,128)(2,1)S(1)} copy-done((bf16[1,2408448]{1,0:T(2,128)(2,1)S(1)}, bf16[1,2408448]{1,0:T(2,128)(2,1)}, u32[]{:S(2)}) %copy-start.23) | copy-done | bytes 4816920
  24.8 4.1 %shard_map.265 = bf16[1792,384]{1,0:T(8,128)(2,1)S(1)} custom-call(s32[4]{0:T(128)S(1)} %pad_add_fusion.at_ref.x_ref, bf16[1,2408448]{1,0:T(2,128)(2,1)S(1)} %copy-done.23, s32[16,112,1]{2,1,0:T(8,128)S(1)} %copy.31.index_ref), custom_call_target="tpu_custom_call" | custom-call | flops 108000002048 | bytes 1024 | tf_op jit(solution)/shard_map/pallas_call | solution.py:98
  32.3 3.3 %collective-permute-done.6 = bf16[2,208,384]{2,1,0:T(8,128)(2,1)S(1)} collective-permute-done((bf16[2,208,384]{2,1,0:T(8,128)(2,1)S(1)}, bf16[2,208,384]{2,1,0:T(8,128)(2,1)S(1)}, u32[]{:S(2)}, u32[]{:S(2)}) %collective-permute-start.6) | collective-permute-done | bytes 319520 | tf_op jit(solution)/shard_map/ppermute | solution.py:635
  35.8 2.8 %shard_map.266 = bf16[1792,384]{1,0:T(8,128)(2,1)S(1)} custom-call(s32[4]{0:T(128)S(1)} %pad_add_fusion.at_ref.x_ref, bf16[1,602112]{1,0:T(2,128)(2,1)S(1)} %copy-done.24), custom_call_target="tpu_custom_call" | custom-call | flops 108000002048 | bytes 1024 | tf_op jit(solution)/shard_map/pallas_call | solution.py:129
  38.8 4.5 %collective-permute-done.5 = bf16[896,384]{1,0:T(8,128)(2,1)S(1)} collective-permute-done((bf16[896,384]{1,0:T(8,128)(2,1)S(1)}, bf16[896,384]{1,0:T(8,128)(2,1)S(1)}, u32[]{:S(2)}, u32[]{:S(2)}) %collective-permute-start.5) | collective-permute-done | bytes 688160 | tf_op jit(solution)/shard_map/ppermute | solution.py:635
  43.9 8.1 %collective-permute-done.8 = bf16[4,208,384]{2,1,0:T(8,128)(2,1)S(1)} collective-permute-done((bf16[4,208,384]{2,1,0:T(8,128)(2,1)S(1)}, bf16[4,208,384]{2,1,0:T(8,128)(2,1)S(1)}, u32[]{:S(2)}, u32[]{:S(2)}) %collective-permute-start.8) | collective-permute-done | bytes 639008 | tf_op jit(solution)/shard_map/ppermute | solution.py:635
  68.2 4.1 %shard_map.270.triple_ref = bf16[896,2304]{1,0:T(8,128)(2,1)S(1)} custom-call(bf16[896,768]{1,0:T(8,128)(2,1)S(1)} %shard_map.268.hidden_ref, bf16[2304,768]{1,0:T(8,128)(2,1)S(1)} %shard_map.269.w_ref, f32[1,2304]{1,0:T(1,128)S(1)} %get-tuple-element.176.bias_ref), custom_call_target="tpu_custom_call" | custom-call | flops 7020000256 | bytes 1024 | tf_op jit(solution)/shard_map/pallas_call | solution.py:247
  72.4 3.2 %collective-permute-done.17 = bf16[2,96,768]{2,1,0:T(8,128)(2,1)S(1)} collective-permute-done((bf16[2,96,768]{2,1,0:T(8,128)(2,1)S(1)}, bf16[2,96,768]{2,1,0:T(8,128)(2,1)S(1)}, u32[]{:S(2)}, u32[]{:S(2)}) %collective-permute-start.17) | collective-permute-done | bytes 294944 | tf_op jit(solution)/shard_map/ppermute | solution.py:635
  75.9 2.5 collective-permute-done.15
  81.7 6.0 %shard_map.271 = (bf16[896,768]{1,0:T(8,128)(2,1)S(1)}, f32[8,12,112,112]{3,2,1,0:T(8,128)}) custom-call(bf16[896,2304]{1,0:T(8,128)(2,1)S(1)} %shard_map.270.triple_ref), custom_call_target="tpu_custom_call" | custom-call | flops 108000002048 | bytes 1024 | tf_op jit(solution)/shard_map/pallas_call | solution.py:302
  87.8 5.4 %collective-permute-done.19 = bf16[4,96,768]{2,1,0:T(8,128)(2,1)S(1)} collective-permute-done((bf16[4,96,768]{2,1,0:T(8,128)(2,1)S(1)}, bf16[4,96,768]{2,1,0:T(8,128)(2,1)S(1)}, u32[]{:S(2)}, u32[]{:S(2)}) %collective-permute-start.19) | collective-permute-done | bytes 589856 | tf_op jit(solution)/shard_map/ppermute | solution.py:635
  102.5 10.2 %shard_map.275 = (bf16[896,3072]{1,0:T(8,128)(2,1)}, f32[896,3072]{1,0:T(8,128)}) custom-call(bf16[896,768]{1,0:T(8,128)(2,1)S(1)} %get-tuple-element.188.hidden_ref, bf16[768,3072]{1,0:T(8,128)(2,1)S(1)} %shard_map.274.w_ref, f32[1,3072]{1,0:T(1,128)S(1)} %get-tuple-element.197.bias_ref), custom_call_target="tpu_custom_call" | custom-call | flops 5400000 | bytes 1024 | tf_op jit(solution)/shard_map/pallas_call | solution.py:353
  112.6 8.4 %shard_map.276 = (bf16[768,3072]{1,0:T(8,128)(2,1)S(1)}, f32[1,3072]{1,0:T(1,128)}) custom-call(bf16[896,768]{1,0:T(8,128)(2,1)S(1)} %get-tuple-element.286.left_ref.cot_ref, bf16[896,3072]{1,0:T(8,128)(2,1)} %get-tuple-element.213.right_ref.active_ref), custom_call_target="tpu_custom_call" | custom-call | flops 5400000 | bytes 1024 | tf_op jit(solution)/shard_map/pallas_call | solution.py:405
  131.6 12.9 %shard_map.279 = (bf16[896,3072]{1,0:T(8,128)(2,1)}, bf16[768,3072]{1,0:T(8,128)(2,1)S(1)}, f32[1,3072]{1,0:T(1,128)S(1)}) custom-call(bf16[896,768]{1,0:T(8,128)(2,1)S(1)} %get-tuple-element.286.left_ref.cot_ref, bf16[768,3072]{1,0:T(8,128)(2,1)S(1)} %shard_map.278.w_ref, f32[896,3072]{1,0:T(8,128)} %get-tuple-element.211.slope_ref, ...), custom_call_target="tpu_custom_call" | custom-call | flops 108000002048 | bytes 1024 | tf_op jit(solution)/shard_map/pallas_call | solution.py:433
  144.4 6.5 %shard_map.280 = bf16[896,768]{1,0:T(8,128)(2,1)S(1)} custom-call(bf16[896,3072]{1,0:T(8,128)(2,1)} %get-tuple-element.213.right_ref.active_ref, bf16[768,3072]{1,0:T(8,128)(2,1)S(1)} %shard_map.278.w_ref, f32[8,768]{1,0:T(8,128)S(1)} %get-tuple-element.263.vec_ref.x_ref, f32[896,768]{1,0:T(8,128)S(1)} %get-tuple-element.214.middle_ref), custom_call_target="tpu_custom_call" | custom-call | flops 5400000 | bytes 1024 | tf_op jit(solution)/shard_map/pallas_call | solution.py:376
  150.9 2.6 shard_map.281
  165.3 16.3 %shard_map.282 = (f32[896,768]{1,0:T(8,128)S(1)}, bf16[896,768]{1,0:T(8,128)(2,1)S(1)}, f32[1,768]{1,0:T(1,128)S(1)}, f32[1,768]{1,0:T(1,128)S(1)}, f32[1,768]{1,0:T(1,128)S(1)}) custom-call(bf16[896,3072]{1,0:T(8,128)(2,1)S(1)} %copy-done.27, bf16[768,3072]{1,0:T(8,128)(2,1)S(1)} %bitcast.85, f32[896,768]{1,0:T(8,128)S(1)} %copy-done.10, ...), custom_call_target="tpu_custom_call" | custom-call | flops 108000002048 | bytes 1024 | tf_op jit(solution)/shard_map/pallas_call | solution.py:490
  181.7 2.5 shard_map.283
  188.0 11.9 %shard_map.284.grad_ref = bf16[896,2304]{1,0:T(8,128)(2,1)S(1)} custom-call(bf16[896,2304]{1,0:T(8,128)(2,1)S(1)} %copy-done.8, f32[8,12,112,112]{3,2,1,0:T(8,128)} %get-tuple-element.215.prob_ref, bf16[896,768]{1,0:T(8,128)(2,1)S(1)} %get-tuple-element.230.grad_ref), custom_call_target="tpu_custom_call" | custom-call | flops 5400000 | bytes 1024 | tf_op jit(solution)/shard_map/pallas_call | solution.py:555
  199.9 4.7 %shard_map.285 = (f32[896,768]{1,0:T(8,128)S(1)}, f32[1,768]{1,0:T(1,128)S(1)}, f32[1,768]{1,0:T(1,128)S(1)}) custom-call(bf16[896,2304]{1,0:T(8,128)(2,1)S(1)} %shard_map.284.grad_ref, bf16[2304,768]{1,0:T(8,128)(2,1)S(1)} %copy-done.2, bf16[896,768]{1,0:T(8,128)(2,1)S(1)} %copy-done.4, f32[896,768]{1,0:T(8,128)S(1)} %get-tuple-element.231.middle_ref, ...), custom_call_target="tpu_custom_call" | custom-call | flops 5400000 | bytes 1024 | tf_op jit(solution)/shard_map/pallas_call | solution.py:613
  207.0 4.7 %shard_map.286 = (bf16[2304,768]{1,0:T(8,128)(2,1)S(1)}, f32[1,2304]{1,0:T(1,128)S(1)}) custom-call(bf16[896,2304]{1,0:T(8,128)(2,1)S(1)} %shard_map.284.grad_ref, bf16[896,768]{1,0:T(8,128)(2,1)S(1)} %copy-done.26), custom_call_target="tpu_custom_call" | custom-call | flops 108000002048 | bytes 1024 | tf_op jit(solution)/shard_map/pallas_call | solution.py:587
  215.1 2.8 %shard_map.287 = (bf16[16,144,384]{2,1,0:T(8,128)(2,1)S(1)}, bf16[16,144,384]{2,1,0:T(8,128)(2,1)S(1)}) custom-call(s32[4]{0:T(128)S(1)} %pad_add_fusion.at_ref.x_ref, bf16[2304,768]{1,0:T(8,128)(2,1)S(1)} %get-tuple-element.239.refs_0_), custom_call_target="tpu_custom_call" | custom-call | flops 5400000 | bytes 1024 | tf_op jit(solution)/shard_map/pallas_call | solution.py:901
  218.0 4.4 %collective-permute-done.39 = bf16[4,96,768]{2,1,0:T(8,128)(2,1)S(1)} collective-permute-done((bf16[4,96,768]{2,1,0:T(8,128)(2,1)S(1)}, bf16[4,96,768]{2,1,0:T(8,128)(2,1)S(1)}, u32[]{:S(2)}, u32[]{:S(2)}) %collective-permute-start.39) | collective-permute-done | bytes 589856 | tf_op jit(solution)/shard_map/ppermute | solution.py:635
  223.8 3.6 %shard_map.290 = bf16[1,602112]{1,0:T(2,128)(2,1)} custom-call(s32[4]{0:T(128)S(1)} %pad_add_fusion.at_ref.x_ref, bf16[896,384]{1,0:T(8,128)(2,1)S(1)} %get-tuple-element.253.keep_ref, bf16[896,384]{1,0:T(8,128)(2,1)S(1)} %collective-permute-done.37.got_ref), custom_call_target="tpu_custom_call" | custom-call | flops 108000002048 | bytes 1024 | tf_op jit(solution)/shard_map/pallas_call | solution.py:196
  230.7 3.0 %collective-permute-start.46 = (bf16[1,96,768]{2,1,0:T(8,128)(2,1)S(1)}, bf16[1,96,768]{2,1,0:T(8,128)(2,1)S(1)}, u32[]{:S(2)}, u32[]{:S(2)}) collective-permute-start(bf16[1,96,768]{2,1,0:T(8,128)(2,1)S(1)} %fusion.9), channel_id=1, source_target_pairs={{0,4},{2,6},{4,0},{6,2},{1,5},{3,7},{5,1},{7,3},{8,12},{10,14},{12... | collective-permute-start | bytes 442376 | tf_op jit(solution)/shard_map/ppermute | solution.py:635
  233.6 3.5 %collective-permute-done.40.got_ref = bf16[896,384]{1,0:T(8,128)(2,1)S(1)} collective-permute-done((bf16[896,384]{1,0:T(8,128)(2,1)S(1)}, bf16[896,384]{1,0:T(8,128)(2,1)S(1)}, u32[]{:S(2)}, u32[]{:S(2)}) %collective-permute-start.40) | collective-permute-done | bytes 688160 | tf_op jit(solution)/shard_map/ppermute | solution.py:635
  237.1 6.8 %shard_map.291 = f32[18816,128]{1,0:T(8,128)} custom-call(s32[4]{0:T(128)S(1)} %pad_add_fusion.at_ref.x_ref, f32[896,384]{1,0:T(8,128)S(1)} %constant_dynamic-slice_fusion.keep_ref, bf16[896,384]{1,0:T(8,128)(2,1)S(1)} %collective-permute-done.40.got_ref, s32[16,112,1]{2,1,0:T(8,128)S(1)} %copy-done.22), custom_call_target="tpu_custom_call" | custom-call | flops 108000002048 | bytes 1024 | tf_op jit(solution)/shard_map/pallas_call | solution.py:169
  244.0 3.3 %collective-permute-start.53 = (bf16[112,384]{1,0:T(8,128)(2,1)S(1)}, bf16[112,384]{1,0:T(8,128)(2,1)S(1)}, u32[]{:S(2)}, u32[]{:S(2)}) collective-permute-start(bf16[112,384]{1,0:T(8,128)(2,1)S(1)} %get-tuple-element.312), channel_id=1, source_target_pairs={{0,6},{2,4},{4,2},{6,0},{1,7},{3,5},{5,3},{7,1},{8,14},{10,12},{12... | collective-permute-start | bytes 258056 | tf_op jit(solution)/shard_map/ppermute | solution.py:635
  257.7 3.3 %collective-permute-start.50 = (bf16[144,384]{1,0:T(8,128)(2,1)S(1)}, bf16[144,384]{1,0:T(8,128)(2,1)S(1)}, u32[]{:S(2)}, u32[]{:S(2)}) collective-permute-start(bf16[144,384]{1,0:T(8,128)(2,1)S(1)} %get-tuple-element.309), channel_id=1, source_target_pairs={{0,6},{2,4},{4,2},{6,0},{1,7},{3,5},{5,3},{7,1},{8,14},{10,12},{12... | collective-permute-start | bytes 331784 | tf_op jit(solution)/shard_map/ppermute | solution.py:635
  269.7 2.8 collective-permute-done.56
  (272 shorter events, 105.4 us)
Async XLA Ops:
  2.7 9.5 %collective-permute-start.3 = (bf16[1,96,384]{2,1,0:T(8,128)(2,1)S(1)}, bf16[1,96,384]{2,1,0:T(8,128)(2,1)S(1)}, u32[]{:S(2)}, u32[]{:S(2)}) collective-permute-start(bf16[1,96,384]{2,1,0:T(8,128)(2,1)S(1)} %bitcast.101), channel_id=1, source_target_pairs={{0,6},{2,4},{4,2},{6,0},{1,7},{3,5},{5,3},{7,1},{8,14},{10,12},{12... | collective-permute-start | bytes 221192 | tf_op jit(solution)/shard_map/ppermute | solution.py:635
  8.4 9.1 %collective-permute-start.4 = (bf16[1,96,768]{2,1,0:T(8,128)(2,1)S(1)}, bf16[1,96,768]{2,1,0:T(8,128)(2,1)S(1)}, u32[]{:S(2)}, u32[]{:S(2)}) collective-permute-start(bf16[1,96,768]{2,1,0:T(8,128)(2,1)S(1)} %bitcast.90), channel_id=1, source_target_pairs={{0,1},{1,0},{2,3},{3,2},{4,5},{5,4},{6,7},{7,6},{8,9},{9,8},{10,11... | collective-permute-start | bytes 442376 | tf_op jit(solution)/shard_map/ppermute | solution.py:635
  14.1 16.6 %collective-permute-start.7 = (bf16[4,96,384]{2,1,0:T(8,128)(2,1)S(1)}, bf16[4,96,384]{2,1,0:T(8,128)(2,1)S(1)}, u32[]{:S(2)}, u32[]{:S(2)}) collective-permute-start(bf16[4,96,384]{2,1,0:T(8,128)(2,1)S(1)} %pad_maximum_fusion.7), channel_id=1, source_target_pairs={{0,1},{1,0},{2,3},{3,2},{4,5},{5,4},{6,7},{7,6},{8,9},{9,8},{10,11... | collective-permute-start | bytes 884744 | tf_op jit(solution)/shard_map/ppermute | solution.py:635
  18.4 17.3 %collective-permute-start.6 = (bf16[2,208,384]{2,1,0:T(8,128)(2,1)S(1)}, bf16[2,208,384]{2,1,0:T(8,128)(2,1)S(1)}, u32[]{:S(2)}, u32[]{:S(2)}) collective-permute-start(bf16[2,208,384]{2,1,0:T(8,128)(2,1)S(1)} %pad_maximum_fusion.6), channel_id=1, source_target_pairs={{0,4},{2,6},{4,0},{6,2},{1,5},{3,7},{5,1},{7,3},{8,12},{10,14},{12... | collective-permute-start | bytes 958472 | tf_op jit(solution)/shard_map/ppermute | solution.py:635
  29.1 14.2 %collective-permute-start.5 = (bf16[896,384]{1,0:T(8,128)(2,1)S(1)}, bf16[896,384]{1,0:T(8,128)(2,1)S(1)}, u32[]{:S(2)}, u32[]{:S(2)}) collective-permute-start(bf16[896,384]{1,0:T(8,128)(2,1)S(1)} %get-tuple-element.308), channel_id=1, source_target_pairs={{0,1},{1,0},{2,3},{3,2},{4,5},{5,4},{6,7},{7,6},{8,9},{9,8},{10,11... | collective-permute-start | bytes 2064392 | tf_op jit(solution)/shard_map/ppermute | solution.py:635
  30.8 13.0 %collective-permute-start.9 = (bf16[8,96,384]{2,1,0:T(8,128)(2,1)S(1)}, bf16[8,96,384]{2,1,0:T(8,128)(2,1)S(1)}, u32[]{:S(2)}, u32[]{:S(2)}) collective-permute-start(bf16[8,96,384]{2,1,0:T(8,128)(2,1)S(1)} %get-tuple-element.316), channel_id=1, source_target_pairs={{0,16},{8,24},{16,0},{24,8},{1,17},{9,25},{17,1},{25,9},{2,18},{10... | collective-permute-start | bytes 1769480 | tf_op jit(solution)/shard_map/ppermute | solution.py:635
  35.7 16.3 %collective-permute-start.8 = (bf16[4,208,384]{2,1,0:T(8,128)(2,1)S(1)}, bf16[4,208,384]{2,1,0:T(8,128)(2,1)S(1)}, u32[]{:S(2)}, u32[]{:S(2)}) collective-permute-start(bf16[4,208,384]{2,1,0:T(8,128)(2,1)S(1)} %pad_maximum_fusion.2), channel_id=1, source_target_pairs={{0,2},{2,0},{4,6},{6,4},{1,3},{3,1},{5,7},{7,5},{8,10},{10,8},{12,... | collective-permute-start | bytes 1916936 | tf_op jit(solution)/shard_map/ppermute | solution.py:635
  53.0 19.3 %collective-permute-start.18 = (bf16[896,384]{1,0:T(8,128)(2,1)S(1)}, bf16[896,384]{1,0:T(8,128)(2,1)S(1)}, u32[]{:S(2)}, u32[]{:S(2)}) collective-permute-start(bf16[896,384]{1,0:T(8,128)(2,1)S(1)} %get-tuple-element.163), channel_id=1, source_target_pairs={{0,1},{1,0},{2,3},{3,2},{4,5},{5,4},{6,7},{7,6},{8,9},{9,8},{10,11... | collective-permute-start | bytes 2064392 | tf_op jit(solution)/shard_map/ppermute | solution.py:635
  55.7 8.8 %collective-permute-start.14 = (bf16[16,96,384]{2,1,0:T(8,128)(2,1)S(1)}, bf16[16,96,384]{2,1,0:T(8,128)(2,1)S(1)}, u32[]{:S(2)}, u32[]{:S(2)}) collective-permute-start(bf16[16,96,384]{2,1,0:T(8,128)(2,1)S(1)} %constant_dynamic-update-slice_fusion.5.refs_2_), channel_id=1, source_target_pairs={{0,8},{8,0},{16,24},{24,16},{1,9},{9,1},{17,25},{25,17},{2,10},{10... | collective-permute-start | bytes 3538952 | tf_op jit(solution)/shard_map/ppermute | solution.py:635
  55.7 10.0 %collective-permute-start.13 = (bf16[8,208,384]{2,1,0:T(8,128)(2,1)S(1)}, bf16[8,208,384]{2,1,0:T(8,128)(2,1)S(1)}, u32[]{:S(2)}, u32[]{:S(2)}) collective-permute-start(bf16[8,208,384]{2,1,0:T(8,128)(2,1)S(1)} %pad_maximum_fusion.refs_0_), channel_id=1, source_target_pairs={{0,8},{8,0},{16,24},{24,16},{1,9},{9,1},{17,25},{25,17},{2,10},{10... | collective-permute-start | bytes 3833864 | tf_op jit(solution)/shard_map/ppermute | solution.py:635
  62.2 13.4 %collective-permute-start.17 = (bf16[2,96,768]{2,1,0:T(8,128)(2,1)S(1)}, bf16[2,96,768]{2,1,0:T(8,128)(2,1)S(1)}, u32[]{:S(2)}, u32[]{:S(2)}) collective-permute-start(bf16[2,96,768]{2,1,0:T(8,128)(2,1)S(1)} %copy-done.32), channel_id=1, source_target_pairs={{0,4},{2,6},{4,0},{6,2},{1,5},{3,7},{5,1},{7,3},{8,12},{10,14},{12... | collective-permute-start | bytes 884744 | tf_op jit(solution)/shard_map/ppermute | solution.py:635
  62.8 13.0 %collective-permute-start.16 = (bf16[4,48,768]{2,1,0:T(8,128)(2,1)S(1)}, bf16[4,48,768]{2,1,0:T(8,128)(2,1)S(1)}, u32[]{:S(2)}, u32[]{:S(2)}) collective-permute-start(bf16[4,48,768]{2,1,0:T(8,128)(2,1)S(1)} %pad_maximum_fusion.10), channel_id=1, source_target_pairs={{0,1},{1,0},{2,3},{3,2},{4,5},{5,4},{6,7},{7,6},{8,9},{9,8},{10,11... | collective-permute-start | bytes 884744 | tf_op jit(solution)/shard_map/ppermute | solution.py:635
  64.5 13.9 %collective-permute-start.15 = (bf16[2,96,768]{2,1,0:T(8,128)(2,1)S(1)}, bf16[2,96,768]{2,1,0:T(8,128)(2,1)S(1)}, u32[]{:S(2)}, u32[]{:S(2)}) collective-permute-start(bf16[2,96,768]{2,1,0:T(8,128)(2,1)S(1)} %pad_maximum_fusion.9), channel_id=1, source_target_pairs={{0,2},{2,0},{4,6},{6,4},{1,3},{3,1},{5,7},{7,5},{8,10},{10,8},{12,... | collective-permute-start | bytes 884744 | tf_op jit(solution)/shard_map/ppermute | solution.py:635
  79.6 16.2 %collective-permute-start.20 = (bf16[4,96,768]{2,1,0:T(8,128)(2,1)S(1)}, bf16[4,96,768]{2,1,0:T(8,128)(2,1)S(1)}, u32[]{:S(2)}, u32[]{:S(2)}) collective-permute-start(bf16[4,96,768]{2,1,0:T(8,128)(2,1)S(1)} %get-tuple-element.189.refs_0_), channel_id=1, source_target_pairs={{0,1},{1,0},{2,3},{3,2},{4,5},{5,4},{6,7},{7,6},{8,9},{9,8},{10,11... | collective-permute-start | bytes 1769480 | tf_op jit(solution)/shard_map/ppermute | solution.py:635
  80.0 13.1 %collective-permute-start.19 = (bf16[4,96,768]{2,1,0:T(8,128)(2,1)S(1)}, bf16[4,96,768]{2,1,0:T(8,128)(2,1)S(1)}, u32[]{:S(2)}, u32[]{:S(2)}) collective-permute-start(bf16[4,96,768]{2,1,0:T(8,128)(2,1)S(1)} %get-tuple-element.330), channel_id=1, source_target_pairs={{0,2},{2,0},{4,6},{6,4},{1,3},{3,1},{5,7},{7,5},{8,10},{10,8},{12,... | collective-permute-start | bytes 1769480 | tf_op jit(solution)/shard_map/ppermute | solution.py:635
  80.2 15.6 %collective-permute-start.21 = (bf16[8,48,768]{2,1,0:T(8,128)(2,1)S(1)}, bf16[8,48,768]{2,1,0:T(8,128)(2,1)S(1)}, u32[]{:S(2)}, u32[]{:S(2)}) collective-permute-start(bf16[8,48,768]{2,1,0:T(8,128)(2,1)S(1)} %pad_maximum_fusion.4.refs_4_), channel_id=1, source_target_pairs={{0,16},{8,24},{16,0},{24,8},{1,17},{9,25},{17,1},{25,9},{2,18},{10... | collective-permute-start | bytes 1769480 | tf_op jit(solution)/shard_map/ppermute | solution.py:635
  93.3 27.8 %collective-permute-start.26 = (bf16[8,96,768]{2,1,0:T(8,128)(2,1)S(1)}, bf16[8,96,768]{2,1,0:T(8,128)(2,1)S(1)}, u32[]{:S(2)}, u32[]{:S(2)}) collective-permute-start(bf16[8,96,768]{2,1,0:T(8,128)(2,1)S(1)} %pad_maximum_fusion.1.refs_0_), channel_id=1, source_target_pairs={{0,16},{8,24},{16,0},{24,8},{1,17},{9,25},{17,1},{25,9},{2,18},{10... | collective-permute-start | bytes 3538952 | tf_op jit(solution)/shard_map/ppermute | solution.py:635
  130.3 29.2 %collective-permute-start.31 = (bf16[4,192,768]{2,1,0:T(8,128)(2,1)}, bf16[4,192,768]{2,1,0:T(8,128)(2,1)}, u32[]{:S(2)}, u32[]{:S(2)}) collective-permute-start(bf16[4,192,768]{2,1,0:T(8,128)(2,1)} %add_convert_fusion.1), channel_id=1, source_target_pairs={{0,1},{1,0},{2,3},{3,2},{4,5},{5,4},{6,7},{7,6},{8,9},{9,8},{10,11... | collective-permute-start | bytes 3538952 | tf_op jit(solution)/shard_map/ppermute | solution.py:635
  161.2 23.6 %collective-permute-start.34 = (bf16[2,192,768]{2,1,0:T(8,128)(2,1)S(1)}, bf16[2,192,768]{2,1,0:T(8,128)(2,1)S(1)}, u32[]{:S(2)}, u32[]{:S(2)}) collective-permute-start(bf16[2,192,768]{2,1,0:T(8,128)(2,1)S(1)} %get-tuple-element.294), channel_id=1, source_target_pairs={{0,2},{2,0},{4,6},{6,4},{1,3},{3,1},{5,7},{7,5},{8,10},{10,8},{12,... | collective-permute-start | bytes 1769480 | tf_op jit(solution)/shard_map/ppermute | solution.py:635
  163.7 42.0 %collective-permute-start.36 = (bf16[8,96,768]{2,1,0:T(8,128)(2,1)S(1)}, bf16[8,96,768]{2,1,0:T(8,128)(2,1)S(1)}, u32[]{:S(2)}, u32[]{:S(2)}) collective-permute-start(bf16[8,96,768]{2,1,0:T(8,128)(2,1)S(1)} %add_convert_fusion), channel_id=1, source_target_pairs={{0,16},{8,24},{16,0},{24,8},{1,17},{9,25},{17,1},{25,9},{2,18},{10... | collective-permute-start | bytes 3538952 | tf_op jit(solution)/shard_map/ppermute | solution.py:635
  184.2 20.7 %collective-permute-start.37 = (bf16[896,384]{1,0:T(8,128)(2,1)S(1)}, bf16[896,384]{1,0:T(8,128)(2,1)S(1)}, u32[]{:S(2)}, u32[]{:S(2)}) collective-permute-start(bf16[896,384]{1,0:T(8,128)(2,1)S(1)} %get-tuple-element.229), channel_id=1, source_target_pairs={{0,1},{1,0},{2,3},{3,2},{4,5},{5,4},{6,7},{7,6},{8,9},{9,8},{10,11... | collective-permute-start | bytes 2064392 | tf_op jit(solution)/shard_map/ppermute | solution.py:635
  184.9 20.0 %collective-permute-start.35 = (bf16[1,192,768]{2,1,0:T(8,128)(2,1)S(1)}, bf16[1,192,768]{2,1,0:T(8,128)(2,1)S(1)}, u32[]{:S(2)}, u32[]{:S(2)}) collective-permute-start(bf16[1,192,768]{2,1,0:T(8,128)(2,1)S(1)} %fusion.7), channel_id=1, source_target_pairs={{0,4},{2,6},{4,0},{6,2},{1,5},{3,7},{5,1},{7,3},{8,12},{10,14},{12... | collective-permute-start | bytes 884744 | tf_op jit(solution)/shard_map/ppermute | solution.py:635
  206.1 16.3 %collective-permute-start.39 = (bf16[4,96,768]{2,1,0:T(8,128)(2,1)S(1)}, bf16[4,96,768]{2,1,0:T(8,128)(2,1)S(1)}, u32[]{:S(2)}, u32[]{:S(2)}) collective-permute-start(bf16[4,96,768]{2,1,0:T(8,128)(2,1)S(1)} %get-tuple-element.292), channel_id=1, source_target_pairs={{0,1},{1,0},{2,3},{3,2},{4,5},{5,4},{6,7},{7,6},{8,9},{9,8},{10,11... | collective-permute-start | bytes 1769480 | tf_op jit(solution)/shard_map/ppermute | solution.py:635
  213.2 15.2 %collective-permute-start.43 = (bf16[8,112,384]{2,1,0:T(8,128)(2,1)S(1)}, bf16[8,112,384]{2,1,0:T(8,128)(2,1)S(1)}, u32[]{:S(2)}, u32[]{:S(2)}) collective-permute-start(bf16[8,112,384]{2,1,0:T(8,128)(2,1)S(1)} %get-tuple-element.249), channel_id=1, source_target_pairs={{0,8},{8,0},{16,24},{24,16},{1,9},{9,1},{17,25},{25,17},{2,10},{10... | collective-permute-start | bytes 2064392 | tf_op jit(solution)/shard_map/ppermute | solution.py:635
  213.5 13.9 %collective-permute-start.61 = (f32[192,768]{1,0:T(8,128)S(1)}, f32[192,768]{1,0:T(8,128)S(1)}, u32[]{:S(2)}, u32[]{:S(2)}) collective-permute-start(f32[192,768]{1,0:T(8,128)S(1)} %convert_add_fusion.4), channel_id=1, source_target_pairs={{0,8},{8,0},{16,24},{24,16},{1,9},{9,1},{17,25},{25,17},{2,10},{10... | collective-permute-start | bytes 1769480 | tf_op jit(solution)/shard_map/ppermute | solution.py:635
  213.9 23.2 %collective-permute-start.40 = (bf16[896,384]{1,0:T(8,128)(2,1)S(1)}, bf16[896,384]{1,0:T(8,128)(2,1)S(1)}, u32[]{:S(2)}, u32[]{:S(2)}) collective-permute-start(bf16[896,384]{1,0:T(8,128)(2,1)S(1)} %constant_dynamic-slice_fusion.1), channel_id=1, source_target_pairs={{0,1},{1,0},{2,3},{3,2},{4,5},{5,4},{6,7},{7,6},{8,9},{9,8},{10,11... | collective-permute-start | bytes 2064392 | tf_op jit(solution)/shard_map/ppermute | solution.py:635
  217.9 11.8 %collective-permute-start.42 = (bf16[16,144,384]{2,1,0:T(8,128)(2,1)S(1)}, bf16[16,144,384]{2,1,0:T(8,128)(2,1)S(1)}, u32[]{:S(2)}, u32[]{:S(2)}) collective-permute-start(bf16[16,144,384]{2,1,0:T(8,128)(2,1)S(1)} %get-tuple-element.240), channel_id=1, source_target_pairs={{0,8},{8,0},{16,24},{24,16},{1,9},{9,1},{17,25},{25,17},{2,10},{10... | collective-permute-start | bytes 5308424 | tf_op jit(solution)/shard_map/ppermute | solution.py:635
  228.6 15.3 %collective-permute-start.47 = (bf16[4,112,384]{2,1,0:T(8,128)(2,1)S(1)}, bf16[4,112,384]{2,1,0:T(8,128)(2,1)S(1)}, u32[]{:S(2)}, u32[]{:S(2)}) collective-permute-start(bf16[4,112,384]{2,1,0:T(8,128)(2,1)S(1)} %get-tuple-element.302), channel_id=1, source_target_pairs={{0,1},{1,0},{2,3},{3,2},{4,5},{5,4},{6,7},{7,6},{8,9},{9,8},{10,11... | collective-permute-start | bytes 1032200 | tf_op jit(solution)/shard_map/ppermute | solution.py:635
  230.1 18.4 %collective-permute-start.44 = (bf16[8,144,384]{2,1,0:T(8,128)(2,1)S(1)}, bf16[8,144,384]{2,1,0:T(8,128)(2,1)S(1)}, u32[]{:S(2)}, u32[]{:S(2)}) collective-permute-start(bf16[8,144,384]{2,1,0:T(8,128)(2,1)S(1)} %get-tuple-element.290), channel_id=1, source_target_pairs={{0,16},{8,24},{16,0},{24,8},{1,17},{9,25},{17,1},{25,9},{2,18},{10... | collective-permute-start | bytes 2654216 | tf_op jit(solution)/shard_map/ppermute | solution.py:635
  230.7 18.9 %collective-permute-start.46 = (bf16[1,96,768]{2,1,0:T(8,128)(2,1)S(1)}, bf16[1,96,768]{2,1,0:T(8,128)(2,1)S(1)}, u32[]{:S(2)}, u32[]{:S(2)}) collective-permute-start(bf16[1,96,768]{2,1,0:T(8,128)(2,1)S(1)} %fusion.9), channel_id=1, source_target_pairs={{0,4},{2,6},{4,0},{6,2},{1,5},{3,7},{5,1},{7,3},{8,12},{10,14},{12... | collective-permute-start | bytes 442376 | tf_op jit(solution)/shard_map/ppermute | solution.py:635
  254.2 8.6 %collective-permute-start.59 = (bf16[96,768]{1,0:T(8,128)(2,1)S(1)}, bf16[96,768]{1,0:T(8,128)(2,1)S(1)}, u32[]{:S(2)}, u32[]{:S(2)}) collective-permute-start(bf16[96,768]{1,0:T(8,128)(2,1)S(1)} %get-tuple-element.281), channel_id=1, source_target_pairs={{0,16},{8,24},{16,0},{24,8},{1,17},{9,25},{17,1},{25,9},{2,18},{10... | collective-permute-start | bytes 442376 | tf_op jit(solution)/shard_map/ppermute | solution.py:635
  264.2 11.3 %collective-permute-start.60 = (f32[2,96,768]{2,1,0:T(8,128)S(1)}, f32[2,96,768]{2,1,0:T(8,128)S(1)}, u32[]{:S(2)}, u32[]{:S(2)}) collective-permute-start(f32[2,96,768]{2,1,0:T(8,128)S(1)} %maximum_select_fusion.6), channel_id=1, source_target_pairs={{0,8},{8,0},{16,24},{24,16},{1,9},{9,1},{17,25},{25,17},{2,10},{10... | collective-permute-start | bytes 1769480 | tf_op jit(solution)/shard_map/ppermute | solution.py:635
  (68 other events, 533.1 us)

commit v6 on v5

--- a/solution.py
+++ b/solution.py
@@ -326,7 +326,7 @@
 
 def mix(mixed, w, rows, vec):
     r = rows.shape[0]
-    m = row_tile(r)
+    m = r // 4 if r % 64 == 0 else row_tile(r)
     row = spec((m, D), lambda i: (i, 0))
     return call(
         mix_body,
@@ -340,10 +340,17 @@
 
 
 def up_body(hidden_ref, w_ref, bias_ref, active_ref, slope_ref):
-    inner = dot(hidden_ref[...], w_ref[...], 1, 0) + bias_ref[...]
-    phi = 0.5 * (1.0 + lax.erf(inner * (0.5**0.5)))
-    active_ref[...] = (inner * phi).astype(BF)
-    slope_ref[...] = phi + inner * (jnp.exp(-0.5 * inner * inner) * 0.3989422804014327)
+    half = hidden_ref.shape[0] // 2
+
+    def step(i, carry):
+        rows = pl.ds(pl.multiple_of(i * half, 16), half)
+        inner = dot(hidden_ref[rows, :], w_ref[...], 1, 0) + bias_ref[...]
+        phi = 0.5 * (1.0 + lax.erf(inner * (0.5**0.5)))
+        active_ref[rows, :] = (inner * phi).astype(BF)
+        slope_ref[rows, :] = phi + inner * (jnp.exp(-0.5 * inner * inner) * 0.3989422804014327)
+        return carry
+
+    lax.fori_loop(0, 2, step, 0)
 
 
 def up(hidden, w, bias):
@@ -389,14 +396,12 @@
     )(active, w, vec, middle)
 
 
-def outer_body(left_ref, right_ref, out_ref, sum_ref, turned):
+def outer_body(left_ref, right_ref, out_ref, turned):
     @pl.when(pl.program_id(0) == 0)
     def _():
         turned[...] = left_ref[...].T
 
-    right = right_ref[...]
-    out_ref[...] = dot(turned[...], right, 1, 0).astype(BF)
-    sum_ref[...] = jnp.sum(right.astype(F32), 0, keepdims=True)
+    out_ref[...] = dot(turned[...], right_ref[...], 1, 0).astype(BF)
 
 
 def outer(left, right):
@@ -406,8 +411,8 @@
         outer_body,
         (width // TILE,),
         [spec((r, rows), lambda j: (0, 0)), spec((r, TILE), lambda j: (0, j))],
-        [spec((rows, TILE), lambda j: (0, j)), spec((1, TILE), lambda j: (0, j))],
-        [struct((rows, width), BF), struct((1, width), F32)],
+        spec((rows, TILE), lambda j: (0, j)),
+        struct((rows, width), BF),
         [pltpu.VMEM((rows, r), BF)],
         us=0.01,
         nbytes=r * rows * 2 + r * width * 2 + rows * width * 2,
@@ -606,7 +611,7 @@
 
 def first_back(grad, w, rows, grad_middle, vecs):
     r, width = grad.shape
-    m = row_tile(r)
+    m = r // 4 if r % 64 == 0 else row_tile(r)
     vec = spec((1, D), lambda i: (0, 0))
     row = spec((m, D), lambda i: (i, 0))
     vec_out = struct((1, D), F32)
@@ -875,6 +880,97 @@
     )(*rows)
 
 
+def build_body(plans, counts, inverse, parts_by, at_ref, tag_ref, *refs):
+    refs, sem = refs[:-1], refs[-1]
+    lists = len(counts)
+    wholes, arrays = (refs[:-lists], refs[-lists:]) if inverse else (refs[lists:], refs[:lists])
+
+    def each(act):
+        first, slot = 0, 0
+        for array, plan, count, by in zip(arrays, plans, counts, parts_by):
+            moves = len(plan(0, 0, 0))
+
+            def step(k, carry, array=array, plan=plan, by=by, first=first, slot=slot, moves=moves):
+                w, n, q = (
+                    at_ref[axis] ^ tag_ref[i, first + k] for i, axis in enumerate((0, 1, by))
+                )
+                for m, (which, (at_row, at_lane), (rows, lanes), (row, lane)) in enumerate(
+                    plan(w, n, q)
+                ):
+                    piece = array.at[k, pl.ds(at_row, rows), pl.ds(at_lane, lanes)]
+                    whole = wholes[which].at[
+                        pl.ds(pl.multiple_of(row, 16), rows),
+                        pl.ds(pl.multiple_of(lane, 128), lanes),
+                    ]
+                    ends = (whole, piece) if inverse else (piece, whole)
+                    act(pltpu.make_async_copy(*ends, sem.at[slot + k * moves + m]))
+                return carry
+
+            lax.fori_loop(0, count, step, 0)
+            first, slot = first + count, slot + count * moves
+
+    each(lambda copy: copy.start())
+    each(lambda copy: copy.wait())
+
+
+def move_pieces(at, arrays, plans, tag_lists, inverse, parts_by, shapes):
+    counts = [len(tags) for tags in tag_lists]
+    moves = sum(count * len(plan(0, 0, 0)) for count, plan in zip(counts, plans))
+    table = jnp.array([tag for tags in tag_lists for tag in tags], jnp.int32).T
+    return pl.pallas_call(
+        partial(build_body, plans, counts, inverse, parts_by),
+        out_shape=[struct(shape, BF) for shape in shapes],
+        grid_spec=pltpu.PrefetchScalarGridSpec(
+            num_scalar_prefetch=2,
+            grid=(1,),
+            in_specs=[ANY] * len(arrays),
+            out_specs=[ANY] * len(shapes),
+            scratch_shapes=[pltpu.SemaphoreType.DMA((moves,))],
+        ),
+        compiler_params=pltpu.CompilerParams(vmem_limit_bytes=4 * MB),
+        cost_estimate=pl.CostEstimate(
+            flops=FLOPS_PER_US // 100, bytes_accessed=1024, transcendentals=0
+        ),
+    )(at, table, *arrays)
+
+
+CORE, DP_INDEX = 2, 3
+
+
+def owner_sums_body(wide, narrow, cols, *refs):
+    out = refs[-1]
+    narrow_refs, qkv_ref, up_ref = refs[:6], refs[6], refs[7]
+    part, units = D // wide, up_ref.shape[1] // wide
+    for w in range(wide):
+        for n in range(narrow):
+            lines = [ref[:, n * cols : (n + 1) * cols] for ref in narrow_refs]
+            lines.append(
+                jnp.concatenate(
+                    [qkv_ref[:, p * D + w * part : p * D + (w + 1) * part] for p in (0, 2)], axis=1
+                )
+            )
+            lines += [
+                up_ref[:, w * units + k : w * units + k + cols] for k in range(0, units, cols)
+            ]
+            lines.append(jnp.zeros((16 - len(lines), cols), F32))
+            at = (w * narrow + n) * 16
+            out[at : at + 16, :] = jnp.concatenate(lines, axis=0).astype(BF)
+
+
+def owner_sums(wide, narrow, cols, *rows):
+    vmem = pl.BlockSpec(memory_space=pltpu.VMEM)
+    return pl.pallas_call(
+        partial(owner_sums_body, wide, narrow, cols),
+        out_shape=struct((wide * narrow * 16, cols), BF),
+        in_specs=[vmem] * len(rows),
+        out_specs=vmem,
+        compiler_params=pltpu.CompilerParams(vmem_limit_bytes=8 * MB),
+        cost_estimate=pl.CostEstimate(
+            flops=FLOPS_PER_US // 100, bytes_accessed=1024, transcendentals=0
+        ),
+    )(*rows)
+
+
 def build_body(plans, tag_lists, inverse, parts_by, at_ref, *refs):
     refs, sem = refs[:-1], refs[-1]
     count = len(tag_lists)
@@ -1192,7 +1288,7 @@
 
         x_first = [(w, n, 0) for n in range(2) for w in (0, 2, 1, 3)]
         y_first = [(w, n, dy) for dy in (0, 2) for n in range(2) for w in (0, 2, 1, 3)]
-        gw_down, _ = outer(cot, in_hbm(active))
+        gw_down = outer(cot, in_hbm(active))
         gb_down = jnp.sum(cot, 0, dtype=F32)[None]
         d_y = d_y.after(gw_down)
         d_c = [p.fetch(DP, 1, d_y.stack) for p in (d_p, d_y)]
@@ -1362,7 +1458,7 @@
         middle, hidden_two = mix(mixed, out_w, rows, vecs)
         active, slope = up(hidden_two, up_w, bias_up)
         result = down(active, down_w, vecs, middle)
-        gw_down, _ = outer(cot, active)
+        gw_down = outer(cot, active)
         gb_down = jnp.sum(cot, 0, dtype=F32)[None]
         grad_inner, gw_up, gb_up = inner_back(cot, down_w, slope, hidden_two)
         grad_middle, branch, gg_two, gs_two, gb_out = middle_back(

time: 282 us -> 268 us (0.950); the launches traced: 277 us -> 268 us
  Pallas kernels: 128 us -> 119 us
    pallas_call x1, Pallas kernels: 16.3 us -> 6.23 us  [middle_back(): call(middle_back_body, (r // m,), [spec((m, units), lambda i: (i, 0)), sp...]
  transfers between devices with their start and end apart: 62 -> 62, of which waited for: 24 -> 25; matrix products, arithmetic and copies ran while one was open for 7% -> 8% of each run, Pallas kernels for 45% -> 43%
where the time goes in v6:
time: 268 us
  Pallas kernels  119 us (44%)
  waiting for transfers between devices  57.2 us (21%)
  starting transfers between devices  56.8 us (21%)
  local copies, waits for them, and re-layouts  16.9 us (6%)
  other arithmetic  16.1 us (6%)
    ppermute x62, waiting for transfers between devices, swap(): return lax.ppermute(value, axis, [(i, i ^ bit) for i in range(size)])  57.2 us
    ppermute x62, starting transfers between devices, swap(): return lax.ppermute(value, axis, [(i, i ^ bit) for i in range(size)])  56.8 us
    pallas_call x8, Pallas kernels, move_pieces(): pl.pallas_call(partial(build_body, plans, tag_lists, inverse, parts_by),...  14.9 us
    pallas_call x1, Pallas kernels, inner_back(): call(inner_back_body, (units // TILE,), [full, col, tile, full], [tile, c...  12.8 us
    pallas_call x1, Pallas kernels, attend_back(): pl.pallas_call(attend_back_body, out_shape=struct(triple.shape, BF), grid...  11.9 us
    unnamed x81, local copies, waits for them, and re-layouts  11.6 us
    pallas_call x1, Pallas kernels, up(): call(up_body, (units // TILE,), [spec((r, D), lambda j: (0, 0)), spec((D,...  10.8 us
    pallas_call x1, Pallas kernels, outer(): call(outer_body, (width // TILE,), [spec((r, rows), lambda j: (0, 0)), sp...  7.61 us
  transfers between devices with their start and end apart: 62, of which 25 were waited for; matrix products, arithmetic and copies ran while one was open for 8% of the time, Pallas kernels for 43%

profile of v6, /device:TPU:0, one launch (start us, length us, event | category | flops | bytes accessed | tf_op | source)
XLA Modules:
  0.0 267.8 jit_solution(6856711471343649406)
XLA Ops:
  2.7 5.1 %collective-permute-start.3 = (bf16[1,96,384]{2,1,0:T(8,128)(2,1)S(1)}, bf16[1,96,384]{2,1,0:T(8,128)(2,1)S(1)}, u32[]{:S(2)}, u32[]{:S(2)}) collective-permute-start(bf16[1,96,384]{2,1,0:T(8,128)(2,1)S(1)} %bitcast.101), channel_id=1, source_target_pairs={{0,6},{2,4},{4,2},{6,0},{1,7},{3,5},{5,3},{7,1},{8,14},{10,12},{12... | collective-permute-start | bytes 221192 | tf_op jit(solution)/shard_map/ppermute | solution.py:640
  18.4 2.7 collective-permute-start.6
  21.0 3.7 %copy-done.23 = bf16[1,2408448]{1,0:T(2,128)(2,1)S(1)} copy-done((bf16[1,2408448]{1,0:T(2,128)(2,1)S(1)}, bf16[1,2408448]{1,0:T(2,128)(2,1)}, u32[]{:S(2)}) %copy-start.23) | copy-done | bytes 4816920
  24.8 4.1 %shard_map.265 = bf16[1792,384]{1,0:T(8,128)(2,1)S(1)} custom-call(s32[4]{0:T(128)S(1)} %pad_add_fusion.at_ref.x_ref, bf16[1,2408448]{1,0:T(2,128)(2,1)S(1)} %copy-done.23, s32[16,112,1]{2,1,0:T(8,128)S(1)} %copy.31.index_ref), custom_call_target="tpu_custom_call" | custom-call | flops 108000002048 | bytes 1024 | tf_op jit(solution)/shard_map/pallas_call | solution.py:98
  32.3 3.3 %collective-permute-done.6 = bf16[2,208,384]{2,1,0:T(8,128)(2,1)S(1)} collective-permute-done((bf16[2,208,384]{2,1,0:T(8,128)(2,1)S(1)}, bf16[2,208,384]{2,1,0:T(8,128)(2,1)S(1)}, u32[]{:S(2)}, u32[]{:S(2)}) %collective-permute-start.6) | collective-permute-done | bytes 319520 | tf_op jit(solution)/shard_map/ppermute | solution.py:640
  35.8 2.8 %shard_map.266 = bf16[1792,384]{1,0:T(8,128)(2,1)S(1)} custom-call(s32[4]{0:T(128)S(1)} %pad_add_fusion.at_ref.x_ref, bf16[1,602112]{1,0:T(2,128)(2,1)S(1)} %copy-done.24), custom_call_target="tpu_custom_call" | custom-call | flops 108000002048 | bytes 1024 | tf_op jit(solution)/shard_map/pallas_call | solution.py:129
  38.8 4.5 %collective-permute-done.5 = bf16[896,384]{1,0:T(8,128)(2,1)S(1)} collective-permute-done((bf16[896,384]{1,0:T(8,128)(2,1)S(1)}, bf16[896,384]{1,0:T(8,128)(2,1)S(1)}, u32[]{:S(2)}, u32[]{:S(2)}) %collective-permute-start.5) | collective-permute-done | bytes 688160 | tf_op jit(solution)/shard_map/ppermute | solution.py:640
  43.9 8.1 %collective-permute-done.8 = bf16[4,208,384]{2,1,0:T(8,128)(2,1)S(1)} collective-permute-done((bf16[4,208,384]{2,1,0:T(8,128)(2,1)S(1)}, bf16[4,208,384]{2,1,0:T(8,128)(2,1)S(1)}, u32[]{:S(2)}, u32[]{:S(2)}) %collective-permute-start.8) | collective-permute-done | bytes 639008 | tf_op jit(solution)/shard_map/ppermute | solution.py:640
  68.2 4.1 %shard_map.270.triple_ref = bf16[896,2304]{1,0:T(8,128)(2,1)S(1)} custom-call(bf16[896,768]{1,0:T(8,128)(2,1)S(1)} %shard_map.268.hidden_ref, bf16[2304,768]{1,0:T(8,128)(2,1)S(1)} %shard_map.269.w_ref, f32[1,2304]{1,0:T(1,128)S(1)} %get-tuple-element.175.bias_ref), custom_call_target="tpu_custom_call" | custom-call | flops 7020000256 | bytes 1024 | tf_op jit(solution)/shard_map/pallas_call | solution.py:247
  72.4 3.2 %collective-permute-done.17 = bf16[2,96,768]{2,1,0:T(8,128)(2,1)S(1)} collective-permute-done((bf16[2,96,768]{2,1,0:T(8,128)(2,1)S(1)}, bf16[2,96,768]{2,1,0:T(8,128)(2,1)S(1)}, u32[]{:S(2)}, u32[]{:S(2)}) %collective-permute-start.17) | collective-permute-done | bytes 294944 | tf_op jit(solution)/shard_map/ppermute | solution.py:640
  75.9 2.5 collective-permute-done.15
  81.7 6.0 %shard_map.271 = (bf16[896,768]{1,0:T(8,128)(2,1)S(1)}, f32[8,12,112,112]{3,2,1,0:T(8,128)}) custom-call(bf16[896,2304]{1,0:T(8,128)(2,1)S(1)} %shard_map.270.triple_ref), custom_call_target="tpu_custom_call" | custom-call | flops 108000002048 | bytes 1024 | tf_op jit(solution)/shard_map/pallas_call | solution.py:302
  87.7 5.4 %collective-permute-done.19 = bf16[4,96,768]{2,1,0:T(8,128)(2,1)S(1)} collective-permute-done((bf16[4,96,768]{2,1,0:T(8,128)(2,1)S(1)}, bf16[4,96,768]{2,1,0:T(8,128)(2,1)S(1)}, u32[]{:S(2)}, u32[]{:S(2)}) %collective-permute-start.19) | collective-permute-done | bytes 589856 | tf_op jit(solution)/shard_map/ppermute | solution.py:640
  96.9 2.8 %shard_map.273 = (f32[896,768]{1,0:T(8,128)S(1)}, bf16[896,768]{1,0:T(8,128)(2,1)S(1)}) custom-call(bf16[896,768]{1,0:T(8,128)(2,1)S(1)} %get-tuple-element.186.mixed_ref, bf16[768,768]{1,0:T(8,128)(2,1)S(1)} %shard_map.272.w_ref, bf16[896,768]{1,0:T(8,128)(2,1)S(1)} %maximum_select_fusion.rows_ref, f32[8,768]{1,0:T(8,128)S(1)} %get-tuple-element.261.vec_ref.x_ref), custom_call_target="tpu_custom_call" | custom-call | flops 8640000000 | bytes 1024 | tf_op jit(solution)/shard_map/pallas_call | solution.py:331
  102.4 10.8 %shard_map.275 = (bf16[896,3072]{1,0:T(8,128)(2,1)}, f32[896,3072]{1,0:T(8,128)}) custom-call(bf16[896,768]{1,0:T(8,128)(2,1)S(1)} %get-tuple-element.187.hidden_ref, bf16[768,3072]{1,0:T(8,128)(2,1)S(1)} %shard_map.274.w_ref, f32[1,3072]{1,0:T(1,128)S(1)} %get-tuple-element.196.bias_ref), custom_call_target="tpu_custom_call" | custom-call | flops 5400000 | bytes 1024 | tf_op jit(solution)/shard_map/pallas_call | solution.py:360
  113.3 7.6 %shard_map.276.refs_0_ = bf16[768,3072]{1,0:T(8,128)(2,1)S(1)} custom-call(bf16[896,768]{1,0:T(8,128)(2,1)S(1)} %get-tuple-element.284.left_ref.cot_ref, bf16[896,3072]{1,0:T(8,128)(2,1)} %get-tuple-element.211.right_ref.active_ref), custom_call_target="tpu_custom_call" | custom-call | flops 5400000 | bytes 1024 | tf_op jit(solution)/shard_map/pallas_call | solution.py:410
  131.5 12.8 %shard_map.279 = (bf16[896,3072]{1,0:T(8,128)(2,1)}, bf16[768,3072]{1,0:T(8,128)(2,1)S(1)}, f32[1,3072]{1,0:T(1,128)S(1)}) custom-call(bf16[896,768]{1,0:T(8,128)(2,1)S(1)} %get-tuple-element.284.left_ref.cot_ref, bf16[768,3072]{1,0:T(8,128)(2,1)S(1)} %shard_map.278.w_ref, f32[896,3072]{1,0:T(8,128)} %get-tuple-element.209.slope_ref, ...), custom_call_target="tpu_custom_call" | custom-call | flops 108000002048 | bytes 1024 | tf_op jit(solution)/shard_map/pallas_call | solution.py:438
  144.3 6.5 %shard_map.280 = bf16[896,768]{1,0:T(8,128)(2,1)S(1)} custom-call(bf16[896,3072]{1,0:T(8,128)(2,1)} %get-tuple-element.211.right_ref.active_ref, bf16[768,3072]{1,0:T(8,128)(2,1)S(1)} %shard_map.278.w_ref, f32[8,768]{1,0:T(8,128)S(1)} %get-tuple-element.261.vec_ref.x_ref, f32[896,768]{1,0:T(8,128)S(1)} %get-tuple-element.212.middle_ref), custom_call_target="tpu_custom_call" | custom-call | flops 5400000 | bytes 1024 | tf_op jit(solution)/shard_map/pallas_call | solution.py:383
  150.8 2.6 shard_map.281
  165.2 6.2 %shard_map.282 = (f32[896,768]{1,0:T(8,128)S(1)}, bf16[896,768]{1,0:T(8,128)(2,1)S(1)}, f32[1,768]{1,0:T(1,128)S(1)}, f32[1,768]{1,0:T(1,128)S(1)}, f32[1,768]{1,0:T(1,128)S(1)}) custom-call(bf16[896,3072]{1,0:T(8,128)(2,1)S(1)} %copy-done.27, bf16[768,3072]{1,0:T(8,128)(2,1)S(1)} %bitcast.85, f32[896,768]{1,0:T(8,128)S(1)} %copy-done.10, ...), custom_call_target="tpu_custom_call" | custom-call | flops 108000002048 | bytes 1024 | tf_op jit(solution)/shard_map/pallas_call | solution.py:495
  179.0 11.9 %shard_map.284.grad_ref = bf16[896,2304]{1,0:T(8,128)(2,1)S(1)} custom-call(bf16[896,2304]{1,0:T(8,128)(2,1)S(1)} %copy-done.8, f32[8,12,112,112]{3,2,1,0:T(8,128)} %get-tuple-element.213.prob_ref, bf16[896,768]{1,0:T(8,128)(2,1)S(1)} %get-tuple-element.228.grad_ref), custom_call_target="tpu_custom_call" | custom-call | flops 5400000 | bytes 1024 | tf_op jit(solution)/shard_map/pallas_call | solution.py:560
  191.0 5.1 %shard_map.285 = (f32[896,768]{1,0:T(8,128)S(1)}, f32[1,768]{1,0:T(1,128)S(1)}, f32[1,768]{1,0:T(1,128)S(1)}) custom-call(bf16[896,2304]{1,0:T(8,128)(2,1)S(1)} %shard_map.284.grad_ref, bf16[2304,768]{1,0:T(8,128)(2,1)S(1)} %copy-done.2, bf16[896,768]{1,0:T(8,128)(2,1)S(1)} %copy-done.4, f32[896,768]{1,0:T(8,128)S(1)} %get-tuple-element.229.middle_ref, ...), custom_call_target="tpu_custom_call" | custom-call | flops 5400000 | bytes 1024 | tf_op jit(solution)/shard_map/pallas_call | solution.py:618
  198.7 4.7 %shard_map.286 = (bf16[2304,768]{1,0:T(8,128)(2,1)S(1)}, f32[1,2304]{1,0:T(1,128)S(1)}) custom-call(bf16[896,2304]{1,0:T(8,128)(2,1)S(1)} %shard_map.284.grad_ref, bf16[896,768]{1,0:T(8,128)(2,1)S(1)} %copy-done.26), custom_call_target="tpu_custom_call" | custom-call | flops 108000002048 | bytes 1024 | tf_op jit(solution)/shard_map/pallas_call | solution.py:592
  206.5 2.8 %shard_map.287 = (bf16[16,144,384]{2,1,0:T(8,128)(2,1)S(1)}, bf16[16,144,384]{2,1,0:T(8,128)(2,1)S(1)}) custom-call(s32[4]{0:T(128)S(1)} %pad_add_fusion.at_ref.x_ref, bf16[2304,768]{1,0:T(8,128)(2,1)S(1)} %get-tuple-element.237.refs_0_), custom_call_target="tpu_custom_call" | custom-call | flops 5400000 | bytes 1024 | tf_op jit(solution)/shard_map/pallas_call | solution.py:997
  209.3 4.4 %collective-permute-done.39 = bf16[4,96,768]{2,1,0:T(8,128)(2,1)S(1)} collective-permute-done((bf16[4,96,768]{2,1,0:T(8,128)(2,1)S(1)}, bf16[4,96,768]{2,1,0:T(8,128)(2,1)S(1)}, u32[]{:S(2)}, u32[]{:S(2)}) %collective-permute-start.39) | collective-permute-done | bytes 589856 | tf_op jit(solution)/shard_map/ppermute | solution.py:640
  215.7 3.6 %shard_map.290 = bf16[1,602112]{1,0:T(2,128)(2,1)} custom-call(s32[4]{0:T(128)S(1)} %pad_add_fusion.at_ref.x_ref, bf16[896,384]{1,0:T(8,128)(2,1)S(1)} %get-tuple-element.251.keep_ref, bf16[896,384]{1,0:T(8,128)(2,1)S(1)} %collective-permute-done.37.got_ref), custom_call_target="tpu_custom_call" | custom-call | flops 108000002048 | bytes 1024 | tf_op jit(solution)/shard_map/pallas_call | solution.py:196
  225.1 3.4 %collective-permute-done.40.got_ref = bf16[896,384]{1,0:T(8,128)(2,1)S(1)} collective-permute-done((bf16[896,384]{1,0:T(8,128)(2,1)S(1)}, bf16[896,384]{1,0:T(8,128)(2,1)S(1)}, u32[]{:S(2)}, u32[]{:S(2)}) %collective-permute-start.40) | collective-permute-done | bytes 688160 | tf_op jit(solution)/shard_map/ppermute | solution.py:640
  228.5 6.8 %shard_map.291 = f32[18816,128]{1,0:T(8,128)} custom-call(s32[4]{0:T(128)S(1)} %pad_add_fusion.at_ref.x_ref, f32[896,384]{1,0:T(8,128)S(1)} %constant_dynamic-slice_fusion.keep_ref, bf16[896,384]{1,0:T(8,128)(2,1)S(1)} %collective-permute-done.40.got_ref, s32[16,112,1]{2,1,0:T(8,128)S(1)} %copy-done.22), custom_call_target="tpu_custom_call" | custom-call | flops 108000002048 | bytes 1024 | tf_op jit(solution)/shard_map/pallas_call | solution.py:169
  235.3 4.1 %collective-permute-start.53 = (bf16[112,384]{1,0:T(8,128)(2,1)S(1)}, bf16[112,384]{1,0:T(8,128)(2,1)S(1)}, u32[]{:S(2)}, u32[]{:S(2)}) collective-permute-start(bf16[112,384]{1,0:T(8,128)(2,1)S(1)} %get-tuple-element.310), channel_id=1, source_target_pairs={{0,6},{2,4},{4,2},{6,0},{1,7},{3,5},{5,3},{7,1},{8,14},{10,12},{12... | collective-permute-start | bytes 258056 | tf_op jit(solution)/shard_map/ppermute | solution.py:640
  242.0 2.9 %collective-permute-done.52 = bf16[112,384]{1,0:T(8,128)(2,1)S(1)} collective-permute-done((bf16[112,384]{1,0:T(8,128)(2,1)S(1)}, bf16[112,384]{1,0:T(8,128)(2,1)S(1)}, u32[]{:S(2)}, u32[]{:S(2)}) %collective-permute-start.52) | collective-permute-done | bytes 86048 | tf_op jit(solution)/shard_map/ppermute | solution.py:640
  249.6 3.7 %collective-permute-start.50 = (bf16[144,384]{1,0:T(8,128)(2,1)S(1)}, bf16[144,384]{1,0:T(8,128)(2,1)S(1)}, u32[]{:S(2)}, u32[]{:S(2)}) collective-permute-start(bf16[144,384]{1,0:T(8,128)(2,1)S(1)} %get-tuple-element.307), channel_id=1, source_target_pairs={{0,6},{2,4},{4,2},{6,0},{1,7},{3,5},{5,3},{7,1},{8,14},{10,12},{12... | collective-permute-start | bytes 331784 | tf_op jit(solution)/shard_map/ppermute | solution.py:640
  261.9 2.7 %collective-permute-done.56 = bf16[144,384]{1,0:T(8,128)(2,1)S(1)} collective-permute-done((bf16[144,384]{1,0:T(8,128)(2,1)S(1)}, bf16[144,384]{1,0:T(8,128)(2,1)S(1)}, u32[]{:S(2)}, u32[]{:S(2)}) %collective-permute-start.56) | collective-permute-done | bytes 110624 | tf_op jit(solution)/shard_map/ppermute | solution.py:640
  (272 shorter events, 105.1 us)
Async XLA Ops:
  2.7 9.5 %collective-permute-start.3 = (bf16[1,96,384]{2,1,0:T(8,128)(2,1)S(1)}, bf16[1,96,384]{2,1,0:T(8,128)(2,1)S(1)}, u32[]{:S(2)}, u32[]{:S(2)}) collective-permute-start(bf16[1,96,384]{2,1,0:T(8,128)(2,1)S(1)} %bitcast.101), channel_id=1, source_target_pairs={{0,6},{2,4},{4,2},{6,0},{1,7},{3,5},{5,3},{7,1},{8,14},{10,12},{12... | collective-permute-start | bytes 221192 | tf_op jit(solution)/shard_map/ppermute | solution.py:640
  8.4 9.1 %collective-permute-start.4 = (bf16[1,96,768]{2,1,0:T(8,128)(2,1)S(1)}, bf16[1,96,768]{2,1,0:T(8,128)(2,1)S(1)}, u32[]{:S(2)}, u32[]{:S(2)}) collective-permute-start(bf16[1,96,768]{2,1,0:T(8,128)(2,1)S(1)} %bitcast.90), channel_id=1, source_target_pairs={{0,1},{1,0},{2,3},{3,2},{4,5},{5,4},{6,7},{7,6},{8,9},{9,8},{10,11... | collective-permute-start | bytes 442376 | tf_op jit(solution)/shard_map/ppermute | solution.py:640
  14.1 16.6 %collective-permute-start.7 = (bf16[4,96,384]{2,1,0:T(8,128)(2,1)S(1)}, bf16[4,96,384]{2,1,0:T(8,128)(2,1)S(1)}, u32[]{:S(2)}, u32[]{:S(2)}) collective-permute-start(bf16[4,96,384]{2,1,0:T(8,128)(2,1)S(1)} %pad_maximum_fusion.7), channel_id=1, source_target_pairs={{0,1},{1,0},{2,3},{3,2},{4,5},{5,4},{6,7},{7,6},{8,9},{9,8},{10,11... | collective-permute-start | bytes 884744 | tf_op jit(solution)/shard_map/ppermute | solution.py:640
  18.4 17.3 %collective-permute-start.6 = (bf16[2,208,384]{2,1,0:T(8,128)(2,1)S(1)}, bf16[2,208,384]{2,1,0:T(8,128)(2,1)S(1)}, u32[]{:S(2)}, u32[]{:S(2)}) collective-permute-start(bf16[2,208,384]{2,1,0:T(8,128)(2,1)S(1)} %pad_maximum_fusion.6), channel_id=1, source_target_pairs={{0,4},{2,6},{4,0},{6,2},{1,5},{3,7},{5,1},{7,3},{8,12},{10,14},{12... | collective-permute-start | bytes 958472 | tf_op jit(solution)/shard_map/ppermute | solution.py:640
  29.1 14.2 %collective-permute-start.5 = (bf16[896,384]{1,0:T(8,128)(2,1)S(1)}, bf16[896,384]{1,0:T(8,128)(2,1)S(1)}, u32[]{:S(2)}, u32[]{:S(2)}) collective-permute-start(bf16[896,384]{1,0:T(8,128)(2,1)S(1)} %get-tuple-element.306), channel_id=1, source_target_pairs={{0,1},{1,0},{2,3},{3,2},{4,5},{5,4},{6,7},{7,6},{8,9},{9,8},{10,11... | collective-permute-start | bytes 2064392 | tf_op jit(solution)/shard_map/ppermute | solution.py:640
  30.8 13.0 %collective-permute-start.9 = (bf16[8,96,384]{2,1,0:T(8,128)(2,1)S(1)}, bf16[8,96,384]{2,1,0:T(8,128)(2,1)S(1)}, u32[]{:S(2)}, u32[]{:S(2)}) collective-permute-start(bf16[8,96,384]{2,1,0:T(8,128)(2,1)S(1)} %get-tuple-element.314), channel_id=1, source_target_pairs={{0,16},{8,24},{16,0},{24,8},{1,17},{9,25},{17,1},{25,9},{2,18},{10... | collective-permute-start | bytes 1769480 | tf_op jit(solution)/shard_map/ppermute | solution.py:640
  35.7 16.3 %collective-permute-start.8 = (bf16[4,208,384]{2,1,0:T(8,128)(2,1)S(1)}, bf16[4,208,384]{2,1,0:T(8,128)(2,1)S(1)}, u32[]{:S(2)}, u32[]{:S(2)}) collective-permute-start(bf16[4,208,384]{2,1,0:T(8,128)(2,1)S(1)} %pad_maximum_fusion.2), channel_id=1, source_target_pairs={{0,2},{2,0},{4,6},{6,4},{1,3},{3,1},{5,7},{7,5},{8,10},{10,8},{12,... | collective-permute-start | bytes 1916936 | tf_op jit(solution)/shard_map/ppermute | solution.py:640
  53.0 19.3 %collective-permute-start.18 = (bf16[896,384]{1,0:T(8,128)(2,1)S(1)}, bf16[896,384]{1,0:T(8,128)(2,1)S(1)}, u32[]{:S(2)}, u32[]{:S(2)}) collective-permute-start(bf16[896,384]{1,0:T(8,128)(2,1)S(1)} %get-tuple-element.162), channel_id=1, source_target_pairs={{0,1},{1,0},{2,3},{3,2},{4,5},{5,4},{6,7},{7,6},{8,9},{9,8},{10,11... | collective-permute-start | bytes 2064392 | tf_op jit(solution)/shard_map/ppermute | solution.py:640
  55.7 8.8 %collective-permute-start.14 = (bf16[16,96,384]{2,1,0:T(8,128)(2,1)S(1)}, bf16[16,96,384]{2,1,0:T(8,128)(2,1)S(1)}, u32[]{:S(2)}, u32[]{:S(2)}) collective-permute-start(bf16[16,96,384]{2,1,0:T(8,128)(2,1)S(1)} %constant_dynamic-update-slice_fusion.5.refs_2_), channel_id=1, source_target_pairs={{0,8},{8,0},{16,24},{24,16},{1,9},{9,1},{17,25},{25,17},{2,10},{10... | collective-permute-start | bytes 3538952 | tf_op jit(solution)/shard_map/ppermute | solution.py:640
  55.7 10.0 %collective-permute-start.13 = (bf16[8,208,384]{2,1,0:T(8,128)(2,1)S(1)}, bf16[8,208,384]{2,1,0:T(8,128)(2,1)S(1)}, u32[]{:S(2)}, u32[]{:S(2)}) collective-permute-start(bf16[8,208,384]{2,1,0:T(8,128)(2,1)S(1)} %pad_maximum_fusion.refs_0_), channel_id=1, source_target_pairs={{0,8},{8,0},{16,24},{24,16},{1,9},{9,1},{17,25},{25,17},{2,10},{10... | collective-permute-start | bytes 3833864 | tf_op jit(solution)/shard_map/ppermute | solution.py:640
  62.2 13.4 %collective-permute-start.17 = (bf16[2,96,768]{2,1,0:T(8,128)(2,1)S(1)}, bf16[2,96,768]{2,1,0:T(8,128)(2,1)S(1)}, u32[]{:S(2)}, u32[]{:S(2)}) collective-permute-start(bf16[2,96,768]{2,1,0:T(8,128)(2,1)S(1)} %copy-done.32), channel_id=1, source_target_pairs={{0,4},{2,6},{4,0},{6,2},{1,5},{3,7},{5,1},{7,3},{8,12},{10,14},{12... | collective-permute-start | bytes 884744 | tf_op jit(solution)/shard_map/ppermute | solution.py:640
  62.8 13.0 %collective-permute-start.16 = (bf16[4,48,768]{2,1,0:T(8,128)(2,1)S(1)}, bf16[4,48,768]{2,1,0:T(8,128)(2,1)S(1)}, u32[]{:S(2)}, u32[]{:S(2)}) collective-permute-start(bf16[4,48,768]{2,1,0:T(8,128)(2,1)S(1)} %pad_maximum_fusion.10), channel_id=1, source_target_pairs={{0,1},{1,0},{2,3},{3,2},{4,5},{5,4},{6,7},{7,6},{8,9},{9,8},{10,11... | collective-permute-start | bytes 884744 | tf_op jit(solution)/shard_map/ppermute | solution.py:640
  64.5 13.9 %collective-permute-start.15 = (bf16[2,96,768]{2,1,0:T(8,128)(2,1)S(1)}, bf16[2,96,768]{2,1,0:T(8,128)(2,1)S(1)}, u32[]{:S(2)}, u32[]{:S(2)}) collective-permute-start(bf16[2,96,768]{2,1,0:T(8,128)(2,1)S(1)} %pad_maximum_fusion.9), channel_id=1, source_target_pairs={{0,2},{2,0},{4,6},{6,4},{1,3},{3,1},{5,7},{7,5},{8,10},{10,8},{12,... | collective-permute-start | bytes 884744 | tf_op jit(solution)/shard_map/ppermute | solution.py:640
  79.6 16.2 %collective-permute-start.20 = (bf16[4,96,768]{2,1,0:T(8,128)(2,1)S(1)}, bf16[4,96,768]{2,1,0:T(8,128)(2,1)S(1)}, u32[]{:S(2)}, u32[]{:S(2)}) collective-permute-start(bf16[4,96,768]{2,1,0:T(8,128)(2,1)S(1)} %get-tuple-element.188.refs_0_), channel_id=1, source_target_pairs={{0,1},{1,0},{2,3},{3,2},{4,5},{5,4},{6,7},{7,6},{8,9},{9,8},{10,11... | collective-permute-start | bytes 1769480 | tf_op jit(solution)/shard_map/ppermute | solution.py:640
  80.0 13.1 %collective-permute-start.19 = (bf16[4,96,768]{2,1,0:T(8,128)(2,1)S(1)}, bf16[4,96,768]{2,1,0:T(8,128)(2,1)S(1)}, u32[]{:S(2)}, u32[]{:S(2)}) collective-permute-start(bf16[4,96,768]{2,1,0:T(8,128)(2,1)S(1)} %get-tuple-element.328), channel_id=1, source_target_pairs={{0,2},{2,0},{4,6},{6,4},{1,3},{3,1},{5,7},{7,5},{8,10},{10,8},{12,... | collective-permute-start | bytes 1769480 | tf_op jit(solution)/shard_map/ppermute | solution.py:640
  80.2 15.6 %collective-permute-start.21 = (bf16[8,48,768]{2,1,0:T(8,128)(2,1)S(1)}, bf16[8,48,768]{2,1,0:T(8,128)(2,1)S(1)}, u32[]{:S(2)}, u32[]{:S(2)}) collective-permute-start(bf16[8,48,768]{2,1,0:T(8,128)(2,1)S(1)} %pad_maximum_fusion.4.refs_4_), channel_id=1, source_target_pairs={{0,16},{8,24},{16,0},{24,8},{1,17},{9,25},{17,1},{25,9},{2,18},{10... | collective-permute-start | bytes 1769480 | tf_op jit(solution)/shard_map/ppermute | solution.py:640
  93.2 27.6 %collective-permute-start.26 = (bf16[8,96,768]{2,1,0:T(8,128)(2,1)S(1)}, bf16[8,96,768]{2,1,0:T(8,128)(2,1)S(1)}, u32[]{:S(2)}, u32[]{:S(2)}) collective-permute-start(bf16[8,96,768]{2,1,0:T(8,128)(2,1)S(1)} %pad_maximum_fusion.1.refs_0_), channel_id=1, source_target_pairs={{0,16},{8,24},{16,0},{24,8},{1,17},{9,25},{17,1},{25,9},{2,18},{10... | collective-permute-start | bytes 3538952 | tf_op jit(solution)/shard_map/ppermute | solution.py:640
  130.2 29.2 %collective-permute-start.31 = (bf16[4,192,768]{2,1,0:T(8,128)(2,1)}, bf16[4,192,768]{2,1,0:T(8,128)(2,1)}, u32[]{:S(2)}, u32[]{:S(2)}) collective-permute-start(bf16[4,192,768]{2,1,0:T(8,128)(2,1)} %add_convert_fusion.1), channel_id=1, source_target_pairs={{0,1},{1,0},{2,3},{3,2},{4,5},{5,4},{6,7},{7,6},{8,9},{9,8},{10,11... | collective-permute-start | bytes 3538952 | tf_op jit(solution)/shard_map/ppermute | solution.py:640
  161.1 15.3 %collective-permute-start.34 = (bf16[2,192,768]{2,1,0:T(8,128)(2,1)S(1)}, bf16[2,192,768]{2,1,0:T(8,128)(2,1)S(1)}, u32[]{:S(2)}, u32[]{:S(2)}) collective-permute-start(bf16[2,192,768]{2,1,0:T(8,128)(2,1)S(1)} %get-tuple-element.292), channel_id=1, source_target_pairs={{0,2},{2,0},{4,6},{6,4},{1,3},{3,1},{5,7},{7,5},{8,10},{10,8},{12,... | collective-permute-start | bytes 1769480 | tf_op jit(solution)/shard_map/ppermute | solution.py:640
  163.6 33.4 %collective-permute-start.36 = (bf16[8,96,768]{2,1,0:T(8,128)(2,1)S(1)}, bf16[8,96,768]{2,1,0:T(8,128)(2,1)S(1)}, u32[]{:S(2)}, u32[]{:S(2)}) collective-permute-start(bf16[8,96,768]{2,1,0:T(8,128)(2,1)S(1)} %add_convert_fusion), channel_id=1, source_target_pairs={{0,16},{8,24},{16,0},{24,8},{1,17},{9,25},{17,1},{25,9},{2,18},{10... | collective-permute-start | bytes 3538952 | tf_op jit(solution)/shard_map/ppermute | solution.py:640
  174.0 22.4 %collective-permute-start.37 = (bf16[896,384]{1,0:T(8,128)(2,1)S(1)}, bf16[896,384]{1,0:T(8,128)(2,1)S(1)}, u32[]{:S(2)}, u32[]{:S(2)}) collective-permute-start(bf16[896,384]{1,0:T(8,128)(2,1)S(1)} %get-tuple-element.227), channel_id=1, source_target_pairs={{0,1},{1,0},{2,3},{3,2},{4,5},{5,4},{6,7},{7,6},{8,9},{9,8},{10,11... | collective-permute-start | bytes 2064392 | tf_op jit(solution)/shard_map/ppermute | solution.py:640
  176.4 19.9 %collective-permute-start.35 = (bf16[1,192,768]{2,1,0:T(8,128)(2,1)S(1)}, bf16[1,192,768]{2,1,0:T(8,128)(2,1)S(1)}, u32[]{:S(2)}, u32[]{:S(2)}) collective-permute-start(bf16[1,192,768]{2,1,0:T(8,128)(2,1)S(1)} %fusion.7), channel_id=1, source_target_pairs={{0,4},{2,6},{4,0},{6,2},{1,5},{3,7},{5,1},{7,3},{8,12},{10,14},{12... | collective-permute-start | bytes 884744 | tf_op jit(solution)/shard_map/ppermute | solution.py:640
  197.4 16.3 %collective-permute-start.39 = (bf16[4,96,768]{2,1,0:T(8,128)(2,1)S(1)}, bf16[4,96,768]{2,1,0:T(8,128)(2,1)S(1)}, u32[]{:S(2)}, u32[]{:S(2)}) collective-permute-start(bf16[4,96,768]{2,1,0:T(8,128)(2,1)S(1)} %get-tuple-element.290), channel_id=1, source_target_pairs={{0,1},{1,0},{2,3},{3,2},{4,5},{5,4},{6,7},{7,6},{8,9},{9,8},{10,11... | collective-permute-start | bytes 1769480 | tf_op jit(solution)/shard_map/ppermute | solution.py:640
  204.9 15.5 %collective-permute-start.43 = (bf16[8,112,384]{2,1,0:T(8,128)(2,1)S(1)}, bf16[8,112,384]{2,1,0:T(8,128)(2,1)S(1)}, u32[]{:S(2)}, u32[]{:S(2)}) collective-permute-start(bf16[8,112,384]{2,1,0:T(8,128)(2,1)S(1)} %get-tuple-element.247), channel_id=1, source_target_pairs={{0,8},{8,0},{16,24},{24,16},{1,9},{9,1},{17,25},{25,17},{2,10},{10... | collective-permute-start | bytes 2064392 | tf_op jit(solution)/shard_map/ppermute | solution.py:640
  205.1 14.2 %collective-permute-start.61 = (f32[192,768]{1,0:T(8,128)S(1)}, f32[192,768]{1,0:T(8,128)S(1)}, u32[]{:S(2)}, u32[]{:S(2)}) collective-permute-start(f32[192,768]{1,0:T(8,128)S(1)} %convert_add_fusion.4), channel_id=1, source_target_pairs={{0,8},{8,0},{16,24},{24,16},{1,9},{9,1},{17,25},{25,17},{2,10},{10... | collective-permute-start | bytes 1769480 | tf_op jit(solution)/shard_map/ppermute | solution.py:640
  205.6 22.9 %collective-permute-start.40 = (bf16[896,384]{1,0:T(8,128)(2,1)S(1)}, bf16[896,384]{1,0:T(8,128)(2,1)S(1)}, u32[]{:S(2)}, u32[]{:S(2)}) collective-permute-start(bf16[896,384]{1,0:T(8,128)(2,1)S(1)} %constant_dynamic-slice_fusion.1), channel_id=1, source_target_pairs={{0,1},{1,0},{2,3},{3,2},{4,5},{5,4},{6,7},{7,6},{8,9},{9,8},{10,11... | collective-permute-start | bytes 2064392 | tf_op jit(solution)/shard_map/ppermute | solution.py:640
  209.3 11.9 %collective-permute-start.42 = (bf16[16,144,384]{2,1,0:T(8,128)(2,1)S(1)}, bf16[16,144,384]{2,1,0:T(8,128)(2,1)S(1)}, u32[]{:S(2)}, u32[]{:S(2)}) collective-permute-start(bf16[16,144,384]{2,1,0:T(8,128)(2,1)S(1)} %get-tuple-element.238), channel_id=1, source_target_pairs={{0,8},{8,0},{16,24},{24,16},{1,9},{9,1},{17,25},{25,17},{2,10},{10... | collective-permute-start | bytes 5308424 | tf_op jit(solution)/shard_map/ppermute | solution.py:640
  213.9 8.8 %collective-permute-start.41 = (bf16[2,96,768]{2,1,0:T(8,128)(2,1)S(1)}, bf16[2,96,768]{2,1,0:T(8,128)(2,1)S(1)}, u32[]{:S(2)}, u32[]{:S(2)}) collective-permute-start(bf16[2,96,768]{2,1,0:T(8,128)(2,1)S(1)} %get-tuple-element.296), channel_id=1, source_target_pairs={{0,2},{2,0},{4,6},{6,4},{1,3},{3,1},{5,7},{7,5},{8,10},{10,8},{12,... | collective-permute-start | bytes 884744 | tf_op jit(solution)/shard_map/ppermute | solution.py:640
  220.5 14.8 %collective-permute-start.47 = (bf16[4,112,384]{2,1,0:T(8,128)(2,1)S(1)}, bf16[4,112,384]{2,1,0:T(8,128)(2,1)S(1)}, u32[]{:S(2)}, u32[]{:S(2)}) collective-permute-start(bf16[4,112,384]{2,1,0:T(8,128)(2,1)S(1)} %get-tuple-element.300), channel_id=1, source_target_pairs={{0,1},{1,0},{2,3},{3,2},{4,5},{5,4},{6,7},{7,6},{8,9},{9,8},{10,11... | collective-permute-start | bytes 1032200 | tf_op jit(solution)/shard_map/ppermute | solution.py:640
  221.6 18.5 %collective-permute-start.44 = (bf16[8,144,384]{2,1,0:T(8,128)(2,1)S(1)}, bf16[8,144,384]{2,1,0:T(8,128)(2,1)S(1)}, u32[]{:S(2)}, u32[]{:S(2)}) collective-permute-start(bf16[8,144,384]{2,1,0:T(8,128)(2,1)S(1)} %get-tuple-element.288), channel_id=1, source_target_pairs={{0,16},{8,24},{16,0},{24,8},{1,17},{9,25},{17,1},{25,9},{2,18},{10... | collective-permute-start | bytes 2654216 | tf_op jit(solution)/shard_map/ppermute | solution.py:640
  222.8 18.5 %collective-permute-start.46 = (bf16[1,96,768]{2,1,0:T(8,128)(2,1)S(1)}, bf16[1,96,768]{2,1,0:T(8,128)(2,1)S(1)}, u32[]{:S(2)}, u32[]{:S(2)}) collective-permute-start(bf16[1,96,768]{2,1,0:T(8,128)(2,1)S(1)} %fusion.9), channel_id=1, source_target_pairs={{0,4},{2,6},{4,0},{6,2},{1,5},{3,7},{5,1},{7,3},{8,12},{10,14},{12... | collective-permute-start | bytes 442376 | tf_op jit(solution)/shard_map/ppermute | solution.py:640
  256.0 10.6 %collective-permute-start.60 = (f32[2,96,768]{2,1,0:T(8,128)S(1)}, f32[2,96,768]{2,1,0:T(8,128)S(1)}, u32[]{:S(2)}, u32[]{:S(2)}) collective-permute-start(f32[2,96,768]{2,1,0:T(8,128)S(1)} %maximum_select_fusion.6), channel_id=1, source_target_pairs={{0,8},{8,0},{16,24},{24,16},{1,9},{9,1},{17,25},{25,17},{2,10},{10... | collective-permute-start | bytes 1769480 | tf_op jit(solution)/shard_map/ppermute | solution.py:640
  (68 other events, 514.0 us)

commit v7 on v5

--- a/solution.py
+++ b/solution.py
@@ -326,7 +326,7 @@
 
 def mix(mixed, w, rows, vec):
     r = rows.shape[0]
-    m = row_tile(r)
+    m = r // 4 if r % 64 == 0 else row_tile(r)
     row = spec((m, D), lambda i: (i, 0))
     return call(
         mix_body,
@@ -389,14 +389,12 @@
     )(active, w, vec, middle)
 
 
-def outer_body(left_ref, right_ref, out_ref, sum_ref, turned):
+def outer_body(left_ref, right_ref, out_ref, turned):
     @pl.when(pl.program_id(0) == 0)
     def _():
         turned[...] = left_ref[...].T
 
-    right = right_ref[...]
-    out_ref[...] = dot(turned[...], right, 1, 0).astype(BF)
-    sum_ref[...] = jnp.sum(right.astype(F32), 0, keepdims=True)
+    out_ref[...] = dot(turned[...], right_ref[...], 1, 0).astype(BF)
 
 
 def outer(left, right):
@@ -406,8 +404,8 @@
         outer_body,
         (width // TILE,),
         [spec((r, rows), lambda j: (0, 0)), spec((r, TILE), lambda j: (0, j))],
-        [spec((rows, TILE), lambda j: (0, j)), spec((1, TILE), lambda j: (0, j))],
-        [struct((rows, width), BF), struct((1, width), F32)],
+        spec((rows, TILE), lambda j: (0, j)),
+        struct((rows, width), BF),
         [pltpu.VMEM((rows, r), BF)],
         us=0.01,
         nbytes=r * rows * 2 + r * width * 2 + rows * width * 2,
@@ -440,6 +438,101 @@
         us=200,
         nbytes=r * D * 4 + D * units * 4 + r * units * 6,
     )(cot, w, slope, hidden)
+
+
+def place(w):
+    return w % 2 * 2 + w // 2
+
+
+def turn_blocks(left_ref, plain, turned, offsets):
+    plain[...] = left_ref[...].T
+    rows = plain.shape[0] // len(offsets)
+    for i, offset in enumerate(offsets):
+        turned[i * rows : (i + 1) * rows, :] = plain[pl.ds(pl.multiple_of(offset, 16), rows), :]
+
+
+def outer_pieces_body(cols, at_ref, left_ref, right_ref, *refs):
+    outs, (plain, turned) = refs[:4], refs[4:]
+
+    @pl.when(pl.program_id(0) == 0)
+    def _():
+        offsets = [
+            (n ^ at_ref[1]) * cols + (at_ref[2] ^ side) * (cols // 2)
+            for side in range(2)
+            for n in range(2)
+        ]
+        turn_blocks(left_ref, plain, turned, offsets)
+
+    grad = dot(turned[...], right_ref[...], 1, 0).astype(BF)
+    half = cols // 2
+    for i, out in enumerate(outs):
+        out[...] = grad[i * half : (i + 1) * half].reshape(out.shape)
+
+
+def outer_pieces(at, left, right, cols, wide):
+    r, width = right.shape
+    rows, units = left.shape[1], width // wide
+    shape = (wide, cols // 2, units)
+    block = spec((1, cols // 2, units), lambda j, at: (place(j ^ at[0]), 0, 0))
+    out = call(
+        partial(outer_pieces_body, cols),
+        (wide,),
+        [spec((r, rows), lambda j, at: (0, 0)), spec((r, units), lambda j, at: (0, j))],
+        [block] * 4,
+        [pltpu.HBM(shape, BF)] * 2 + [struct(shape, BF)] * 2,
+        [pltpu.VMEM((rows, r), BF)] * 2,
+        prefetch=1,
+        us=0.01,
+        nbytes=r * rows * 2 + r * width * 2 + rows * width * 2,
+    )(at, left, right)
+    return out[:2], out[2:]
+
+
+def inner_back_pieces_body(cols, at_ref, cot_ref, w_ref, slope_ref, hidden_ref, *refs):
+    grad_ref, outs, gb_ref, plain, turned = refs[0], refs[1:5], refs[5], refs[6], refs[7]
+    part = cols // 4
+
+    @pl.when(pl.program_id(0) == 0)
+    def _():
+        offsets = [
+            (n ^ at_ref[1]) * cols + (at_ref[3] ^ (2 * dy) ^ side) * part
+            for side in range(2)
+            for dy in range(2)
+            for n in range(2)
+        ]
+        turn_blocks(hidden_ref, plain, turned, offsets)
+
+    grad = (dot(cot_ref[...], w_ref[...], 1, 0) * slope_ref[...]).astype(BF)
+    grad_ref[...] = grad
+    gb_ref[...] = jnp.sum(grad.astype(F32), 0, keepdims=True)
+    outer_grad = dot(turned[...], grad, 1, 0).astype(BF)
+    for i, out in enumerate(outs):
+        out[...] = outer_grad[2 * i * part : 2 * (i + 1) * part].reshape(out.shape)
+
+
+def inner_back_pieces(at, cot, w, slope, hidden, cols, wide):
+    r, width = slope.shape
+    units, part = width // wide, cols // 4
+    shape = (2, wide, part, units)
+    full = spec((r, D), lambda j, at: (0, 0))
+    tile = spec((r, units), lambda j, at: (0, j))
+    block = spec((2, 1, part, units), lambda j, at: (0, place(j ^ at[0]), 0, 0))
+    out = call(
+        partial(inner_back_pieces_body, cols),
+        (wide,),
+        [full, spec((D, units), lambda j, at: (0, j)), tile, full],
+        [tile] + [block] * 4 + [spec((1, units), lambda j, at: (0, j))],
+        [pltpu.HBM((r, width), BF)]
+        + [pltpu.HBM(shape, BF)] * 2
+        + [struct(shape, BF)] * 2
+        + [struct((1, width), F32)],
+        [pltpu.VMEM((D, r), BF)] * 2,
+        prefetch=1,
+        us=200,
+        nbytes=r * D * 4 + D * width * 4 + r * width * 6,
+    )(at, cot, w, slope, hidden)
+    pieces = [piece.reshape(2 * wide, part, units) for piece in out[1:5]]
+    return out[0], pieces[:2], pieces[2:], out[5]
 
 
 def norm_pull(grad, normed, inv, gain):
@@ -606,7 +699,7 @@
 
 def first_back(grad, w, rows, grad_middle, vecs):
     r, width = grad.shape
-    m = row_tile(r)
+    m = r // 4 if r % 64 == 0 else row_tile(r)
     vec = spec((1, D), lambda i: (0, 0))
     row = spec((m, D), lambda i: (i, 0))
     vec_out = struct((1, D), F32)
@@ -838,9 +931,6 @@
 IN_HBM = pl.BlockSpec(memory_space=pltpu.HBM)
 
 
-CORE, DP_INDEX = 2, 3
-
-
 def owner_sums_body(wide, narrow, cols, *refs):
     out = refs[-1]
     narrow_refs, qkv_ref, up_ref = refs[:6], refs[6], refs[7]
@@ -875,34 +965,51 @@
     )(*rows)
 
 
-def build_body(plans, tag_lists, inverse, parts_by, at_ref, *refs):
+def build_body(plans, counts, inverse, parts_by, at_ref, tag_ref, *refs):
     refs, sem = refs[:-1], refs[-1]
-    count = len(tag_lists)
-    wholes, arrays = (refs[:-count], refs[-count:]) if inverse else (refs[count:], refs[:count])
-    copies = []
-    for array, tags, plan, by in zip(arrays, tag_lists, plans, parts_by):
-        for k, (dw, dn, dq) in enumerate(tags):
-            w, n, q = at_ref[0] ^ dw, at_ref[1] ^ dn, at_ref[by] ^ dq
-            for which, (at_row, at_lane), (rows, lanes), (row, lane) in plan(w, n, q):
-                piece = array.at[k, pl.ds(at_row, rows), pl.ds(at_lane, lanes)]
-                whole = wholes[which].at[
-                    pl.ds(pl.multiple_of(row, 16), rows), pl.ds(pl.multiple_of(lane, 128), lanes)
-                ]
-                ends = (whole, piece) if inverse else (piece, whole)
-                copies.append(pltpu.make_async_copy(*ends, sem.at[len(copies)]))
-    for copy in copies:
-        copy.start()
-    for copy in copies:
-        copy.wait()
-
-
-def move_pieces(at, arrays, plans, tag_lists, inverse, parts_by, shapes):
-    moves = sum(len(tags) * len(plan(0, 0, 0)) for tags, plan in zip(tag_lists, plans))
+    lists = len(counts)
+    wholes, arrays = (refs[:-lists], refs[-lists:]) if inverse else (refs[lists:], refs[:lists])
+
+    def each(act):
+        first, slot = 0, 0
+        for array, plan, count, by in zip(arrays, plans, counts, parts_by):
+            moves = len(plan(0, 0, 0))
+
+            def step(k, carry, array=array, plan=plan, by=by, first=first, slot=slot, moves=moves):
+                w, n, q = (
+                    at_ref[axis] ^ tag_ref[i, first + k] for i, axis in enumerate((0, 1, by))
+                )
+                for m, (which, (at_row, at_lane), (rows, lanes), (row, lane)) in enumerate(
+                    plan(w, n, q)
+                ):
+                    piece = array.at[k, pl.ds(at_row, rows), pl.ds(at_lane, lanes)]
+                    whole = wholes[which].at[
+                        pl.ds(pl.multiple_of(row, 16), rows),
+                        pl.ds(pl.multiple_of(lane, 128), lanes),
+                    ]
+                    ends = (whole, piece) if inverse else (piece, whole)
+                    act(pltpu.make_async_copy(*ends, sem.at[slot + k * moves + m]))
+                return carry
+
+            lax.fori_loop(0, count, step, 0, unroll=4)
+            first, slot = first + count, slot + count * moves
+
+    each(lambda copy: copy.start())
+    each(lambda copy: copy.wait())
+
+
+def move_pieces(at, arrays, plans, tag_lists, inverse, parts_by, shapes, pinned=0):
+    counts = [len(tags) for tags in tag_lists]
+    moves = sum(count * len(plan(0, 0, 0)) for count, plan in zip(counts, plans))
+    table = jnp.array([tag for tags in tag_lists for tag in tags], jnp.int32).T
     return pl.pallas_call(
-        partial(build_body, plans, tag_lists, inverse, parts_by),
-        out_shape=[struct(shape, BF) for shape in shapes],
+        partial(build_body, plans, counts, inverse, parts_by),
+        out_shape=[
+            pltpu.HBM(shape, BF) if i < pinned else struct(shape, BF)
+            for i, shape in enumerate(shapes)
+        ],
         grid_spec=pltpu.PrefetchScalarGridSpec(
-            num_scalar_prefetch=1,
+            num_scalar_prefetch=2,
             grid=(1,),
             in_specs=[ANY] * len(arrays),
             out_specs=[ANY] * len(shapes),
@@ -912,7 +1019,7 @@
         cost_estimate=pl.CostEstimate(
             flops=FLOPS_PER_US // 100, bytes_accessed=1024, transcendentals=0
         ),
-    )(at, *arrays)
+    )(at, table, *arrays)
 
 
 CORE, DP_INDEX = 2, 3
@@ -925,16 +1032,10 @@
     return move_pieces(at, arrays, plans, tags, False, parts_by, [shape])[0]
 
 
-def cut_grads(at, grads, plan, tags, shape, part_at=CORE, split=False):
-    half = len(tags) // 2
-    some = (tags[:half], tags[half:]) if split else (tags,)
-    tag_lists = [[(w, n, q ^ dc) for w, n, q in part] for dc in range(2) for part in some]
-    shapes = [(len(part),) + shape for part in tag_lists]
-    count = len(tag_lists)
-    out = move_pieces(
-        at, grads, [plan] * count, tag_lists, True, [part_at] * count, shapes
-    )
-    return (out[:2], out[2:]) if split else out
+def cut_grads(at, grads, plan, tags, shape, part_at=CORE):
+    lists = [[(w, n, q ^ dc) for w, n, q in tags] for dc in range(2)]
+    shapes = [(len(tags),) + shape] * 2
+    return move_pieces(at, grads, [plan] * 2, lists, True, [part_at] * 2, shapes, 1)
 
 
 def fence_body(x_ref, out_ref):
@@ -956,8 +1057,8 @@
 
 
 class Chain:
-    def __init__(self, *args, **options):
-        self.keep, self.send = cut_grads(*args, **options)
+    def __init__(self, keep, send):
+        self.keep, self.send = keep, send
 
     def go(self, axis, bit):
         if isinstance(self.send, (list, tuple)):
@@ -1118,7 +1219,7 @@
 
         b_x, a_z = b_p.fetch(NARROW, 1), a_p.fetch(WIDE, 2)
         rows_out = pick_rows(
-            hold(at, a_p.stack, b_p.stack, d_p.stack), patches, index, cols
+            hold(at, a_p.stack, b_p.stack, d_p.stack), in_hbm(patches), index, cols
         )
         own = rows_out.shape[0] // 2
         rows_send = rows_out[:own]
@@ -1192,37 +1293,22 @@
 
         x_first = [(w, n, 0) for n in range(2) for w in (0, 2, 1, 3)]
         y_first = [(w, n, dy) for dy in (0, 2) for n in range(2) for w in (0, 2, 1, 3)]
-        gw_down, _ = outer(cot, in_hbm(active))
+        gd_keep, gd_send = outer_pieces(at, cot, in_hbm(active), cols, wide)
         gb_down = jnp.sum(cot, 0, dtype=F32)[None]
-        d_y = d_y.after(gw_down)
+        d_y = d_y.after(*gd_send)
         d_c = [p.fetch(DP, 1, d_y.stack) for p in (d_p, d_y)]
-        g_d = Chain(
-            at,
-            [hold(gw_down, d_y.stack)],
-            half_flat,
-            x_first,
-            (cols // 2, units),
-            split=True,
-        )
+        g_d = Chain(gd_keep, [hold(piece, d_y.stack) for piece in gd_send])
         g_d.go(DP, 1)
         d_c = [p.after(*g_d.send) for p in d_c]
         down_w = build_weights(at, whole, ([d_p, d_y] + d_c, part_flat, DP_INDEX))
         g_d.fold(down_w)
         g_d.go(NARROW, 1)
-        grad_inner, gw_up, gb_up = inner_back(
-            cot, hold(down_w, g_d.send), in_hbm(slope), hidden_two
+        grad_inner, gu_keep, gu_send, gb_up = inner_back_pieces(
+            at, cot, hold(down_w, g_d.send), in_hbm(slope), hidden_two, cols, wide
         )
 
         result = down(hold(in_hbm(active), grad_inner), down_w, vecs, middle)
-        g_u = Chain(
-            at,
-            [hold(gw_up, result)],
-            part_flat,
-            y_first,
-            (cols // 4, units),
-            DP_INDEX,
-            split=True,
-        )
+        g_u = Chain(gu_keep, [hold(piece, result) for piece in gu_send])
         g_u.go(DP, 1)
         g_d.fold(*g_u.send)
         g_d.go(WIDE, 1)
@@ -1264,7 +1350,7 @@
         )
 
         part = heads_cols // 4
-        g_q = Chain(
+        g_q = cut_grads(
             at,
             [gw_qkv],
             qkv_plan(cols, heads_cols, 4, {p: (p * part, 0) for p in range(3)}),
@@ -1272,11 +1358,12 @@
             (3 * part, cols),
             DP_INDEX,
         )
+        g_q = Chain(*g_q)
         g_q.go(DP, 1)
         rest_plan = joined(
             out_plan(cols, heads_cols, 2, (0, 0), 0), sums_plan(cols, narrow, (half, 0), 1)
         )
-        g_r = Chain(at, [gw_out, sums], rest_plan, x_first, (half + 16, cols))
+        g_r = Chain(*cut_grads(at, [gw_out, sums], rest_plan, x_first, (half + 16, cols)))
         g_r.go(DP, 1)
         d_sum = d_sum + hold(d_got, g_r.send).astype(F32)
         d_got = swap(d_sum, DP, 1)
@@ -1284,12 +1371,11 @@
         g_u.go(WIDE, 1)
         rows_send = hold(part_of(grad_rows, theirs), g_r.send).astype(BF)
         rows_back = swap(rows_send, NARROW, 1)
-        keep = hold(part_of(result, mine), g_q.send, d_sum, g_u.send, rows_send)
-        block_output = flat_rows(at, keep, result_got, cols)
-
-        g_q.fold(block_output)
+        token = fence(hold(vecs, g_q.send, d_sum, g_u.send, rows_send))
+
+        g_q.fold(token)
         g_q.go(DP, 2)
-        g_r.fold(block_output)
+        g_r.fold(token, g_q.send)
         g_r.go(NARROW, 1)
         g_u.fold(g_q.send, g_r.send)
         g_u.go(WIDE, 2)
@@ -1301,17 +1387,18 @@
 
         g_q.fold(grad_patches)
         g_q.go(NARROW, 1)
-        g_r.spread(grad_patches)
+        g_r.spread(grad_patches, g_q.send)
         u_sum = g_u.total(g_q.send, *g_r.send)
-        token = fence(hold(vecs, g_q.send, u_sum, *g_r.send))
-        g_q.spread(token)
-        r_sum = g_r.all_of(token)
+        keep = hold(part_of(result, mine), g_q.send, u_sum, *g_r.send)
+        block_output = flat_rows(at, keep, result_got, cols)
+        g_q.spread(block_output)
+        r_sum = g_r.all_of(block_output)
         r_got = swap(r_sum.astype(BF), DP, 2)
         u_got = swap(u_sum.astype(BF), DP, 2)
         token = fence(hold(token, r_sum, u_sum, *g_q.send))
         q_sum = g_q.all_of(token)
         q_got = [swap(q_sum.astype(BF), DP, bit) for bit in (1, 2, 3)]
-        r_sum = r_sum + hold(r_got, token).astype(F32)
+        r_sum = r_sum + hold(r_got, q_sum).astype(F32)
         r_got = swap(r_sum[:half], DP, 1)
         u_sum = in_order(u_sum, hold(u_got, token).astype(F32), at[3] // 2)
         u_got = swap(u_sum, DP, 1)
@@ -1362,7 +1449,7 @@
         middle, hidden_two = mix(mixed, out_w, rows, vecs)
         active, slope = up(hidden_two, up_w, bias_up)
         result = down(active, down_w, vecs, middle)
-        gw_down, _ = outer(cot, active)
+        gw_down = outer(cot, active)
         gb_down = jnp.sum(cot, 0, dtype=F32)[None]
         grad_inner, gw_up, gb_up = inner_back(cot, down_w, slope, hidden_two)
         grad_middle, branch, gg_two, gs_two, gb_out = middle_back(

time: 282 us -> 267 us (0.947); the launches traced: 277 us -> 266 us
  local copies, waits for them, and re-layouts: 17.4 us -> 10.9 us
  Pallas kernels: 128 us -> 122 us
    pallas_call x1, Pallas kernels: 16.3 us -> 6.45 us  [middle_back(): call(middle_back_body, (r // m,), [spec((m, units), lambda i: (i, 0)), sp...]
    unnamed x81 -> x99, local copies, waits for them, and re-layouts: 12 us -> 5.57 us
    pallas_call x10 -> x8, Pallas kernels: 36 us -> 35.8 us  [the longest x1 14.4 us: inner_back_pieces(): call(partial(inner_back_pieces_body, cols), (wide,), [full, spec((D, unit...]
  transfers between devices with their start and end apart: 62 -> 62, of which waited for: 24 -> 25; matrix products, arithmetic and copies ran while one was open for 7% -> 8% of each run, Pallas kernels for 45% -> 45%
where the time goes in v7:
time: 267 us; the launch traced here: 266 us
  Pallas kernels  122 us (46%)
  starting transfers between devices  58.1 us (22%)
  waiting for transfers between devices  56.8 us (21%)
  other arithmetic  16.6 us (6%)
  local copies, waits for them, and re-layouts  10.9 us (4%)
    ppermute x62, starting transfers between devices, swap(): return lax.ppermute(value, axis, [(i, i ^ bit) for i in range(size)])  58.1 us
    ppermute x62, waiting for transfers between devices, swap(): return lax.ppermute(value, axis, [(i, i ^ bit) for i in range(size)])  56.8 us
    pallas_call x1, Pallas kernels, inner_back_pieces(): call(partial(inner_back_pieces_body, cols), (wide,), [full, spec((D, unit...  14.4 us
    pallas_call x6, Pallas kernels, move_pieces(): pl.pallas_call(partial(build_body, plans, counts, inverse, parts_by), out...  12.4 us
    pallas_call x1, Pallas kernels, attend_back(): pl.pallas_call(attend_back_body, out_shape=struct(triple.shape, BF), grid...  12 us
    pallas_call x1, Pallas kernels, up(): call(up_body, (units // TILE,), [spec((r, D), lambda j: (0, 0)), spec((D,...  10.1 us
    pallas_call x1, Pallas kernels, outer_pieces(): call(partial(outer_pieces_body, cols), (wide,), [spec((r, rows), lambda j...  8.98 us
    pallas_call x1, Pallas kernels, put_rows(): call(partial(put_body, cols, count), (pairs // count,), [rows, rows, spec...  6.79 us
  transfers between devices with their start and end apart: 62, of which 25 were waited for; matrix products, arithmetic and copies ran while one was open for 8% of the time, Pallas kernels for 45%

profile of v7, /device:TPU:0, one launch (start us, length us, event | category | flops | bytes accessed | tf_op | source)
XLA Modules:
  0.0 266.0 jit_solution(10701414330274478403)
XLA Ops:
  2.7 5.1 %collective-permute-start.3 = (bf16[1,96,384]{2,1,0:T(8,128)(2,1)S(1)}, bf16[1,96,384]{2,1,0:T(8,128)(2,1)S(1)}, u32[]{:S(2)}, u32[]{:S(2)}) collective-permute-start(bf16[1,96,384]{2,1,0:T(8,128)(2,1)S(1)} %bitcast.105), channel_id=1, source_target_pairs={{0,6},{2,4},{4,2},{6,0},{1,7},{3,5},{5,3},{7,1},{8,14},{10,12},{12... | collective-permute-start | bytes 221192 | tf_op jit(solution)/shard_map/ppermute | solution.py:728
  18.4 2.7 %collective-permute-start.6 = (bf16[2,208,384]{2,1,0:T(8,128)(2,1)S(1)}, bf16[2,208,384]{2,1,0:T(8,128)(2,1)S(1)}, u32[]{:S(2)}, u32[]{:S(2)}) collective-permute-start(bf16[2,208,384]{2,1,0:T(8,128)(2,1)S(1)} %pad_maximum_fusion.6), channel_id=1, source_target_pairs={{0,4},{2,6},{4,0},{6,2},{1,5},{3,7},{5,1},{7,3},{8,12},{10,14},{12... | collective-permute-start | bytes 958472 | tf_op jit(solution)/shard_map/ppermute | solution.py:728
  21.0 6.7 %shard_map.319 = bf16[1792,384]{1,0:T(8,128)(2,1)S(1)} custom-call(s32[4]{0:T(128)S(1)} %pad_add_fusion.at_ref.x_ref, bf16[1,2408448]{1,0:T(2,128)(2,1)} %patch_ref.1, s32[16,112,1]{2,1,0:T(8,128)S(1)} %copy.38.index_ref), custom_call_target="tpu_custom_call" | custom-call | flops 108000002048 | bytes 1024 | tf_op jit(solution)/shard_map/pallas_call | solution.py:98
  31.2 5.2 %collective-permute-done.6 = bf16[2,208,384]{2,1,0:T(8,128)(2,1)S(1)} collective-permute-done((bf16[2,208,384]{2,1,0:T(8,128)(2,1)S(1)}, bf16[2,208,384]{2,1,0:T(8,128)(2,1)S(1)}, u32[]{:S(2)}, u32[]{:S(2)}) %collective-permute-start.6) | collective-permute-done | bytes 319520 | tf_op jit(solution)/shard_map/ppermute | solution.py:728
  36.6 2.8 %shard_map.320 = bf16[1792,384]{1,0:T(8,128)(2,1)S(1)} custom-call(s32[4]{0:T(128)S(1)} %pad_add_fusion.at_ref.x_ref, bf16[1,602112]{1,0:T(2,128)(2,1)S(1)} %copy-done.25), custom_call_target="tpu_custom_call" | custom-call | flops 108000002048 | bytes 1024 | tf_op jit(solution)/shard_map/pallas_call | solution.py:129
  39.6 2.5 collective-permute-done.5
  42.7 9.3 %collective-permute-done.8 = bf16[4,208,384]{2,1,0:T(8,128)(2,1)S(1)} collective-permute-done((bf16[4,208,384]{2,1,0:T(8,128)(2,1)S(1)}, bf16[4,208,384]{2,1,0:T(8,128)(2,1)S(1)}, u32[]{:S(2)}, u32[]{:S(2)}) %collective-permute-start.8) | collective-permute-done | bytes 639008 | tf_op jit(solution)/shard_map/ppermute | solution.py:728
  65.4 2.7 %shard_map.323.w_ref = bf16[2304,768]{1,0:T(8,128)(2,1)S(1)} custom-call(s32[4]{0:T(128)S(1)} %pad_add_fusion.at_ref.x_ref, s32[3,48]{1,0:T(4,128)S(1)} %copy-done.22, bf16[8,208,384]{2,1,0:T(8,128)(2,1)S(1)} %pad_maximum_fusion.refs_0_, bf16[8,208,384]{2,1,0:T(8,128)(2,1)S(1)} %collective-permute-done.13.refs_1_, ...), custom_call_target="tpu_custom_call" | custom-call | flops 5400000 | bytes 1024 | tf_op jit(solution)/shard_map/pallas_call | solution.py:1005
  68.1 4.1 %shard_map.324.triple_ref = bf16[896,2304]{1,0:T(8,128)(2,1)S(1)} custom-call(bf16[896,768]{1,0:T(8,128)(2,1)S(1)} %shard_map.322.hidden_ref, bf16[2304,768]{1,0:T(8,128)(2,1)S(1)} %shard_map.323.w_ref, f32[1,2304]{1,0:T(1,128)S(1)} %get-tuple-element.176.bias_ref), custom_call_target="tpu_custom_call" | custom-call | flops 7020000256 | bytes 1024 | tf_op jit(solution)/shard_map/pallas_call | solution.py:247
  80.1 6.0 %shard_map.325 = (bf16[896,768]{1,0:T(8,128)(2,1)S(1)}, f32[8,12,112,112]{3,2,1,0:T(8,128)}) custom-call(bf16[896,2304]{1,0:T(8,128)(2,1)S(1)} %shard_map.324.triple_ref), custom_call_target="tpu_custom_call" | custom-call | flops 108000002048 | bytes 1024 | tf_op jit(solution)/shard_map/pallas_call | solution.py:302
  86.1 5.4 %collective-permute-done.19 = bf16[4,96,768]{2,1,0:T(8,128)(2,1)S(1)} collective-permute-done((bf16[4,96,768]{2,1,0:T(8,128)(2,1)S(1)}, bf16[4,96,768]{2,1,0:T(8,128)(2,1)S(1)}, u32[]{:S(2)}, u32[]{:S(2)}) %collective-permute-start.19) | collective-permute-done | bytes 589856 | tf_op jit(solution)/shard_map/ppermute | solution.py:728
  95.4 2.8 %shard_map.327 = (f32[896,768]{1,0:T(8,128)S(1)}, bf16[896,768]{1,0:T(8,128)(2,1)S(1)}) custom-call(bf16[896,768]{1,0:T(8,128)(2,1)S(1)} %get-tuple-element.187.mixed_ref, bf16[768,768]{1,0:T(8,128)(2,1)S(1)} %shard_map.326.w_ref, bf16[896,768]{1,0:T(8,128)(2,1)S(1)} %maximum_select_fusion.rows_ref, f32[8,768]{1,0:T(8,128)S(1)} %get-tuple-element.254.vec_ref.x_ref), custom_call_target="tpu_custom_call" | custom-call | flops 8640000000 | bytes 1024 | tf_op jit(solution)/shard_map/pallas_call | solution.py:331
  99.0 2.4 shard_map.328.w_ref
  101.4 10.1 %shard_map.329 = (bf16[896,3072]{1,0:T(8,128)(2,1)}, f32[896,3072]{1,0:T(8,128)}) custom-call(bf16[896,768]{1,0:T(8,128)(2,1)S(1)} %get-tuple-element.188.hidden_ref, bf16[768,3072]{1,0:T(8,128)(2,1)S(1)} %shard_map.328.w_ref, f32[1,3072]{1,0:T(1,128)S(1)} %get-tuple-element.197.bias_ref), custom_call_target="tpu_custom_call" | custom-call | flops 5400000 | bytes 1024 | tf_op jit(solution)/shard_map/pallas_call | solution.py:353
  111.5 9.0 %shard_map.330 = (bf16[4,192,768]{2,1,0:T(8,128)(2,1)}, bf16[4,192,768]{2,1,0:T(8,128)(2,1)}, bf16[4,192,768]{2,1,0:T(8,128)(2,1)S(1)}, bf16[4,192,768]{2,1,0:T(8,128)(2,1)S(1)}) custom-call(s32[4]{0:T(128)S(1)} %pad_add_fusion.at_ref.x_ref, bf16[896,768]{1,0:T(8,128)(2,1)S(1)} %get-tuple-element.288.left_ref.cot_ref, ...), custom_call_target="tpu_custom_call" | custom-call | flops 5400000 | bytes 1024 | tf_op jit(solution)/shard_map/pallas_call | solution.py:477
  131.0 14.4 %shard_map.332 = (bf16[896,3072]{1,0:T(8,128)(2,1)}, bf16[2,4,96,768]{3,2,1,0:T(8,128)(2,1)}, bf16[2,4,96,768]{3,2,1,0:T(8,128)(2,1)}, bf16[2,4,96,768]{3,2,1,0:...) custom-call(s32[4]{0:T(128)S(1)} %pad_add_fusion.at_ref.x_ref, ...), custom_call_target="tpu_custom_call" | custom-call | flops 108000002048 | bytes 1024 | tf_op jit(solution)/shard_map/pallas_call | solution.py:520
  145.4 6.5 %shard_map.333 = bf16[896,768]{1,0:T(8,128)(2,1)S(1)} custom-call(bf16[896,3072]{1,0:T(8,128)(2,1)} %get-tuple-element.213.right_ref.active_ref, bf16[768,3072]{1,0:T(8,128)(2,1)S(1)} %shard_map.331.w_ref, f32[8,768]{1,0:T(8,128)S(1)} %get-tuple-element.254.vec_ref.x_ref, f32[896,768]{1,0:T(8,128)S(1)} %get-tuple-element.214.middle_ref), custom_call_target="tpu_custom_call" | custom-call | flops 5400000 | bytes 1024 | tf_op jit(solution)/shard_map/pallas_call | solution.py:376
  155.5 2.6 collective-permute-done.31
  163.6 6.4 %shard_map.334 = (f32[896,768]{1,0:T(8,128)S(1)}, bf16[896,768]{1,0:T(8,128)(2,1)S(1)}, f32[1,768]{1,0:T(1,128)S(1)}, f32[1,768]{1,0:T(1,128)S(1)}, f32[1,768]{1,0:T(1,128)S(1)}) custom-call(bf16[896,3072]{1,0:T(8,128)(2,1)S(1)} %copy-done.30, bf16[768,3072]{1,0:T(8,128)(2,1)S(1)} %bitcast.89, f32[896,768]{1,0:T(8,128)S(1)} %copy-done.10, ...), custom_call_target="tpu_custom_call" | custom-call | flops 108000002048 | bytes 1024 | tf_op jit(solution)/shard_map/pallas_call | solution.py:583
  170.1 2.5 shard_map.335
  178.2 12.0 %shard_map.336.grad_ref = bf16[896,2304]{1,0:T(8,128)(2,1)S(1)} custom-call(bf16[896,2304]{1,0:T(8,128)(2,1)S(1)} %copy-done.8, f32[8,12,112,112]{3,2,1,0:T(8,128)} %get-tuple-element.215.prob_ref, bf16[896,768]{1,0:T(8,128)(2,1)S(1)} %get-tuple-element.230.grad_ref), custom_call_target="tpu_custom_call" | custom-call | flops 5400000 | bytes 1024 | tf_op jit(solution)/shard_map/pallas_call | solution.py:648
  190.2 5.2 %shard_map.337 = (f32[896,768]{1,0:T(8,128)S(1)}, f32[1,768]{1,0:T(1,128)S(1)}, f32[1,768]{1,0:T(1,128)S(1)}) custom-call(bf16[896,2304]{1,0:T(8,128)(2,1)S(1)} %shard_map.336.grad_ref, bf16[2304,768]{1,0:T(8,128)(2,1)S(1)} %copy-done.2, bf16[896,768]{1,0:T(8,128)(2,1)S(1)} %copy-done.4, f32[896,768]{1,0:T(8,128)S(1)} %get-tuple-element.231.middle_ref, ...), custom_call_target="tpu_custom_call" | custom-call | flops 5400000 | bytes 1024 | tf_op jit(solution)/shard_map/pallas_call | solution.py:706
  198.4 4.8 %shard_map.338 = (bf16[2304,768]{1,0:T(8,128)(2,1)S(1)}, f32[1,2304]{1,0:T(1,128)S(1)}) custom-call(bf16[896,2304]{1,0:T(8,128)(2,1)S(1)} %shard_map.336.grad_ref, bf16[896,768]{1,0:T(8,128)(2,1)S(1)} %copy-done.29), custom_call_target="tpu_custom_call" | custom-call | flops 108000002048 | bytes 1024 | tf_op jit(solution)/shard_map/pallas_call | solution.py:680
  206.2 2.7 %shard_map.339 = (bf16[16,144,384]{2,1,0:T(8,128)(2,1)}, bf16[16,144,384]{2,1,0:T(8,128)(2,1)S(1)}) custom-call(s32[4]{0:T(128)S(1)} %copy-done.18, s32[3,32]{1,0:T(4,128)S(1)} %copy-done.19, bf16[2304,768]{1,0:T(8,128)(2,1)S(1)} %get-tuple-element.239.refs_0_), custom_call_target="tpu_custom_call" | custom-call | flops 5400000 | bytes 1024 | tf_op jit(solution)/shard_map/pallas_call | solution.py:1005
  209.0 2.5 collective-permute-done.40
  211.6 2.7 %collective-permute-start.43 = (bf16[2,96,768]{2,1,0:T(8,128)(2,1)S(1)}, bf16[2,96,768]{2,1,0:T(8,128)(2,1)S(1)}, u32[]{:S(2)}, u32[]{:S(2)}) collective-permute-start(bf16[2,96,768]{2,1,0:T(8,128)(2,1)S(1)} %get-tuple-element.300), channel_id=1, source_target_pairs={{0,2},{2,0},{4,6},{6,4},{1,3},{3,1},{5,7},{7,5},{8,10},{10,8},{12,... | collective-permute-start | bytes 884744 | tf_op jit(solution)/shard_map/ppermute | solution.py:728
  220.5 5.7 %collective-permute-done.42.got_ref = bf16[896,384]{1,0:T(8,128)(2,1)S(1)} collective-permute-done((bf16[896,384]{1,0:T(8,128)(2,1)S(1)}, bf16[896,384]{1,0:T(8,128)(2,1)S(1)}, u32[]{:S(2)}, u32[]{:S(2)}) %collective-permute-start.42) | collective-permute-done | bytes 688160 | tf_op jit(solution)/shard_map/ppermute | solution.py:728
  226.2 6.8 %shard_map.343 = f32[18816,128]{1,0:T(8,128)} custom-call(s32[4]{0:T(128)S(1)} %copy-done.18, f32[896,384]{1,0:T(8,128)S(1)} %constant_dynamic-slice_fusion.keep_ref, bf16[896,384]{1,0:T(8,128)(2,1)S(1)} %collective-permute-done.42.got_ref, s32[16,112,1]{2,1,0:T(8,128)S(1)} %copy-done.16), custom_call_target="tpu_custom_call" | custom-call | flops 108000002048 | bytes 1024 | tf_op jit(solution)/shard_map/pallas_call | solution.py:169
  236.6 2.4 collective-permute-start.53
  242.5 3.6 %shard_map.344 = bf16[1,602112]{1,0:T(2,128)(2,1)} custom-call(s32[4]{0:T(128)S(1)} %copy-done.18, bf16[896,384]{1,0:T(8,128)(2,1)S(1)} %get-tuple-element.263.keep_ref, bf16[896,384]{1,0:T(8,128)(2,1)S(1)} %copy-done.27), custom_call_target="tpu_custom_call" | custom-call | flops 108000002048 | bytes 1024 | tf_op jit(solution)/shard_map/pallas_call | solution.py:196
  247.8 2.4 collective-permute-start.50
  254.4 2.3 collective-permute-done.49
  (288 shorter events, 102.0 us)
Async XLA Ops:
  2.7 9.5 %collective-permute-start.3 = (bf16[1,96,384]{2,1,0:T(8,128)(2,1)S(1)}, bf16[1,96,384]{2,1,0:T(8,128)(2,1)S(1)}, u32[]{:S(2)}, u32[]{:S(2)}) collective-permute-start(bf16[1,96,384]{2,1,0:T(8,128)(2,1)S(1)} %bitcast.105), channel_id=1, source_target_pairs={{0,6},{2,4},{4,2},{6,0},{1,7},{3,5},{5,3},{7,1},{8,14},{10,12},{12... | collective-permute-start | bytes 221192 | tf_op jit(solution)/shard_map/ppermute | solution.py:728
  14.1 15.5 %collective-permute-start.7 = (bf16[4,96,384]{2,1,0:T(8,128)(2,1)S(1)}, bf16[4,96,384]{2,1,0:T(8,128)(2,1)S(1)}, u32[]{:S(2)}, u32[]{:S(2)}) collective-permute-start(bf16[4,96,384]{2,1,0:T(8,128)(2,1)S(1)} %pad_maximum_fusion.7), channel_id=1, source_target_pairs={{0,1},{1,0},{2,3},{3,2},{4,5},{5,4},{6,7},{7,6},{8,9},{9,8},{10,11... | collective-permute-start | bytes 884744 | tf_op jit(solution)/shard_map/ppermute | solution.py:728
  18.4 18.1 %collective-permute-start.6 = (bf16[2,208,384]{2,1,0:T(8,128)(2,1)S(1)}, bf16[2,208,384]{2,1,0:T(8,128)(2,1)S(1)}, u32[]{:S(2)}, u32[]{:S(2)}) collective-permute-start(bf16[2,208,384]{2,1,0:T(8,128)(2,1)S(1)} %pad_maximum_fusion.6), channel_id=1, source_target_pairs={{0,4},{2,6},{4,0},{6,2},{1,5},{3,7},{5,1},{7,3},{8,12},{10,14},{12... | collective-permute-start | bytes 958472 | tf_op jit(solution)/shard_map/ppermute | solution.py:728
  27.9 14.2 %collective-permute-start.5 = (bf16[896,384]{1,0:T(8,128)(2,1)S(1)}, bf16[896,384]{1,0:T(8,128)(2,1)S(1)}, u32[]{:S(2)}, u32[]{:S(2)}) collective-permute-start(bf16[896,384]{1,0:T(8,128)(2,1)S(1)} %get-tuple-element.308), channel_id=1, source_target_pairs={{0,1},{1,0},{2,3},{3,2},{4,5},{5,4},{6,7},{7,6},{8,9},{9,8},{10,11... | collective-permute-start | bytes 2064392 | tf_op jit(solution)/shard_map/ppermute | solution.py:728
  29.5 9.9 %collective-permute-start.10 = (bf16[1,48,768]{2,1,0:T(8,128)(2,1)S(1)}, bf16[1,48,768]{2,1,0:T(8,128)(2,1)S(1)}, u32[]{:S(2)}, u32[]{:S(2)}) collective-permute-start(bf16[1,48,768]{2,1,0:T(8,128)(2,1)S(1)} %bitcast.98), channel_id=1, source_target_pairs={{0,4},{2,6},{4,0},{6,2},{1,5},{3,7},{5,1},{7,3},{8,12},{10,14},{12... | collective-permute-start | bytes 221192 | tf_op jit(solution)/shard_map/ppermute | solution.py:728
  29.6 13.0 %collective-permute-start.9 = (bf16[8,96,384]{2,1,0:T(8,128)(2,1)S(1)}, bf16[8,96,384]{2,1,0:T(8,128)(2,1)S(1)}, u32[]{:S(2)}, u32[]{:S(2)}) collective-permute-start(bf16[8,96,384]{2,1,0:T(8,128)(2,1)S(1)} %get-tuple-element.316), channel_id=1, source_target_pairs={{0,16},{8,24},{16,0},{24,8},{1,17},{9,25},{17,1},{25,9},{2,18},{10... | collective-permute-start | bytes 1769480 | tf_op jit(solution)/shard_map/ppermute | solution.py:728
  36.5 15.5 %collective-permute-start.8 = (bf16[4,208,384]{2,1,0:T(8,128)(2,1)S(1)}, bf16[4,208,384]{2,1,0:T(8,128)(2,1)S(1)}, u32[]{:S(2)}, u32[]{:S(2)}) collective-permute-start(bf16[4,208,384]{2,1,0:T(8,128)(2,1)S(1)} %pad_maximum_fusion.2), channel_id=1, source_target_pairs={{0,2},{2,0},{4,6},{6,4},{1,3},{3,1},{5,7},{7,5},{8,10},{10,8},{12,... | collective-permute-start | bytes 1916936 | tf_op jit(solution)/shard_map/ppermute | solution.py:728
  53.1 19.2 %collective-permute-start.18 = (bf16[896,384]{1,0:T(8,128)(2,1)S(1)}, bf16[896,384]{1,0:T(8,128)(2,1)S(1)}, u32[]{:S(2)}, u32[]{:S(2)}) collective-permute-start(bf16[896,384]{1,0:T(8,128)(2,1)S(1)} %get-tuple-element.163), channel_id=1, source_target_pairs={{0,1},{1,0},{2,3},{3,2},{4,5},{5,4},{6,7},{7,6},{8,9},{9,8},{10,11... | collective-permute-start | bytes 2064392 | tf_op jit(solution)/shard_map/ppermute | solution.py:728
  55.9 9.5 %collective-permute-start.13 = (bf16[8,208,384]{2,1,0:T(8,128)(2,1)S(1)}, bf16[8,208,384]{2,1,0:T(8,128)(2,1)S(1)}, u32[]{:S(2)}, u32[]{:S(2)}) collective-permute-start(bf16[8,208,384]{2,1,0:T(8,128)(2,1)S(1)} %pad_maximum_fusion.refs_0_), channel_id=1, source_target_pairs={{0,8},{8,0},{16,24},{24,16},{1,9},{9,1},{17,25},{25,17},{2,10},{10... | collective-permute-start | bytes 3833864 | tf_op jit(solution)/shard_map/ppermute | solution.py:728
  61.5 12.9 %collective-permute-start.17 = (bf16[2,96,768]{2,1,0:T(8,128)(2,1)S(1)}, bf16[2,96,768]{2,1,0:T(8,128)(2,1)S(1)}, u32[]{:S(2)}, u32[]{:S(2)}) collective-permute-start(bf16[2,96,768]{2,1,0:T(8,128)(2,1)S(1)} %copy-done.41), channel_id=1, source_target_pairs={{0,4},{2,6},{4,0},{6,2},{1,5},{3,7},{5,1},{7,3},{8,12},{10,14},{12... | collective-permute-start | bytes 884744 | tf_op jit(solution)/shard_map/ppermute | solution.py:728
  62.2 12.8 %collective-permute-start.16 = (bf16[4,48,768]{2,1,0:T(8,128)(2,1)S(1)}, bf16[4,48,768]{2,1,0:T(8,128)(2,1)S(1)}, u32[]{:S(2)}, u32[]{:S(2)}) collective-permute-start(bf16[4,48,768]{2,1,0:T(8,128)(2,1)S(1)} %pad_maximum_fusion.10), channel_id=1, source_target_pairs={{0,1},{1,0},{2,3},{3,2},{4,5},{5,4},{6,7},{7,6},{8,9},{9,8},{10,11... | collective-permute-start | bytes 884744 | tf_op jit(solution)/shard_map/ppermute | solution.py:728
  63.7 13.0 %collective-permute-start.15 = (bf16[2,96,768]{2,1,0:T(8,128)(2,1)S(1)}, bf16[2,96,768]{2,1,0:T(8,128)(2,1)S(1)}, u32[]{:S(2)}, u32[]{:S(2)}) collective-permute-start(bf16[2,96,768]{2,1,0:T(8,128)(2,1)S(1)} %pad_maximum_fusion.9), channel_id=1, source_target_pairs={{0,2},{2,0},{4,6},{6,4},{1,3},{3,1},{5,7},{7,5},{8,10},{10,8},{12,... | collective-permute-start | bytes 884744 | tf_op jit(solution)/shard_map/ppermute | solution.py:728
  78.0 16.4 %collective-permute-start.20 = (bf16[4,96,768]{2,1,0:T(8,128)(2,1)S(1)}, bf16[4,96,768]{2,1,0:T(8,128)(2,1)S(1)}, u32[]{:S(2)}, u32[]{:S(2)}) collective-permute-start(bf16[4,96,768]{2,1,0:T(8,128)(2,1)S(1)} %get-tuple-element.189.refs_0_), channel_id=1, source_target_pairs={{0,1},{1,0},{2,3},{3,2},{4,5},{5,4},{6,7},{7,6},{8,9},{9,8},{10,11... | collective-permute-start | bytes 1769480 | tf_op jit(solution)/shard_map/ppermute | solution.py:728
  78.5 13.0 %collective-permute-start.19 = (bf16[4,96,768]{2,1,0:T(8,128)(2,1)S(1)}, bf16[4,96,768]{2,1,0:T(8,128)(2,1)S(1)}, u32[]{:S(2)}, u32[]{:S(2)}) collective-permute-start(bf16[4,96,768]{2,1,0:T(8,128)(2,1)S(1)} %get-tuple-element.330), channel_id=1, source_target_pairs={{0,2},{2,0},{4,6},{6,4},{1,3},{3,1},{5,7},{7,5},{8,10},{10,8},{12,... | collective-permute-start | bytes 1769480 | tf_op jit(solution)/shard_map/ppermute | solution.py:728
  78.5 15.8 %collective-permute-start.21 = (bf16[8,48,768]{2,1,0:T(8,128)(2,1)S(1)}, bf16[8,48,768]{2,1,0:T(8,128)(2,1)S(1)}, u32[]{:S(2)}, u32[]{:S(2)}) collective-permute-start(bf16[8,48,768]{2,1,0:T(8,128)(2,1)S(1)} %pad_maximum_fusion.4.refs_4_), channel_id=1, source_target_pairs={{0,16},{8,24},{16,0},{24,8},{1,17},{9,25},{17,1},{25,9},{2,18},{10... | collective-permute-start | bytes 1769480 | tf_op jit(solution)/shard_map/ppermute | solution.py:728
  91.6 28.8 %collective-permute-start.26 = (bf16[8,96,768]{2,1,0:T(8,128)(2,1)S(1)}, bf16[8,96,768]{2,1,0:T(8,128)(2,1)S(1)}, u32[]{:S(2)}, u32[]{:S(2)}) collective-permute-start(bf16[8,96,768]{2,1,0:T(8,128)(2,1)S(1)} %pad_maximum_fusion.1.refs_0_), channel_id=1, source_target_pairs={{0,16},{8,24},{16,0},{24,8},{1,17},{9,25},{17,1},{25,9},{2,18},{10... | collective-permute-start | bytes 3538952 | tf_op jit(solution)/shard_map/ppermute | solution.py:728
  129.7 28.3 %collective-permute-start.31 = (bf16[4,192,768]{2,1,0:T(8,128)(2,1)}, bf16[4,192,768]{2,1,0:T(8,128)(2,1)}, u32[]{:S(2)}, u32[]{:S(2)}) collective-permute-start(bf16[4,192,768]{2,1,0:T(8,128)(2,1)} %add_convert_fusion), channel_id=1, source_target_pairs={{0,1},{1,0},{2,3},{3,2},{4,5},{5,4},{6,7},{7,6},{8,9},{9,8},{10,11... | collective-permute-start | bytes 3538952 | tf_op jit(solution)/shard_map/ppermute | solution.py:728
  159.8 14.6 %collective-permute-start.34 = (bf16[2,192,768]{2,1,0:T(8,128)(2,1)S(1)}, bf16[2,192,768]{2,1,0:T(8,128)(2,1)S(1)}, u32[]{:S(2)}, u32[]{:S(2)}) collective-permute-start(bf16[2,192,768]{2,1,0:T(8,128)(2,1)S(1)} %get-tuple-element.296), channel_id=1, source_target_pairs={{0,2},{2,0},{4,6},{6,4},{1,3},{3,1},{5,7},{7,5},{8,10},{10,8},{12,... | collective-permute-start | bytes 1769480 | tf_op jit(solution)/shard_map/ppermute | solution.py:728
  162.0 34.5 %collective-permute-start.36 = (bf16[8,96,768]{2,1,0:T(8,128)(2,1)S(1)}, bf16[8,96,768]{2,1,0:T(8,128)(2,1)S(1)}, u32[]{:S(2)}, u32[]{:S(2)}) collective-permute-start(bf16[8,96,768]{2,1,0:T(8,128)(2,1)S(1)} %fusion), channel_id=1, source_target_pairs={{0,16},{8,24},{16,0},{24,8},{1,17},{9,25},{17,1},{25,9},{2,18},{10... | collective-permute-start | bytes 3538952 | tf_op jit(solution)/shard_map/ppermute | solution.py:728
  172.6 23.0 %collective-permute-start.37 = (bf16[896,384]{1,0:T(8,128)(2,1)S(1)}, bf16[896,384]{1,0:T(8,128)(2,1)S(1)}, u32[]{:S(2)}, u32[]{:S(2)}) collective-permute-start(bf16[896,384]{1,0:T(8,128)(2,1)S(1)} %get-tuple-element.229), channel_id=1, source_target_pairs={{0,1},{1,0},{2,3},{3,2},{4,5},{5,4},{6,7},{7,6},{8,9},{9,8},{10,11... | collective-permute-start | bytes 2064392 | tf_op jit(solution)/shard_map/ppermute | solution.py:728
  174.5 21.1 %collective-permute-start.35 = (bf16[1,192,768]{2,1,0:T(8,128)(2,1)S(1)}, bf16[1,192,768]{2,1,0:T(8,128)(2,1)S(1)}, u32[]{:S(2)}, u32[]{:S(2)}) collective-permute-start(bf16[1,192,768]{2,1,0:T(8,128)(2,1)S(1)} %fusion.8), channel_id=1, source_target_pairs={{0,4},{2,6},{4,0},{6,2},{1,5},{3,7},{5,1},{7,3},{8,12},{10,14},{12... | collective-permute-start | bytes 884744 | tf_op jit(solution)/shard_map/ppermute | solution.py:728
  196.8 14.7 %collective-permute-start.40 = (bf16[4,96,768]{2,1,0:T(8,128)(2,1)S(1)}, bf16[4,96,768]{2,1,0:T(8,128)(2,1)S(1)}, u32[]{:S(2)}, u32[]{:S(2)}) collective-permute-start(bf16[4,96,768]{2,1,0:T(8,128)(2,1)S(1)} %get-tuple-element.294), channel_id=1, source_target_pairs={{0,1},{1,0},{2,3},{3,2},{4,5},{5,4},{6,7},{7,6},{8,9},{9,8},{10,11... | collective-permute-start | bytes 1769480 | tf_op jit(solution)/shard_map/ppermute | solution.py:728
  205.0 13.0 %collective-permute-start.44 = (bf16[8,112,384]{2,1,0:T(8,128)(2,1)S(1)}, bf16[8,112,384]{2,1,0:T(8,128)(2,1)S(1)}, u32[]{:S(2)}, u32[]{:S(2)}) collective-permute-start(bf16[8,112,384]{2,1,0:T(8,128)(2,1)S(1)} %get-tuple-element.250), channel_id=1, source_target_pairs={{0,8},{8,0},{16,24},{24,16},{1,9},{9,1},{17,25},{25,17},{2,10},{10... | collective-permute-start | bytes 2064392 | tf_op jit(solution)/shard_map/ppermute | solution.py:728
  205.7 20.5 %collective-permute-start.42 = (bf16[896,384]{1,0:T(8,128)(2,1)S(1)}, bf16[896,384]{1,0:T(8,128)(2,1)S(1)}, u32[]{:S(2)}, u32[]{:S(2)}) collective-permute-start(bf16[896,384]{1,0:T(8,128)(2,1)S(1)} %constant_dynamic-slice_fusion.1), channel_id=1, source_target_pairs={{0,1},{1,0},{2,3},{3,2},{4,5},{5,4},{6,7},{7,6},{8,9},{9,8},{10,11... | collective-permute-start | bytes 2064392 | tf_op jit(solution)/shard_map/ppermute | solution.py:728
  216.6 18.3 %collective-permute-start.41 = (bf16[8,144,384]{2,1,0:T(8,128)(2,1)S(1)}, bf16[8,144,384]{2,1,0:T(8,128)(2,1)S(1)}, u32[]{:S(2)}, u32[]{:S(2)}) collective-permute-start(bf16[8,144,384]{2,1,0:T(8,128)(2,1)S(1)} %get-tuple-element.291), channel_id=1, source_target_pairs={{0,16},{8,24},{16,0},{24,8},{1,17},{9,25},{17,1},{25,9},{2,18},{10... | collective-permute-start | bytes 2654216 | tf_op jit(solution)/shard_map/ppermute | solution.py:728
  218.2 18.4 %collective-permute-start.46 = (bf16[4,112,384]{2,1,0:T(8,128)(2,1)S(1)}, bf16[4,112,384]{2,1,0:T(8,128)(2,1)S(1)}, u32[]{:S(2)}, u32[]{:S(2)}) collective-permute-start(bf16[4,112,384]{2,1,0:T(8,128)(2,1)S(1)} %get-tuple-element.302), channel_id=1, source_target_pairs={{0,1},{1,0},{2,3},{3,2},{4,5},{5,4},{6,7},{7,6},{8,9},{9,8},{10,11... | collective-permute-start | bytes 1032200 | tf_op jit(solution)/shard_map/ppermute | solution.py:728
  219.5 21.6 %collective-permute-start.45 = (bf16[1,96,768]{2,1,0:T(8,128)(2,1)S(1)}, bf16[1,96,768]{2,1,0:T(8,128)(2,1)S(1)}, u32[]{:S(2)}, u32[]{:S(2)}) collective-permute-start(bf16[1,96,768]{2,1,0:T(8,128)(2,1)S(1)} %fusion.10), channel_id=1, source_target_pairs={{0,4},{2,6},{4,0},{6,2},{1,5},{3,7},{5,1},{7,3},{8,12},{10,14},{12... | collective-permute-start | bytes 442376 | tf_op jit(solution)/shard_map/ppermute | solution.py:728
  235.0 12.7 %collective-permute-start.47 = (bf16[4,144,384]{2,1,0:T(8,128)(2,1)S(1)}, bf16[4,144,384]{2,1,0:T(8,128)(2,1)S(1)}, u32[]{:S(2)}, u32[]{:S(2)}) collective-permute-start(bf16[4,144,384]{2,1,0:T(8,128)(2,1)S(1)} %get-tuple-element.298), channel_id=1, source_target_pairs={{0,1},{1,0},{2,3},{3,2},{4,5},{5,4},{6,7},{7,6},{8,9},{9,8},{10,11... | collective-permute-start | bytes 1327112 | tf_op jit(solution)/shard_map/ppermute | solution.py:728
  236.6 9.4 %collective-permute-start.53 = (bf16[112,384]{1,0:T(8,128)(2,1)S(1)}, bf16[112,384]{1,0:T(8,128)(2,1)S(1)}, u32[]{:S(2)}, u32[]{:S(2)}) collective-permute-start(bf16[112,384]{1,0:T(8,128)(2,1)S(1)} %get-tuple-element.312), channel_id=1, source_target_pairs={{0,6},{2,4},{4,2},{6,0},{1,7},{3,5},{5,3},{7,1},{8,14},{10,12},{12... | collective-permute-start | bytes 258056 | tf_op jit(solution)/shard_map/ppermute | solution.py:728
  241.9 10.9 %collective-permute-start.59 = (bf16[96,768]{1,0:T(8,128)(2,1)}, bf16[96,768]{1,0:T(8,128)(2,1)}, u32[]{:S(2)}, u32[]{:S(2)}) collective-permute-start(bf16[96,768]{1,0:T(8,128)(2,1)} %get-tuple-element.281), channel_id=1, source_target_pairs={{0,16},{8,24},{16,0},{24,8},{1,17},{9,25},{17,1},{25,9},{2,18},{10... | collective-permute-start | bytes 442376 | tf_op jit(solution)/shard_map/ppermute | solution.py:728
  246.2 12.6 %collective-permute-start.57 = (bf16[112,384]{1,0:T(8,128)(2,1)S(1)}, bf16[112,384]{1,0:T(8,128)(2,1)S(1)}, u32[]{:S(2)}, u32[]{:S(2)}) collective-permute-start(bf16[112,384]{1,0:T(8,128)(2,1)S(1)} %get-tuple-element.283), channel_id=1, source_target_pairs={{0,16},{8,24},{16,0},{24,8},{1,17},{9,25},{17,1},{25,9},{2,18},{10... | collective-permute-start | bytes 258056 | tf_op jit(solution)/shard_map/ppermute | solution.py:728
  253.9 11.0 %collective-permute-start.60 = (f32[2,96,768]{2,1,0:T(8,128)S(1)}, f32[2,96,768]{2,1,0:T(8,128)S(1)}, u32[]{:S(2)}, u32[]{:S(2)}) collective-permute-start(f32[2,96,768]{2,1,0:T(8,128)S(1)} %maximum_select_fusion.6), channel_id=1, source_target_pairs={{0,8},{8,0},{16,24},{24,16},{1,9},{9,1},{17,25},{25,17},{2,10},{10... | collective-permute-start | bytes 1769480 | tf_op jit(solution)/shard_map/ppermute | solution.py:728
  (77 other events, 721.9 us)

commit v8 on v7

--- a/solution.py
+++ b/solution.py
@@ -756,15 +756,6 @@
     return Pieces(piece[None], [(0, 0, 0)])
 
 
-def dp_sum(total):
-    total = total.astype(F32)
-    bit = 2
-    while bit < lax.axis_size(DP):
-        total = total + swap(total.astype(BF), DP, bit).astype(F32)
-        bit *= 2
-    return total
-
-
 def qkv_plan(cols, heads_cols, parts, spots):
     rows = heads_cols // parts
 
@@ -1087,11 +1078,6 @@
         return self.keep[0].astype(F32) + hold(self.got, *deps)[0].astype(F32)
 
 
-def doubled(value, bit, index):
-    other = swap(value, DP, bit)
-    return jnp.where(index == 0, jnp.stack([value, other]), jnp.stack([other, value]))
-
-
 def halves_summed(kept, got):
     def halves(stack):
         if isinstance(stack, (list, tuple)):
@@ -1101,11 +1087,6 @@
 
     first, second = [a.astype(F32) + b.astype(F32) for a, b in zip(halves(kept), halves(got))]
     return first, second.astype(BF)
-
-
-def core_half(at, shard):
-    rows = shard.shape[0] // 2
-    return lax.dynamic_slice_in_dim(shard, at[2] * rows, rows, axis=0)
 
 
 def quarter(at, shard):

time: 267 us -> 267 us (level)
  no operation moved by 1% of the time
where the time goes in v8:
time: 267 us; the launch traced here: 266 us
  Pallas kernels  122 us (46%)
  starting transfers between devices  58.1 us (22%)
  waiting for transfers between devices  56.8 us (21%)
  other arithmetic  16.6 us (6%)
  local copies, waits for them, and re-layouts  10.9 us (4%)
    ppermute x62, starting transfers between devices, swap(): return lax.ppermute(value, axis, [(i, i ^ bit) for i in range(size)])  58.1 us
    ppermute x62, waiting for transfers between devices, swap(): return lax.ppermute(value, axis, [(i, i ^ bit) for i in range(size)])  56.8 us
    pallas_call x1, Pallas kernels, inner_back_pieces(): call(partial(inner_back_pieces_body, cols), (wide,), [full, spec((D, unit...  14.4 us
    pallas_call x6, Pallas kernels, move_pieces(): pl.pallas_call(partial(build_body, plans, counts, inverse, parts_by), out...  12.4 us
    pallas_call x1, Pallas kernels, attend_back(): pl.pallas_call(attend_back_body, out_shape=struct(triple.shape, BF), grid...  12 us
    pallas_call x1, Pallas kernels, up(): call(up_body, (units // TILE,), [spec((r, D), lambda j: (0, 0)), spec((D,...  10.1 us
    pallas_call x1, Pallas kernels, outer_pieces(): call(partial(outer_pieces_body, cols), (wide,), [spec((r, rows), lambda j...  8.98 us
    pallas_call x1, Pallas kernels, put_rows(): call(partial(put_body, cols, count), (pairs // count,), [rows, rows, spec...  6.79 us
  transfers between devices with their start and end apart: 62, of which 25 were waited for; matrix products, arithmetic and copies ran while one was open for 8% of the time, Pallas kernels for 45%

profile of v8, /device:TPU:0, one launch (start us, length us, event | category | flops | bytes accessed | tf_op | source)
XLA Modules:
  0.0 266.0 jit_solution(10701414330274478403)
XLA Ops:
  2.7 5.1 %collective-permute-start.3 = (bf16[1,96,384]{2,1,0:T(8,128)(2,1)S(1)}, bf16[1,96,384]{2,1,0:T(8,128)(2,1)S(1)}, u32[]{:S(2)}, u32[]{:S(2)}) collective-permute-start(bf16[1,96,384]{2,1,0:T(8,128)(2,1)S(1)} %bitcast.105), channel_id=1, source_target_pairs={{0,6},{2,4},{4,2},{6,0},{1,7},{3,5},{5,3},{7,1},{8,14},{10,12},{12... | collective-permute-start | bytes 221192 | tf_op jit(solution)/shard_map/ppermute | solution.py:728
  18.4 2.7 %collective-permute-start.6 = (bf16[2,208,384]{2,1,0:T(8,128)(2,1)S(1)}, bf16[2,208,384]{2,1,0:T(8,128)(2,1)S(1)}, u32[]{:S(2)}, u32[]{:S(2)}) collective-permute-start(bf16[2,208,384]{2,1,0:T(8,128)(2,1)S(1)} %pad_maximum_fusion.6), channel_id=1, source_target_pairs={{0,4},{2,6},{4,0},{6,2},{1,5},{3,7},{5,1},{7,3},{8,12},{10,14},{12... | collective-permute-start | bytes 958472 | tf_op jit(solution)/shard_map/ppermute | solution.py:728
  21.0 6.7 %shard_map.319 = bf16[1792,384]{1,0:T(8,128)(2,1)S(1)} custom-call(s32[4]{0:T(128)S(1)} %pad_add_fusion.at_ref.x_ref, bf16[1,2408448]{1,0:T(2,128)(2,1)} %patch_ref.1, s32[16,112,1]{2,1,0:T(8,128)S(1)} %copy.38.index_ref), custom_call_target="tpu_custom_call" | custom-call | flops 108000002048 | bytes 1024 | tf_op jit(solution)/shard_map/pallas_call | solution.py:98
  31.2 5.2 %collective-permute-done.6 = bf16[2,208,384]{2,1,0:T(8,128)(2,1)S(1)} collective-permute-done((bf16[2,208,384]{2,1,0:T(8,128)(2,1)S(1)}, bf16[2,208,384]{2,1,0:T(8,128)(2,1)S(1)}, u32[]{:S(2)}, u32[]{:S(2)}) %collective-permute-start.6) | collective-permute-done | bytes 319520 | tf_op jit(solution)/shard_map/ppermute | solution.py:728
  36.6 2.8 %shard_map.320 = bf16[1792,384]{1,0:T(8,128)(2,1)S(1)} custom-call(s32[4]{0:T(128)S(1)} %pad_add_fusion.at_ref.x_ref, bf16[1,602112]{1,0:T(2,128)(2,1)S(1)} %copy-done.25), custom_call_target="tpu_custom_call" | custom-call | flops 108000002048 | bytes 1024 | tf_op jit(solution)/shard_map/pallas_call | solution.py:129
  39.6 2.5 collective-permute-done.5
  42.7 9.3 %collective-permute-done.8 = bf16[4,208,384]{2,1,0:T(8,128)(2,1)S(1)} collective-permute-done((bf16[4,208,384]{2,1,0:T(8,128)(2,1)S(1)}, bf16[4,208,384]{2,1,0:T(8,128)(2,1)S(1)}, u32[]{:S(2)}, u32[]{:S(2)}) %collective-permute-start.8) | collective-permute-done | bytes 639008 | tf_op jit(solution)/shard_map/ppermute | solution.py:728
  65.4 2.7 %shard_map.323.w_ref = bf16[2304,768]{1,0:T(8,128)(2,1)S(1)} custom-call(s32[4]{0:T(128)S(1)} %pad_add_fusion.at_ref.x_ref, s32[3,48]{1,0:T(4,128)S(1)} %copy-done.22, bf16[8,208,384]{2,1,0:T(8,128)(2,1)S(1)} %pad_maximum_fusion.refs_0_, bf16[8,208,384]{2,1,0:T(8,128)(2,1)S(1)} %collective-permute-done.13.refs_1_, ...), custom_call_target="tpu_custom_call" | custom-call | flops 5400000 | bytes 1024 | tf_op jit(solution)/shard_map/pallas_call | solution.py:996
  68.1 4.1 %shard_map.324.triple_ref = bf16[896,2304]{1,0:T(8,128)(2,1)S(1)} custom-call(bf16[896,768]{1,0:T(8,128)(2,1)S(1)} %shard_map.322.hidden_ref, bf16[2304,768]{1,0:T(8,128)(2,1)S(1)} %shard_map.323.w_ref, f32[1,2304]{1,0:T(1,128)S(1)} %get-tuple-element.176.bias_ref), custom_call_target="tpu_custom_call" | custom-call | flops 7020000256 | bytes 1024 | tf_op jit(solution)/shard_map/pallas_call | solution.py:247
  80.1 6.0 %shard_map.325 = (bf16[896,768]{1,0:T(8,128)(2,1)S(1)}, f32[8,12,112,112]{3,2,1,0:T(8,128)}) custom-call(bf16[896,2304]{1,0:T(8,128)(2,1)S(1)} %shard_map.324.triple_ref), custom_call_target="tpu_custom_call" | custom-call | flops 108000002048 | bytes 1024 | tf_op jit(solution)/shard_map/pallas_call | solution.py:302
  86.1 5.4 %collective-permute-done.19 = bf16[4,96,768]{2,1,0:T(8,128)(2,1)S(1)} collective-permute-done((bf16[4,96,768]{2,1,0:T(8,128)(2,1)S(1)}, bf16[4,96,768]{2,1,0:T(8,128)(2,1)S(1)}, u32[]{:S(2)}, u32[]{:S(2)}) %collective-permute-start.19) | collective-permute-done | bytes 589856 | tf_op jit(solution)/shard_map/ppermute | solution.py:728
  95.4 2.8 %shard_map.327 = (f32[896,768]{1,0:T(8,128)S(1)}, bf16[896,768]{1,0:T(8,128)(2,1)S(1)}) custom-call(bf16[896,768]{1,0:T(8,128)(2,1)S(1)} %get-tuple-element.187.mixed_ref, bf16[768,768]{1,0:T(8,128)(2,1)S(1)} %shard_map.326.w_ref, bf16[896,768]{1,0:T(8,128)(2,1)S(1)} %maximum_select_fusion.rows_ref, f32[8,768]{1,0:T(8,128)S(1)} %get-tuple-element.254.vec_ref.x_ref), custom_call_target="tpu_custom_call" | custom-call | flops 8640000000 | bytes 1024 | tf_op jit(solution)/shard_map/pallas_call | solution.py:331
  99.0 2.4 shard_map.328.w_ref
  101.4 10.1 %shard_map.329 = (bf16[896,3072]{1,0:T(8,128)(2,1)}, f32[896,3072]{1,0:T(8,128)}) custom-call(bf16[896,768]{1,0:T(8,128)(2,1)S(1)} %get-tuple-element.188.hidden_ref, bf16[768,3072]{1,0:T(8,128)(2,1)S(1)} %shard_map.328.w_ref, f32[1,3072]{1,0:T(1,128)S(1)} %get-tuple-element.197.bias_ref), custom_call_target="tpu_custom_call" | custom-call | flops 5400000 | bytes 1024 | tf_op jit(solution)/shard_map/pallas_call | solution.py:353
  111.5 9.0 %shard_map.330 = (bf16[4,192,768]{2,1,0:T(8,128)(2,1)}, bf16[4,192,768]{2,1,0:T(8,128)(2,1)}, bf16[4,192,768]{2,1,0:T(8,128)(2,1)S(1)}, bf16[4,192,768]{2,1,0:T(8,128)(2,1)S(1)}) custom-call(s32[4]{0:T(128)S(1)} %pad_add_fusion.at_ref.x_ref, bf16[896,768]{1,0:T(8,128)(2,1)S(1)} %get-tuple-element.288.left_ref.cot_ref, ...), custom_call_target="tpu_custom_call" | custom-call | flops 5400000 | bytes 1024 | tf_op jit(solution)/shard_map/pallas_call | solution.py:477
  131.0 14.4 %shard_map.332 = (bf16[896,3072]{1,0:T(8,128)(2,1)}, bf16[2,4,96,768]{3,2,1,0:T(8,128)(2,1)}, bf16[2,4,96,768]{3,2,1,0:T(8,128)(2,1)}, bf16[2,4,96,768]{3,2,1,0:...) custom-call(s32[4]{0:T(128)S(1)} %pad_add_fusion.at_ref.x_ref, ...), custom_call_target="tpu_custom_call" | custom-call | flops 108000002048 | bytes 1024 | tf_op jit(solution)/shard_map/pallas_call | solution.py:520
  145.4 6.5 %shard_map.333 = bf16[896,768]{1,0:T(8,128)(2,1)S(1)} custom-call(bf16[896,3072]{1,0:T(8,128)(2,1)} %get-tuple-element.213.right_ref.active_ref, bf16[768,3072]{1,0:T(8,128)(2,1)S(1)} %shard_map.331.w_ref, f32[8,768]{1,0:T(8,128)S(1)} %get-tuple-element.254.vec_ref.x_ref, f32[896,768]{1,0:T(8,128)S(1)} %get-tuple-element.214.middle_ref), custom_call_target="tpu_custom_call" | custom-call | flops 5400000 | bytes 1024 | tf_op jit(solution)/shard_map/pallas_call | solution.py:376
  155.5 2.6 collective-permute-done.31
  163.6 6.4 %shard_map.334 = (f32[896,768]{1,0:T(8,128)S(1)}, bf16[896,768]{1,0:T(8,128)(2,1)S(1)}, f32[1,768]{1,0:T(1,128)S(1)}, f32[1,768]{1,0:T(1,128)S(1)}, f32[1,768]{1,0:T(1,128)S(1)}) custom-call(bf16[896,3072]{1,0:T(8,128)(2,1)S(1)} %copy-done.30, bf16[768,3072]{1,0:T(8,128)(2,1)S(1)} %bitcast.89, f32[896,768]{1,0:T(8,128)S(1)} %copy-done.10, ...), custom_call_target="tpu_custom_call" | custom-call | flops 108000002048 | bytes 1024 | tf_op jit(solution)/shard_map/pallas_call | solution.py:583
  170.1 2.5 shard_map.335
  178.2 12.0 %shard_map.336.grad_ref = bf16[896,2304]{1,0:T(8,128)(2,1)S(1)} custom-call(bf16[896,2304]{1,0:T(8,128)(2,1)S(1)} %copy-done.8, f32[8,12,112,112]{3,2,1,0:T(8,128)} %get-tuple-element.215.prob_ref, bf16[896,768]{1,0:T(8,128)(2,1)S(1)} %get-tuple-element.230.grad_ref), custom_call_target="tpu_custom_call" | custom-call | flops 5400000 | bytes 1024 | tf_op jit(solution)/shard_map/pallas_call | solution.py:648
  190.2 5.2 %shard_map.337 = (f32[896,768]{1,0:T(8,128)S(1)}, f32[1,768]{1,0:T(1,128)S(1)}, f32[1,768]{1,0:T(1,128)S(1)}) custom-call(bf16[896,2304]{1,0:T(8,128)(2,1)S(1)} %shard_map.336.grad_ref, bf16[2304,768]{1,0:T(8,128)(2,1)S(1)} %copy-done.2, bf16[896,768]{1,0:T(8,128)(2,1)S(1)} %copy-done.4, f32[896,768]{1,0:T(8,128)S(1)} %get-tuple-element.231.middle_ref, ...), custom_call_target="tpu_custom_call" | custom-call | flops 5400000 | bytes 1024 | tf_op jit(solution)/shard_map/pallas_call | solution.py:706
  198.4 4.8 %shard_map.338 = (bf16[2304,768]{1,0:T(8,128)(2,1)S(1)}, f32[1,2304]{1,0:T(1,128)S(1)}) custom-call(bf16[896,2304]{1,0:T(8,128)(2,1)S(1)} %shard_map.336.grad_ref, bf16[896,768]{1,0:T(8,128)(2,1)S(1)} %copy-done.29), custom_call_target="tpu_custom_call" | custom-call | flops 108000002048 | bytes 1024 | tf_op jit(solution)/shard_map/pallas_call | solution.py:680
  206.2 2.7 %shard_map.339 = (bf16[16,144,384]{2,1,0:T(8,128)(2,1)}, bf16[16,144,384]{2,1,0:T(8,128)(2,1)S(1)}) custom-call(s32[4]{0:T(128)S(1)} %copy-done.18, s32[3,32]{1,0:T(4,128)S(1)} %copy-done.19, bf16[2304,768]{1,0:T(8,128)(2,1)S(1)} %get-tuple-element.239.refs_0_), custom_call_target="tpu_custom_call" | custom-call | flops 5400000 | bytes 1024 | tf_op jit(solution)/shard_map/pallas_call | solution.py:996
  209.0 2.5 collective-permute-done.40
  211.6 2.7 %collective-permute-start.43 = (bf16[2,96,768]{2,1,0:T(8,128)(2,1)S(1)}, bf16[2,96,768]{2,1,0:T(8,128)(2,1)S(1)}, u32[]{:S(2)}, u32[]{:S(2)}) collective-permute-start(bf16[2,96,768]{2,1,0:T(8,128)(2,1)S(1)} %get-tuple-element.300), channel_id=1, source_target_pairs={{0,2},{2,0},{4,6},{6,4},{1,3},{3,1},{5,7},{7,5},{8,10},{10,8},{12,... | collective-permute-start | bytes 884744 | tf_op jit(solution)/shard_map/ppermute | solution.py:728
  220.5 5.7 %collective-permute-done.42.got_ref = bf16[896,384]{1,0:T(8,128)(2,1)S(1)} collective-permute-done((bf16[896,384]{1,0:T(8,128)(2,1)S(1)}, bf16[896,384]{1,0:T(8,128)(2,1)S(1)}, u32[]{:S(2)}, u32[]{:S(2)}) %collective-permute-start.42) | collective-permute-done | bytes 688160 | tf_op jit(solution)/shard_map/ppermute | solution.py:728
  226.2 6.8 %shard_map.343 = f32[18816,128]{1,0:T(8,128)} custom-call(s32[4]{0:T(128)S(1)} %copy-done.18, f32[896,384]{1,0:T(8,128)S(1)} %constant_dynamic-slice_fusion.keep_ref, bf16[896,384]{1,0:T(8,128)(2,1)S(1)} %collective-permute-done.42.got_ref, s32[16,112,1]{2,1,0:T(8,128)S(1)} %copy-done.16), custom_call_target="tpu_custom_call" | custom-call | flops 108000002048 | bytes 1024 | tf_op jit(solution)/shard_map/pallas_call | solution.py:169
  236.6 2.4 collective-permute-start.53
  242.5 3.6 %shard_map.344 = bf16[1,602112]{1,0:T(2,128)(2,1)} custom-call(s32[4]{0:T(128)S(1)} %copy-done.18, bf16[896,384]{1,0:T(8,128)(2,1)S(1)} %get-tuple-element.263.keep_ref, bf16[896,384]{1,0:T(8,128)(2,1)S(1)} %copy-done.27), custom_call_target="tpu_custom_call" | custom-call | flops 108000002048 | bytes 1024 | tf_op jit(solution)/shard_map/pallas_call | solution.py:196
  247.8 2.4 collective-permute-start.50
  254.4 2.3 collective-permute-done.49
  (288 shorter events, 102.0 us)
Async XLA Ops:
  2.7 9.5 %collective-permute-start.3 = (bf16[1,96,384]{2,1,0:T(8,128)(2,1)S(1)}, bf16[1,96,384]{2,1,0:T(8,128)(2,1)S(1)}, u32[]{:S(2)}, u32[]{:S(2)}) collective-permute-start(bf16[1,96,384]{2,1,0:T(8,128)(2,1)S(1)} %bitcast.105), channel_id=1, source_target_pairs={{0,6},{2,4},{4,2},{6,0},{1,7},{3,5},{5,3},{7,1},{8,14},{10,12},{12... | collective-permute-start | bytes 221192 | tf_op jit(solution)/shard_map/ppermute | solution.py:728
  14.1 15.5 %collective-permute-start.7 = (bf16[4,96,384]{2,1,0:T(8,128)(2,1)S(1)}, bf16[4,96,384]{2,1,0:T(8,128)(2,1)S(1)}, u32[]{:S(2)}, u32[]{:S(2)}) collective-permute-start(bf16[4,96,384]{2,1,0:T(8,128)(2,1)S(1)} %pad_maximum_fusion.7), channel_id=1, source_target_pairs={{0,1},{1,0},{2,3},{3,2},{4,5},{5,4},{6,7},{7,6},{8,9},{9,8},{10,11... | collective-permute-start | bytes 884744 | tf_op jit(solution)/shard_map/ppermute | solution.py:728
  18.4 18.1 %collective-permute-start.6 = (bf16[2,208,384]{2,1,0:T(8,128)(2,1)S(1)}, bf16[2,208,384]{2,1,0:T(8,128)(2,1)S(1)}, u32[]{:S(2)}, u32[]{:S(2)}) collective-permute-start(bf16[2,208,384]{2,1,0:T(8,128)(2,1)S(1)} %pad_maximum_fusion.6), channel_id=1, source_target_pairs={{0,4},{2,6},{4,0},{6,2},{1,5},{3,7},{5,1},{7,3},{8,12},{10,14},{12... | collective-permute-start | bytes 958472 | tf_op jit(solution)/shard_map/ppermute | solution.py:728
  27.9 14.2 %collective-permute-start.5 = (bf16[896,384]{1,0:T(8,128)(2,1)S(1)}, bf16[896,384]{1,0:T(8,128)(2,1)S(1)}, u32[]{:S(2)}, u32[]{:S(2)}) collective-permute-start(bf16[896,384]{1,0:T(8,128)(2,1)S(1)} %get-tuple-element.308), channel_id=1, source_target_pairs={{0,1},{1,0},{2,3},{3,2},{4,5},{5,4},{6,7},{7,6},{8,9},{9,8},{10,11... | collective-permute-start | bytes 2064392 | tf_op jit(solution)/shard_map/ppermute | solution.py:728
  29.5 9.9 %collective-permute-start.10 = (bf16[1,48,768]{2,1,0:T(8,128)(2,1)S(1)}, bf16[1,48,768]{2,1,0:T(8,128)(2,1)S(1)}, u32[]{:S(2)}, u32[]{:S(2)}) collective-permute-start(bf16[1,48,768]{2,1,0:T(8,128)(2,1)S(1)} %bitcast.98), channel_id=1, source_target_pairs={{0,4},{2,6},{4,0},{6,2},{1,5},{3,7},{5,1},{7,3},{8,12},{10,14},{12... | collective-permute-start | bytes 221192 | tf_op jit(solution)/shard_map/ppermute | solution.py:728
  29.6 13.0 %collective-permute-start.9 = (bf16[8,96,384]{2,1,0:T(8,128)(2,1)S(1)}, bf16[8,96,384]{2,1,0:T(8,128)(2,1)S(1)}, u32[]{:S(2)}, u32[]{:S(2)}) collective-permute-start(bf16[8,96,384]{2,1,0:T(8,128)(2,1)S(1)} %get-tuple-element.316), channel_id=1, source_target_pairs={{0,16},{8,24},{16,0},{24,8},{1,17},{9,25},{17,1},{25,9},{2,18},{10... | collective-permute-start | bytes 1769480 | tf_op jit(solution)/shard_map/ppermute | solution.py:728
  36.5 15.5 %collective-permute-start.8 = (bf16[4,208,384]{2,1,0:T(8,128)(2,1)S(1)}, bf16[4,208,384]{2,1,0:T(8,128)(2,1)S(1)}, u32[]{:S(2)}, u32[]{:S(2)}) collective-permute-start(bf16[4,208,384]{2,1,0:T(8,128)(2,1)S(1)} %pad_maximum_fusion.2), channel_id=1, source_target_pairs={{0,2},{2,0},{4,6},{6,4},{1,3},{3,1},{5,7},{7,5},{8,10},{10,8},{12,... | collective-permute-start | bytes 1916936 | tf_op jit(solution)/shard_map/ppermute | solution.py:728
  53.1 19.2 %collective-permute-start.18 = (bf16[896,384]{1,0:T(8,128)(2,1)S(1)}, bf16[896,384]{1,0:T(8,128)(2,1)S(1)}, u32[]{:S(2)}, u32[]{:S(2)}) collective-permute-start(bf16[896,384]{1,0:T(8,128)(2,1)S(1)} %get-tuple-element.163), channel_id=1, source_target_pairs={{0,1},{1,0},{2,3},{3,2},{4,5},{5,4},{6,7},{7,6},{8,9},{9,8},{10,11... | collective-permute-start | bytes 2064392 | tf_op jit(solution)/shard_map/ppermute | solution.py:728
  55.9 9.5 %collective-permute-start.13 = (bf16[8,208,384]{2,1,0:T(8,128)(2,1)S(1)}, bf16[8,208,384]{2,1,0:T(8,128)(2,1)S(1)}, u32[]{:S(2)}, u32[]{:S(2)}) collective-permute-start(bf16[8,208,384]{2,1,0:T(8,128)(2,1)S(1)} %pad_maximum_fusion.refs_0_), channel_id=1, source_target_pairs={{0,8},{8,0},{16,24},{24,16},{1,9},{9,1},{17,25},{25,17},{2,10},{10... | collective-permute-start | bytes 3833864 | tf_op jit(solution)/shard_map/ppermute | solution.py:728
  61.5 12.9 %collective-permute-start.17 = (bf16[2,96,768]{2,1,0:T(8,128)(2,1)S(1)}, bf16[2,96,768]{2,1,0:T(8,128)(2,1)S(1)}, u32[]{:S(2)}, u32[]{:S(2)}) collective-permute-start(bf16[2,96,768]{2,1,0:T(8,128)(2,1)S(1)} %copy-done.41), channel_id=1, source_target_pairs={{0,4},{2,6},{4,0},{6,2},{1,5},{3,7},{5,1},{7,3},{8,12},{10,14},{12... | collective-permute-start | bytes 884744 | tf_op jit(solution)/shard_map/ppermute | solution.py:728
  62.2 12.8 %collective-permute-start.16 = (bf16[4,48,768]{2,1,0:T(8,128)(2,1)S(1)}, bf16[4,48,768]{2,1,0:T(8,128)(2,1)S(1)}, u32[]{:S(2)}, u32[]{:S(2)}) collective-permute-start(bf16[4,48,768]{2,1,0:T(8,128)(2,1)S(1)} %pad_maximum_fusion.10), channel_id=1, source_target_pairs={{0,1},{1,0},{2,3},{3,2},{4,5},{5,4},{6,7},{7,6},{8,9},{9,8},{10,11... | collective-permute-start | bytes 884744 | tf_op jit(solution)/shard_map/ppermute | solution.py:728
  63.7 13.0 %collective-permute-start.15 = (bf16[2,96,768]{2,1,0:T(8,128)(2,1)S(1)}, bf16[2,96,768]{2,1,0:T(8,128)(2,1)S(1)}, u32[]{:S(2)}, u32[]{:S(2)}) collective-permute-start(bf16[2,96,768]{2,1,0:T(8,128)(2,1)S(1)} %pad_maximum_fusion.9), channel_id=1, source_target_pairs={{0,2},{2,0},{4,6},{6,4},{1,3},{3,1},{5,7},{7,5},{8,10},{10,8},{12,... | collective-permute-start | bytes 884744 | tf_op jit(solution)/shard_map/ppermute | solution.py:728
  78.0 16.4 %collective-permute-start.20 = (bf16[4,96,768]{2,1,0:T(8,128)(2,1)S(1)}, bf16[4,96,768]{2,1,0:T(8,128)(2,1)S(1)}, u32[]{:S(2)}, u32[]{:S(2)}) collective-permute-start(bf16[4,96,768]{2,1,0:T(8,128)(2,1)S(1)} %get-tuple-element.189.refs_0_), channel_id=1, source_target_pairs={{0,1},{1,0},{2,3},{3,2},{4,5},{5,4},{6,7},{7,6},{8,9},{9,8},{10,11... | collective-permute-start | bytes 1769480 | tf_op jit(solution)/shard_map/ppermute | solution.py:728
  78.5 13.0 %collective-permute-start.19 = (bf16[4,96,768]{2,1,0:T(8,128)(2,1)S(1)}, bf16[4,96,768]{2,1,0:T(8,128)(2,1)S(1)}, u32[]{:S(2)}, u32[]{:S(2)}) collective-permute-start(bf16[4,96,768]{2,1,0:T(8,128)(2,1)S(1)} %get-tuple-element.330), channel_id=1, source_target_pairs={{0,2},{2,0},{4,6},{6,4},{1,3},{3,1},{5,7},{7,5},{8,10},{10,8},{12,... | collective-permute-start | bytes 1769480 | tf_op jit(solution)/shard_map/ppermute | solution.py:728
  78.5 15.8 %collective-permute-start.21 = (bf16[8,48,768]{2,1,0:T(8,128)(2,1)S(1)}, bf16[8,48,768]{2,1,0:T(8,128)(2,1)S(1)}, u32[]{:S(2)}, u32[]{:S(2)}) collective-permute-start(bf16[8,48,768]{2,1,0:T(8,128)(2,1)S(1)} %pad_maximum_fusion.4.refs_4_), channel_id=1, source_target_pairs={{0,16},{8,24},{16,0},{24,8},{1,17},{9,25},{17,1},{25,9},{2,18},{10... | collective-permute-start | bytes 1769480 | tf_op jit(solution)/shard_map/ppermute | solution.py:728
  91.6 28.8 %collective-permute-start.26 = (bf16[8,96,768]{2,1,0:T(8,128)(2,1)S(1)}, bf16[8,96,768]{2,1,0:T(8,128)(2,1)S(1)}, u32[]{:S(2)}, u32[]{:S(2)}) collective-permute-start(bf16[8,96,768]{2,1,0:T(8,128)(2,1)S(1)} %pad_maximum_fusion.1.refs_0_), channel_id=1, source_target_pairs={{0,16},{8,24},{16,0},{24,8},{1,17},{9,25},{17,1},{25,9},{2,18},{10... | collective-permute-start | bytes 3538952 | tf_op jit(solution)/shard_map/ppermute | solution.py:728
  129.7 28.3 %collective-permute-start.31 = (bf16[4,192,768]{2,1,0:T(8,128)(2,1)}, bf16[4,192,768]{2,1,0:T(8,128)(2,1)}, u32[]{:S(2)}, u32[]{:S(2)}) collective-permute-start(bf16[4,192,768]{2,1,0:T(8,128)(2,1)} %add_convert_fusion), channel_id=1, source_target_pairs={{0,1},{1,0},{2,3},{3,2},{4,5},{5,4},{6,7},{7,6},{8,9},{9,8},{10,11... | collective-permute-start | bytes 3538952 | tf_op jit(solution)/shard_map/ppermute | solution.py:728
  159.8 14.6 %collective-permute-start.34 = (bf16[2,192,768]{2,1,0:T(8,128)(2,1)S(1)}, bf16[2,192,768]{2,1,0:T(8,128)(2,1)S(1)}, u32[]{:S(2)}, u32[]{:S(2)}) collective-permute-start(bf16[2,192,768]{2,1,0:T(8,128)(2,1)S(1)} %get-tuple-element.296), channel_id=1, source_target_pairs={{0,2},{2,0},{4,6},{6,4},{1,3},{3,1},{5,7},{7,5},{8,10},{10,8},{12,... | collective-permute-start | bytes 1769480 | tf_op jit(solution)/shard_map/ppermute | solution.py:728
  162.0 34.5 %collective-permute-start.36 = (bf16[8,96,768]{2,1,0:T(8,128)(2,1)S(1)}, bf16[8,96,768]{2,1,0:T(8,128)(2,1)S(1)}, u32[]{:S(2)}, u32[]{:S(2)}) collective-permute-start(bf16[8,96,768]{2,1,0:T(8,128)(2,1)S(1)} %fusion), channel_id=1, source_target_pairs={{0,16},{8,24},{16,0},{24,8},{1,17},{9,25},{17,1},{25,9},{2,18},{10... | collective-permute-start | bytes 3538952 | tf_op jit(solution)/shard_map/ppermute | solution.py:728
  172.6 23.0 %collective-permute-start.37 = (bf16[896,384]{1,0:T(8,128)(2,1)S(1)}, bf16[896,384]{1,0:T(8,128)(2,1)S(1)}, u32[]{:S(2)}, u32[]{:S(2)}) collective-permute-start(bf16[896,384]{1,0:T(8,128)(2,1)S(1)} %get-tuple-element.229), channel_id=1, source_target_pairs={{0,1},{1,0},{2,3},{3,2},{4,5},{5,4},{6,7},{7,6},{8,9},{9,8},{10,11... | collective-permute-start | bytes 2064392 | tf_op jit(solution)/shard_map/ppermute | solution.py:728
  174.5 21.1 %collective-permute-start.35 = (bf16[1,192,768]{2,1,0:T(8,128)(2,1)S(1)}, bf16[1,192,768]{2,1,0:T(8,128)(2,1)S(1)}, u32[]{:S(2)}, u32[]{:S(2)}) collective-permute-start(bf16[1,192,768]{2,1,0:T(8,128)(2,1)S(1)} %fusion.8), channel_id=1, source_target_pairs={{0,4},{2,6},{4,0},{6,2},{1,5},{3,7},{5,1},{7,3},{8,12},{10,14},{12... | collective-permute-start | bytes 884744 | tf_op jit(solution)/shard_map/ppermute | solution.py:728
  196.8 14.7 %collective-permute-start.40 = (bf16[4,96,768]{2,1,0:T(8,128)(2,1)S(1)}, bf16[4,96,768]{2,1,0:T(8,128)(2,1)S(1)}, u32[]{:S(2)}, u32[]{:S(2)}) collective-permute-start(bf16[4,96,768]{2,1,0:T(8,128)(2,1)S(1)} %get-tuple-element.294), channel_id=1, source_target_pairs={{0,1},{1,0},{2,3},{3,2},{4,5},{5,4},{6,7},{7,6},{8,9},{9,8},{10,11... | collective-permute-start | bytes 1769480 | tf_op jit(solution)/shard_map/ppermute | solution.py:728
  205.0 13.0 %collective-permute-start.44 = (bf16[8,112,384]{2,1,0:T(8,128)(2,1)S(1)}, bf16[8,112,384]{2,1,0:T(8,128)(2,1)S(1)}, u32[]{:S(2)}, u32[]{:S(2)}) collective-permute-start(bf16[8,112,384]{2,1,0:T(8,128)(2,1)S(1)} %get-tuple-element.250), channel_id=1, source_target_pairs={{0,8},{8,0},{16,24},{24,16},{1,9},{9,1},{17,25},{25,17},{2,10},{10... | collective-permute-start | bytes 2064392 | tf_op jit(solution)/shard_map/ppermute | solution.py:728
  205.7 20.5 %collective-permute-start.42 = (bf16[896,384]{1,0:T(8,128)(2,1)S(1)}, bf16[896,384]{1,0:T(8,128)(2,1)S(1)}, u32[]{:S(2)}, u32[]{:S(2)}) collective-permute-start(bf16[896,384]{1,0:T(8,128)(2,1)S(1)} %constant_dynamic-slice_fusion.1), channel_id=1, source_target_pairs={{0,1},{1,0},{2,3},{3,2},{4,5},{5,4},{6,7},{7,6},{8,9},{9,8},{10,11... | collective-permute-start | bytes 2064392 | tf_op jit(solution)/shard_map/ppermute | solution.py:728
  216.6 18.3 %collective-permute-start.41 = (bf16[8,144,384]{2,1,0:T(8,128)(2,1)S(1)}, bf16[8,144,384]{2,1,0:T(8,128)(2,1)S(1)}, u32[]{:S(2)}, u32[]{:S(2)}) collective-permute-start(bf16[8,144,384]{2,1,0:T(8,128)(2,1)S(1)} %get-tuple-element.291), channel_id=1, source_target_pairs={{0,16},{8,24},{16,0},{24,8},{1,17},{9,25},{17,1},{25,9},{2,18},{10... | collective-permute-start | bytes 2654216 | tf_op jit(solution)/shard_map/ppermute | solution.py:728
  218.2 18.4 %collective-permute-start.46 = (bf16[4,112,384]{2,1,0:T(8,128)(2,1)S(1)}, bf16[4,112,384]{2,1,0:T(8,128)(2,1)S(1)}, u32[]{:S(2)}, u32[]{:S(2)}) collective-permute-start(bf16[4,112,384]{2,1,0:T(8,128)(2,1)S(1)} %get-tuple-element.302), channel_id=1, source_target_pairs={{0,1},{1,0},{2,3},{3,2},{4,5},{5,4},{6,7},{7,6},{8,9},{9,8},{10,11... | collective-permute-start | bytes 1032200 | tf_op jit(solution)/shard_map/ppermute | solution.py:728
  219.5 21.6 %collective-permute-start.45 = (bf16[1,96,768]{2,1,0:T(8,128)(2,1)S(1)}, bf16[1,96,768]{2,1,0:T(8,128)(2,1)S(1)}, u32[]{:S(2)}, u32[]{:S(2)}) collective-permute-start(bf16[1,96,768]{2,1,0:T(8,128)(2,1)S(1)} %fusion.10), channel_id=1, source_target_pairs={{0,4},{2,6},{4,0},{6,2},{1,5},{3,7},{5,1},{7,3},{8,12},{10,14},{12... | collective-permute-start | bytes 442376 | tf_op jit(solution)/shard_map/ppermute | solution.py:728
  235.0 12.7 %collective-permute-start.47 = (bf16[4,144,384]{2,1,0:T(8,128)(2,1)S(1)}, bf16[4,144,384]{2,1,0:T(8,128)(2,1)S(1)}, u32[]{:S(2)}, u32[]{:S(2)}) collective-permute-start(bf16[4,144,384]{2,1,0:T(8,128)(2,1)S(1)} %get-tuple-element.298), channel_id=1, source_target_pairs={{0,1},{1,0},{2,3},{3,2},{4,5},{5,4},{6,7},{7,6},{8,9},{9,8},{10,11... | collective-permute-start | bytes 1327112 | tf_op jit(solution)/shard_map/ppermute | solution.py:728
  236.6 9.4 %collective-permute-start.53 = (bf16[112,384]{1,0:T(8,128)(2,1)S(1)}, bf16[112,384]{1,0:T(8,128)(2,1)S(1)}, u32[]{:S(2)}, u32[]{:S(2)}) collective-permute-start(bf16[112,384]{1,0:T(8,128)(2,1)S(1)} %get-tuple-element.312), channel_id=1, source_target_pairs={{0,6},{2,4},{4,2},{6,0},{1,7},{3,5},{5,3},{7,1},{8,14},{10,12},{12... | collective-permute-start | bytes 258056 | tf_op jit(solution)/shard_map/ppermute | solution.py:728
  241.9 10.9 %collective-permute-start.59 = (bf16[96,768]{1,0:T(8,128)(2,1)}, bf16[96,768]{1,0:T(8,128)(2,1)}, u32[]{:S(2)}, u32[]{:S(2)}) collective-permute-start(bf16[96,768]{1,0:T(8,128)(2,1)} %get-tuple-element.281), channel_id=1, source_target_pairs={{0,16},{8,24},{16,0},{24,8},{1,17},{9,25},{17,1},{25,9},{2,18},{10... | collective-permute-start | bytes 442376 | tf_op jit(solution)/shard_map/ppermute | solution.py:728
  246.2 12.6 %collective-permute-start.57 = (bf16[112,384]{1,0:T(8,128)(2,1)S(1)}, bf16[112,384]{1,0:T(8,128)(2,1)S(1)}, u32[]{:S(2)}, u32[]{:S(2)}) collective-permute-start(bf16[112,384]{1,0:T(8,128)(2,1)S(1)} %get-tuple-element.283), channel_id=1, source_target_pairs={{0,16},{8,24},{16,0},{24,8},{1,17},{9,25},{17,1},{25,9},{2,18},{10... | collective-permute-start | bytes 258056 | tf_op jit(solution)/shard_map/ppermute | solution.py:728
  253.9 11.0 %collective-permute-start.60 = (f32[2,96,768]{2,1,0:T(8,128)S(1)}, f32[2,96,768]{2,1,0:T(8,128)S(1)}, u32[]{:S(2)}, u32[]{:S(2)}) collective-permute-start(f32[2,96,768]{2,1,0:T(8,128)S(1)} %maximum_select_fusion.6), channel_id=1, source_target_pairs={{0,8},{8,0},{16,24},{24,16},{1,9},{9,1},{17,25},{25,17},{2,10},{10... | collective-permute-start | bytes 1769480 | tf_op jit(solution)/shard_map/ppermute | solution.py:728
  (77 other events, 721.9 us)

commit v9 on v8

--- a/solution.py
+++ b/solution.py
@@ -107,6 +107,7 @@
         [pltpu.VMEM((width // 128, 128), F32)],
         prefetch=1,
         us=200,
+        vmem=16,
         nbytes=pairs * width * 4,
     )(at, patches, index)
 
@@ -135,6 +136,7 @@
         [pltpu.VMEM((width // 128, 128), F32)],
         prefetch=1,
         us=200,
+        vmem=12,
         nbytes=pairs * width * 4,
     )(at, cotangent)
 
@@ -174,6 +176,7 @@
         struct((pairs // count * tall, 128), F32),
         prefetch=1,
         us=200,
+        vmem=14,
         nbytes=pairs * (tall * 512 + ROWS * cols * 4),
     )(at, keep, got, index)
 
@@ -202,6 +205,7 @@
         [pltpu.VMEM((width // 128, 128), F32)],
         prefetch=1,
         us=200,
+        vmem=12,
         nbytes=pairs * width * 6,
     )(at, keep, got)
 
@@ -234,6 +238,7 @@
         spec((ROWS, D), lambda i: (i, 0)),
         struct((r, D), BF),
         us=200,
+        vmem=10,
         nbytes=r * D * 4,
     )(rows, vec)
 
@@ -255,6 +260,7 @@
         spec((r, TILE), lambda j: (0, j)),
         struct((r, 3 * D), BF),
         us=13,
+        vmem=16,
         nbytes=r * D * 8 + 3 * D * D * 2,
     )(hidden, w, bias)
 
@@ -306,6 +312,7 @@
         [spec((ROWS, D), lambda g: (g, 0)), spec((1, HEADS, ROWS, ROWS), lambda g: (g, 0, 0, 0))],
         [struct((groups * ROWS, D), BF), pltpu.HBM((groups, HEADS, ROWS, ROWS), F32)],
         us=200,
+        vmem=16,
         nbytes=groups * ROWS * (8 * D + HEADS * 512),
     )(triple)
 
@@ -335,6 +342,7 @@
         [row, row],
         [struct((r, D), F32), struct((r, D), BF)],
         us=16,
+        vmem=16,
         nbytes=r * D * 10 + D * D * 2,
     )(mixed, w, rows, vec)
 
@@ -618,6 +626,7 @@
         [struct((r, D), BF), struct((D, D), BF)],
         [pltpu.VMEM((D, r), BF)],
         us=0.01,
+        vmem=16,
         nbytes=r * D * 8 + D * D * 4,
     )(branch, branch, w, mixed)
 
@@ -661,7 +670,7 @@
         ),
         input_output_aliases={3: 0} if given else {},
         compiler_params=pltpu.CompilerParams(
-            dimension_semantics=("arbitrary",), vmem_limit_bytes=24 * MB
+            dimension_semantics=("arbitrary",), vmem_limit_bytes=16 * MB
         ),
         cost_estimate=pl.CostEstimate(
             flops=FLOPS_PER_US // 100, bytes_accessed=1024, transcendentals=0
@@ -684,6 +693,7 @@
         [spec((TILE, D), lambda j: (j, 0)), spec((1, TILE), lambda j: (0, j))],
         [struct((width, D), BF), struct((1, width), F32)],
         us=200,
+        vmem=16,
         nbytes=r * width * 2 + r * D * 2 + width * D * 2,
     )(grad, hidden)
 
@@ -716,6 +726,7 @@
         [row, vec, vec],
         [struct((r, D), F32), vec_out, vec_out],
         us=0.01,
+        vmem=22,
         nbytes=r * width * 2 + D * width * 2 + r * D * 10,
     )(grad, w, rows, grad_middle, vecs)
 
@@ -1210,7 +1221,7 @@
         v_z = v_p.fetch(WIDE, 2, rows_send)
         rows_got = swap(rows_send, NARROW, 1)
         cot_out = cot_rows(hold(at, rows_send, a_p.stack, b_p.stack), cotangent, pairs, cols)
-        a_p, b_p = a_p.join(a_z.after(cot_out)), b_p.join(b_y.after(cot_out))
+        a_p, b_p = a_p.join(a_z.after(cot_out)), b_p.after(cot_out).join(b_y.after(cot_out))
         v_p = v_p.join(v_z.after(cot_out))
         rows = join_cols(rows_out[own:], hold(rows_got, cot_out))
 

time: 267 us -> 267 us (level)
  starting transfers between devices: 58.1 us -> 62.7 us
    ppermute x62, starting transfers between devices: 58.1 us -> 62.7 us  [swap(): return lax.ppermute(value, axis, [(i, i ^ bit) for i in range(size)])]
    unnamed x99 -> x97, local copies, waits for them, and re-layouts: 5.57 us -> 3.01 us
  transfers between devices with their start and end apart: 62 -> 62, of which waited for: 25 -> 22; matrix products, arithmetic and copies ran while one was open for 8% -> 7% of each run, Pallas kernels for 45% -> 45%
where the time goes in v9:
time: 267 us; the launch traced here: 266 us
  Pallas kernels  122 us (46%)
  starting transfers between devices  62.7 us (23%)
  waiting for transfers between devices  54.7 us (20%)
  other arithmetic  16.7 us (6%)
  local copies, waits for them, and re-layouts  8.38 us (3%)
    ppermute x62, starting transfers between devices, swap(): return lax.ppermute(value, axis, [(i, i ^ bit) for i in range(size)])  62.7 us
    ppermute x62, waiting for transfers between devices, swap(): return lax.ppermute(value, axis, [(i, i ^ bit) for i in range(size)])  54.7 us
    pallas_call x1, Pallas kernels, inner_back_pieces(): call(partial(inner_back_pieces_body, cols), (wide,), [full, spec((D, unit...  14.4 us
    pallas_call x6, Pallas kernels, move_pieces(): pl.pallas_call(partial(build_body, plans, counts, inverse, parts_by), out...  12.4 us
    pallas_call x1, Pallas kernels, attend_back(): pl.pallas_call(attend_back_body, out_shape=struct(triple.shape, BF), grid...  12 us
    pallas_call x1, Pallas kernels, up(): call(up_body, (units // TILE,), [spec((r, D), lambda j: (0, 0)), spec((D,...  10.1 us
    pallas_call x1, Pallas kernels, outer_pieces(): call(partial(outer_pieces_body, cols), (wide,), [spec((r, rows), lambda j...  8.98 us
    pallas_call x1, Pallas kernels, put_rows(): call(partial(put_body, cols, count), (pairs // count,), [rows, rows, spec...  6.78 us
  transfers between devices with their start and end apart: 62, of which 22 were waited for; matrix products, arithmetic and copies ran while one was open for 7% of the time, Pallas kernels for 45%

profile of v9, /device:TPU:0, one launch (start us, length us, event | category | flops | bytes accessed | tf_op | source)
XLA Modules:
  0.0 266.2 jit_solution(12304413796134936068)
XLA Ops:
  2.7 5.1 %collective-permute-start.3 = (bf16[1,96,384]{2,1,0:T(8,128)(2,1)S(1)}, bf16[1,96,384]{2,1,0:T(8,128)(2,1)S(1)}, u32[]{:S(2)}, u32[]{:S(2)}) collective-permute-start(bf16[1,96,384]{2,1,0:T(8,128)(2,1)S(1)} %bitcast.104), channel_id=1, source_target_pairs={{0,6},{2,4},{4,2},{6,0},{1,7},{3,5},{5,3},{7,1},{8,14},{10,12},{12... | collective-permute-start | bytes 221192 | tf_op jit(solution)/shard_map/ppermute | solution.py:739
  11.6 2.4 collective-permute-done.2
  17.6 3.5 %collective-permute-start.6 = (bf16[2,208,384]{2,1,0:T(8,128)(2,1)S(1)}, bf16[2,208,384]{2,1,0:T(8,128)(2,1)S(1)}, u32[]{:S(2)}, u32[]{:S(2)}) collective-permute-start(bf16[2,208,384]{2,1,0:T(8,128)(2,1)S(1)} %pad_maximum_fusion.6), channel_id=1, source_target_pairs={{0,4},{2,6},{4,0},{6,2},{1,5},{3,7},{5,1},{7,3},{8,12},{10,14},{12... | collective-permute-start | bytes 958472 | tf_op jit(solution)/shard_map/ppermute | solution.py:739
  21.0 6.7 %shard_map.319 = bf16[1792,384]{1,0:T(8,128)(2,1)S(1)} custom-call(s32[4]{0:T(128)S(1)} %pad_add_fusion.at_ref.x_ref, bf16[1,2408448]{1,0:T(2,128)(2,1)} %patch_ref.1, s32[16,112,1]{2,1,0:T(8,128)S(1)} %copy.38.index_ref), custom_call_target="tpu_custom_call" | custom-call | flops 108000002048 | bytes 1024 | tf_op jit(solution)/shard_map/pallas_call | solution.py:98
  31.2 3.1 %collective-permute-done.6 = bf16[2,208,384]{2,1,0:T(8,128)(2,1)S(1)} collective-permute-done((bf16[2,208,384]{2,1,0:T(8,128)(2,1)S(1)}, bf16[2,208,384]{2,1,0:T(8,128)(2,1)S(1)}, u32[]{:S(2)}, u32[]{:S(2)}) %collective-permute-start.6) | collective-permute-done | bytes 319520 | tf_op jit(solution)/shard_map/ppermute | solution.py:739
  35.4 2.8 %shard_map.320 = bf16[1792,384]{1,0:T(8,128)(2,1)S(1)} custom-call(s32[4]{0:T(128)S(1)} %pad_add_fusion.at_ref.x_ref, bf16[1,602112]{1,0:T(2,128)(2,1)S(1)} %copy-done.25), custom_call_target="tpu_custom_call" | custom-call | flops 108000002048 | bytes 1024 | tf_op jit(solution)/shard_map/pallas_call | solution.py:130
  38.5 3.2 %collective-permute-done.5 = bf16[896,384]{1,0:T(8,128)(2,1)S(1)} collective-permute-done((bf16[896,384]{1,0:T(8,128)(2,1)S(1)}, bf16[896,384]{1,0:T(8,128)(2,1)S(1)}, u32[]{:S(2)}, u32[]{:S(2)}) %collective-permute-start.5) | collective-permute-done | bytes 688160 | tf_op jit(solution)/shard_map/ppermute | solution.py:739
  42.1 8.0 %collective-permute-done.8 = bf16[4,208,384]{2,1,0:T(8,128)(2,1)S(1)} collective-permute-done((bf16[4,208,384]{2,1,0:T(8,128)(2,1)S(1)}, bf16[4,208,384]{2,1,0:T(8,128)(2,1)S(1)}, u32[]{:S(2)}, u32[]{:S(2)}) %collective-permute-start.8) | collective-permute-done | bytes 639008 | tf_op jit(solution)/shard_map/ppermute | solution.py:739
  51.4 2.8 %collective-permute-start.11 = (bf16[1,96,768]{2,1,0:T(8,128)(2,1)S(1)}, bf16[1,96,768]{2,1,0:T(8,128)(2,1)S(1)}, u32[]{:S(2)}, u32[]{:S(2)}) collective-permute-start(bf16[1,96,768]{2,1,0:T(8,128)(2,1)S(1)} %bitcast.101), channel_id=1, source_target_pairs={{0,4},{2,6},{4,0},{6,2},{1,5},{3,7},{5,1},{7,3},{8,12},{10,14},{12... | collective-permute-start | bytes 442376 | tf_op jit(solution)/shard_map/ppermute | solution.py:739
  63.9 2.7 %shard_map.323.w_ref = bf16[2304,768]{1,0:T(8,128)(2,1)S(1)} custom-call(s32[4]{0:T(128)S(1)} %pad_add_fusion.at_ref.x_ref, s32[3,48]{1,0:T(4,128)S(1)} %copy-done.22, bf16[8,208,384]{2,1,0:T(8,128)(2,1)S(1)} %pad_maximum_fusion.refs_0_, bf16[8,208,384]{2,1,0:T(8,128)(2,1)S(1)} %collective-permute-done.13.refs_1_, ...), custom_call_target="tpu_custom_call" | custom-call | flops 5400000 | bytes 1024 | tf_op jit(solution)/shard_map/pallas_call | solution.py:1007
  66.6 4.1 %shard_map.324.triple_ref = bf16[896,2304]{1,0:T(8,128)(2,1)S(1)} custom-call(bf16[896,768]{1,0:T(8,128)(2,1)S(1)} %shard_map.322.hidden_ref, bf16[2304,768]{1,0:T(8,128)(2,1)S(1)} %shard_map.323.w_ref, f32[1,2304]{1,0:T(1,128)S(1)} %get-tuple-element.178.bias_ref), custom_call_target="tpu_custom_call" | custom-call | flops 7020000256 | bytes 1024 | tf_op jit(solution)/shard_map/pallas_call | solution.py:252
  70.8 3.7 %collective-permute-done.17 = bf16[2,96,768]{2,1,0:T(8,128)(2,1)S(1)} collective-permute-done((bf16[2,96,768]{2,1,0:T(8,128)(2,1)S(1)}, bf16[2,96,768]{2,1,0:T(8,128)(2,1)S(1)}, u32[]{:S(2)}, u32[]{:S(2)}) %collective-permute-start.17) | collective-permute-done | bytes 294944 | tf_op jit(solution)/shard_map/ppermute | solution.py:739
  78.3 6.0 %shard_map.325 = (bf16[896,768]{1,0:T(8,128)(2,1)S(1)}, f32[8,12,112,112]{3,2,1,0:T(8,128)}) custom-call(bf16[896,2304]{1,0:T(8,128)(2,1)S(1)} %shard_map.324.triple_ref), custom_call_target="tpu_custom_call" | custom-call | flops 108000002048 | bytes 1024 | tf_op jit(solution)/shard_map/pallas_call | solution.py:308
  84.4 6.6 %collective-permute-done.19 = bf16[4,96,768]{2,1,0:T(8,128)(2,1)S(1)} collective-permute-done((bf16[4,96,768]{2,1,0:T(8,128)(2,1)S(1)}, bf16[4,96,768]{2,1,0:T(8,128)(2,1)S(1)}, u32[]{:S(2)}, u32[]{:S(2)}) %collective-permute-start.19) | collective-permute-done | bytes 589856 | tf_op jit(solution)/shard_map/ppermute | solution.py:739
  94.9 2.8 %shard_map.327 = (f32[896,768]{1,0:T(8,128)S(1)}, bf16[896,768]{1,0:T(8,128)(2,1)S(1)}) custom-call(bf16[896,768]{1,0:T(8,128)(2,1)S(1)} %get-tuple-element.189.mixed_ref, bf16[768,768]{1,0:T(8,128)(2,1)S(1)} %shard_map.326.w_ref, bf16[896,768]{1,0:T(8,128)(2,1)S(1)} %maximum_select_fusion.rows_ref, f32[8,768]{1,0:T(8,128)S(1)} %get-tuple-element.256.vec_ref.x_ref), custom_call_target="tpu_custom_call" | custom-call | flops 8640000000 | bytes 1024 | tf_op jit(solution)/shard_map/pallas_call | solution.py:338
  100.8 10.1 %shard_map.329 = (bf16[896,3072]{1,0:T(8,128)(2,1)}, f32[896,3072]{1,0:T(8,128)}) custom-call(bf16[896,768]{1,0:T(8,128)(2,1)S(1)} %get-tuple-element.190.hidden_ref, bf16[768,3072]{1,0:T(8,128)(2,1)S(1)} %shard_map.328.w_ref, f32[1,3072]{1,0:T(1,128)S(1)} %get-tuple-element.199.bias_ref), custom_call_target="tpu_custom_call" | custom-call | flops 5400000 | bytes 1024 | tf_op jit(solution)/shard_map/pallas_call | solution.py:361
  110.9 9.0 %shard_map.330 = (bf16[4,192,768]{2,1,0:T(8,128)(2,1)}, bf16[4,192,768]{2,1,0:T(8,128)(2,1)}, bf16[4,192,768]{2,1,0:T(8,128)(2,1)S(1)}, bf16[4,192,768]{2,1,0:T(8,128)(2,1)S(1)}) custom-call(s32[4]{0:T(128)S(1)} %pad_add_fusion.at_ref.x_ref, bf16[896,768]{1,0:T(8,128)(2,1)S(1)} %get-tuple-element.290.left_ref.cot_ref, ...), custom_call_target="tpu_custom_call" | custom-call | flops 5400000 | bytes 1024 | tf_op jit(solution)/shard_map/pallas_call | solution.py:485
  130.9 14.4 %shard_map.332 = (bf16[896,3072]{1,0:T(8,128)(2,1)}, bf16[2,4,96,768]{3,2,1,0:T(8,128)(2,1)}, bf16[2,4,96,768]{3,2,1,0:T(8,128)(2,1)}, bf16[2,4,96,768]{3,2,1,0:...) custom-call(s32[4]{0:T(128)S(1)} %pad_add_fusion.at_ref.x_ref, ...), custom_call_target="tpu_custom_call" | custom-call | flops 108000002048 | bytes 1024 | tf_op jit(solution)/shard_map/pallas_call | solution.py:528
  145.3 6.6 %shard_map.333 = bf16[896,768]{1,0:T(8,128)(2,1)S(1)} custom-call(bf16[896,3072]{1,0:T(8,128)(2,1)} %get-tuple-element.215.right_ref.active_ref, bf16[768,3072]{1,0:T(8,128)(2,1)S(1)} %shard_map.331.w_ref, f32[8,768]{1,0:T(8,128)S(1)} %get-tuple-element.256.vec_ref.x_ref, f32[896,768]{1,0:T(8,128)S(1)} %get-tuple-element.216.middle_ref), custom_call_target="tpu_custom_call" | custom-call | flops 5400000 | bytes 1024 | tf_op jit(solution)/shard_map/pallas_call | solution.py:384
  162.0 6.4 %shard_map.334 = (f32[896,768]{1,0:T(8,128)S(1)}, bf16[896,768]{1,0:T(8,128)(2,1)S(1)}, f32[1,768]{1,0:T(1,128)S(1)}, f32[1,768]{1,0:T(1,128)S(1)}, f32[1,768]{1,0:T(1,128)S(1)}) custom-call(bf16[896,3072]{1,0:T(8,128)(2,1)S(1)} %copy-done.30, bf16[768,3072]{1,0:T(8,128)(2,1)S(1)} %bitcast.88, f32[896,768]{1,0:T(8,128)S(1)} %copy-done.10, ...), custom_call_target="tpu_custom_call" | custom-call | flops 108000002048 | bytes 1024 | tf_op jit(solution)/shard_map/pallas_call | solution.py:591
  168.4 2.5 shard_map.335
  176.6 12.0 %shard_map.336.grad_ref = bf16[896,2304]{1,0:T(8,128)(2,1)S(1)} custom-call(bf16[896,2304]{1,0:T(8,128)(2,1)S(1)} %copy-done.8, f32[8,12,112,112]{3,2,1,0:T(8,128)} %get-tuple-element.217.prob_ref, bf16[896,768]{1,0:T(8,128)(2,1)S(1)} %get-tuple-element.232.grad_ref), custom_call_target="tpu_custom_call" | custom-call | flops 5400000 | bytes 1024 | tf_op jit(solution)/shard_map/pallas_call | solution.py:657
  188.6 5.1 %shard_map.337 = (f32[896,768]{1,0:T(8,128)S(1)}, f32[1,768]{1,0:T(1,128)S(1)}, f32[1,768]{1,0:T(1,128)S(1)}) custom-call(bf16[896,2304]{1,0:T(8,128)(2,1)S(1)} %shard_map.336.grad_ref, bf16[2304,768]{1,0:T(8,128)(2,1)S(1)} %copy-done.2, bf16[896,768]{1,0:T(8,128)(2,1)S(1)} %copy-done.4, f32[896,768]{1,0:T(8,128)S(1)} %get-tuple-element.233.middle_ref, ...), custom_call_target="tpu_custom_call" | custom-call | flops 5400000 | bytes 1024 | tf_op jit(solution)/shard_map/pallas_call | solution.py:716
  196.8 4.8 %shard_map.338 = (bf16[2304,768]{1,0:T(8,128)(2,1)S(1)}, f32[1,2304]{1,0:T(1,128)S(1)}) custom-call(bf16[896,2304]{1,0:T(8,128)(2,1)S(1)} %shard_map.336.grad_ref, bf16[896,768]{1,0:T(8,128)(2,1)S(1)} %copy-done.29), custom_call_target="tpu_custom_call" | custom-call | flops 108000002048 | bytes 1024 | tf_op jit(solution)/shard_map/pallas_call | solution.py:689
  205.2 2.7 %shard_map.339 = (bf16[16,144,384]{2,1,0:T(8,128)(2,1)}, bf16[16,144,384]{2,1,0:T(8,128)(2,1)S(1)}) custom-call(s32[4]{0:T(128)S(1)} %copy-done.18, s32[3,32]{1,0:T(4,128)S(1)} %copy-done.19, bf16[2304,768]{1,0:T(8,128)(2,1)S(1)} %get-tuple-element.241.refs_0_), custom_call_target="tpu_custom_call" | custom-call | flops 5400000 | bytes 1024 | tf_op jit(solution)/shard_map/pallas_call | solution.py:1007
  208.0 3.0 %collective-permute-done.40 = bf16[4,96,768]{2,1,0:T(8,128)(2,1)S(1)} collective-permute-done((bf16[4,96,768]{2,1,0:T(8,128)(2,1)S(1)}, bf16[4,96,768]{2,1,0:T(8,128)(2,1)S(1)}, u32[]{:S(2)}, u32[]{:S(2)}) %collective-permute-start.40) | collective-permute-done | bytes 589856 | tf_op jit(solution)/shard_map/ppermute | solution.py:739
  217.9 3.4 %collective-permute-start.45 = (bf16[1,96,768]{2,1,0:T(8,128)(2,1)S(1)}, bf16[1,96,768]{2,1,0:T(8,128)(2,1)S(1)}, u32[]{:S(2)}, u32[]{:S(2)}) collective-permute-start(bf16[1,96,768]{2,1,0:T(8,128)(2,1)S(1)} %fusion.10), channel_id=1, source_target_pairs={{0,4},{2,6},{4,0},{6,2},{1,5},{3,7},{5,1},{7,3},{8,12},{10,14},{12... | collective-permute-start | bytes 442376 | tf_op jit(solution)/shard_map/ppermute | solution.py:739
  221.3 4.4 %collective-permute-done.42.got_ref = bf16[896,384]{1,0:T(8,128)(2,1)S(1)} collective-permute-done((bf16[896,384]{1,0:T(8,128)(2,1)S(1)}, bf16[896,384]{1,0:T(8,128)(2,1)S(1)}, u32[]{:S(2)}, u32[]{:S(2)}) %collective-permute-start.42) | collective-permute-done | bytes 688160 | tf_op jit(solution)/shard_map/ppermute | solution.py:739
  225.7 6.8 %shard_map.343 = f32[18816,128]{1,0:T(8,128)} custom-call(s32[4]{0:T(128)S(1)} %copy-done.18, f32[896,384]{1,0:T(8,128)S(1)} %constant_dynamic-slice_fusion.keep_ref, bf16[896,384]{1,0:T(8,128)(2,1)S(1)} %collective-permute-done.42.got_ref, s32[16,112,1]{2,1,0:T(8,128)S(1)} %copy-done.16), custom_call_target="tpu_custom_call" | custom-call | flops 108000002048 | bytes 1024 | tf_op jit(solution)/shard_map/pallas_call | solution.py:171
  235.1 3.0 %collective-permute-start.53 = (bf16[112,384]{1,0:T(8,128)(2,1)S(1)}, bf16[112,384]{1,0:T(8,128)(2,1)S(1)}, u32[]{:S(2)}, u32[]{:S(2)}) collective-permute-start(bf16[112,384]{1,0:T(8,128)(2,1)S(1)} %get-tuple-element.314), channel_id=1, source_target_pairs={{0,6},{2,4},{4,2},{6,0},{1,7},{3,5},{5,3},{7,1},{8,14},{10,12},{12... | collective-permute-start | bytes 258056 | tf_op jit(solution)/shard_map/ppermute | solution.py:739
  241.9 3.6 %shard_map.344 = bf16[1,602112]{1,0:T(2,128)(2,1)} custom-call(s32[4]{0:T(128)S(1)} %copy-done.18, bf16[896,384]{1,0:T(8,128)(2,1)S(1)} %get-tuple-element.265.keep_ref, bf16[896,384]{1,0:T(8,128)(2,1)S(1)} %copy-done.27), custom_call_target="tpu_custom_call" | custom-call | flops 108000002048 | bytes 1024 | tf_op jit(solution)/shard_map/pallas_call | solution.py:199
  246.2 3.0 %collective-permute-start.50 = (bf16[144,384]{1,0:T(8,128)(2,1)S(1)}, bf16[144,384]{1,0:T(8,128)(2,1)S(1)}, u32[]{:S(2)}, u32[]{:S(2)}) collective-permute-start(bf16[144,384]{1,0:T(8,128)(2,1)S(1)} %get-tuple-element.311), channel_id=1, source_target_pairs={{0,6},{2,4},{4,2},{6,0},{1,7},{3,5},{5,3},{7,1},{8,14},{10,12},{12... | collective-permute-start | bytes 331784 | tf_op jit(solution)/shard_map/ppermute | solution.py:739
  (287 shorter events, 100.5 us)
Async XLA Ops:
  2.7 8.9 %collective-permute-start.3 = (bf16[1,96,384]{2,1,0:T(8,128)(2,1)S(1)}, bf16[1,96,384]{2,1,0:T(8,128)(2,1)S(1)}, u32[]{:S(2)}, u32[]{:S(2)}) collective-permute-start(bf16[1,96,384]{2,1,0:T(8,128)(2,1)S(1)} %bitcast.104), channel_id=1, source_target_pairs={{0,6},{2,4},{4,2},{6,0},{1,7},{3,5},{5,3},{7,1},{8,14},{10,12},{12... | collective-permute-start | bytes 221192 | tf_op jit(solution)/shard_map/ppermute | solution.py:739
  14.1 15.5 %collective-permute-start.7 = (bf16[4,96,384]{2,1,0:T(8,128)(2,1)S(1)}, bf16[4,96,384]{2,1,0:T(8,128)(2,1)S(1)}, u32[]{:S(2)}, u32[]{:S(2)}) collective-permute-start(bf16[4,96,384]{2,1,0:T(8,128)(2,1)S(1)} %pad_maximum_fusion.7), channel_id=1, source_target_pairs={{0,1},{1,0},{2,3},{3,2},{4,5},{5,4},{6,7},{7,6},{8,9},{9,8},{10,11... | collective-permute-start | bytes 884744 | tf_op jit(solution)/shard_map/ppermute | solution.py:739
  17.6 16.6 %collective-permute-start.6 = (bf16[2,208,384]{2,1,0:T(8,128)(2,1)S(1)}, bf16[2,208,384]{2,1,0:T(8,128)(2,1)S(1)}, u32[]{:S(2)}, u32[]{:S(2)}) collective-permute-start(bf16[2,208,384]{2,1,0:T(8,128)(2,1)S(1)} %pad_maximum_fusion.6), channel_id=1, source_target_pairs={{0,4},{2,6},{4,0},{6,2},{1,5},{3,7},{5,1},{7,3},{8,12},{10,14},{12... | collective-permute-start | bytes 958472 | tf_op jit(solution)/shard_map/ppermute | solution.py:739
  27.9 13.7 %collective-permute-start.5 = (bf16[896,384]{1,0:T(8,128)(2,1)S(1)}, bf16[896,384]{1,0:T(8,128)(2,1)S(1)}, u32[]{:S(2)}, u32[]{:S(2)}) collective-permute-start(bf16[896,384]{1,0:T(8,128)(2,1)S(1)} %get-tuple-element.310), channel_id=1, source_target_pairs={{0,1},{1,0},{2,3},{3,2},{4,5},{5,4},{6,7},{7,6},{8,9},{9,8},{10,11... | collective-permute-start | bytes 2064392 | tf_op jit(solution)/shard_map/ppermute | solution.py:739
  29.6 12.5 %collective-permute-start.9 = (bf16[8,96,384]{2,1,0:T(8,128)(2,1)S(1)}, bf16[8,96,384]{2,1,0:T(8,128)(2,1)S(1)}, u32[]{:S(2)}, u32[]{:S(2)}) collective-permute-start(bf16[8,96,384]{2,1,0:T(8,128)(2,1)S(1)} %constant_dynamic-update-slice_fusion), channel_id=1, source_target_pairs={{0,16},{8,24},{16,0},{24,8},{1,17},{9,25},{17,1},{25,9},{2,18},{10... | collective-permute-start | bytes 1769480 | tf_op jit(solution)/shard_map/ppermute | solution.py:739
  34.3 15.8 %collective-permute-start.8 = (bf16[4,208,384]{2,1,0:T(8,128)(2,1)S(1)}, bf16[4,208,384]{2,1,0:T(8,128)(2,1)S(1)}, u32[]{:S(2)}, u32[]{:S(2)}) collective-permute-start(bf16[4,208,384]{2,1,0:T(8,128)(2,1)S(1)} %pad_maximum_fusion.2), channel_id=1, source_target_pairs={{0,2},{2,0},{4,6},{6,4},{1,3},{3,1},{5,7},{7,5},{8,10},{10,8},{12,... | collective-permute-start | bytes 1916936 | tf_op jit(solution)/shard_map/ppermute | solution.py:739
  51.2 19.6 %collective-permute-start.18 = (bf16[896,384]{1,0:T(8,128)(2,1)S(1)}, bf16[896,384]{1,0:T(8,128)(2,1)S(1)}, u32[]{:S(2)}, u32[]{:S(2)}) collective-permute-start(bf16[896,384]{1,0:T(8,128)(2,1)S(1)} %get-tuple-element.165), channel_id=1, source_target_pairs={{0,1},{1,0},{2,3},{3,2},{4,5},{5,4},{6,7},{7,6},{8,9},{9,8},{10,11... | collective-permute-start | bytes 2064392 | tf_op jit(solution)/shard_map/ppermute | solution.py:739
  60.3 14.1 %collective-permute-start.17 = (bf16[2,96,768]{2,1,0:T(8,128)(2,1)S(1)}, bf16[2,96,768]{2,1,0:T(8,128)(2,1)S(1)}, u32[]{:S(2)}, u32[]{:S(2)}) collective-permute-start(bf16[2,96,768]{2,1,0:T(8,128)(2,1)S(1)} %copy-done.41), channel_id=1, source_target_pairs={{0,4},{2,6},{4,0},{6,2},{1,5},{3,7},{5,1},{7,3},{8,12},{10,14},{12... | collective-permute-start | bytes 884744 | tf_op jit(solution)/shard_map/ppermute | solution.py:739
  60.8 13.7 %collective-permute-start.16 = (bf16[4,48,768]{2,1,0:T(8,128)(2,1)S(1)}, bf16[4,48,768]{2,1,0:T(8,128)(2,1)S(1)}, u32[]{:S(2)}, u32[]{:S(2)}) collective-permute-start(bf16[4,48,768]{2,1,0:T(8,128)(2,1)S(1)} %pad_maximum_fusion.10), channel_id=1, source_target_pairs={{0,1},{1,0},{2,3},{3,2},{4,5},{5,4},{6,7},{7,6},{8,9},{9,8},{10,11... | collective-permute-start | bytes 884744 | tf_op jit(solution)/shard_map/ppermute | solution.py:739
  61.8 12.8 %collective-permute-start.15 = (bf16[2,96,768]{2,1,0:T(8,128)(2,1)S(1)}, bf16[2,96,768]{2,1,0:T(8,128)(2,1)S(1)}, u32[]{:S(2)}, u32[]{:S(2)}) collective-permute-start(bf16[2,96,768]{2,1,0:T(8,128)(2,1)S(1)} %pad_maximum_fusion.9), channel_id=1, source_target_pairs={{0,2},{2,0},{4,6},{6,4},{1,3},{3,1},{5,7},{7,5},{8,10},{10,8},{12,... | collective-permute-start | bytes 884744 | tf_op jit(solution)/shard_map/ppermute | solution.py:739
  75.8 18.0 %collective-permute-start.20 = (bf16[4,96,768]{2,1,0:T(8,128)(2,1)S(1)}, bf16[4,96,768]{2,1,0:T(8,128)(2,1)S(1)}, u32[]{:S(2)}, u32[]{:S(2)}) collective-permute-start(bf16[4,96,768]{2,1,0:T(8,128)(2,1)S(1)} %get-tuple-element.191.refs_0_), channel_id=1, source_target_pairs={{0,1},{1,0},{2,3},{3,2},{4,5},{5,4},{6,7},{7,6},{8,9},{9,8},{10,11... | collective-permute-start | bytes 1769480 | tf_op jit(solution)/shard_map/ppermute | solution.py:739
  76.8 14.2 %collective-permute-start.19 = (bf16[4,96,768]{2,1,0:T(8,128)(2,1)S(1)}, bf16[4,96,768]{2,1,0:T(8,128)(2,1)S(1)}, u32[]{:S(2)}, u32[]{:S(2)}) collective-permute-start(bf16[4,96,768]{2,1,0:T(8,128)(2,1)S(1)} %get-tuple-element.322), channel_id=1, source_target_pairs={{0,2},{2,0},{4,6},{6,4},{1,3},{3,1},{5,7},{7,5},{8,10},{10,8},{12,... | collective-permute-start | bytes 1769480 | tf_op jit(solution)/shard_map/ppermute | solution.py:739
  76.8 17.0 %collective-permute-start.21 = (bf16[8,48,768]{2,1,0:T(8,128)(2,1)S(1)}, bf16[8,48,768]{2,1,0:T(8,128)(2,1)S(1)}, u32[]{:S(2)}, u32[]{:S(2)}) collective-permute-start(bf16[8,48,768]{2,1,0:T(8,128)(2,1)S(1)} %pad_maximum_fusion.4.refs_4_), channel_id=1, source_target_pairs={{0,16},{8,24},{16,0},{24,8},{1,17},{9,25},{17,1},{25,9},{2,18},{10... | collective-permute-start | bytes 1769480 | tf_op jit(solution)/shard_map/ppermute | solution.py:739
  91.1 28.8 %collective-permute-start.26 = (bf16[8,96,768]{2,1,0:T(8,128)(2,1)S(1)}, bf16[8,96,768]{2,1,0:T(8,128)(2,1)S(1)}, u32[]{:S(2)}, u32[]{:S(2)}) collective-permute-start(bf16[8,96,768]{2,1,0:T(8,128)(2,1)S(1)} %pad_maximum_fusion.1.refs_0_), channel_id=1, source_target_pairs={{0,16},{8,24},{16,0},{24,8},{1,17},{9,25},{17,1},{25,9},{2,18},{10... | collective-permute-start | bytes 3538952 | tf_op jit(solution)/shard_map/ppermute | solution.py:739
  129.2 28.3 %collective-permute-start.31 = (bf16[4,192,768]{2,1,0:T(8,128)(2,1)}, bf16[4,192,768]{2,1,0:T(8,128)(2,1)}, u32[]{:S(2)}, u32[]{:S(2)}) collective-permute-start(bf16[4,192,768]{2,1,0:T(8,128)(2,1)} %add_convert_fusion), channel_id=1, source_target_pairs={{0,1},{1,0},{2,3},{3,2},{4,5},{5,4},{6,7},{7,6},{8,9},{9,8},{10,11... | collective-permute-start | bytes 3538952 | tf_op jit(solution)/shard_map/ppermute | solution.py:739
  159.3 14.6 %collective-permute-start.34 = (bf16[2,192,768]{2,1,0:T(8,128)(2,1)S(1)}, bf16[2,192,768]{2,1,0:T(8,128)(2,1)S(1)}, u32[]{:S(2)}, u32[]{:S(2)}) collective-permute-start(bf16[2,192,768]{2,1,0:T(8,128)(2,1)S(1)} %get-tuple-element.298), channel_id=1, source_target_pairs={{0,2},{2,0},{4,6},{6,4},{1,3},{3,1},{5,7},{7,5},{8,10},{10,8},{12,... | collective-permute-start | bytes 1769480 | tf_op jit(solution)/shard_map/ppermute | solution.py:739
  161.4 34.1 %collective-permute-start.36 = (bf16[8,96,768]{2,1,0:T(8,128)(2,1)S(1)}, bf16[8,96,768]{2,1,0:T(8,128)(2,1)S(1)}, u32[]{:S(2)}, u32[]{:S(2)}) collective-permute-start(bf16[8,96,768]{2,1,0:T(8,128)(2,1)S(1)} %fusion), channel_id=1, source_target_pairs={{0,16},{8,24},{16,0},{24,8},{1,17},{9,25},{17,1},{25,9},{2,18},{10... | collective-permute-start | bytes 3538952 | tf_op jit(solution)/shard_map/ppermute | solution.py:739
  170.9 22.9 %collective-permute-start.37 = (bf16[896,384]{1,0:T(8,128)(2,1)S(1)}, bf16[896,384]{1,0:T(8,128)(2,1)S(1)}, u32[]{:S(2)}, u32[]{:S(2)}) collective-permute-start(bf16[896,384]{1,0:T(8,128)(2,1)S(1)} %get-tuple-element.231), channel_id=1, source_target_pairs={{0,1},{1,0},{2,3},{3,2},{4,5},{5,4},{6,7},{7,6},{8,9},{9,8},{10,11... | collective-permute-start | bytes 2064392 | tf_op jit(solution)/shard_map/ppermute | solution.py:739
  173.9 20.0 %collective-permute-start.35 = (bf16[1,192,768]{2,1,0:T(8,128)(2,1)S(1)}, bf16[1,192,768]{2,1,0:T(8,128)(2,1)S(1)}, u32[]{:S(2)}, u32[]{:S(2)}) collective-permute-start(bf16[1,192,768]{2,1,0:T(8,128)(2,1)S(1)} %fusion.8), channel_id=1, source_target_pairs={{0,4},{2,6},{4,0},{6,2},{1,5},{3,7},{5,1},{7,3},{8,12},{10,14},{12... | collective-permute-start | bytes 884744 | tf_op jit(solution)/shard_map/ppermute | solution.py:739
  194.0 9.5 %collective-permute-start.39 = (bf16[192,768]{1,0:T(8,128)(2,1)S(1)}, bf16[192,768]{1,0:T(8,128)(2,1)S(1)}, u32[]{:S(2)}, u32[]{:S(2)}) collective-permute-start(bf16[192,768]{1,0:T(8,128)(2,1)S(1)} %get-tuple-element.291), channel_id=1, source_target_pairs={{0,16},{8,24},{16,0},{24,8},{1,17},{9,25},{17,1},{25,9},{2,18},{10... | collective-permute-start | bytes 884744 | tf_op jit(solution)/shard_map/ppermute | solution.py:739
  195.8 15.2 %collective-permute-start.40 = (bf16[4,96,768]{2,1,0:T(8,128)(2,1)S(1)}, bf16[4,96,768]{2,1,0:T(8,128)(2,1)S(1)}, u32[]{:S(2)}, u32[]{:S(2)}) collective-permute-start(bf16[4,96,768]{2,1,0:T(8,128)(2,1)S(1)} %get-tuple-element.296), channel_id=1, source_target_pairs={{0,1},{1,0},{2,3},{3,2},{4,5},{5,4},{6,7},{7,6},{8,9},{9,8},{10,11... | collective-permute-start | bytes 1769480 | tf_op jit(solution)/shard_map/ppermute | solution.py:739
  203.4 12.8 %collective-permute-start.44 = (bf16[8,112,384]{2,1,0:T(8,128)(2,1)S(1)}, bf16[8,112,384]{2,1,0:T(8,128)(2,1)S(1)}, u32[]{:S(2)}, u32[]{:S(2)}) collective-permute-start(bf16[8,112,384]{2,1,0:T(8,128)(2,1)S(1)} %get-tuple-element.252), channel_id=1, source_target_pairs={{0,8},{8,0},{16,24},{24,16},{1,9},{9,1},{17,25},{25,17},{2,10},{10... | collective-permute-start | bytes 2064392 | tf_op jit(solution)/shard_map/ppermute | solution.py:739
  203.6 9.0 %collective-permute-start.61 = (f32[192,768]{1,0:T(8,128)S(1)}, f32[192,768]{1,0:T(8,128)S(1)}, u32[]{:S(2)}, u32[]{:S(2)}) collective-permute-start(f32[192,768]{1,0:T(8,128)S(1)} %convert_add_fusion.5), channel_id=1, source_target_pairs={{0,8},{8,0},{16,24},{24,16},{1,9},{9,1},{17,25},{25,17},{2,10},{10... | collective-permute-start | bytes 1769480 | tf_op jit(solution)/shard_map/ppermute | solution.py:739
  204.1 21.6 %collective-permute-start.42 = (bf16[896,384]{1,0:T(8,128)(2,1)S(1)}, bf16[896,384]{1,0:T(8,128)(2,1)S(1)}, u32[]{:S(2)}, u32[]{:S(2)}) collective-permute-start(bf16[896,384]{1,0:T(8,128)(2,1)S(1)} %constant_dynamic-slice_fusion.1), channel_id=1, source_target_pairs={{0,1},{1,0},{2,3},{3,2},{4,5},{5,4},{6,7},{7,6},{8,9},{9,8},{10,11... | collective-permute-start | bytes 2064392 | tf_op jit(solution)/shard_map/ppermute | solution.py:739
  214.9 19.0 %collective-permute-start.41 = (bf16[8,144,384]{2,1,0:T(8,128)(2,1)S(1)}, bf16[8,144,384]{2,1,0:T(8,128)(2,1)S(1)}, u32[]{:S(2)}, u32[]{:S(2)}) collective-permute-start(bf16[8,144,384]{2,1,0:T(8,128)(2,1)S(1)} %get-tuple-element.293), channel_id=1, source_target_pairs={{0,16},{8,24},{16,0},{24,8},{1,17},{9,25},{17,1},{25,9},{2,18},{10... | collective-permute-start | bytes 2654216 | tf_op jit(solution)/shard_map/ppermute | solution.py:739
  216.4 18.7 %collective-permute-start.46 = (bf16[4,112,384]{2,1,0:T(8,128)(2,1)S(1)}, bf16[4,112,384]{2,1,0:T(8,128)(2,1)S(1)}, u32[]{:S(2)}, u32[]{:S(2)}) collective-permute-start(bf16[4,112,384]{2,1,0:T(8,128)(2,1)S(1)} %get-tuple-element.304), channel_id=1, source_target_pairs={{0,1},{1,0},{2,3},{3,2},{4,5},{5,4},{6,7},{7,6},{8,9},{9,8},{10,11... | collective-permute-start | bytes 1032200 | tf_op jit(solution)/shard_map/ppermute | solution.py:739
  217.9 21.6 %collective-permute-start.45 = (bf16[1,96,768]{2,1,0:T(8,128)(2,1)S(1)}, bf16[1,96,768]{2,1,0:T(8,128)(2,1)S(1)}, u32[]{:S(2)}, u32[]{:S(2)}) collective-permute-start(bf16[1,96,768]{2,1,0:T(8,128)(2,1)S(1)} %fusion.10), channel_id=1, source_target_pairs={{0,4},{2,6},{4,0},{6,2},{1,5},{3,7},{5,1},{7,3},{8,12},{10,14},{12... | collective-permute-start | bytes 442376 | tf_op jit(solution)/shard_map/ppermute | solution.py:739
  234.0 12.1 %collective-permute-start.47 = (bf16[4,144,384]{2,1,0:T(8,128)(2,1)S(1)}, bf16[4,144,384]{2,1,0:T(8,128)(2,1)S(1)}, u32[]{:S(2)}, u32[]{:S(2)}) collective-permute-start(bf16[4,144,384]{2,1,0:T(8,128)(2,1)S(1)} %get-tuple-element.300), channel_id=1, source_target_pairs={{0,1},{1,0},{2,3},{3,2},{4,5},{5,4},{6,7},{7,6},{8,9},{9,8},{10,11... | collective-permute-start | bytes 1327112 | tf_op jit(solution)/shard_map/ppermute | solution.py:739
  235.1 10.4 %collective-permute-start.53 = (bf16[112,384]{1,0:T(8,128)(2,1)S(1)}, bf16[112,384]{1,0:T(8,128)(2,1)S(1)}, u32[]{:S(2)}, u32[]{:S(2)}) collective-permute-start(bf16[112,384]{1,0:T(8,128)(2,1)S(1)} %get-tuple-element.314), channel_id=1, source_target_pairs={{0,6},{2,4},{4,2},{6,0},{1,7},{3,5},{5,3},{7,1},{8,14},{10,12},{12... | collective-permute-start | bytes 258056 | tf_op jit(solution)/shard_map/ppermute | solution.py:739
  240.4 10.9 %collective-permute-start.59 = (bf16[96,768]{1,0:T(8,128)(2,1)}, bf16[96,768]{1,0:T(8,128)(2,1)}, u32[]{:S(2)}, u32[]{:S(2)}) collective-permute-start(bf16[96,768]{1,0:T(8,128)(2,1)} %get-tuple-element.283), channel_id=1, source_target_pairs={{0,16},{8,24},{16,0},{24,8},{1,17},{9,25},{17,1},{25,9},{2,18},{10... | collective-permute-start | bytes 442376 | tf_op jit(solution)/shard_map/ppermute | solution.py:739
  245.5 11.7 %collective-permute-start.57 = (bf16[112,384]{1,0:T(8,128)(2,1)S(1)}, bf16[112,384]{1,0:T(8,128)(2,1)S(1)}, u32[]{:S(2)}, u32[]{:S(2)}) collective-permute-start(bf16[112,384]{1,0:T(8,128)(2,1)S(1)} %get-tuple-element.285), channel_id=1, source_target_pairs={{0,16},{8,24},{16,0},{24,8},{1,17},{9,25},{17,1},{25,9},{2,18},{10... | collective-permute-start | bytes 258056 | tf_op jit(solution)/shard_map/ppermute | solution.py:739
  252.3 12.7 %collective-permute-start.60 = (f32[2,96,768]{2,1,0:T(8,128)S(1)}, f32[2,96,768]{2,1,0:T(8,128)S(1)}, u32[]{:S(2)}, u32[]{:S(2)}) collective-permute-start(f32[2,96,768]{2,1,0:T(8,128)S(1)} %maximum_select_fusion.6), channel_id=1, source_target_pairs={{0,8},{8,0},{16,24},{24,16},{1,9},{9,1},{17,25},{25,17},{2,10},{10... | collective-permute-start | bytes 1769480 | tf_op jit(solution)/shard_map/ppermute | solution.py:739
  (76 other events, 700.0 us)
